TPU v7x, 32 devices: a whole 2x2x4 slice. The times are simulated.
32 devices in a mesh: ctx: 16 (over z, y, core), fsdp: 2 (over x).
Axes of the slice: x: 2, y: 2, z: 4, core: 2. Of those that a mesh axis runs over, the one named last changes fastest.
Arguments:
- tokens: bfloat16 [2, 2048, 768], P('fsdp', 'ctx'), may hold values from -6 to 6
- segments: int32 [2, 2048], P('fsdp', 'ctx'), may hold values from 0 to 7, as said below
- routes: int32 [4096, 2], P(('ctx', 'fsdp')), may hold values from 0 to 7, all different within a row; in each aligned block of 128 rows (0 to 127, 128 to 255, ...) at most 40 rows name the same one
- bucket_table: int32 [2048], replicated, may hold values from 0 to 31, as said below
- attn_gain: bfloat16 [768], P('fsdp'), may hold values from 0.5 to 1.5
- qkv_weight: bfloat16 [768, 2304], P('fsdp'), may hold values from -0.21875 to 0.21875
- out_weight: bfloat16 [768, 768], P('fsdp'), may hold values from -1.25 to 1.25
- bias_table: bfloat16 [32, 12], P('fsdp'), may hold values from -4 to 4
- moe_gain: bfloat16 [768], P('fsdp'), may hold values from 0.5 to 1.5
- router_weight: bfloat16 [768, 8], P('fsdp'), may hold values from -0.15625 to 0.15625
- up_weight: bfloat16 [8, 768, 3072], P('fsdp'), may hold values from -0.21875 to 0.21875
- down_weight: bfloat16 [8, 768, 3072], P('fsdp'), may hold values from -0.21875 to 0.21875
- cotangent: bfloat16 [2, 2048, 768], P('fsdp', 'ctx'), may hold values from -6 to 6
Outputs:
- layer_out: bfloat16 [2, 2048, 768], P('fsdp', 'ctx')
- tokens_grad: bfloat16 [2, 2048, 768], P('fsdp', 'ctx')
- attn_gain_grad: float32 [768], P('fsdp')
- qkv_grad: float32 [768, 2304], P('fsdp', 'ctx')
- out_grad: float32 [768, 768], P('fsdp', 'ctx')
- bias_grad: float32 [32, 12], P('fsdp')
- moe_gain_grad: float32 [768], P('fsdp')
- router_grad: float32 [768, 8], P('fsdp')
- up_grad: float32 [8, 768, 3072], P('fsdp', 'ctx')
- down_grad: float32 [8, 768, 3072], P('fsdp', 'ctx')
Inputs may be any that keep to these rules, and one draw needn't show every extreme that they name: `segments`: in the order of positions p, document numbers never fall; they are 0 at position 0 and 7 at position 2047. `bucket_table`: never falls with the distance; 0 at distance 0 and 31 at distance 2048 - 1. `routes`: each row names 2 different experts; among the 128 rows of one device no expert is named more than 40 times.
All inputs are finite; a program needn't handle non-finite values.
Results may differ from a plain program's by a relative error of at most 0.02.
Values may be sent and summed in bfloat16 or wider, within the bound.
No kernel may reach another device: no remote copies, remote signals or barrier semaphores. Data moves between devices by JAX's collectives and lax.ppermute only.
A program may use at most 512 MiB of HBM per device.

v0:
```python
import jax
import jax.numpy as jnp
from jax import lax
from jax.sharding import PartitionSpec as P

HEADS = 12
HEAD_DIM = 64
EXPERTS = 8
TOP = 2
BUCKETS = 32
CAP = 40


LOG2E = 1.4426950408889634
EPS = 1e-06
LOWEST = -1e30
PRECISION_FULL = lax.Precision.HIGHEST


def normalize(values, weight):
    inv_rms = lax.rsqrt(jnp.mean(values * values, axis=-1, keepdims=True) + EPS)
    return values * inv_rms * weight


def place_of(row_index, tok_seq, blocks_ctx):
    half_len = tok_seq // 2
    owner_idx = row_index // tok_seq
    within = row_index % tok_seq
    late_place = (2 * blocks_ctx - 1 - owner_idx) * half_len + within - half_len
    return jnp.where(within < half_len, owner_idx * half_len + within, late_place)


def pair_terms(query_places, key_places, query_segs, key_segs, bucket_table, bias_table):
    distance = jnp.maximum(query_places[:, None] - key_places[None, :], 0)
    buckets = jnp.take(bucket_table, distance, axis=0)
    bucket_ids = jnp.arange(bias_table.shape[0], dtype=jnp.int32)
    one_hot = (buckets[:, :, None] == bucket_ids[None, None, :]).astype(jnp.bfloat16)
    bias_vals = jnp.einsum("qkb,bh->hqk", one_hot, bias_table, preferred_element_type=jnp.float32)
    allowed = (query_segs[:, :, None] == key_segs[:, None, :]) & (
        key_places[None, None, :] <= query_places[None, :, None]
    )
    return (one_hot, bias_vals, allowed)


def scaled_scores(queries, key_vecs, bias_vals, allowed):
    raw_scores = jnp.einsum(
        "sqhd,skhd->shqk", queries, key_vecs, preferred_element_type=jnp.float32
    ) * HEAD_DIM ** (-0.5)
    return jnp.where(allowed[:, None], (raw_scores + bias_vals[None]) * LOG2E, -jnp.inf)


def over_shards(step_fn, running, shard_group, tok_seq):
    shard_count = shard_group[0].shape[1] // tok_seq

    def visit_shard(shard_idx, current):
        shard_part = tuple(
            (
                lax.dynamic_slice_in_dim(member, shard_idx * tok_seq, tok_seq, 1)
                for member in shard_group
            )
        )
        return step_fn(current, shard_part, shard_idx * tok_seq)

    return lax.fori_loop(0, shard_count, visit_shard, running)


def gelu_grad(inputs, upstream):
    pullback = jax.vjp(lambda argument: jax.nn.gelu(argument, approximate=False), inputs)[1]
    return pullback(upstream)[0]


def per_device(
    tokens,
    segments,
    routes,
    bucket_table,
    attn_gain,
    qkv_weight,
    out_weight,
    bias_table,
    moe_gain,
    router_weight,
    up_weight,
    down_weight,
    cotangent,
):
    seq_dev, tok_seq, width = tokens.shape
    tok_dev = seq_dev * tok_seq
    blocks_ctx = lax.axis_size("ctx")
    my_rows = lax.axis_index("ctx") * tok_seq + jnp.arange(tok_seq, dtype=jnp.int32)
    my_places = place_of(my_rows, tok_seq, blocks_ctx)
    seg_local = segments.astype(jnp.bfloat16)
    head_scale = HEAD_DIM ** (-0.5)
    attn_scale, qkv_full, out_full, bias_full, moe_scale, router_full = (
        lax.all_gather(attn_gain, "fsdp", axis=0, tiled=True),
        lax.all_gather(qkv_weight, "fsdp", axis=0, tiled=True),
        lax.all_gather(out_weight, "fsdp", axis=0, tiled=True),
        lax.all_gather(bias_table, "fsdp", axis=0, tiled=True),
        lax.all_gather(moe_gain, "fsdp", axis=0, tiled=True),
        lax.all_gather(router_weight, "fsdp", axis=0, tiled=True),
    )
    attn_scale = attn_scale.astype(jnp.float32)
    moe_scale = moe_scale.astype(jnp.float32)
    token_vals = tokens.astype(jnp.float32)
    attention_input = normalize(token_vals, attn_scale).astype(jnp.bfloat16)
    projected_rows = jnp.einsum(
        "scd,de->sce", attention_input, qkv_full, preferred_element_type=jnp.float32
    ).astype(jnp.bfloat16)
    query_flat = projected_rows[..., :width]
    key_flat = projected_rows[..., width : 2 * width]
    value_flat = projected_rows[..., 2 * width :]
    queries = query_flat.reshape(seq_dev, tok_seq, HEADS, HEAD_DIM)
    key_vecs = key_flat.reshape(seq_dev, tok_seq, HEADS, HEAD_DIM)
    value_vecs = value_flat.reshape(seq_dev, tok_seq, HEADS, HEAD_DIM)

    def forward_step(current, shard_part, first_row):
        max_run, sum_run, acc_run = current
        piece_keys, piece_values, piece_segs = shard_part
        key_count = piece_keys.shape[1]
        key_places = place_of(
            first_row + jnp.arange(key_count, dtype=jnp.int32), tok_seq, blocks_ctx
        )
        unused_hot, bias_vals, allowed = pair_terms(
            my_places, key_places, seg_local, piece_segs, bucket_table, bias_full
        )
        scaled = scaled_scores(
            queries, piece_keys.reshape(seq_dev, key_count, HEADS, HEAD_DIM), bias_vals, allowed
        )
        new_max = jnp.maximum(max_run, jnp.ceil(jnp.max(scaled, axis=-1)))
        numerator = jnp.exp2(scaled - new_max[..., None])
        factor = jnp.exp2(max_run - new_max)
        sum_new = sum_run * factor + jnp.sum(numerator, axis=-1)
        update = jnp.einsum(
            "shqk,skhd->sqhd",
            numerator.astype(jnp.bfloat16),
            piece_values.reshape(seq_dev, key_count, HEADS, HEAD_DIM),
            preferred_element_type=jnp.float32,
        )
        acc_new = acc_run * jnp.transpose(factor, (0, 2, 1))[..., None] + update
        return (new_max, sum_new, acc_new)

    start_state = (
        jnp.full((seq_dev, HEADS, tok_seq), LOWEST, jnp.float32),
        jnp.zeros((seq_dev, HEADS, tok_seq), jnp.float32),
        jnp.zeros((seq_dev, tok_seq, HEADS, HEAD_DIM), jnp.float32),
    )
    row_max, row_sum, numer_acc = over_shards(
        forward_step,
        start_state,
        (
            lax.all_gather(key_flat, "ctx", axis=1, tiled=True),
            lax.all_gather(value_flat, "ctx", axis=1, tiled=True),
            lax.all_gather(seg_local, "ctx", axis=1, tiled=True),
        ),
        tok_seq,
    )
    sum_heads = jnp.transpose(row_sum, (0, 2, 1))[..., None]
    context_pre = numer_acc / sum_heads
    context_rows = context_pre.reshape(seq_dev, tok_seq, width).astype(jnp.bfloat16)
    attention_output = jnp.einsum(
        "scd,de->sce", context_rows, out_full, preferred_element_type=jnp.float32
    )
    residual = (token_vals + attention_output).reshape(tok_dev, width)
    moe_in = normalize(residual, moe_scale).astype(jnp.bfloat16)
    logits = jnp.dot(moe_in, router_full, preferred_element_type=jnp.float32)
    expert_ids = jnp.arange(EXPERTS, dtype=jnp.int32)
    route_hot = (routes[:, :, None] == expert_ids[None, None, :]).astype(jnp.float32)
    chosen = jnp.sum(logits[:, None, :] * route_hot, axis=-1)
    gate_vals = jax.nn.softmax(chosen, axis=-1)
    flat_routes = routes.reshape(-1)
    flat_hot = (flat_routes[:, None] == expert_ids[None, :]).astype(jnp.int32)
    before = jnp.cumsum(flat_hot, axis=0) - flat_hot
    places = flat_routes * CAP + jnp.sum(before * flat_hot, axis=1)
    owners = (
        jnp.full((EXPERTS * CAP,), -1, jnp.int32)
        .at[places]
        .set(jnp.arange(tok_dev * TOP, dtype=jnp.int32))
    )
    filled = (owners >= 0)[:, None]
    safe_owner = jnp.maximum(owners, 0)
    source_rows = safe_owner // TOP
    dispatch = jnp.where(filled, moe_in[source_rows], jnp.zeros((), jnp.bfloat16)).reshape(
        EXPERTS, CAP, width
    )
    up_piece = lax.all_gather(up_weight, "fsdp", axis=0, tiled=True)
    down_piece = lax.all_gather(down_weight, "fsdp", axis=0, tiled=True)
    rows_in = dispatch
    upper_vals = jnp.einsum("ecd,edf->ecf", rows_in, up_piece, preferred_element_type=jnp.float32)
    active = jax.nn.gelu(upper_vals, approximate=False).astype(jnp.bfloat16)
    result = jnp.einsum(
        "ecf,edf->ecd", active, down_piece, preferred_element_type=jnp.float32
    ).astype(jnp.bfloat16)
    picked = (
        result.reshape(EXPERTS * CAP, width)[places]
        .reshape(tok_dev, TOP, width)
        .astype(jnp.float32)
    )
    layer_rows = residual + jnp.sum(gate_vals[:, :, None] * picked, axis=1)
    layer_out = layer_rows.reshape(seq_dev, tok_seq, width).astype(jnp.bfloat16)
    grad_rows = cotangent.astype(jnp.float32).reshape(tok_dev, width)
    gate_grad = jnp.sum(grad_rows[:, None, :] * picked, axis=-1)
    chosen_grad = gate_vals * (gate_grad - jnp.sum(gate_vals * gate_grad, axis=1, keepdims=True))
    logit_grad = jnp.sum(chosen_grad[:, :, None] * route_hot, axis=1)
    router_grad = jnp.dot(
        moe_in.T, logit_grad, precision=PRECISION_FULL, preferred_element_type=jnp.float32
    )
    moe_in_grad = jnp.dot(
        logit_grad, router_full.T, precision=PRECISION_FULL, preferred_element_type=jnp.float32
    )
    flat_gates = gate_vals.reshape(-1)
    slot_grad = (
        jnp.where(filled, flat_gates[safe_owner][:, None] * grad_rows[source_rows], 0.0)
        .astype(jnp.bfloat16)
        .reshape(EXPERTS, CAP, width)
    )
    up_piece = lax.all_gather(up_weight, "fsdp", axis=0, tiled=True)
    down_piece = lax.all_gather(down_weight, "fsdp", axis=0, tiled=True)
    active_grad = jnp.einsum(
        "ecd,edf->ecf", slot_grad, down_piece, preferred_element_type=jnp.float32
    )
    upper_grad = gelu_grad(upper_vals, active_grad).astype(jnp.bfloat16)
    input_grad = jnp.einsum(
        "ecf,edf->ecd", upper_grad, up_piece, preferred_element_type=jnp.float32
    ).astype(jnp.bfloat16)
    rows_in = dispatch
    active_part = jax.nn.gelu(upper_vals, approximate=False).astype(jnp.bfloat16)
    up_term = jnp.einsum("ecd,ecf->edf", rows_in, upper_grad, preferred_element_type=jnp.float32)
    down_term = jnp.einsum(
        "ecd,ecf->edf", slot_grad, active_part, preferred_element_type=jnp.float32
    )
    expert_grads = lax.psum_scatter(
        jnp.stack([up_term, down_term], axis=2).astype(jnp.bfloat16),
        "fsdp",
        scatter_dimension=0,
        tiled=True,
    )
    copy_grad = (
        input_grad.reshape(EXPERTS * CAP, width)[places]
        .reshape(tok_dev, TOP, width)
        .astype(jnp.float32)
    )
    moe_in_grad = moe_in_grad + jnp.sum(copy_grad, axis=1)
    moe_pullback = jax.vjp(normalize, residual, moe_scale)[1]
    resid_norm_grad, moe_gain_grad = moe_pullback(moe_in_grad)
    resid_grad = grad_rows + resid_norm_grad
    attn_grad = resid_grad.reshape(seq_dev, tok_seq, width).astype(jnp.bfloat16)
    out_grad = jnp.einsum(
        "scd,sce->de", context_rows, attn_grad, preferred_element_type=jnp.float32
    )
    context_grad = jnp.einsum(
        "sce,de->scd", attn_grad, out_full, preferred_element_type=jnp.float32
    ).reshape(seq_dev, tok_seq, HEADS, HEAD_DIM)
    scaled_grad = (context_grad / sum_heads).astype(jnp.bfloat16)
    correction = jnp.transpose(jnp.sum(context_grad * context_pre, axis=-1), (0, 2, 1)) / row_sum
    grad_flat = scaled_grad.reshape(seq_dev, tok_seq, width)

    def query_step(current, shard_part, first_row):
        query_run, bias_run = current
        piece_keys, piece_values, piece_segs = shard_part
        key_count = piece_keys.shape[1]
        key_places = place_of(
            first_row + jnp.arange(key_count, dtype=jnp.int32), tok_seq, blocks_ctx
        )
        one_hot, bias_vals, allowed = pair_terms(
            my_places, key_places, seg_local, piece_segs, bucket_table, bias_full
        )
        key_heads = piece_keys.reshape(seq_dev, key_count, HEADS, HEAD_DIM)
        scaled = scaled_scores(queries, key_heads, bias_vals, allowed)
        numerator = jnp.exp2(scaled - row_max[..., None])
        prob_grad = jnp.einsum(
            "sqhd,skhd->shqk",
            scaled_grad,
            piece_values.reshape(seq_dev, key_count, HEADS, HEAD_DIM),
            preferred_element_type=jnp.float32,
        )
        score_grad = numerator * (prob_grad - correction[..., None])
        query_new = query_run + jnp.einsum(
            "shqk,skhd->sqhd",
            score_grad.astype(jnp.bfloat16),
            key_heads,
            preferred_element_type=jnp.float32,
        )
        bias_new = bias_run + jnp.einsum(
            "hqk,qkb->bh",
            jnp.sum(score_grad, axis=0),
            one_hot.astype(jnp.float32),
            precision=PRECISION_FULL,
        )
        return (query_new, bias_new)

    query_init = (
        jnp.zeros((seq_dev, tok_seq, HEADS, HEAD_DIM), jnp.float32),
        jnp.zeros((BUCKETS, HEADS), jnp.float32),
    )
    query_grad_acc, bias_grad = over_shards(
        query_step,
        query_init,
        (
            lax.all_gather(key_flat, "ctx", axis=1, tiled=True),
            lax.all_gather(value_flat, "ctx", axis=1, tiled=True),
            lax.all_gather(seg_local, "ctx", axis=1, tiled=True),
        ),
        tok_seq,
    )
    row_max_all, correction_all = (
        lax.all_gather(row_max, "ctx", axis=2, tiled=True),
        lax.all_gather(correction, "ctx", axis=2, tiled=True),
    )

    def key_step(current, shard_part, first_row):
        key_run, value_run = current
        piece_queries, piece_grads, piece_segs = shard_part
        query_count = piece_queries.shape[1]
        query_places = place_of(
            first_row + jnp.arange(query_count, dtype=jnp.int32), tok_seq, blocks_ctx
        )
        unused_hot, bias_vals, allowed = pair_terms(
            query_places, my_places, piece_segs, seg_local, bucket_table, bias_full
        )
        query_heads = piece_queries.reshape(seq_dev, query_count, HEADS, HEAD_DIM)
        grad_heads = piece_grads.reshape(seq_dev, query_count, HEADS, HEAD_DIM)
        scaled = scaled_scores(query_heads, key_vecs, bias_vals, allowed)
        max_part = lax.dynamic_slice_in_dim(row_max_all, first_row, query_count, 2)
        corr_part = lax.dynamic_slice_in_dim(correction_all, first_row, query_count, 2)
        numerator = jnp.exp2(scaled - max_part[..., None])
        value_new = value_run + jnp.einsum(
            "shqk,sqhd->skhd",
            numerator.astype(jnp.bfloat16),
            grad_heads,
            preferred_element_type=jnp.float32,
        )
        prob_grad = jnp.einsum(
            "sqhd,skhd->shqk", grad_heads, value_vecs, preferred_element_type=jnp.float32
        )
        score_grad = numerator * (prob_grad - corr_part[..., None])
        key_new = key_run + jnp.einsum(
            "shqk,sqhd->skhd",
            score_grad.astype(jnp.bfloat16),
            query_heads,
            preferred_element_type=jnp.float32,
        )
        return (key_new, value_new)

    key_init = (
        jnp.zeros((seq_dev, tok_seq, HEADS, HEAD_DIM), jnp.float32),
        jnp.zeros((seq_dev, tok_seq, HEADS, HEAD_DIM), jnp.float32),
    )
    key_grad_acc, value_grad_acc = over_shards(
        key_step,
        key_init,
        (
            lax.all_gather(query_flat, "ctx", axis=1, tiled=True),
            lax.all_gather(grad_flat, "ctx", axis=1, tiled=True),
            lax.all_gather(seg_local, "ctx", axis=1, tiled=True),
        ),
        tok_seq,
    )
    proj_grad = jnp.concatenate(
        [
            (query_grad_acc * head_scale).reshape(seq_dev, tok_seq, width),
            (key_grad_acc * head_scale).reshape(seq_dev, tok_seq, width),
            value_grad_acc.reshape(seq_dev, tok_seq, width),
        ],
        axis=-1,
    ).astype(jnp.bfloat16)
    qkv_grad = jnp.einsum(
        "scd,sce->de", attention_input, proj_grad, preferred_element_type=jnp.float32
    )
    attn_in_grad = jnp.einsum(
        "sce,de->scd", proj_grad, qkv_full, preferred_element_type=jnp.float32
    )
    attn_pullback = jax.vjp(normalize, token_vals, attn_scale)[1]
    token_norm_grad, attn_gain_grad = attn_pullback(attn_in_grad)
    tokens_grad = (resid_grad.reshape(seq_dev, tok_seq, width) + token_norm_grad).astype(
        jnp.bfloat16
    )
    attn_part, qkv_part, out_part, bias_part, moe_part, router_part = (
        lax.psum_scatter(
            attn_gain_grad.astype(jnp.bfloat16), "fsdp", scatter_dimension=0, tiled=True
        ).astype(jnp.float32),
        lax.psum_scatter(
            qkv_grad.astype(jnp.bfloat16), "fsdp", scatter_dimension=0, tiled=True
        ).astype(jnp.float32),
        lax.psum_scatter(
            out_grad.astype(jnp.bfloat16), "fsdp", scatter_dimension=0, tiled=True
        ).astype(jnp.float32),
        lax.psum_scatter(
            bias_grad.astype(jnp.bfloat16), "fsdp", scatter_dimension=0, tiled=True
        ).astype(jnp.float32),
        lax.psum_scatter(
            moe_gain_grad.astype(jnp.bfloat16), "fsdp", scatter_dimension=0, tiled=True
        ).astype(jnp.float32),
        lax.psum_scatter(
            router_grad.astype(jnp.bfloat16), "fsdp", scatter_dimension=0, tiled=True
        ).astype(jnp.float32),
    )
    attn_sum, bias_sum, moe_sum, router_sum = lax.psum(
        (attn_part, bias_part, moe_part, router_part), "ctx"
    )
    qkv_sum, out_sum, expert_sum = (
        lax.psum_scatter(
            qkv_part.astype(jnp.bfloat16), "ctx", scatter_dimension=1, tiled=True
        ).astype(jnp.float32),
        lax.psum_scatter(
            out_part.astype(jnp.bfloat16), "ctx", scatter_dimension=1, tiled=True
        ).astype(jnp.float32),
        lax.psum_scatter(expert_grads, "ctx", scatter_dimension=1, tiled=True).astype(jnp.float32),
    )
    return (
        layer_out,
        tokens_grad,
        attn_sum,
        qkv_sum,
        out_sum,
        bias_sum,
        moe_sum,
        router_sum,
        expert_sum[:, :, 0],
        expert_sum[:, :, 1],
    )


def solution(mesh):
    return jax.shard_map(
        per_device,
        mesh=mesh,
        in_specs=(
            P("fsdp", "ctx", None),
            P("fsdp", "ctx"),
            P(("ctx", "fsdp"), None),
            P(),
            P("fsdp"),
            P("fsdp", None),
            P("fsdp", None),
            P("fsdp", None),
            P("fsdp"),
            P("fsdp", None),
            P("fsdp", None, None),
            P("fsdp", None, None),
            P("fsdp", "ctx", None),
        ),
        out_specs=(
            P("fsdp", "ctx", None),
            P("fsdp", "ctx", None),
            P("fsdp"),
            P("fsdp", "ctx"),
            P("fsdp", "ctx"),
            P("fsdp", None),
            P("fsdp"),
            P("fsdp", None),
            P("fsdp", "ctx", None),
            P("fsdp", "ctx", None),
        ),
        check_vma=False,
    )
```

profile of v0, /device:TPU:11, one launch (start us, length us, event | category | flops | bytes accessed | tf_op | source)
XLA Modules:
  0.0 7126.3 jit_solution(15006108718030150369)
XLA Ops:
  161.7 1500.1 %while.56 = (s32[]{:T(128)}, f32[1,12,128]{2,1,0:T(8,128)S(1)}, f32[1,12,128]{2,1,0:T(8,128)S(1)}, f32[1,128,12,64]{1,3,2,0:T(8,128)S(1)}, bf16[1,128]{1,0:T(2,1...) while((s32[]{:T(128)}, f32[1,12,128]{2,1,0:T(8,128)S(1)}, ...), condition=%wide.region_4.6_spmd.clone, body=%wide.region_1.5_spmd.clone.sunk | while | flops 66114056 | bytes 8296423 | solution.py:64
  162.0 90.5 %gather_fusion = s32[16384]{0:T(1024)S(1)} fusion(s32[2048]{0:T(1024)S(1)} %get-tuple-element.1917, s32[16384]{0:T(1024)S(1)} %bitcast_clamp_fusion.6), kind=kCustom, calls=%fused_computation.clone.clone.1 | custom fusion | bytes 196608 | tf_op jit(solution)/shard_map/while/body/eval_jaxpr/jit(_take)/gather | solution.py:35
  255.8 90.5 %gather_fusion = s32[16384]{0:T(1024)S(1)} fusion(s32[2048]{0:T(1024)S(1)} %get-tuple-element.1917, s32[16384]{0:T(1024)S(1)} %bitcast_clamp_fusion.6), kind=kCustom, calls=%fused_computation.clone.clone.1 | custom fusion | bytes 196608 | tf_op jit(solution)/shard_map/while/body/eval_jaxpr/jit(_take)/gather | solution.py:35
  349.5 90.5 %gather_fusion = s32[16384]{0:T(1024)S(1)} fusion(s32[2048]{0:T(1024)S(1)} %get-tuple-element.1917, s32[16384]{0:T(1024)S(1)} %bitcast_clamp_fusion.6), kind=kCustom, calls=%fused_computation.clone.clone.1 | custom fusion | bytes 196608 | tf_op jit(solution)/shard_map/while/body/eval_jaxpr/jit(_take)/gather | solution.py:35
  443.2 90.5 %gather_fusion = s32[16384]{0:T(1024)S(1)} fusion(s32[2048]{0:T(1024)S(1)} %get-tuple-element.1917, s32[16384]{0:T(1024)S(1)} %bitcast_clamp_fusion.6), kind=kCustom, calls=%fused_computation.clone.clone.1 | custom fusion | bytes 196608 | tf_op jit(solution)/shard_map/while/body/eval_jaxpr/jit(_take)/gather | solution.py:35
  537.0 90.5 %gather_fusion = s32[16384]{0:T(1024)S(1)} fusion(s32[2048]{0:T(1024)S(1)} %get-tuple-element.1917, s32[16384]{0:T(1024)S(1)} %bitcast_clamp_fusion.6), kind=kCustom, calls=%fused_computation.clone.clone.1 | custom fusion | bytes 196608 | tf_op jit(solution)/shard_map/while/body/eval_jaxpr/jit(_take)/gather | solution.py:35
  630.9 90.5 %gather_fusion = s32[16384]{0:T(1024)S(1)} fusion(s32[2048]{0:T(1024)S(1)} %get-tuple-element.1917, s32[16384]{0:T(1024)S(1)} %bitcast_clamp_fusion.6), kind=kCustom, calls=%fused_computation.clone.clone.1 | custom fusion | bytes 196608 | tf_op jit(solution)/shard_map/while/body/eval_jaxpr/jit(_take)/gather | solution.py:35
  724.7 90.5 %gather_fusion = s32[16384]{0:T(1024)S(1)} fusion(s32[2048]{0:T(1024)S(1)} %get-tuple-element.1917, s32[16384]{0:T(1024)S(1)} %bitcast_clamp_fusion.6), kind=kCustom, calls=%fused_computation.clone.clone.1 | custom fusion | bytes 196608 | tf_op jit(solution)/shard_map/while/body/eval_jaxpr/jit(_take)/gather | solution.py:35
  818.4 90.5 %gather_fusion = s32[16384]{0:T(1024)S(1)} fusion(s32[2048]{0:T(1024)S(1)} %get-tuple-element.1917, s32[16384]{0:T(1024)S(1)} %bitcast_clamp_fusion.6), kind=kCustom, calls=%fused_computation.clone.clone.1 | custom fusion | bytes 196608 | tf_op jit(solution)/shard_map/while/body/eval_jaxpr/jit(_take)/gather | solution.py:35
  912.2 90.5 %gather_fusion = s32[16384]{0:T(1024)S(1)} fusion(s32[2048]{0:T(1024)S(1)} %get-tuple-element.1917, s32[16384]{0:T(1024)S(1)} %bitcast_clamp_fusion.6), kind=kCustom, calls=%fused_computation.clone.clone.1 | custom fusion | bytes 196608 | tf_op jit(solution)/shard_map/while/body/eval_jaxpr/jit(_take)/gather | solution.py:35
  1005.9 90.5 %gather_fusion = s32[16384]{0:T(1024)S(1)} fusion(s32[2048]{0:T(1024)S(1)} %get-tuple-element.1917, s32[16384]{0:T(1024)S(1)} %bitcast_clamp_fusion.6), kind=kCustom, calls=%fused_computation.clone.clone.1 | custom fusion | bytes 196608 | tf_op jit(solution)/shard_map/while/body/eval_jaxpr/jit(_take)/gather | solution.py:35
  1099.6 90.5 %gather_fusion = s32[16384]{0:T(1024)S(1)} fusion(s32[2048]{0:T(1024)S(1)} %get-tuple-element.1917, s32[16384]{0:T(1024)S(1)} %bitcast_clamp_fusion.6), kind=kCustom, calls=%fused_computation.clone.clone.1 | custom fusion | bytes 196608 | tf_op jit(solution)/shard_map/while/body/eval_jaxpr/jit(_take)/gather | solution.py:35
  1193.4 90.5 %gather_fusion = s32[16384]{0:T(1024)S(1)} fusion(s32[2048]{0:T(1024)S(1)} %get-tuple-element.1917, s32[16384]{0:T(1024)S(1)} %bitcast_clamp_fusion.6), kind=kCustom, calls=%fused_computation.clone.clone.1 | custom fusion | bytes 196608 | tf_op jit(solution)/shard_map/while/body/eval_jaxpr/jit(_take)/gather | solution.py:35
  1287.1 90.5 %gather_fusion = s32[16384]{0:T(1024)S(1)} fusion(s32[2048]{0:T(1024)S(1)} %get-tuple-element.1917, s32[16384]{0:T(1024)S(1)} %bitcast_clamp_fusion.6), kind=kCustom, calls=%fused_computation.clone.clone.1 | custom fusion | bytes 196608 | tf_op jit(solution)/shard_map/while/body/eval_jaxpr/jit(_take)/gather | solution.py:35
  1380.9 90.5 %gather_fusion = s32[16384]{0:T(1024)S(1)} fusion(s32[2048]{0:T(1024)S(1)} %get-tuple-element.1917, s32[16384]{0:T(1024)S(1)} %bitcast_clamp_fusion.6), kind=kCustom, calls=%fused_computation.clone.clone.1 | custom fusion | bytes 196608 | tf_op jit(solution)/shard_map/while/body/eval_jaxpr/jit(_take)/gather | solution.py:35
  1474.6 90.5 %gather_fusion = s32[16384]{0:T(1024)S(1)} fusion(s32[2048]{0:T(1024)S(1)} %get-tuple-element.1917, s32[16384]{0:T(1024)S(1)} %bitcast_clamp_fusion.6), kind=kCustom, calls=%fused_computation.clone.clone.1 | custom fusion | bytes 196608 | tf_op jit(solution)/shard_map/while/body/eval_jaxpr/jit(_take)/gather | solution.py:35
  1568.4 90.5 %gather_fusion = s32[16384]{0:T(1024)S(1)} fusion(s32[2048]{0:T(1024)S(1)} %get-tuple-element.1917, s32[16384]{0:T(1024)S(1)} %bitcast_clamp_fusion.6), kind=kCustom, calls=%fused_computation.clone.clone.1 | custom fusion | bytes 196608 | tf_op jit(solution)/shard_map/while/body/eval_jaxpr/jit(_take)/gather | solution.py:35
  1779.6 1535.2 %while.57 = (s32[]{:T(128)}, f32[1,128,12,64]{1,3,2,0:T(8,128)S(1)}, f32[32,12]{0,1:T(8,128)S(1)}, bf16[1,2048,768]{1,2,0:T(8,128)(2,1)}, bf16[1,128]{1,0:T(2,12...) while((s32[]{:T(128)}, ...), condition=%wide.region_21.23_spmd.clone, body=%wide.region_20.22_spmd.clone.sunk | while | flops 166797056 | bytes 8803318 | solution.py:64
  1780.7 90.5 %gather_fusion.1 = s32[16384]{0:T(1024)S(1)} fusion(s32[2048]{0:T(1024)S(1)} %get-tuple-element.2022, s32[16384]{0:T(1024)S(1)} %bitcast_clamp_fusion.7), kind=kCustom, calls=%fused_computation.1.clone.clone.1 | custom fusion | bytes 196608 | tf_op jit(solution)/shard_map/while/body/eval_jaxpr/jit(_take)/gather | solution.py:35
  1876.7 90.5 %gather_fusion.1 = s32[16384]{0:T(1024)S(1)} fusion(s32[2048]{0:T(1024)S(1)} %get-tuple-element.2022, s32[16384]{0:T(1024)S(1)} %bitcast_clamp_fusion.7), kind=kCustom, calls=%fused_computation.1.clone.clone.1 | custom fusion | bytes 196608 | tf_op jit(solution)/shard_map/while/body/eval_jaxpr/jit(_take)/gather | solution.py:35
  1972.6 90.5 %gather_fusion.1 = s32[16384]{0:T(1024)S(1)} fusion(s32[2048]{0:T(1024)S(1)} %get-tuple-element.2022, s32[16384]{0:T(1024)S(1)} %bitcast_clamp_fusion.7), kind=kCustom, calls=%fused_computation.1.clone.clone.1 | custom fusion | bytes 196608 | tf_op jit(solution)/shard_map/while/body/eval_jaxpr/jit(_take)/gather | solution.py:35
  2068.5 90.5 %gather_fusion.1 = s32[16384]{0:T(1024)S(1)} fusion(s32[2048]{0:T(1024)S(1)} %get-tuple-element.2022, s32[16384]{0:T(1024)S(1)} %bitcast_clamp_fusion.7), kind=kCustom, calls=%fused_computation.1.clone.clone.1 | custom fusion | bytes 196608 | tf_op jit(solution)/shard_map/while/body/eval_jaxpr/jit(_take)/gather | solution.py:35
  2164.5 90.5 %gather_fusion.1 = s32[16384]{0:T(1024)S(1)} fusion(s32[2048]{0:T(1024)S(1)} %get-tuple-element.2022, s32[16384]{0:T(1024)S(1)} %bitcast_clamp_fusion.7), kind=kCustom, calls=%fused_computation.1.clone.clone.1 | custom fusion | bytes 196608 | tf_op jit(solution)/shard_map/while/body/eval_jaxpr/jit(_take)/gather | solution.py:35
  2260.4 90.5 %gather_fusion.1 = s32[16384]{0:T(1024)S(1)} fusion(s32[2048]{0:T(1024)S(1)} %get-tuple-element.2022, s32[16384]{0:T(1024)S(1)} %bitcast_clamp_fusion.7), kind=kCustom, calls=%fused_computation.1.clone.clone.1 | custom fusion | bytes 196608 | tf_op jit(solution)/shard_map/while/body/eval_jaxpr/jit(_take)/gather | solution.py:35
  2356.4 90.5 %gather_fusion.1 = s32[16384]{0:T(1024)S(1)} fusion(s32[2048]{0:T(1024)S(1)} %get-tuple-element.2022, s32[16384]{0:T(1024)S(1)} %bitcast_clamp_fusion.7), kind=kCustom, calls=%fused_computation.1.clone.clone.1 | custom fusion | bytes 196608 | tf_op jit(solution)/shard_map/while/body/eval_jaxpr/jit(_take)/gather | solution.py:35
  2452.3 90.5 %gather_fusion.1 = s32[16384]{0:T(1024)S(1)} fusion(s32[2048]{0:T(1024)S(1)} %get-tuple-element.2022, s32[16384]{0:T(1024)S(1)} %bitcast_clamp_fusion.7), kind=kCustom, calls=%fused_computation.1.clone.clone.1 | custom fusion | bytes 196608 | tf_op jit(solution)/shard_map/while/body/eval_jaxpr/jit(_take)/gather | solution.py:35
  2548.2 90.5 %gather_fusion.1 = s32[16384]{0:T(1024)S(1)} fusion(s32[2048]{0:T(1024)S(1)} %get-tuple-element.2022, s32[16384]{0:T(1024)S(1)} %bitcast_clamp_fusion.7), kind=kCustom, calls=%fused_computation.1.clone.clone.1 | custom fusion | bytes 196608 | tf_op jit(solution)/shard_map/while/body/eval_jaxpr/jit(_take)/gather | solution.py:35
  2644.2 90.5 %gather_fusion.1 = s32[16384]{0:T(1024)S(1)} fusion(s32[2048]{0:T(1024)S(1)} %get-tuple-element.2022, s32[16384]{0:T(1024)S(1)} %bitcast_clamp_fusion.7), kind=kCustom, calls=%fused_computation.1.clone.clone.1 | custom fusion | bytes 196608 | tf_op jit(solution)/shard_map/while/body/eval_jaxpr/jit(_take)/gather | solution.py:35
  2740.1 90.5 %gather_fusion.1 = s32[16384]{0:T(1024)S(1)} fusion(s32[2048]{0:T(1024)S(1)} %get-tuple-element.2022, s32[16384]{0:T(1024)S(1)} %bitcast_clamp_fusion.7), kind=kCustom, calls=%fused_computation.1.clone.clone.1 | custom fusion | bytes 196608 | tf_op jit(solution)/shard_map/while/body/eval_jaxpr/jit(_take)/gather | solution.py:35
  2836.1 90.5 %gather_fusion.1 = s32[16384]{0:T(1024)S(1)} fusion(s32[2048]{0:T(1024)S(1)} %get-tuple-element.2022, s32[16384]{0:T(1024)S(1)} %bitcast_clamp_fusion.7), kind=kCustom, calls=%fused_computation.1.clone.clone.1 | custom fusion | bytes 196608 | tf_op jit(solution)/shard_map/while/body/eval_jaxpr/jit(_take)/gather | solution.py:35
  2932.0 90.5 %gather_fusion.1 = s32[16384]{0:T(1024)S(1)} fusion(s32[2048]{0:T(1024)S(1)} %get-tuple-element.2022, s32[16384]{0:T(1024)S(1)} %bitcast_clamp_fusion.7), kind=kCustom, calls=%fused_computation.1.clone.clone.1 | custom fusion | bytes 196608 | tf_op jit(solution)/shard_map/while/body/eval_jaxpr/jit(_take)/gather | solution.py:35
  3123.9 90.5 %gather_fusion.1 = s32[16384]{0:T(1024)S(1)} fusion(s32[2048]{0:T(1024)S(1)} %get-tuple-element.2022, s32[16384]{0:T(1024)S(1)} %bitcast_clamp_fusion.7), kind=kCustom, calls=%fused_computation.1.clone.clone.1 | custom fusion | bytes 196608 | tf_op jit(solution)/shard_map/while/body/eval_jaxpr/jit(_take)/gather | solution.py:35
  3219.8 90.5 %gather_fusion.1 = s32[16384]{0:T(1024)S(1)} fusion(s32[2048]{0:T(1024)S(1)} %get-tuple-element.2022, s32[16384]{0:T(1024)S(1)} %bitcast_clamp_fusion.7), kind=kCustom, calls=%fused_computation.1.clone.clone.1 | custom fusion | bytes 196608 | tf_op jit(solution)/shard_map/while/body/eval_jaxpr/jit(_take)/gather | solution.py:35
  3334.3 1529.1 %while.58 = (s32[]{:T(128)}, f32[1,128,12,64]{1,3,2,0:T(8,128)S(1)}, f32[1,128,12,64]{1,3,2,0:T(8,128)S(1)}, bf16[1,2048,768]{2,1,0:T(8,128)(2,1)}, bf16[1,2048]...) while((s32[]{:T(128)}, ...), condition=%wide.region_23.25_spmd.clone, body=%wide.region_22.24_spmd.clone.sunk | while | flops 116333568 | bytes 8792058 | solution.py:64
  3336.2 90.5 %gather_fusion.2 = s32[16384]{0:T(1024)S(1)} fusion(s32[2048]{0:T(1024)S(1)} %get-tuple-element.1968, s32[16384]{0:T(1024)S(1)} %bitcast_clamp_fusion.8), kind=kCustom, calls=%fused_computation.2.clone.clone.1 | custom fusion | bytes 196608 | tf_op jit(solution)/shard_map/while/body/eval_jaxpr/jit(_take)/gather | solution.py:35
  3431.7 90.5 %gather_fusion.2 = s32[16384]{0:T(1024)S(1)} fusion(s32[2048]{0:T(1024)S(1)} %get-tuple-element.1968, s32[16384]{0:T(1024)S(1)} %bitcast_clamp_fusion.8), kind=kCustom, calls=%fused_computation.2.clone.clone.1 | custom fusion | bytes 196608 | tf_op jit(solution)/shard_map/while/body/eval_jaxpr/jit(_take)/gather | solution.py:35
  3527.2 90.5 %gather_fusion.2 = s32[16384]{0:T(1024)S(1)} fusion(s32[2048]{0:T(1024)S(1)} %get-tuple-element.1968, s32[16384]{0:T(1024)S(1)} %bitcast_clamp_fusion.8), kind=kCustom, calls=%fused_computation.2.clone.clone.1 | custom fusion | bytes 196608 | tf_op jit(solution)/shard_map/while/body/eval_jaxpr/jit(_take)/gather | solution.py:35
  3622.8 90.5 %gather_fusion.2 = s32[16384]{0:T(1024)S(1)} fusion(s32[2048]{0:T(1024)S(1)} %get-tuple-element.1968, s32[16384]{0:T(1024)S(1)} %bitcast_clamp_fusion.8), kind=kCustom, calls=%fused_computation.2.clone.clone.1 | custom fusion | bytes 196608 | tf_op jit(solution)/shard_map/while/body/eval_jaxpr/jit(_take)/gather | solution.py:35
  3813.9 90.5 %gather_fusion.2 = s32[16384]{0:T(1024)S(1)} fusion(s32[2048]{0:T(1024)S(1)} %get-tuple-element.1968, s32[16384]{0:T(1024)S(1)} %bitcast_clamp_fusion.8), kind=kCustom, calls=%fused_computation.2.clone.clone.1 | custom fusion | bytes 196608 | tf_op jit(solution)/shard_map/while/body/eval_jaxpr/jit(_take)/gather | solution.py:35
  3909.5 90.5 %gather_fusion.2 = s32[16384]{0:T(1024)S(1)} fusion(s32[2048]{0:T(1024)S(1)} %get-tuple-element.1968, s32[16384]{0:T(1024)S(1)} %bitcast_clamp_fusion.8), kind=kCustom, calls=%fused_computation.2.clone.clone.1 | custom fusion | bytes 196608 | tf_op jit(solution)/shard_map/while/body/eval_jaxpr/jit(_take)/gather | solution.py:35
  4005.0 90.5 %gather_fusion.2 = s32[16384]{0:T(1024)S(1)} fusion(s32[2048]{0:T(1024)S(1)} %get-tuple-element.1968, s32[16384]{0:T(1024)S(1)} %bitcast_clamp_fusion.8), kind=kCustom, calls=%fused_computation.2.clone.clone.1 | custom fusion | bytes 196608 | tf_op jit(solution)/shard_map/while/body/eval_jaxpr/jit(_take)/gather | solution.py:35
  4100.6 90.5 %gather_fusion.2 = s32[16384]{0:T(1024)S(1)} fusion(s32[2048]{0:T(1024)S(1)} %get-tuple-element.1968, s32[16384]{0:T(1024)S(1)} %bitcast_clamp_fusion.8), kind=kCustom, calls=%fused_computation.2.clone.clone.1 | custom fusion | bytes 196608 | tf_op jit(solution)/shard_map/while/body/eval_jaxpr/jit(_take)/gather | solution.py:35
  4387.2 90.5 %gather_fusion.2 = s32[16384]{0:T(1024)S(1)} fusion(s32[2048]{0:T(1024)S(1)} %get-tuple-element.1968, s32[16384]{0:T(1024)S(1)} %bitcast_clamp_fusion.8), kind=kCustom, calls=%fused_computation.2.clone.clone.1 | custom fusion | bytes 196608 | tf_op jit(solution)/shard_map/while/body/eval_jaxpr/jit(_take)/gather | solution.py:35
  4482.8 90.5 %gather_fusion.2 = s32[16384]{0:T(1024)S(1)} fusion(s32[2048]{0:T(1024)S(1)} %get-tuple-element.1968, s32[16384]{0:T(1024)S(1)} %bitcast_clamp_fusion.8), kind=kCustom, calls=%fused_computation.2.clone.clone.1 | custom fusion | bytes 196608 | tf_op jit(solution)/shard_map/while/body/eval_jaxpr/jit(_take)/gather | solution.py:35
  4578.3 90.5 %gather_fusion.2 = s32[16384]{0:T(1024)S(1)} fusion(s32[2048]{0:T(1024)S(1)} %get-tuple-element.1968, s32[16384]{0:T(1024)S(1)} %bitcast_clamp_fusion.8), kind=kCustom, calls=%fused_computation.2.clone.clone.1 | custom fusion | bytes 196608 | tf_op jit(solution)/shard_map/while/body/eval_jaxpr/jit(_take)/gather | solution.py:35
  4673.9 90.5 %gather_fusion.2 = s32[16384]{0:T(1024)S(1)} fusion(s32[2048]{0:T(1024)S(1)} %get-tuple-element.1968, s32[16384]{0:T(1024)S(1)} %bitcast_clamp_fusion.8), kind=kCustom, calls=%fused_computation.2.clone.clone.1 | custom fusion | bytes 196608 | tf_op jit(solution)/shard_map/while/body/eval_jaxpr/jit(_take)/gather | solution.py:35
  4963.8 1630.8 %all-reduce.7.cloned.1.call-done = bf16[8,768,2,3072]{3,1,0,2:T(8,128)(2,1)} async-done(((bf16[8,768,2,3072]{3,1,0,2:T(8,128)(2,1)}), bf16[8,768,2,3072]{3,1,0,2:T(8,128)(2,1)}) %all-reduce.7.cloned.1.call-update) | async-done | bytes 75497488
  6744.3 370.0 %reduce-scatter.23.cloned.1.call-done = bf16[4,48,2,3072]{3,1,0,2:T(8,128)(2,1)} async-done(((bf16[4,768,2,3072]{3,1,0,2:T(8,128)(2,1)}), bf16[4,48,2,3072]{3,1,0,2:T(8,128)(2,1)}) %reduce-scatter.23.cloned.1.call-update) | async-done | bytes 2359312 | tf_op jit(solution)/shard_map/reduce_scatter | solution.py:407
  (964 shorter events, 1210.2 us)
Async XLA Ops:
  7.2 52.0 all-gather.12.cloned.1.call-start
  7.9 102.1 %all-gather.16.cloned.1.call-start = ((), (), s32[]{:S(2)}) async-start(), calls=%async_computation.9 | async-start | bytes 3342336 | tf_op jit(solution)/shard_map/all_gather | solution.py:152
  11.8 52.3 copy-start.32
  13.5 50.7 copy-start.52
  62.8 42.5 copy-start.19
  62.8 94.2 %all-gather.14.cloned.1.call-start = ((), (), s32[]{:S(2)}) async-start(), calls=%async_computation.8 | async-start | bytes 3342336 | tf_op jit(solution)/shard_map/all_gather | solution.py:151
  63.5 1617.7 %all-gather.18.cloned.1.call-start = ((), (), s32[]{:S(2)}) async-start(), calls=%async_computation.10 | async-start | bytes 1769472 | tf_op jit(solution)/shard_map/all_gather | solution.py:97
  64.1 1625.3 %all-gather.20.cloned.1.call-start = ((), (), s32[]{:S(2)}) async-start(), calls=%async_computation.11 | async-start | bytes 56623104 | tf_op jit(solution)/shard_map/all_gather | solution.py:185
  64.7 11.0 copy-start.28
  64.8 1643.0 %all-gather.22.cloned.1.call-start = ((), (), s32[]{:S(2)}) async-start(), calls=%async_computation.12 | async-start | bytes 56623104 | tf_op jit(solution)/shard_map/all_gather | solution.py:186
  65.3 3268.9 %all-gather.24.cloned.1.call-start = ((), (), s32[]{:S(2)}) async-start(), calls=%async_computation.13 | async-start | bytes 3342336 | tf_op jit(solution)/shard_map/all_gather | solution.py:352
  75.1 1632.6 %copy-start.34 = (pred[8,40]{1,0:T(8,128)(4,1)}, pred[8,40]{1,0:T(8,128)(4,1)S(1)}, u32[]{:S(2)}) copy-start(pred[8,40]{1,0:T(8,128)(4,1)S(1)} %broadcast_in_dim.242) | copy-start | bytes 964
  75.8 23.7 copy-start.54
  75.8 27.8 copy-start.23
  75.8 28.7 copy-start.22
  105.5 3228.7 %all-gather.26.cloned.1.call-start = ((), (), s32[]{:S(2)}) async-start(), calls=%async_computation.17 | async-start | bytes 3342336 | tf_op jit(solution)/shard_map/all_gather | solution.py:353
  114.8 46.9 copy-start
  161.7 1519.5 %copy-start.13 = (bf16[1,128,768]{2,1,0:T(8,128)(2,1)S(1)}, bf16[1,128,768]{2,1,0:T(8,128)(2,1)}, u32[]{:S(2)}) copy-start(bf16[1,128,768]{2,1,0:T(8,128)(2,1)} %param.21) | copy-start | bytes 589828
  1661.7 18.4 copy-start.26
  1661.7 21.4 copy-start.49
  1682.9 24.8 copy-start.63
  1682.9 92.5 %copy-start.10 = (f32[1,128,768]{2,1,0:T(8,128)}, f32[1,128,768]{2,1,0:T(8,128)S(1)}, u32[]{:S(2)}) copy-start(f32[1,128,768]{2,1,0:T(8,128)S(1)} %get-tuple-element.1590) | copy-start | bytes 1179652
  1685.2 22.5 copy-start.17
  1689.4 18.3 copy-start.58
  1729.4 17.7 copy-start.8
  1776.5 1556.1 %copy-start.15 = (f32[128,768]{1,0:T(8,128)}, f32[128,768]{1,0:T(8,128)S(1)}, u32[]{:S(2)}) copy-start(f32[128,768]{1,0:T(8,128)S(1)} %fusion.84) | copy-start | bytes 1179652
  1779.5 3176.9 %reduce-scatter.21.cloned.1.call-start = ((), (), s32[]{:S(2)}) async-start(), calls=%async_computation.15 | async-start | bytes 1769472 | tf_op jit(solution)/shard_map/reduce_scatter | solution.py:384
  1779.5 1553.1 %copy-start.21 = (bf16[1,128,12,64]{1,3,2,0:T(8,128)(2,1)S(1)}, bf16[1,128,12,64]{1,3,2,0:T(8,128)(2,1)}, u32[]{:S(2)}) copy-start(bf16[1,128,12,64]{1,3,2,0:T(8,128)(2,1)} %copy-done.20) | copy-start | bytes 589828
  1779.5 1554.7 %copy-start.5 = (f32[1,128,12,64]{1,3,2,0:T(8,128)S(1)}, f32[1,128,12,64]{1,3,2,0:T(8,128)}, u32[]{:S(2)}) copy-start(f32[1,128,12,64]{1,3,2,0:T(8,128)} %custom-call.5) | copy-start | bytes 1179652
  1779.5 1554.7 %copy-start.6 = (f32[1,128,12,64]{1,3,2,0:T(8,128)S(1)}, f32[1,128,12,64]{1,3,2,0:T(8,128)}, u32[]{:S(2)}) copy-start(f32[1,128,12,64]{1,3,2,0:T(8,128)} %custom-call.6) | copy-start | bytes 1179652
  1779.6 1554.7 %copy-start.12 = (bf16[1,128,768]{1,2,0:T(8,128)(2,1)S(1)}, bf16[1,128,768]{1,2,0:T(8,128)(2,1)}, u32[]{:S(2)}) copy-start(bf16[1,128,768]{1,2,0:T(8,128)(2,1)} %copy.234) | copy-start | bytes 589828
  1779.6 1554.7 %copy-start.36 = (bf16[1,128,768]{1,2,0:T(8,128)(2,1)S(1)}, bf16[1,128,768]{1,2,0:T(8,128)(2,1)}, u32[]{:S(2)}) copy-start(bf16[1,128,768]{1,2,0:T(8,128)(2,1)} %copy.232) | copy-start | bytes 589828
  3314.7 17.8 copy-start.30
  3334.1 1624.5 %reduce-scatter.19.cloned.1.call-start = ((), (), s32[]{:S(2)}) async-start(), calls=%async_computation.14 | async-start | bytes 5308416 | tf_op jit(solution)/shard_map/reduce_scatter | solution.py:381
  3334.3 1529.2 %copy-start.14 = (bf16[1,128,768]{2,1,0:T(8,128)(2,1)S(1)}, bf16[1,128,768]{2,1,0:T(8,128)(2,1)}, u32[]{:S(2)}) copy-start(bf16[1,128,768]{2,1,0:T(8,128)(2,1)} %param.21) | copy-start | bytes 589828
  3334.3 1529.2 %copy-start.33 = (f32[768]{0:T(1024)S(1)}, f32[768]{0:T(1024)}, u32[]{:S(2)}) copy-start(f32[768]{0:T(1024)} %copy-done.32) | copy-start | bytes 9220
  3334.3 1529.2 %copy-start.53 = (f32[128]{0:T(128)S(1)}, f32[128]{0:T(128)}, u32[]{:S(2)}) copy-start(f32[128]{0:T(128)} %copy-done.52) | copy-start | bytes 1540
  4866.6 17.0 copy-start.38
  4866.6 17.0 copy-start.59
  4866.6 1728.0 %all-reduce.7.cloned.1.call-start = ((), (), s32[]{:S(2)}) async-start(), calls=%async_computation.22 | async-start | bytes 150994944
  4953.6 1668.8 %reduce-scatter.29.cloned.1.call-start = ((), (), s32[]{:S(2)}) async-start(), calls=%async_computation.20 | async-start | bytes 12288
  4954.9 1668.2 %reduce-scatter.31.cloned.1.call-start = ((), (), s32[]{:S(2)}) async-start(), calls=%async_computation.21 | async-start | bytes 294912
  4956.3 1722.7 %reduce-scatter.27.cloned.1.call-start = ((), (), s32[]{:S(2)}) async-start(), calls=%async_computation.19 | async-start | bytes 626688
  4958.5 1784.0 %reduce-scatter.25.cloned.1.call-start = ((), (), s32[]{:S(2)}) async-start(), calls=%async_computation.18 | async-start | bytes 1880064
  4962.5 2151.8 %reduce-scatter.23.cloned.1.call-start = ((), (), s32[]{:S(2)}) async-start(), calls=%async_computation.16 | async-start | bytes 40108032 | tf_op jit(solution)/shard_map/reduce_scatter | solution.py:407
  6620.5 63.5 copy-start.48
  6620.5 117.6 %copy-start.62 = (f32[128]{0:T(128)S(1)}, f32[128]{0:T(128)}, u32[]{:S(2)}) copy-start(f32[128]{0:T(128)} %copy-done.61) | copy-start | bytes 1540
  6620.6 117.6 %copy-start.16 = (f32[128,768]{1,0:T(8,128)S(1)}, f32[128,768]{1,0:T(8,128)}, u32[]{:S(2)}) copy-start(f32[128,768]{1,0:T(8,128)} %copy-done.15) | copy-start | bytes 1179652
  (35 other events, 118.1 us)
Sparse Core Ops, SparseCore 0:
  9.6 49.5 all-gather.11
  62.9 47.0 all-gather.15
  112.9 43.9 all-gather.13
  158.3 19.8 all-gather.17
  179.6 437.0 all-gather.19
  618.2 437.0 all-gather.21
  1058.1 46.9 all-gather.23
  1779.6 45.6 all-gather.25
  3334.2 21.4 reduce-scatter.20
  4866.7 47.3 reduce-scatter.18
  4953.7 1640.9 all-reduce.6
  6597.3 9.2 reduce-scatter.28
  6609.5 11.4 reduce-scatter.30
  6625.4 53.5 reduce-scatter.26
  6683.2 59.2 reduce-scatter.24
  6746.6 367.6 reduce-scatter.22
where the time goes:
time: 7140 us; the launch traced here: 7130 us
  local copies, waits for them, and re-layouts  4520 us (63%)
  waiting for transfers between devices  2150 us (30%)
  matrix products  227 us (3%)
  blocking collectives  124 us (2%)
  other arithmetic  78.6 us (1%)
    gather x48, local copies, waits for them, and re-layouts, pair_terms(): buckets = jnp.take(bucket_table, distance, axis=0)  4350 us
    unnamed x21, waiting for transfers between devices  1690 us
    reduce_scatter x1, waiting for transfers between devices, per_device(): lax.psum_scatter(expert_grads, 'ctx', scatter_dimension=1, tiled=True)  370 us
  transfers between devices with their start and end apart: 16, of which 7 were waited for; matrix products, arithmetic and copies ran while one was open for 68% of the time, Pallas kernels for 0%

commit v1 on v0

v1 whole, which is shorter than its diff:
```python
import functools

import jax
import jax.numpy as jnp
from jax import lax
from jax.experimental import pallas as pl
from jax.experimental.pallas import tpu as pltpu
from jax.sharding import Mesh, PartitionSpec as P

HEADS = 12
HEAD_DIM = 64
EXPERTS = 8
TOP = 2
BUCKETS = 32
DOCS = 8
CAP = 40
GROUPS = 4
GHEADS = HEADS // GROUPS
GWIDTH = GHEADS * HEAD_DIM
CHUNK = 256

LOG2E = 1.4426950408889634
EPS = 1e-06
LOWEST = -1e30
FULL = lax.Precision.HIGHEST
BF = jnp.bfloat16
F32 = jnp.float32


def normalize(values, weight):
    inv_rms = lax.rsqrt(jnp.mean(values * values, axis=-1, keepdims=True) + EPS)
    return values * inv_rms * weight


def dot(a, b, dims=((1,), (0,))):
    return lax.dot_general(a, b, (dims, ((), ())), preferred_element_type=F32)


def gelu_both(upper, upstream):
    value, pullback = jax.vjp(lambda a: jax.nn.gelu(a, approximate=False), upper)
    return value, pullback(upstream)[0]


def xor_perm(mask, size):
    return [(i, i ^ mask) for i in range(size)]


def bits_of(size):
    bit = size // 2
    while bit:
        yield bit
        bit //= 2


def strip_width(blocks, half):
    need = half * (blocks - 1) + CHUNK + half
    return -(-need // 128) * 128


def strips_kernel(g_ref, out_ref):
    half = out_ref.shape[1]
    row = jnp.broadcast_to(g_ref[0], (half, g_ref.shape[2]))
    out_ref[0] = pltpu.roll(row, 0, 1, stride=1, stride_axis=0)


def make_strips(lines, half):
    count, _, width = lines.shape
    return pl.pallas_call(
        strips_kernel,
        grid=(count,),
        in_specs=[pl.BlockSpec((1, 1, width), lambda i: (i, 0, 0))],
        out_specs=pl.BlockSpec((1, half, width), lambda i: (i, 0, 0)),
        out_shape=jax.ShapeDtypeStruct((count, half, width), F32),
    )(lines)


def order_keys(me, kv_ref, kpos, half):
    members, groups = kv_ref.shape[0], kv_ref.shape[1]
    shards = members * groups
    for block in range(2 * shards):
        owner = block if block < shards else 2 * shards - 1 - block
        late = 0 if block < shards else half
        slot = (owner % members) ^ me
        kpos[block * half : (block + 1) * half, :] = kv_ref[
            slot, owner // members, late : late + half, :
        ]


def tile_terms(block, chunk, half, blocks, start):
    shift = blocks - 1 - (block - (CHUNK // half) * chunk)
    parity = lax.rem(shift, 2)
    lane = pl.multiple_of((shift - parity) * half, 128)
    keys = chunk * CHUNK + lax.broadcasted_iota(jnp.int32, (half, CHUNK), 1)
    rows = block * half + lax.broadcasted_iota(jnp.int32, (half, CHUNK), 0)
    return parity, lane, (keys <= rows) & (keys >= start)


def forward_kernel(half, blocks, info, q_ref, kv_ref, strip_ref, start_ref, o_ref, stat_ref, kpos):
    step = pl.program_id(0)

    @pl.when(step == 0)
    def _():
        order_keys(info[2, 0], kv_ref, kpos, half)

    block, first = info[0, step], info[1, step]
    q = q_ref[...]
    start = start_ref[...]

    def visit(chunk, carry):
        parity, lane, allowed = tile_terms(block, chunk, half, blocks, start)
        rows = pl.ds(pl.multiple_of(chunk * CHUNK, CHUNK), CHUNK)
        out = []
        for n in range(GHEADS):
            peak, total, acc = carry[n]
            cols = slice(n * HEAD_DIM, (n + 1) * HEAD_DIM)
            vcols = slice(GWIDTH + n * HEAD_DIM, GWIDTH + (n + 1) * HEAD_DIM)
            raw = dot(q[:, cols], kpos[rows, cols], ((1,), (1,)))
            t = raw * (HEAD_DIM**-0.5 * LOG2E) + strip_ref[parity * GHEADS + n, :, pl.ds(lane, CHUNK)]
            t = jnp.where(allowed, t, LOWEST)
            new = jnp.maximum(peak, jnp.ceil(jnp.max(t, axis=1, keepdims=True)))
            e = jnp.exp2(t - new)
            fade = jnp.exp2(peak - new)
            total = total * fade + jnp.sum(e, axis=1, keepdims=True)
            acc = acc * fade + dot(e.astype(BF), kpos[rows, vcols])
            out.append((new, total, acc))
        return tuple(out)

    init = tuple(
        (
            jnp.full((half, 1), LOWEST, F32),
            jnp.zeros((half, 1), F32),
            jnp.zeros((half, HEAD_DIM), F32),
        )
        for _ in range(GHEADS)
    )
    done = lax.fori_loop(first, block // (CHUNK // half) + 1, visit, init)
    for n in range(GHEADS):
        peak, total, acc = done[n]
        o_ref[:, n * HEAD_DIM : (n + 1) * HEAD_DIM] = acc / total
        stat_ref[:, n : n + 1] = peak
        stat_ref[:, GHEADS + n : GHEADS + n + 1] = total


def backward_kernel(
    half, blocks, info, q_ref, kv_ref, strip_ref, start_ref, do_ref, o_ref, stat_ref,
    dq_ref, dkv_ref, dline_ref, kpos, dkv, dstrip,
):
    step = pl.program_id(0)
    width = dstrip.shape[2]

    @pl.when(step == 0)
    def _():
        order_keys(info[2, 0], kv_ref, kpos, half)
        dkv[...] = jnp.zeros_like(dkv)
        dstrip[...] = jnp.zeros_like(dstrip)

    block, first = info[0, step], info[1, step]
    q = q_ref[...]
    start = start_ref[...]
    peaks, scaled, corr = [], [], []
    for n in range(GHEADS):
        cols = slice(n * HEAD_DIM, (n + 1) * HEAD_DIM)
        total = stat_ref[:, GHEADS + n : GHEADS + n + 1]
        do = do_ref[:, cols].astype(F32)
        peaks.append(stat_ref[:, n : n + 1])
        scaled.append((do / total).astype(BF))
        corr.append(jnp.sum(do * o_ref[:, cols], axis=1, keepdims=True) / total)

    def visit(chunk, carry):
        parity, lane, allowed = tile_terms(block, chunk, half, blocks, start)
        rows = pl.ds(pl.multiple_of(chunk * CHUNK, CHUNK), CHUNK)
        out = []
        for n in range(GHEADS):
            cols = slice(n * HEAD_DIM, (n + 1) * HEAD_DIM)
            vcols = slice(GWIDTH + n * HEAD_DIM, GWIDTH + (n + 1) * HEAD_DIM)
            strip = parity * GHEADS + n
            raw = dot(q[:, cols], kpos[rows, cols], ((1,), (1,)))
            t = raw * (HEAD_DIM**-0.5 * LOG2E) + strip_ref[strip, :, pl.ds(lane, CHUNK)]
            e = jnp.exp2(jnp.where(allowed, t, LOWEST) - peaks[n])
            dp = dot(scaled[n], kpos[rows, vcols], ((1,), (1,)))
            s = e * (dp - corr[n])
            low = s.astype(BF)
            out.append(carry[n] + dot(low, kpos[rows, cols]))
            dkv[rows, cols] += dot(low, q[:, cols], ((0,), (0,)))
            dkv[rows, vcols] += dot(e.astype(BF), scaled[n], ((0,), (0,)))
            dstrip[strip, :, pl.ds(lane, CHUNK)] += s
        return tuple(out)

    init = tuple(jnp.zeros((half, HEAD_DIM), F32) for _ in range(GHEADS))
    done = lax.fori_loop(first, block // (CHUNK // half) + 1, visit, init)
    for n in range(GHEADS):
        dq_ref[:, n * HEAD_DIM : (n + 1) * HEAD_DIM] = (done[n] * HEAD_DIM**-0.5).astype(BF)

    @pl.when(step == pl.num_programs(0) - 1)
    def _():
        me = info[2, 0]
        members, groups = dkv_ref.shape[0], dkv_ref.shape[1]
        shards = members * groups
        for b in range(2 * shards):
            owner = b if b < shards else 2 * shards - 1 - b
            late = 0 if b < shards else half
            part = dkv[b * half : (b + 1) * half, :]
            lanes = lax.broadcasted_iota(jnp.int32, part.shape, 1)
            part = part * jnp.where(lanes < GWIDTH, HEAD_DIM**-0.5, 1.0)
            dkv_ref[(owner % members) ^ me, owner // members, late : late + half, :] = part.astype(BF)
        for n in range(GHEADS):
            for parity in range(2):
                x = dstrip[parity * GHEADS + n]
                rows = half
                while rows > 8:
                    rows //= 2
                    x = x[:rows] + pltpu.roll(x[rows:], width - rows, 1)
                sub = lax.broadcasted_iota(jnp.int32, x.shape, 0)
                for bit in (4, 2, 1):
                    x = jnp.where((sub & bit) != 0, pltpu.roll(x, width - bit, 1), x)
                line = jnp.sum(x, axis=0, keepdims=True)
                if parity == 0:
                    even = line
                else:
                    dline_ref[n : n + 1, :] = even + pltpu.roll(line, half, 1)


def whole(shape):
    return pl.BlockSpec(shape, lambda i, info: (0,) * len(shape))


def attend(info, q, kv, strips, start, blocks):
    rows = q.shape[0]
    half = strips.shape[1]
    block = lambda width: pl.BlockSpec((half, width), lambda i, info: (i, 0))
    return pl.pallas_call(
        functools.partial(forward_kernel, half, blocks),
        grid_spec=pltpu.PrefetchScalarGridSpec(
            num_scalar_prefetch=1,
            grid=(rows // half,),
            in_specs=[block(GWIDTH), whole(kv.shape), whole(strips.shape), block(1)],
            out_specs=[block(GWIDTH), block(8)],
            scratch_shapes=[pltpu.VMEM((blocks * half, 2 * GWIDTH), BF)],
        ),
        out_shape=[
            jax.ShapeDtypeStruct((rows, GWIDTH), F32),
            jax.ShapeDtypeStruct((rows, 8), F32),
        ],
        compiler_params=pltpu.CompilerParams(vmem_limit_bytes=48 << 20),
        name="attend",
    )(info, q, kv, strips, start)


def attend_back(info, q, kv, strips, start, do, o, stat, blocks):
    rows = q.shape[0]
    half = strips.shape[1]
    width = strips.shape[2]
    block = lambda width: pl.BlockSpec((half, width), lambda i, info: (i, 0))
    return pl.pallas_call(
        functools.partial(backward_kernel, half, blocks),
        grid_spec=pltpu.PrefetchScalarGridSpec(
            num_scalar_prefetch=1,
            grid=(rows // half,),
            in_specs=[
                block(GWIDTH), whole(kv.shape), whole(strips.shape), block(1),
                block(GWIDTH), block(GWIDTH), block(8),
            ],
            out_specs=[block(GWIDTH), whole(kv.shape), whole((GHEADS, width))],
            scratch_shapes=[
                pltpu.VMEM((blocks * half, 2 * GWIDTH), BF),
                pltpu.VMEM((blocks * half, 2 * GWIDTH), F32),
                pltpu.VMEM(strips.shape, F32),
            ],
        ),
        out_shape=[
            jax.ShapeDtypeStruct((rows, GWIDTH), BF),
            jax.ShapeDtypeStruct(kv.shape, BF),
            jax.ShapeDtypeStruct((GHEADS, width), F32),
        ],
        compiler_params=pltpu.CompilerParams(vmem_limit_bytes=56 << 20),
        name="attend_back",
    )(info, q, kv, strips, start, do, o, stat)


def gather_members(x):
    size = lax.axis_size("m")
    held = {0: x[None]}
    for bit in bits_of(size):
        keys = sorted(held)
        sent = jnp.concatenate([held[k] for k in keys]) if len(keys) > 1 else held[keys[0]]
        came = lax.ppermute(sent, "m", xor_perm(bit, size))
        for i, k in enumerate(keys):
            held[k | bit] = came[i : i + 1]
    return jnp.concatenate([held[k] for k in range(size)])


def reduce_members(x):
    size = lax.axis_size("m")
    held = {k: x[k] for k in range(size)}
    bit = 1
    while bit < size:
        keep = [k for k in sorted(held) if not k & bit]
        sent = jnp.stack([held[k | bit] for k in keep]).astype(BF)
        came = lax.ppermute(sent, "m", xor_perm(bit, size))
        held = {k: held[k].astype(F32) + came[i].astype(F32) for i, k in enumerate(keep)}
        bit *= 2
    return held[0]


def halve(x, axis, bit):
    mine = lax.rem(lax.axis_index(axis) // bit, 2)
    keep = lax.dynamic_index_in_dim(x, mine, 0, False)
    send = lax.dynamic_index_in_dim(x, 1 - mine, 0, False)
    came = lax.ppermute(send.astype(BF), axis, xor_perm(bit, lax.axis_size(axis)))
    return keep.astype(F32) + came.astype(F32)


def butterfly(x):
    for axis in ("fsdp", "m", "h"):
        size = lax.axis_size(axis)
        for bit in bits_of(size):
            x = x + lax.ppermute(x, axis, xor_perm(bit, size))
    return x


class Rows:
    def __init__(self):
        self.split = lax.axis_size("fsdp") == 2 and lax.axis_size("m") % 2 == 0
        self.f = lax.axis_index("fsdp")
        self.core = lax.rem(lax.axis_index("m"), 2)

    def gather(self, w):
        if not self.split:
            return lax.all_gather(w, "fsdp", axis=0, tiled=True)
        half = w.shape[0] // 2
        part = lax.dynamic_slice_in_dim(w, self.core * half, half, 0)
        first = lax.ppermute(part, "fsdp", xor_perm(1, 2))
        second = lax.ppermute(first, "m", xor_perm(1, lax.axis_size("m")))
        return jnp.concatenate([w, first, second])

    def into(self, x):
        if not self.split:
            return x
        half = x.shape[-1] // 2
        low, high = x[..., :half], x[..., half:]
        own = jnp.where(self.f == 0, low, high)
        other = jnp.where(self.f == 0, high, low)
        a, b = other[..., : half // 2], other[..., half // 2 :]
        return jnp.concatenate(
            [own, jnp.where(self.core == 0, a, b), jnp.where(self.core == 0, b, a)], axis=-1
        )

    def back(self, y):
        if not self.split:
            return y
        half = y.shape[-1] // 2
        own, first, second = y[..., :half], y[..., half : half + half // 2], y[..., half + half // 2 :]
        other = jnp.concatenate(
            [jnp.where(self.core == 0, first, second), jnp.where(self.core == 0, second, first)], axis=-1
        )
        return jnp.concatenate(
            [jnp.where(self.f == 0, own, other), jnp.where(self.f == 0, other, own)], axis=-1
        )


def per_device(
    tokens, segments, routes, bucket_table, attn_gain, qkv_weight, out_weight, bias_table,
    moe_gain, router_weight, up_weight, down_weight, cotangent,
):
    tok, width = tokens.shape[1], tokens.shape[2]
    half = tok // 2
    h, m, f = lax.axis_index("h"), lax.axis_index("m"), lax.axis_index("fsdp")
    members, n_fsdp = lax.axis_size("m"), lax.axis_size("fsdp")
    shards = GROUPS * members
    blocks = 2 * shards
    length = shards * tok
    here = EXPERTS // n_fsdp
    spread = here > 1
    ffn = up_weight.shape[2]
    rows_f = width // n_fsdp
    order = Rows()

    qkv_full = order.gather(qkv_weight)
    out_full = order.gather(out_weight)
    pad = jnp.zeros((1, rows_f), BF)
    bias_flat = bias_table.reshape(1, -1)
    bias_rows = -(-bias_flat.shape[1] // rows_f)
    bias_flat = jnp.pad(bias_flat, ((0, 0), (0, bias_rows * rows_f - bias_flat.shape[1])))
    small = jnp.concatenate(
        [attn_gain[None], moe_gain[None], router_weight.T, bias_flat.reshape(bias_rows, rows_f)]
        + [pad] * (16 - 10 - bias_rows)
    )
    small = lax.all_gather(small, "fsdp", axis=0)
    attn_scale = small[:, 0].reshape(width).astype(F32)
    moe_scale = small[:, 1].reshape(width).astype(F32)
    router_t = jnp.transpose(small[:, 2:10], (1, 0, 2)).reshape(EXPERTS, width)
    bias_full = small[:, 10 : 10 + bias_rows].reshape(n_fsdp, -1)[:, : bias_table.size]
    bias_full = bias_full.reshape(BUCKETS, HEADS)

    seg_all = lax.all_to_all(
        jnp.broadcast_to(segments, (shards, tok)), ("h", "m"), 0, 0, tiled=True
    )
    docs = jnp.arange(DOCS, dtype=jnp.int32)
    starts = jnp.sum((seg_all[None] < docs[:, None, None]).astype(jnp.int32), axis=(1, 2))
    seg_q = lax.dynamic_index_in_dim(seg_all.reshape(GROUPS, members, tok), m, 1, False).reshape(-1)
    start_q = jnp.sum(jnp.where(seg_q[:, None] == docs, starts, 0), axis=1)
    owner = jnp.arange(GROUPS, dtype=jnp.int32) * members + m
    block_q = jnp.stack([owner, blocks - 1 - owner], axis=1).reshape(-1)
    first_q = jnp.min(start_q.reshape(2 * GROUPS, half), axis=1) // CHUNK
    info = jnp.stack([block_q, first_q, jnp.full_like(block_q, m)])
    start_col = start_q[:, None]

    wide = strip_width(blocks, half)
    top = half * (blocks - 1)
    line = jnp.concatenate(
        [
            bucket_table[: top + 1][::-1],
            jnp.full((wide - length,), -1, jnp.int32),
            bucket_table[top + 1 :][::-1],
        ]
    )
    hot = (line[None] == jnp.arange(BUCKETS, dtype=jnp.int32)[:, None]).astype(BF)
    bias_mine = lax.dynamic_slice_in_dim(bias_full, h * GHEADS, GHEADS, 1)
    lines = dot(bias_mine, hot, ((0,), (0,))) * LOG2E
    lines = jnp.concatenate([lines, jnp.roll(lines, -half, axis=1)])[:, None]
    strips = make_strips(lines, half)

    hot_routes = (routes.reshape(-1)[:, None] == jnp.arange(EXPERTS)[None]).astype(F32)
    earlier = jnp.arange(tok * TOP)
    earlier = (earlier[None, :] < earlier[:, None]).astype(BF)
    before = dot(earlier, hot_routes.astype(BF))
    slot = jnp.sum(before * hot_routes, axis=1).astype(jnp.int32).reshape(tok, TOP)
    target = (routes % here) * n_fsdp + routes // here
    place = target * CAP + slot
    slots = jnp.arange(EXPERTS * CAP, dtype=jnp.int32)
    pick = [slots[:, None] == place[None, :, k] for k in range(TOP)]
    pick_any = (pick[0] | pick[1]).astype(BF)
    exchange = ("h", "fsdp") if spread else ("fsdp",)

    def deal(rows):
        send = rows.reshape(EXPERTS, CAP, rows.shape[-1])
        return lax.all_to_all(send, exchange, 0, 0, tiled=True).reshape(rows.shape)

    dy_slots = deal(dot(pick_any, cotangent[0]).astype(BF))

    x = tokens[0].astype(F32)
    attn_in = normalize(x, attn_scale).astype(BF)
    proj = dot(order.into(attn_in), qkv_full).astype(BF)
    proj = jnp.transpose(proj.reshape(tok, 3, GROUPS, GWIDTH), (2, 0, 1, 3)).reshape(GROUPS, tok, 3 * GWIDTH)
    proj = lax.all_to_all(proj, "h", 0, 0, tiled=True)
    q = proj[..., :GWIDTH].reshape(GROUPS * tok, GWIDTH)
    kv = gather_members(proj[..., GWIDTH:])
    o_pre, stat = attend(info, q, kv, strips, start_col, blocks)
    context = lax.all_to_all(o_pre.astype(BF).reshape(GROUPS, tok, GWIDTH), "h", 0, 0, tiled=True)
    context = jnp.transpose(context, (1, 0, 2)).reshape(tok, width)
    residual = x + dot(order.into(context), out_full)

    moe_in = normalize(residual, moe_scale).astype(BF)
    logits = dot(moe_in, router_t, ((1,), (1,)))
    route_hot = hot_routes.reshape(tok, TOP, EXPERTS)
    chosen = jnp.sum(logits[:, None, :] * route_hot, axis=-1)
    gates = jax.nn.softmax(chosen, axis=-1)
    gate_slots = sum(
        jnp.sum(jnp.where(pick[k], gates[None, :, k], 0.0), axis=1, keepdims=True) for k in range(TOP)
    )
    high = lax.reduce_precision(gate_slots, 8, 7)
    mid = lax.reduce_precision(gate_slots - high, 8, 7)
    low = gate_slots - high - mid
    extra = jnp.concatenate([high, mid, low, jnp.zeros((slots.shape[0], 125), F32)], axis=1)
    rows_out = jnp.concatenate([dot(pick_any, moe_in).astype(BF), extra.astype(BF)], axis=1)

    came = deal(rows_out)
    rows_in = came[:, :width]
    gate_in = jnp.sum(came[:, width : width + 3].astype(F32), axis=1, keepdims=True)
    mine = h if spread else 0
    up = lax.dynamic_index_in_dim(up_weight, mine, 0, False)
    down = lax.dynamic_index_in_dim(down_weight, mine, 0, False)
    slot_grad = (gate_in * dy_slots.astype(F32)).astype(BF)
    upper = dot(rows_in, up)
    active_grad = dot(slot_grad, down)
    active, upper_grad = gelu_both(upper, active_grad)
    active, upper_grad = active.astype(BF), upper_grad.astype(BF)
    expert_out = dot(active, down, ((1,), (1,))).astype(BF)
    dispatch_grad = dot(upper_grad, up, ((1,), (1,))).astype(BF)
    back = deal(jnp.concatenate([expert_out, dispatch_grad], axis=1))
    result, input_grad = back[:, :width], back[:, width:]

    def members_first(rows):
        if not spread:
            return rows
        cut = rows.reshape(rows.shape[0], GROUPS, members, width // shards)
        return jnp.transpose(cut, (0, 2, 1, 3)).reshape(rows.shape)

    up_term = dot(members_first(rows_in), upper_grad, ((0,), (0,))).astype(BF)
    down_term = dot(members_first(slot_grad), active, ((0,), (0,))).astype(BF)
    terms = jnp.concatenate([up_term, down_term], axis=1)
    terms = lax.psum_scatter(terms, "m" if spread else ("h", "m"), scatter_dimension=0, tiled=True)
    terms = terms.reshape(here, width // shards, 2 * ffn)
    if spread:
        terms = lax.all_to_all(terms, "h", 0, 0, tiled=True)
    up_grad, down_grad = terms[..., :ffn].astype(F32), terms[..., ffn:].astype(F32)

    dy = cotangent[0].astype(F32)
    picked = [dot(pick[k].astype(BF), result, ((0,), (0,))) for k in range(TOP)]
    layer_out = residual + gates[:, :1] * picked[0] + gates[:, 1:] * picked[1]
    gate_grad = jnp.stack([jnp.sum(dy * p, axis=1) for p in picked], axis=1)
    chosen_grad = gates * (gate_grad - jnp.sum(gates * gate_grad, axis=1, keepdims=True))
    logit_grad = jnp.sum(chosen_grad[:, :, None] * route_hot, axis=1)
    router_grad = lax.dot_general(
        logit_grad, moe_in.astype(F32), (((0,), (0,)), ((), ())), precision=FULL
    )
    moe_in_grad = lax.dot_general(
        logit_grad, router_t.astype(F32), (((1,), (0,)), ((), ())), precision=FULL
    )
    moe_in_grad = moe_in_grad + dot(pick_any, input_grad, ((0,), (0,)))
    norm_grad, moe_gain_grad = jax.vjp(normalize, residual, moe_scale)[1](moe_in_grad)
    resid_grad = dy + norm_grad
    attn_grad = resid_grad.astype(BF)

    out_term = dot(attn_grad, context, ((0,), (0,))).astype(BF)
    out_term = lax.psum_scatter(out_term, ("h", "m"), scatter_dimension=0, tiled=True)
    out_term = lax.psum_scatter(out_term.T, "fsdp", scatter_dimension=0, tiled=True)
    out_grad = out_term.astype(F32)
    do = order.back(dot(attn_grad, out_full, ((1,), (1,)))).astype(BF)
    do = jnp.transpose(do.reshape(tok, GROUPS, GWIDTH), (1, 0, 2))
    do = lax.all_to_all(do, "h", 0, 0, tiled=True).reshape(GROUPS * tok, GWIDTH)

    dq, dkv, dline = attend_back(info, q, kv, strips, start_col, do, o_pre, stat, blocks)
    dkv = reduce_members(dkv).astype(BF)
    dproj = jnp.concatenate([dq.reshape(GROUPS, tok, GWIDTH), dkv], axis=2)
    bias_mine = lax.dot_general(
        hot.astype(F32), dline, (((1,), (1,)), ((), ())), precision=FULL
    )

    ain = lax.all_gather(attn_in, "h", axis=0).reshape(GROUPS * tok, width)
    flat = dproj.reshape(GROUPS * tok, 3 * GWIDTH)
    term = dot(flat, ain, ((0,), (0,)))
    unit = GWIDTH // members
    term = term.reshape(3, members, unit, width)
    for bit in bits_of(members):
        cut = jnp.transpose(term.reshape(3, 2, -1, unit, width), (1, 0, 2, 3, 4))
        term = halve(cut, "m", bit)
    for bit in bits_of(n_fsdp):
        cut = jnp.stack(jnp.split(term, 2, axis=-1))
        term = halve(cut, "fsdp", bit)
    term = term.reshape(3, unit, rows_f).astype(BF)
    me = h * members + m
    parts = []
    for r in range(3):
        source = [((3 * d + r) % shards, d) for d in range(shards)]
        target_of = [0] * shards
        for s, d in source:
            target_of[s] = (3 * d + r) // shards
        which = jnp.sum(jnp.where(jnp.arange(shards) == me, jnp.asarray(target_of), 0))
        send = lax.dynamic_index_in_dim(term, which, 0, False)
        parts.append(lax.ppermute(send, ("h", "m"), source))
    qkv_grad = jnp.concatenate(parts).astype(F32).T

    dproj = lax.all_to_all(dproj, "h", 0, 0, tiled=True)
    dproj = jnp.transpose(dproj.reshape(GROUPS, tok, 3, GWIDTH), (1, 2, 0, 3)).reshape(tok, 3 * width)
    attn_in_grad = order.back(dot(dproj, qkv_full, ((1,), (1,))))
    token_grad, attn_gain_grad = jax.vjp(normalize, x, attn_scale)[1](attn_in_grad)
    tokens_grad = (resid_grad + token_grad).astype(BF)

    bias_own = lax.dynamic_update_slice_in_dim(jnp.zeros((BUCKETS, HEADS), F32), bias_mine, h * GHEADS, 1)
    pack = jnp.concatenate(
        [router_grad, attn_gain_grad[None], moe_gain_grad[None]]
        + [jnp.pad(bias_own.reshape(1, -1), ((0, 0), (0, width - bias_own.size)))]
    )
    pack = butterfly(pack)
    mine_f = lax.dynamic_slice_in_dim(pack[:10], f * rows_f, rows_f, 1)
    bias_grad = pack[10, : bias_own.size].reshape(BUCKETS, HEADS)
    bias_grad = lax.dynamic_slice_in_dim(bias_grad, f * (BUCKETS // n_fsdp), BUCKETS // n_fsdp, 0)
    return (
        layer_out.astype(BF)[None],
        tokens_grad[None],
        mine_f[8],
        qkv_grad,
        out_grad,
        bias_grad,
        mine_f[9],
        mine_f[:8].T,
        up_grad,
        down_grad,
    )


def solution(mesh):
    n_ctx, n_fsdp = mesh.shape["ctx"], mesh.shape["fsdp"]
    cut = Mesh(mesh.devices.reshape(GROUPS, n_ctx // GROUPS, n_fsdp), ("h", "m", "fsdp"))
    ctx = ("h", "m")
    return jax.shard_map(
        per_device,
        mesh=cut,
        in_specs=(
            P("fsdp", ctx, None),
            P("fsdp", ctx),
            P(("h", "m", "fsdp"), None),
            P(),
            P("fsdp"),
            P("fsdp", None),
            P("fsdp", None),
            P("fsdp", None),
            P("fsdp"),
            P("fsdp", None),
            P("fsdp", None, None),
            P("fsdp", None, None),
            P("fsdp", ctx, None),
        ),
        out_specs=(
            P("fsdp", ctx, None),
            P("fsdp", ctx, None),
            P("fsdp"),
            P("fsdp", ctx),
            P("fsdp", ctx),
            P("fsdp", None),
            P("fsdp"),
            P("fsdp", None),
            P("fsdp", ctx, None),
            P("fsdp", ctx, None),
        ),
        check_vma=False,
    )
```

time: 7140 us -> 463 us (0.06)
  local copies, waits for them, and re-layouts: 4520 us -> 65.8 us
  waiting for transfers between devices: 2150 us -> 92.3 us
  matrix products: 227 us -> 45.1 us
  starting transfers between devices: 0.94 us -> 77.1 us
    gather x53 -> x0, local copies, waits for them, and re-layouts: 4360 us -> none  [the longest x48 4350 us: pair_terms(): buckets = jnp.take(bucket_table, distance, axis=0)]
    unnamed x21 -> x4, waiting for transfers between devices: 1690 us -> 0.05 us
    reduce_scatter x3 -> x2, waiting for transfers between devices: 370 us -> 55.2 us  [the longest x1 55.2 us: per_device(): lax.psum_scatter(out_term, ('h', 'm'), scatter_dimension=0, tiled=True)]
    dot_general x207 -> x23, matrix products: 227 us -> 45.1 us  [the longest x20 42.1 us: dot(): return lax.dot_general(a, b, (dims, ((), ())), preferred_element_type=F32)]
    all_gather x8 -> x0, waiting for transfers between devices: 92.4 us -> none  [the longest x1 45.7 us: per_device(): lax.all_gather(qkv_weight, 'fsdp', axis=0, tiled=True)]
  transfers between devices with their start and end apart: 16 -> 29, of which waited for: 7 -> 12; matrix products, arithmetic and copies ran while one was open for 68% -> 21% of each run, Pallas kernels for 0% -> 11%
where the time goes in v1:
time: 463 us; the launch traced here: 455 us
  waiting for transfers between devices  92.3 us (20%)
  starting transfers between devices  77.1 us (17%)
  blocking collectives  71.5 us (15%)
  local copies, waits for them, and re-layouts  65.8 us (14%)
  Pallas kernels  50.8 us (11%)
  matrix products  45.1 us (10%)
  other arithmetic  32.1 us (7%)
  between operations  20.7 us (4%)
    reduce_scatter x1, waiting for transfers between devices, per_device(): lax.psum_scatter(out_term, ('h', 'm'), scatter_dimension=0, tiled=True)  55.2 us
    dot_general x20, matrix products, dot(): return lax.dot_general(a, b, (dims, ((), ())), preferred_element_type=F32)  42.1 us
    all_to_all x1, blocking collectives, deal(): return lax.all_to_all(send, exchange, 0, 0, tiled=True).reshape(rows.shape)  27.5 us
    pallas_call x1, Pallas kernels, attend_back(): pl.pallas_call(functools.partial(backward_kernel, half, blocks), grid_spe...  27.3 us
    pallas_call x1, Pallas kernels, attend(): pl.pallas_call(functools.partial(forward_kernel, half, blocks), grid_spec...  18.9 us
    all_gather x1, blocking collectives, per_device(): small = lax.all_gather(small, 'fsdp', axis=0)  18.4 us
    unnamed x109, local copies, waits for them, and re-layouts  17.6 us
    all_gather x1, blocking collectives, per_device(): ain = lax.all_gather(attn_in, 'h', axis=0).reshape(GROUPS * tok, width)  15.5 us
  transfers between devices with their start and end apart: 29, of which 12 were waited for; matrix products, arithmetic and copies ran while one was open for 21% of the time, Pallas kernels for 11%

profile of v1, /device:TPU:11, one launch (start us, length us, event | category | flops | bytes accessed | tf_op | source)
XLA Modules:
  0.0 455.4 jit_solution(12092906457080298752)
XLA Ops:
  7.2 1.8 constant_dynamic-slice_fusion.1
  15.7 2.2 concatenate.81
  17.9 18.4 %all-gather = bf16[32,384]{1,0:T(8,128)(2,1)S(1)} all-gather(bf16[16,384]{1,0:T(8,128)(2,1)S(1)} %concatenate.81), channel_id=2, replica_groups=mesh['h'=4,'m'=4,'fsdp'=2] {'fsdp'}, dimensions={0}, use_global_device_ids=true | all-gather | bytes 36864 | tf_op jit(solution)/shard_map/all_gather | solution.py:388
  55.8 1.8 collective-permute-done.1
  57.6 1.8 copy-done.6
  61.3 4.7 %all-to-all-start.1 = ((bf16[4,128,576]{1,2,0:T(8,128)(2,1)}), bf16[4,128,576]{1,2,0:T(8,128)(2,1)S(1)}, u32[]{:S(2)}, u32[]{:S(2)}) async-start(bf16[4,128,576]{1,2,0:T(8,128)(2,1)} %bitcast.10), calls=%async_computation.1 | async-start | bytes 1179648 | tf_op jit(solution)/shard_map/all_to_all | solution.py:445
  66.5 11.9 %all-to-all-done.1 = bf16[4,128,576]{1,2,0:T(8,128)(2,1)S(1)} async-done(((bf16[4,128,576]{1,2,0:T(8,128)(2,1)}), bf16[4,128,576]{1,2,0:T(8,128)(2,1)S(1)}, u32[]{:S(2)}, u32[]{:S(2)}) %all-to-all-start.1) | async-done | bytes 589856 | tf_op jit(solution)/shard_map/all_to_all | solution.py:445
  79.0 8.2 %all-to-all-start = ((s32[16,1,128]{2,1,0:T(1,128)}), s32[16,1,128]{2,1,0:T(1,128)S(1)}, u32[]{:S(2)}, u32[]{:S(2)}) async-start(s32[16,1,128]{2,1,0:T(1,128)} %broadcast_in_dim.103), calls=%async_computation | async-start | bytes 16384 | tf_op jit(solution)/shard_map/all_to_all | solution.py:395
  89.6 4.6 %shard_map.234.strip_ref = f32[6,64,2304]{2,1,0:T(8,128)} custom-call(f32[6,1,2304]{2,1,0:T(1,128)} %broadcast_in_dim.110.g_ref), custom_call_target="tpu_custom_call" | custom-call | tf_op jit(solution)/shard_map/pallas_call | solution.py:68
  95.4 2.5 collective-permute-done.2
  103.6 18.9 %attend.1 = (f32[512,192]{1,0:T(8,128)S(1)}, f32[512,8]{1,0:T(8,128)S(1)}) custom-call(s32[3,8]{1,0:T(4,128)S(1)} %add_add_fusion.2.info, bf16[512,192]{1,0:T(8,128)(2,1)S(1)} %bitcast.187, bf16[4,4,128,384]{3,2,1,0:T(8,128)(2,1)S(1)} %pad_maximum_fusion.1.kv_ref, f32[6,64,2304]{2,1,0:T(8,128)} %shard_map.234.strip_ref, s32[512,1]{1,0:T(8,128)S(1)} %copy.203.start_ref), custom_call_target="tpu_custom_call" | custom-call | tf_op jit(solution)/shard_map/attend/pallas_call | solution.py:231
  124.1 4.5 all-to-all-start.2
  128.6 1.9 constant_dynamic-update-slice_fusion.5
  130.6 1.7 constant_dynamic-update-slice_fusion.4
  132.3 1.7 constant_dynamic-update-slice_fusion.3
  134.0 8.1 %all-to-all-start.4 = ((bf16[8,40,768]{2,1,0:T(8,128)(2,1)}), bf16[8,40,768]{2,1,0:T(8,128)(2,1)S(1)}, u32[]{:S(2)}, u32[]{:S(2)}) async-start(bf16[8,40,768]{2,1,0:T(8,128)(2,1)} %bitcast.28), calls=%async_computation.4 | async-start | bytes 983040 | tf_op jit(solution)/shard_map/all_to_all | solution.py:437
  146.8 4.8 %all-to-all-done.4 = bf16[8,40,768]{2,1,0:T(8,128)(2,1)S(1)} async-done(((bf16[8,40,768]{2,1,0:T(8,128)(2,1)}), bf16[8,40,768]{2,1,0:T(8,128)(2,1)S(1)}, u32[]{:S(2)}, u32[]{:S(2)}) %all-to-all-start.4) | async-done | bytes 491552 | tf_op jit(solution)/shard_map/all_to_all | solution.py:437
  151.6 6.2 %all-to-all-start.3 = ((bf16[8,40,896]{2,1,0:T(8,128)(2,1)}), bf16[8,40,896]{2,1,0:T(8,128)(2,1)}, u32[]{:S(2)}, u32[]{:S(2)}) async-start(bf16[8,40,896]{2,1,0:T(8,128)(2,1)} %bitcast.23), calls=%async_computation.3 | async-start | bytes 1146880 | tf_op jit(solution)/shard_map/all_to_all | solution.py:437
  157.8 3.7 reshape.484
  161.6 8.1 %all-to-all-done.3 = bf16[8,40,896]{2,1,0:T(8,128)(2,1)} async-done(((bf16[8,40,896]{2,1,0:T(8,128)(2,1)}), bf16[8,40,896]{2,1,0:T(8,128)(2,1)}, u32[]{:S(2)}, u32[]{:S(2)}) %all-to-all-start.3) | async-done | bytes 573472 | tf_op jit(solution)/shard_map/all_to_all | solution.py:437
  170.6 1.8 slice.217
  174.2 2.8 copy.229
  178.4 11.2 %multiply_convert_fusion = (bf16[320,3072]{1,0:T(8,128)(2,1)S(1)}, f32[320,3072]{1,0:T(8,128)S(1)}, f32[320,3072]{1,0:T(8,128)S(1)}) fusion(bf16[4,768,3072]{2,1,0:T(8,128)(2,1)} %param.26, s32[]{:T(128)S(6)} %select_n.200, bf16[320,896]{1,0:T(8,128)(2,1)} %bitcast.24), kind=kOutput, calls=%fused_computation.18 | convolution fusion | flops 1573847040 | bytes 15040516 | tf_op jit(solution)/shard_map/dot_general | solution.py:36
  189.6 2.8 convolution_convert_fusion
  192.6 5.2 %add_convert_fusion = bf16[320,3072]{1,0:T(8,128)(2,1)S(1)} fusion(f32[320,3072]{1,0:T(8,128)S(1)} %get-tuple-element.33, f32[320,3072]{1,0:T(8,128)S(1)} %get-tuple-element.69, bf16[320,768]{1,0:T(8,128)(2,1)S(1)} %bitcast.213, bf16[4,768,3072]{2,1,0:T(8,128)(2,1)} %param.27, s32[]{:T(128)S(6)} %select_n.200), kind=kOutput, calls=%fused_computation.17 | convolution fusion | flops 1523712000 | bytes 15040516 | tf_op jit(solution)/shard_map/dot_general | solution.py:36
  197.8 2.8 convolution_convert_fusion.1
  200.7 4.0 pad_maximum_fusion
  206.2 4.2 fusion.21
  210.4 4.1 fusion.24
  214.6 27.5 %all_to_all.46 = bf16[8,40,1536]{2,1,0:T(8,128)(2,1)S(1)} all-to-all(bf16[8,40,1536]{2,1,0:T(8,128)(2,1)S(1)} %bitcast.192), channel_id=1, replica_groups=mesh['h'=4,'m'=4,'fsdp'=2] {'h','fsdp'}, dimensions={0} | all-to-all | bytes 1966080 | tf_op jit(solution)/shard_map/all_to_all | solution.py:437
  245.7 10.1 %all_to_all.47 = bf16[4,128,192]{1,2,0:T(8,128)(2,1)S(1)} all-to-all(bf16[4,128,192]{1,2,0:T(8,128)(2,1)S(1)} %maximum_bitcast_fusion.1), channel_id=1, replica_groups=mesh['h'=4,'m'=4,'fsdp'=2] {'h'}, dimensions={0} | all-to-all | bytes 393216 | tf_op jit(solution)/shard_map/all_to_all | solution.py:521
  256.6 27.3 %attend_back.1 = (bf16[512,192]{1,0:T(8,128)(2,1)}, bf16[4,4,128,384]{3,2,1,0:T(8,128)(2,1)}, f32[3,2304]{1,0:T(4,128)}) custom-call(s32[3,8]{1,0:T(4,128)} %copy-done.5, bf16[512,192]{1,0:T(8,128)(2,1)} %bitcast.188, bf16[4,4,128,384]{3,2,1,0:T(8,128)(2,1)} %copy-done, f32[6,64,2304]{2,1,0:T(8,128)} %shard_map.234.strip_ref, s32[512,1]{1,0:T(8,128)} %copy-done.2, ...), custom_call_target="tpu_custom_call" | custom-call | tf_op jit(solution)/shard_map/attend_back/pallas_call | solution.py:254
  285.3 5.6 %collective-permute-start.6 = (bf16[2,4,128,384]{3,2,1,0:T(8,128)(2,1)S(1)}, bf16[2,4,128,384]{3,2,1,0:T(8,128)(2,1)S(1)}, u32[]{:S(2)}, u32[]{:S(2)}) collective-permute-start(bf16[2,4,128,384]{3,2,1,0:T(8,128)(2,1)S(1)} %pad_maximum_fusion.4), channel_id=1, source_target_pairs={{0,2},{2,0},{4,6},{6,4},{1,3},{3,1},{5,7},{7,5},{8,10},{10,8},{12,... | collective-permute-start | bytes 2359304 | tf_op jit(solution)/shard_map/ppermute | solution.py:299
  291.0 1.8 collective-permute-done.6
  296.2 15.5 %all_gather.12 = bf16[4,128,768]{2,1,0:T(8,128)(2,1)S(1)} all-gather(bf16[1,128,768]{2,1,0:T(8,128)(2,1)S(1)} %fusion.46), channel_id=1, replica_groups=mesh['h'=4,'m'=4,'fsdp'=2] {'h'}, dimensions={0}, use_global_device_ids=true | all-gather | bytes 983040 | tf_op jit(solution)/shard_map/all_gather | solution.py:530
  314.3 1.7 fusion.125
  320.2 5.9 %all-to-all-start.7 = ((bf16[4,128,576]{1,2,0:T(8,128)(2,1)}), bf16[4,128,576]{1,2,0:T(8,128)(2,1)S(1)}, u32[]{:S(2)}, u32[]{:S(2)}) async-start(bf16[4,128,576]{1,2,0:T(8,128)(2,1)} %copy.222), calls=%async_computation.7 | async-start | bytes 1179648 | tf_op jit(solution)/shard_map/all_to_all | solution.py:554
  335.7 2.7 collective-permute-start.14
  340.0 6.8 %all-to-all-start.8 = ((bf16[4,48,6144]{2,1,0:T(8,128)(2,1)}), bf16[4,48,6144]{2,1,0:T(8,128)(2,1)}, u32[]{:S(2)}, u32[]{:S(2)}) async-start(bf16[4,48,6144]{2,1,0:T(8,128)(2,1)} %bitcast.200), calls=%async_computation.10 | async-start | bytes 4718592 | tf_op jit(solution)/shard_map/all_to_all | solution.py:495
  349.4 3.8 collective-permute-start.15
  357.8 55.2 %reduce-scatter.6.cloned.1.call-done = bf16[48,768]{1,0:T(8,128)(2,1)} async-done(((bf16[768,768]{1,0:T(8,128)(2,1)}), bf16[48,768]{1,0:T(8,128)(2,1)}) %reduce-scatter.6.cloned.1.call-update) | async-done | bytes 73744 | tf_op jit(solution)/shard_map/reduce_scatter | solution.py:516
  413.0 1.7 copy.232
  420.3 2.0 collective-permute-start.18
  422.3 4.9 %collective-permute-start.17 = (bf16[48,384]{1,0:T(8,128)(2,1)S(1)}, bf16[48,384]{1,0:T(8,128)(2,1)S(1)}, u32[]{:S(2)}, u32[]{:S(2)}) collective-permute-start(bf16[48,384]{1,0:T(8,128)(2,1)S(1)} %get-tuple-element.57), channel_id=1, source_target_pairs={{2,0},{8,2},{14,4},{20,6},{26,8},{0,10},{6,12},{12,14},{18,16},{24... | collective-permute-start | bytes 110600 | tf_op jit(solution)/shard_map/ppermute | solution.py:551
  427.3 2.9 collective-permute-start.16
  436.7 2.8 collective-permute-done.11
  440.1 1.9 fusion.70
  444.5 4.4 slice_convert_fusion
  (298 shorter events, 93.4 us)
Async XLA Ops:
  7.2 48.4 %copy-start.14 = (bf16[384,2304]{1,0:T(8,128)(2,1)S(1)}, bf16[384,2304]{1,0:T(8,128)(2,1)}, u32[]{:S(2)}) copy-start(bf16[384,2304]{1,0:T(8,128)(2,1)} %param.21) | copy-start | bytes 5308420
  9.0 91.9 %collective-permute-start.4 = (bf16[192,768]{1,0:T(8,128)(2,1)}, bf16[192,768]{1,0:T(8,128)(2,1)}, u32[]{:S(2)}, u32[]{:S(2)}) collective-permute-start(bf16[192,768]{1,0:T(8,128)(2,1)} %constant_dynamic-slice_fusion.1), channel_id=1, source_target_pairs={{0,1},{1,0},{2,3},{3,2},{4,5},{5,4},{6,7},{7,6},{8,9},{9,8},{10,11... | collective-permute-start | bytes 884744 | tf_op jit(solution)/shard_map/ppermute | solution.py:332
  10.5 43.4 %collective-permute-start = (bf16[192,2304]{1,0:T(8,128)(2,1)S(1)}, bf16[192,2304]{1,0:T(8,128)(2,1)S(1)}, u32[]{:S(2)}, u32[]{:S(2)}) collective-permute-start(bf16[192,2304]{1,0:T(8,128)(2,1)S(1)} %constant_dynamic-slice_fusion.2), channel_id=1, source_target_pairs={{0,1},{1,0},{2,3},{3,2},{4,5},{5,4},{6,7},{7,6},{8,9},{9,8},{10,11... | collective-permute-start | bytes 2654216 | tf_op jit(solution)/shard_map/ppermute | solution.py:332
  52.8 238.1 %copy-start.37 = (f32[128]{0:T(128)}, f32[128]{0:T(128)S(1)}, u32[]{:S(2)}) copy-start(f32[128]{0:T(128)S(1)} %fusion.110) | copy-start | bytes 1540
  53.9 3.7 collective-permute-start.1
  59.5 18.9 %copy-start.40 = (s32[1,128]{1,0:T(1,128)S(1)}, s32[1,128]{1,0:T(1,128)}, u32[]{:S(2)}) copy-start(s32[1,128]{1,0:T(1,128)} %param.17) | copy-start | bytes 1540
  60.5 33.9 %copy-start.21 = (bf16[1,128,768]{2,1,0:T(8,128)(2,1)S(1)}, bf16[1,128,768]{2,1,0:T(8,128)(2,1)}, u32[]{:S(2)}) copy-start(bf16[1,128,768]{2,1,0:T(8,128)(2,1)} %param.28) | copy-start | bytes 589828
  61.3 17.1 %all-to-all-start.1 = ((bf16[4,128,576]{1,2,0:T(8,128)(2,1)}), bf16[4,128,576]{1,2,0:T(8,128)(2,1)S(1)}, u32[]{:S(2)}, u32[]{:S(2)}) async-start(bf16[4,128,576]{1,2,0:T(8,128)(2,1)} %bitcast.10), calls=%async_computation.1 | async-start | bytes 1179648 | tf_op jit(solution)/shard_map/all_to_all | solution.py:445
  79.0 21.1 %all-to-all-start = ((s32[16,1,128]{2,1,0:T(1,128)}), s32[16,1,128]{2,1,0:T(1,128)S(1)}, u32[]{:S(2)}, u32[]{:S(2)}) async-start(s32[16,1,128]{2,1,0:T(1,128)} %broadcast_in_dim.103), calls=%async_computation | async-start | bytes 16384 | tf_op jit(solution)/shard_map/all_to_all | solution.py:395
  87.4 10.5 %collective-permute-start.2 = (bf16[1,4,128,384]{3,2,1,0:T(8,128)(2,1)S(1)}, bf16[1,4,128,384]{3,2,1,0:T(8,128)(2,1)S(1)}, u32[]{:S(2)}, u32[]{:S(2)}) collective-permute-start(bf16[1,4,128,384]{3,2,1,0:T(8,128)(2,1)S(1)} %bitcast.193), channel_id=1, source_target_pairs={{0,4},{2,6},{4,0},{6,2},{1,5},{3,7},{5,1},{7,3},{8,12},{10,14},{12... | collective-permute-start | bytes 1179656 | tf_op jit(solution)/shard_map/ppermute | solution.py:286
  99.0 3.3 collective-permute-start.3
  100.8 21.7 %copy-start.2 = (s32[512,1]{1,0:T(8,128)}, s32[512,1]{1,0:T(8,128)S(1)}, u32[]{:S(2)}) copy-start(s32[512,1]{1,0:T(8,128)S(1)} %copy.203.start_ref) | copy-start | bytes 6148
  100.9 21.6 %copy-start.5 = (s32[3,8]{1,0:T(4,128)}, s32[3,8]{1,0:T(4,128)S(1)}, u32[]{:S(2)}) copy-start(s32[3,8]{1,0:T(4,128)S(1)} %add_add_fusion.2.info) | copy-start | bytes 292
  100.9 31.4 %collective-permute-start.5 = (bf16[192,768]{1,0:T(8,128)(2,1)}, bf16[192,768]{1,0:T(8,128)(2,1)}, u32[]{:S(2)}, u32[]{:S(2)}) collective-permute-start(bf16[192,768]{1,0:T(8,128)(2,1)} %collective-permute-done.4), channel_id=1, source_target_pairs={{0,2},{2,0},{4,6},{6,4},{1,3},{3,1},{5,7},{7,5},{8,10},{10,8},{12,... | collective-permute-start | bytes 884744 | tf_op jit(solution)/shard_map/ppermute | solution.py:333
  101.1 21.4 %copy-start.1 = (bf16[4,128,192]{2,1,0:T(8,128)(2,1)}, bf16[4,128,192]{2,1,0:T(8,128)(2,1)S(1)}, u32[]{:S(2)}) copy-start(bf16[4,128,192]{2,1,0:T(8,128)(2,1)S(1)} %copy.200) | copy-start | bytes 589828
  103.6 27.0 %copy-start = (bf16[4,4,128,384]{3,2,1,0:T(8,128)(2,1)}, bf16[4,4,128,384]{3,2,1,0:T(8,128)(2,1)S(1)}, u32[]{:S(2)}) copy-start(bf16[4,4,128,384]{3,2,1,0:T(8,128)(2,1)S(1)} %pad_maximum_fusion.1.kv_ref) | copy-start | bytes 4718596
  103.6 26.9 %copy-start.34 = (bf16[32,384]{1,0:T(8,128)(2,1)S(1)}, bf16[32,384]{1,0:T(8,128)(2,1)}, u32[]{:S(2)}) copy-start(bf16[32,384]{1,0:T(8,128)(2,1)} %copy-done.33) | copy-start | bytes 73732
  103.6 26.9 %copy-start.35 = (f32[2,384]{1,0:T(2,128)S(1)}, f32[2,384]{1,0:T(2,128)}, u32[]{:S(2)}) copy-start(f32[2,384]{1,0:T(2,128)} %get-tuple-element.30) | copy-start | bytes 9220
  123.2 21.0 %copy-start.3 = (f32[512,192]{1,0:T(8,128)}, f32[512,192]{1,0:T(8,128)S(1)}, u32[]{:S(2)}) copy-start(f32[512,192]{1,0:T(8,128)S(1)} %get-tuple-element.15.o_ref) | copy-start | bytes 1179652
  123.2 19.3 %copy-start.9 = (bf16[1,128,768]{2,1,0:T(8,128)(2,1)S(1)}, bf16[1,128,768]{2,1,0:T(8,128)(2,1)}, u32[]{:S(2)}) copy-start(bf16[1,128,768]{2,1,0:T(8,128)(2,1)} %param.16) | copy-start | bytes 589828
  124.1 9.9 %all-to-all-start.2 = ((bf16[4,128,192]{1,2,0:T(8,128)(2,1)}), bf16[4,128,192]{1,2,0:T(8,128)(2,1)S(1)}, u32[]{:S(2)}, u32[]{:S(2)}) async-start(bf16[4,128,192]{1,2,0:T(8,128)(2,1)} %copy.204), calls=%async_computation.2 | async-start | bytes 393216 | tf_op jit(solution)/shard_map/all_to_all | solution.py:449
  134.0 17.6 %all-to-all-start.4 = ((bf16[8,40,768]{2,1,0:T(8,128)(2,1)}), bf16[8,40,768]{2,1,0:T(8,128)(2,1)S(1)}, u32[]{:S(2)}, u32[]{:S(2)}) async-start(bf16[8,40,768]{2,1,0:T(8,128)(2,1)} %bitcast.28), calls=%async_computation.4 | async-start | bytes 983040 | tf_op jit(solution)/shard_map/all_to_all | solution.py:437
  144.4 13.4 %copy-start.15 = (bf16[128,768]{1,0:T(8,128)(2,1)}, bf16[128,768]{1,0:T(8,128)(2,1)S(1)}, u32[]{:S(2)}) copy-start(bf16[128,768]{1,0:T(8,128)(2,1)S(1)} %multiply_convert_fusion.3) | copy-start | bytes 589828
  151.6 18.0 %all-to-all-start.3 = ((bf16[8,40,896]{2,1,0:T(8,128)(2,1)}), bf16[8,40,896]{2,1,0:T(8,128)(2,1)}, u32[]{:S(2)}, u32[]{:S(2)}) async-start(bf16[8,40,896]{2,1,0:T(8,128)(2,1)} %bitcast.23), calls=%async_computation.3 | async-start | bytes 1146880 | tf_op jit(solution)/shard_map/all_to_all | solution.py:437
  157.8 181.4 %reduce-scatter.8.cloned.1.call-start = ((), (), s32[]{:S(2)}) async-start(), calls=%async_computation.13 | async-start | bytes 11796480 | tf_op jit(solution)/shard_map/reduce_scatter | solution.py:492
  214.6 30.1 %copy-start.8 = (bf16[768,768]{1,0:T(8,128)(2,1)S(1)}, bf16[768,768]{1,0:T(8,128)(2,1)}, u32[]{:S(2)}) copy-start(bf16[768,768]{1,0:T(8,128)(2,1)} %constant_dynamic-update-slice_fusion.3) | copy-start | bytes 3538948
  244.6 81.6 %copy-start.11 = (f32[128,768]{1,0:T(8,128)}, f32[128,768]{1,0:T(8,128)S(1)}, u32[]{:S(2)}) copy-start(f32[128,768]{1,0:T(8,128)S(1)} %convert_add_fusion) | copy-start | bytes 1179652
  283.9 29.1 %copy-start.25 = (bf16[512,192]{1,0:T(8,128)(2,1)S(1)}, bf16[512,192]{1,0:T(8,128)(2,1)}, u32[]{:S(2)}) copy-start(bf16[512,192]{1,0:T(8,128)(2,1)} %get-tuple-element.17) | copy-start | bytes 589828
  285.3 7.5 %collective-permute-start.6 = (bf16[2,4,128,384]{3,2,1,0:T(8,128)(2,1)S(1)}, bf16[2,4,128,384]{3,2,1,0:T(8,128)(2,1)S(1)}, u32[]{:S(2)}, u32[]{:S(2)}) collective-permute-start(bf16[2,4,128,384]{3,2,1,0:T(8,128)(2,1)S(1)} %pad_maximum_fusion.4), channel_id=1, source_target_pairs={{0,2},{2,0},{4,6},{6,4},{1,3},{3,1},{5,7},{7,5},{8,10},{10,8},{12,... | collective-permute-start | bytes 2359304 | tf_op jit(solution)/shard_map/ppermute | solution.py:299
  294.1 17.5 %collective-permute-start.7 = (bf16[1,4,128,384]{3,2,1,0:T(8,128)(2,1)S(1)}, bf16[1,4,128,384]{3,2,1,0:T(8,128)(2,1)S(1)}, u32[]{:S(2)}, u32[]{:S(2)}) collective-permute-start(bf16[1,4,128,384]{3,2,1,0:T(8,128)(2,1)S(1)} %add_convert_fusion.2), channel_id=1, source_target_pairs={{0,4},{2,6},{4,0},{6,2},{1,5},{3,7},{5,1},{7,3},{8,12},{10,14},{12... | collective-permute-start | bytes 1179656 | tf_op jit(solution)/shard_map/ppermute | solution.py:299
  314.3 11.9 %copy-start.23 = (bf16[4,128,192]{1,2,0:T(8,128)(2,1)S(1)}, bf16[4,128,192]{1,2,0:T(8,128)(2,1)}, u32[]{:S(2)}) copy-start(bf16[4,128,192]{1,2,0:T(8,128)(2,1)} %copy-done.22) | copy-start | bytes 589828
  316.9 16.1 %collective-permute-start.13 = (bf16[3,2,48,768]{3,2,1,0:T(8,128)(2,1)}, bf16[3,2,48,768]{3,2,1,0:T(8,128)(2,1)}, u32[]{:S(2)}, u32[]{:S(2)}) collective-permute-start(bf16[3,2,48,768]{3,2,1,0:T(8,128)(2,1)} %fusion.36), channel_id=1, source_target_pairs={{0,4},{2,6},{4,0},{6,2},{1,5},{3,7},{5,1},{7,3},{8,12},{10,14},{12... | collective-permute-start | bytes 1327112 | tf_op jit(solution)/shard_map/ppermute | solution.py:309
  319.1 19.3 %copy-start.16 = (bf16[128,768]{1,0:T(8,128)(2,1)S(1)}, bf16[128,768]{1,0:T(8,128)(2,1)}, u32[]{:S(2)}) copy-start(bf16[128,768]{1,0:T(8,128)(2,1)} %copy-done.15) | copy-start | bytes 589828
  320.2 19.0 %all-to-all-start.7 = ((bf16[4,128,576]{1,2,0:T(8,128)(2,1)}), bf16[4,128,576]{1,2,0:T(8,128)(2,1)S(1)}, u32[]{:S(2)}, u32[]{:S(2)}) async-start(bf16[4,128,576]{1,2,0:T(8,128)(2,1)} %copy.222), calls=%async_computation.7 | async-start | bytes 1179648 | tf_op jit(solution)/shard_map/all_to_all | solution.py:554
  326.2 86.8 %reduce-scatter.6.cloned.1.call-start = ((), (), s32[]{:S(2)}) async-start(), calls=%async_computation.12 | async-start | bytes 1253376 | tf_op jit(solution)/shard_map/reduce_scatter | solution.py:516
  335.7 11.2 %collective-permute-start.14 = (bf16[3,1,48,768]{3,2,1,0:T(8,128)(2,1)}, bf16[3,1,48,768]{3,2,1,0:T(8,128)(2,1)}, u32[]{:S(2)}, u32[]{:S(2)}) collective-permute-start(bf16[3,1,48,768]{3,2,1,0:T(8,128)(2,1)} %dynamic-slice_convert_fusion.1), channel_id=1, source_target_pairs={{0,2},{2,0},{4,6},{6,4},{1,3},{3,1},{5,7},{7,5},{8,10},{10,8},{12,... | collective-permute-start | bytes 663560 | tf_op jit(solution)/shard_map/ppermute | solution.py:309
  340.0 76.9 %copy-start.7 = (bf16[768,2304]{1,0:T(8,128)(2,1)S(1)}, bf16[768,2304]{1,0:T(8,128)(2,1)}, u32[]{:S(2)}) copy-start(bf16[768,2304]{1,0:T(8,128)(2,1)} %copy-done.6) | copy-start | bytes 10616836
  340.0 104.5 %all-to-all-start.8 = ((bf16[4,48,6144]{2,1,0:T(8,128)(2,1)}), bf16[4,48,6144]{2,1,0:T(8,128)(2,1)}, u32[]{:S(2)}, u32[]{:S(2)}) async-start(bf16[4,48,6144]{2,1,0:T(8,128)(2,1)} %bitcast.200), calls=%async_computation.10 | async-start | bytes 4718592 | tf_op jit(solution)/shard_map/all_to_all | solution.py:495
  346.8 84.1 %reduce-scatter.10.cloned.1.call-start = ((), (), s32[]{:S(2)}) async-start(), calls=%async_computation.14 | async-start | bytes 294912
  349.4 65.3 %collective-permute-start.15 = (bf16[3,1,48,384]{3,2,0,1:T(8,128)(2,1)}, bf16[3,1,48,384]{3,2,0,1:T(8,128)(2,1)}, u32[]{:S(2)}, u32[]{:S(2)}) collective-permute-start(bf16[3,1,48,384]{3,2,0,1:T(8,128)(2,1)} %fusion.74), channel_id=1, source_target_pairs={{0,1},{1,0},{2,3},{3,2},{4,5},{5,4},{6,7},{7,6},{8,9},{9,8},{10,11... | collective-permute-start | bytes 331784 | tf_op jit(solution)/shard_map/ppermute | solution.py:309
  418.7 11.4 %collective-permute-start.8 = (f32[11,768]{1,0:T(8,128)S(1)}, f32[11,768]{1,0:T(8,128)S(1)}, u32[]{:S(2)}, u32[]{:S(2)}) collective-permute-start(f32[11,768]{1,0:T(8,128)S(1)} %select_maximum_fusion), channel_id=1, source_target_pairs={{0,1},{1,0},{2,3},{3,2},{4,5},{5,4},{6,7},{7,6},{8,9},{9,8},{10,11... | collective-permute-start | bytes 101384 | tf_op jit(solution)/shard_map/ppermute | solution.py:317
  420.3 14.4 %collective-permute-start.18 = (bf16[48,384]{1,0:T(8,128)(2,1)S(1)}, bf16[48,384]{1,0:T(8,128)(2,1)S(1)}, u32[]{:S(2)}, u32[]{:S(2)}) collective-permute-start(bf16[48,384]{1,0:T(8,128)(2,1)S(1)} %get-tuple-element.56), channel_id=1, source_target_pairs={{4,0},{10,2},{16,4},{22,6},{28,8},{2,10},{8,12},{14,14},{20,16},{2... | collective-permute-start | bytes 110600 | tf_op jit(solution)/shard_map/ppermute | solution.py:551
  422.3 12.4 %collective-permute-start.17 = (bf16[48,384]{1,0:T(8,128)(2,1)S(1)}, bf16[48,384]{1,0:T(8,128)(2,1)S(1)}, u32[]{:S(2)}, u32[]{:S(2)}) collective-permute-start(bf16[48,384]{1,0:T(8,128)(2,1)S(1)} %get-tuple-element.57), channel_id=1, source_target_pairs={{2,0},{8,2},{14,4},{20,6},{26,8},{0,10},{6,12},{12,14},{18,16},{24... | collective-permute-start | bytes 110600 | tf_op jit(solution)/shard_map/ppermute | solution.py:551
  427.3 7.4 %collective-permute-start.16 = (bf16[48,384]{1,0:T(8,128)(2,1)S(1)}, bf16[48,384]{1,0:T(8,128)(2,1)S(1)}, u32[]{:S(2)}, u32[]{:S(2)}) collective-permute-start(bf16[48,384]{1,0:T(8,128)(2,1)S(1)} %get-tuple-element.55), channel_id=1, source_target_pairs={{0,0},{6,2},{12,4},{18,6},{24,8},{30,10},{4,12},{10,14},{16,16},{2... | collective-permute-start | bytes 110600 | tf_op jit(solution)/shard_map/ppermute | solution.py:551
  430.2 4.0 collective-permute-start.9
  434.2 1.3 collective-permute-start.10
  435.6 3.9 collective-permute-start.11
  439.5 3.0 collective-permute-start.12
  (29 other events, 120.7 us)
Sparse Core Ops, SparseCore 0:
  204.8 82.3 reduce-scatter.7
  331.2 81.7 reduce-scatter.5
  415.8 12.3 reduce-scatter.9

commit v2 on v1

v2 whole, which is shorter than its diff:
```python
import functools

import jax
import jax.numpy as jnp
from jax import lax
from jax.experimental import pallas as pl
from jax.experimental.pallas import tpu as pltpu
from jax.sharding import Mesh, PartitionSpec as P

HEADS = 12
HEAD_DIM = 64
EXPERTS = 8
TOP = 2
BUCKETS = 32
DOCS = 8
CAP = 40
GROUPS = 4
GHEADS = HEADS // GROUPS
GWIDTH = GHEADS * HEAD_DIM
CHUNK = 256

LOG2E = 1.4426950408889634
EPS = 1e-06
LOWEST = -1e30
FULL = lax.Precision.HIGHEST
BF = jnp.bfloat16
F32 = jnp.float32
MEMBERS = ("r", "core")
CTX = ("h", "r", "core")


def normalize(values, weight):
    inv_rms = lax.rsqrt(jnp.mean(values * values, axis=-1, keepdims=True) + EPS)
    return values * inv_rms * weight


def dot(a, b, dims=((1,), (0,))):
    return lax.dot_general(a, b, (dims, ((), ())), preferred_element_type=F32)


def exact_dot(a, b, dims):
    return lax.dot_general(a, b, (dims, ((), ())), precision=FULL)


def xor_perm(mask, size):
    return [(i, i ^ mask) for i in range(size)]


def bits_of(size):
    bit = size // 2
    while bit:
        yield bit
        bit //= 2


def strip_width(blocks, half):
    need = half * (blocks - 1) + CHUNK + half
    return -(-need // 128) * 128


def strips_kernel(g_ref, out_ref):
    half = out_ref.shape[1] // GHEADS
    rolled = [
        pltpu.roll(
            jnp.broadcast_to(g_ref[n : n + 1, :], (half, g_ref.shape[1])), 0, 1, stride=1, stride_axis=0
        )
        for n in range(GHEADS)
    ]
    out_ref[...] = jnp.concatenate(rolled).T


def make_strips(lines, half):
    return pl.pallas_call(
        strips_kernel,
        out_shape=jax.ShapeDtypeStruct((lines.shape[1], GHEADS * half), F32),
        cost_estimate=pl.CostEstimate(flops=3 * 10**9, bytes_accessed=2 * 10**6, transcendentals=0),
        name="strips",
    )(lines)


def own_blocks(size, half):
    a = lax.broadcasted_iota(jnp.int32, (size, size), 0) // half
    b = lax.broadcasted_iota(jnp.int32, (size, size), 1) // half
    return a == b


def spread_rows(x, same):
    return jnp.where(same, jnp.concatenate([x] * GHEADS), 0.0)


def fold_rows(x, same, half):
    y = jnp.where(same, x, 0.0).T
    return sum(y[n * half : (n + 1) * half] for n in range(GHEADS))


def group_of(slot, h):
    return lax.rem(h + GROUPS - slot, GROUPS)


def place_of(slot, early, me, h, members, blocks):
    owner = group_of(slot, h) * members + me
    return owner if early else blocks - 1 - owner


def bounds(block, chunk, half, blocks, start):
    top = (blocks - 1 - (block - (CHUNK // half) * chunk)) * half
    lane = lax.broadcasted_iota(jnp.int32, (1, GHEADS * half), 1)
    last = block * half + lax.rem(lane, half) - chunk * CHUNK
    return pl.multiple_of(top, half), last, start - chunk * CHUNK


def forward_kernel(half, blocks, members, pos, q_ref, *refs):
    kvs, refs = refs[:members], refs[members:]
    strip_ref, o_ref, low_ref, stat_ref, k_out, v_out, kt_out, k_ref, v_ref, kt_ref, vt, sems = refs
    size = GHEADS * half
    me, h = pos[0], pos[1]
    tok = 2 * half
    same = own_blocks(size, half)
    key = lax.broadcasted_iota(jnp.int32, (CHUNK, size), 0)
    per = CHUNK // half

    @pl.loop(0, GROUPS)
    def _(slot):
        for j in range(members):
            for early in (True, False):
                block = place_of(slot, early, jnp.bitwise_xor(me, j), h, members, blocks)
                at = pl.ds(pl.multiple_of(lax.rem(block, per) * half, half), half)
                rows = kvs[j][slot, 0 if early else half : half if early else tok, :]
                k_ref[block // per, at, :] = rows[:, :GWIDTH]
                v_ref[block // per, at, :] = rows[:, GWIDTH:]

    @pl.loop(0, blocks // per)
    def _(chunk):
        kt_ref[chunk] = k_ref[chunk].astype(F32).T.astype(BF)
        vt[chunk] = v_ref[chunk].astype(F32).T.astype(BF)

    copies = [
        pltpu.make_async_copy(src, dst, sems.at[i])
        for i, (src, dst) in enumerate(((k_ref, k_out), (v_ref, v_out), (kt_ref, kt_out)))
    ]
    for copy in copies:
        copy.start()

    docs = jnp.concatenate([kv[a, tok : tok + 1, :tok].astype(F32) for kv in kvs for a in range(GROUPS)])
    begins = [jnp.sum(jnp.where(docs < s, 1.0, 0.0)) for s in range(1, DOCS)]

    @pl.loop(0, q_ref.shape[0] // half)
    def _(i):
        slot, late = i // 2, lax.rem(i, 2)
        owner = group_of(slot, h) * members + me
        block = jnp.where(late == 0, owner, blocks - 1 - owner)
        at = pl.ds(pl.multiple_of(i * half, half), half)
        qt = spread_rows(q_ref[at, :].astype(F32), same).T.astype(BF)
        doc = kvs[0][slot, tok : tok + 1, :tok].astype(F32)
        doc = jnp.where(late == 0, doc[:, :half], doc[:, half:])
        begin = jnp.zeros((1, half), F32)
        for s in range(1, DOCS):
            begin = jnp.where(doc == s, begins[s - 1], begin)
        first = jnp.min(begin).astype(jnp.int32) // CHUNK
        begin = jnp.concatenate([begin] * GHEADS, axis=1)
        start = begin.astype(jnp.int32)

        def visit(chunk, carry):
            peak, total, acc = carry
            top, last, begin = bounds(block, chunk, half, blocks, start)
            t = dot(k_ref[chunk], qt) * (HEAD_DIM**-0.5 * LOG2E) + strip_ref[pl.ds(top, CHUNK), :]
            t = jnp.where((key <= last) & (key >= begin), t, LOWEST)
            new = jnp.maximum(peak, jnp.ceil(jnp.max(t, axis=0, keepdims=True)))
            e = jnp.exp2(t - new)
            fade = jnp.exp2(peak - new)
            total = total * fade + jnp.sum(e, axis=0, keepdims=True)
            acc = acc * fade + dot(vt[chunk], e.astype(BF))
            return new, total, acc

        init = (
            jnp.full((1, size), LOWEST, F32),
            jnp.zeros((1, size), F32),
            jnp.zeros((GWIDTH, size), F32),
        )
        peak, total, acc = lax.fori_loop(first, block // per + 1, visit, init)
        out = fold_rows(acc / total, same, half)
        o_ref[at, :] = out
        low_ref[group_of(slot, h), pl.ds(pl.multiple_of(late * half, half), half), :] = out.astype(BF)
        stat_ref[i, 0:1, :] = peak
        stat_ref[i, 1:2, :] = total
        stat_ref[i, 2:3, :] = begin

    for copy in copies:
        copy.wait()


def backward_kernel(half, blocks, members, pos, q_ref, strip_ref, do_ref, o_ref, stat_ref, *refs):
    (k_in, v_in, kt_in, dq_ref), refs = refs[:4], refs[4:]
    dkvs, refs = refs[:members], refs[members:]
    dline_ref, k_ref, v_ref, kt_ref, dk, dv, dstrip, sems = refs
    size = GHEADS * half
    me, h = pos[0], pos[1]
    width = dstrip.shape[0]
    per = CHUNK // half
    copies = [
        pltpu.make_async_copy(src, dst, sems.at[i])
        for i, (src, dst) in enumerate(((k_in, k_ref), (v_in, v_ref), (kt_in, kt_ref)))
    ]
    for copy in copies:
        copy.start()
    same = own_blocks(size, half)
    key = lax.broadcasted_iota(jnp.int32, (CHUNK, size), 0)

    @pl.loop(0, blocks // per)
    def _(chunk):
        dk[chunk] = jnp.zeros(dk.shape[1:], F32)
        dv[chunk] = jnp.zeros(dv.shape[1:], F32)

    @pl.loop(0, width // 128)
    def _(j):
        dstrip[pl.ds(pl.multiple_of(j * 128, 128), 128), :] = jnp.zeros((128, size), F32)

    for copy in copies:
        copy.wait()

    @pl.loop(0, q_ref.shape[0] // half)
    def _(i):
        slot, late = i // 2, lax.rem(i, 2)
        owner = group_of(slot, h) * members + me
        block = jnp.where(late == 0, owner, blocks - 1 - owner)
        at = pl.ds(pl.multiple_of(i * half, half), half)
        peak, total, start = (stat_ref[i, n : n + 1, :] for n in range(3))
        first = jnp.min(start).astype(jnp.int32) // CHUNK
        start = start.astype(jnp.int32)
        qs = spread_rows(q_ref[at, :].astype(F32), same)
        qt, qs = qs.T.astype(BF), qs.astype(BF)
        do = do_ref[group_of(slot, h), pl.ds(pl.multiple_of(late * half, half), half), :].astype(F32)
        corr = jnp.sum(spread_rows(do * o_ref[at, :], same).T, axis=0, keepdims=True) / total
        gt = spread_rows(do, same).T / total
        gs = gt.T.astype(BF)
        gt = gt.astype(BF)

        def visit(chunk, dq):
            top, last, begin = bounds(block, chunk, half, blocks, start)
            t = dot(k_ref[chunk], qt) * (HEAD_DIM**-0.5 * LOG2E) + strip_ref[pl.ds(top, CHUNK), :]
            t = jnp.where((key <= last) & (key >= begin), t - peak, LOWEST)
            e = jnp.exp2(t)
            s = e * (dot(v_ref[chunk], gt) - corr)
            low = s.astype(BF)
            dk[chunk] += dot(low, qs)
            dv[chunk] += dot(e.astype(BF), gs)
            dstrip[pl.ds(top, CHUNK), :] += s
            return dq + dot(kt_ref[chunk], low)

        dq = lax.fori_loop(first, block // per + 1, visit, jnp.zeros((GWIDTH, size), F32))
        dq_ref[at, :] = (fold_rows(dq, same, half) * HEAD_DIM**-0.5).astype(BF)

    @pl.loop(0, GROUPS)
    def _(slot):
        for j in range(members):
            for early in (True, False):
                block = place_of(slot, early, jnp.bitwise_xor(me, j), h, members, blocks)
                at = pl.ds(pl.multiple_of(lax.rem(block, per) * half, half), half)
                part = jnp.concatenate(
                    [dk[block // per, at, :] * HEAD_DIM**-0.5, dv[block // per, at, :]], axis=1
                )
                dkvs[j][slot, 0 if early else half : half if early else 2 * half, :] = part.astype(BF)

    lines = dstrip[...].T
    for n in range(GHEADS):
        x = lines[n * half : (n + 1) * half]
        rows = half
        while rows > 8:
            rows //= 2
            x = x[:rows] + pltpu.roll(x[rows:], width - rows, 1)
        sub = lax.broadcasted_iota(jnp.int32, x.shape, 0)
        for bit in (4, 2, 1):
            x = jnp.where((sub & bit) != 0, pltpu.roll(x, width - bit, 1), x)
        dline_ref[n : n + 1, :] = jnp.sum(x, axis=0, keepdims=True)


VMEM_SPEC = pl.BlockSpec(memory_space=pltpu.VMEM)
SMEM_SPEC = pl.BlockSpec(memory_space=pltpu.SMEM)
HBM_SPEC = pl.BlockSpec(memory_space=pltpu.HBM)


def key_shapes(blocks, half):
    chunks = blocks * half // CHUNK
    return ((chunks, CHUNK, GWIDTH), (chunks, CHUNK, GWIDTH), (chunks, GWIDTH, CHUNK))


def attend(pos, q, kvs, strips, blocks):
    rows = q.shape[0]
    half = strips.shape[1] // GHEADS
    shapes = key_shapes(blocks, half)
    return pl.pallas_call(
        functools.partial(forward_kernel, half, blocks, len(kvs)),
        in_specs=[SMEM_SPEC] + [VMEM_SPEC] * (2 + len(kvs)),
        out_specs=[VMEM_SPEC] * 3 + [HBM_SPEC] * 3,
        scratch_shapes=[pltpu.VMEM(s, BF) for s in shapes + shapes[2:]] + [pltpu.SemaphoreType.DMA((3,))],
        out_shape=[
            jax.ShapeDtypeStruct((rows, GWIDTH), F32),
            jax.ShapeDtypeStruct((GROUPS, rows // GROUPS, GWIDTH), BF),
            jax.ShapeDtypeStruct((rows // half, 8, GHEADS * half), F32),
        ]
        + [jax.ShapeDtypeStruct(s, BF) for s in shapes],
        compiler_params=pltpu.CompilerParams(vmem_limit_bytes=40 << 20),
        cost_estimate=pl.CostEstimate(flops=10**10, bytes_accessed=10**7, transcendentals=10**6),
        name="attend",
    )(pos, q, *kvs, strips)


def attend_back(pos, q, keys, strips, do, o, stat, members, blocks):
    rows = q.shape[0]
    half = strips.shape[1] // GHEADS
    shapes = key_shapes(blocks, half)
    kv = jax.ShapeDtypeStruct((GROUPS, 2 * half, 2 * GWIDTH), BF)
    return pl.pallas_call(
        functools.partial(backward_kernel, half, blocks, members),
        in_specs=[SMEM_SPEC] + [VMEM_SPEC] * 5 + [HBM_SPEC] * 3,
        out_specs=[VMEM_SPEC] * (2 + members),
        scratch_shapes=[pltpu.VMEM(s, BF) for s in shapes]
        + [pltpu.VMEM(s, F32) for s in shapes[:2]]
        + [pltpu.VMEM(strips.shape, F32), pltpu.SemaphoreType.DMA((3,))],
        out_shape=[jax.ShapeDtypeStruct((rows, GWIDTH), BF)]
        + [kv] * members
        + [jax.ShapeDtypeStruct((GHEADS, strips.shape[0]), F32)],
        compiler_params=pltpu.CompilerParams(vmem_limit_bytes=48 << 20),
        cost_estimate=pl.CostEstimate(flops=15 * 10**9, bytes_accessed=10**7, transcendentals=10**6),
        name="attend_back",
    )(pos, q, strips, do, o, stat, *keys)


FBLOCK = 768


def three_parts(x):
    high = x.astype(BF).astype(F32)
    mid = (x - high).astype(BF).astype(F32)
    low = x - high - mid
    lane = lax.broadcasted_iota(jnp.int32, (x.shape[0], 128), 1)
    return jnp.where(lane == 0, high, jnp.where(lane == 1, mid, jnp.where(lane == 2, low, 0.0))).astype(BF)


def expert_kernel(
    cuts, info, came_ref, dy_ref, up_ref, down_ref, out_ref, back_ref, act_ref, lhs_ref,
    grad, out_acc, back_acc,
):
    step = pl.program_id(0)
    width = dy_ref.shape[1]

    @pl.when(step == 0)
    def _():
        gate = jnp.sum(came_ref[:, width:].astype(F32), axis=1, keepdims=True)
        grad[...] = (gate * dy_ref[...].astype(F32)).astype(BF)
        out_acc[...] = jnp.zeros_like(out_acc)
        back_acc[...] = jnp.zeros_like(back_acc)
        outer, inner = cuts
        unit = width // (outer * inner)
        for n, value in enumerate((came_ref[:, :width], grad[...])):
            turned = value.astype(F32).T.astype(BF)
            if outer == 1:
                lhs_ref[n] = turned
                continue
            for b in range(inner):
                slot = jnp.bitwise_xor(info[1], b)
                first = (slot & 1) * (inner // 2) + slot // 2
                for a in range(outer):
                    dest = lax.rem(a + outer - info[0], outer)
                    row = pl.multiple_of((first * outer + dest) * unit, 16)
                    lhs_ref[n, pl.ds(row, unit), :] = turned[(a * inner + b) * unit : (a * inner + b + 1) * unit]

    up, down = up_ref[0], down_ref[0]
    upper = dot(came_ref[:, :width], up)
    active_grad = dot(grad[...], down)
    cdf = 0.5 + 0.5 * lax.erf(upper * 0.7071067811865476)
    active = (upper * cdf).astype(BF)
    upper_grad = (active_grad * (cdf + upper * (0.3989422804014327 * jnp.exp(-0.5 * upper * upper)))).astype(BF)
    act_ref[0] = upper_grad
    act_ref[1] = active
    back_acc[...] += dot(upper_grad, up, ((1,), (1,)))
    out_acc[...] += dot(active, down, ((1,), (1,)))

    @pl.when(step == pl.num_programs(0) - 1)
    def _():
        out = out_acc[...].astype(BF)
        out_ref[...] = out
        back_ref[:, :width] = back_acc[...].astype(BF)
        gate_grad = jnp.sum(dy_ref[...].astype(F32) * out.astype(F32), axis=1, keepdims=True)
        back_ref[:, width:] = three_parts(gate_grad)


def expert(info, came, dy, up, down, cuts):
    rows, width = dy.shape
    ffn = up.shape[2]
    whole = lambda *shape: pl.BlockSpec(shape, lambda j, info: (0,) * len(shape))
    weight = pl.BlockSpec((1, width, FBLOCK), lambda j, info: (info[0], 0, j))
    return pl.pallas_call(
        functools.partial(expert_kernel, cuts),
        grid_spec=pltpu.PrefetchScalarGridSpec(
            num_scalar_prefetch=1,
            grid=(ffn // FBLOCK,),
            in_specs=[whole(*came.shape), whole(rows, width), weight, weight],
            out_specs=[
                whole(rows, width),
                whole(*came.shape),
                pl.BlockSpec((2, rows, FBLOCK), lambda j, info: (0, 0, j)),
                whole(2, width, rows),
            ],
            scratch_shapes=[
                pltpu.VMEM((rows, width), BF),
                pltpu.VMEM((rows, width), F32),
                pltpu.VMEM((rows, width), F32),
            ],
        ),
        out_shape=[
            jax.ShapeDtypeStruct((rows, width), BF),
            jax.ShapeDtypeStruct(came.shape, BF),
            jax.ShapeDtypeStruct((2, rows, ffn), BF),
            jax.ShapeDtypeStruct((2, width, rows), BF),
        ],
        compiler_params=pltpu.CompilerParams(vmem_limit_bytes=48 << 20),
        cost_estimate=pl.CostEstimate(flops=11 * 10**9, bytes_accessed=2 * 10**7, transcendentals=10**6),
        name="expert",
    )(info, came, dy, up, down)


def weight_kernel(lhs_ref, act_ref, keep_ref, pass_ref, send_ref):
    rows = keep_ref.shape[0]
    keep_ref[...] = dot(lhs_ref[0, :rows, :], act_ref[0]).astype(BF)
    pass_ref[...] = dot(lhs_ref[0, rows : 2 * rows, :], act_ref[0]).astype(BF)
    send_ref[...] = dot(lhs_ref[0, 2 * rows :, :], act_ref[0]).astype(BF)


def weight_terms(lhs, act, which):
    _, width, rows = lhs.shape
    ffn = act.shape[2]
    cuts = (width // 4, width // 4, width // 2)
    return pl.pallas_call(
        weight_kernel,
        grid=(ffn // FBLOCK,),
        in_specs=[
            pl.BlockSpec((1, width, rows), lambda j: (which, 0, 0)),
            pl.BlockSpec((1, rows, FBLOCK), lambda j: (which, 0, j)),
        ],
        out_specs=[pl.BlockSpec((c, FBLOCK), lambda j: (0, j)) for c in cuts],
        out_shape=[jax.ShapeDtypeStruct((c, ffn), BF) for c in cuts],
        compiler_params=pltpu.CompilerParams(vmem_limit_bytes=32 << 20),
        cost_estimate=pl.CostEstimate(flops=35 * 10**8, bytes_accessed=10**7, transcendentals=0),
        name="weight_terms",
    )(lhs, act)


def together(*values):
    return lax.optimization_barrier(values)


def turn(shift):
    return [(i, (i + shift) % GROUPS) for i in range(GROUPS)]


def gather_groups(x):
    came = {k: lax.ppermute(x, "h", turn(k)) for k in (2, 1, 3)}
    return jnp.stack([x] + [came[k] for k in range(1, GROUPS)])


def gather_members(x):
    size = lax.axis_size(MEMBERS)
    held = {0: x}
    for bit in bits_of(size):
        for k in sorted(held):
            held[k | bit] = lax.ppermute(held[k], MEMBERS, xor_perm(bit, size))
    return [held[k] for k in range(size)]


def part_of(x, mine):
    low, high = jnp.split(x, 2, axis=-1)
    return jnp.where(mine == 0, low, high), jnp.where(mine == 0, high, low)


def swap(x, axis, bit):
    return lax.ppermute(x, axis, xor_perm(bit, lax.axis_size(axis))).astype(F32)


def two_parts(x):
    high = lax.reduce_precision(x, 8, 7)
    return jnp.concatenate([high, x - high]).astype(BF)


def from_fsdp(part):
    if lax.axis_size("fsdp") != 2:
        return lax.all_gather(part, "fsdp", axis=0)
    came = lax.ppermute(part, "fsdp", xor_perm(1, 2))
    return jnp.where(lax.axis_index("fsdp") == 0, jnp.stack([part, came]), jnp.stack([came, part]))


def swap_groups(x):
    return lax.all_to_all(x, "h", 0, 0, tiled=True)


def per_device(
    tokens, segments, routes, bucket_table, attn_gain, qkv_weight, out_weight, bias_table,
    moe_gain, router_weight, up_weight, down_weight, cotangent,
):
    tok, width = tokens.shape[1], tokens.shape[2]
    half = tok // 2
    h, m, f = lax.axis_index("h"), lax.axis_index(MEMBERS), lax.axis_index("fsdp")
    core = lax.axis_index("core")
    members, n_fsdp = lax.axis_size(MEMBERS), lax.axis_size("fsdp")
    shards = GROUPS * members
    blocks = 2 * shards
    length = shards * tok
    here = EXPERTS // n_fsdp
    spread = here > 1
    ffn = up_weight.shape[2]
    rows_f = width // n_fsdp
    rows_c = width // shards
    pos = jnp.stack([m, h]).astype(jnp.int32)

    extra = jnp.pad(segments.astype(BF), ((0, 7), (0, width - tok)))
    mixed = gather_groups(jnp.concatenate([tokens[0], extra]))

    bias_flat = bias_table.reshape(1, -1)
    bias_rows = -(-bias_flat.shape[1] // rows_f)
    bias_flat = jnp.pad(bias_flat, ((0, 0), (0, bias_rows * rows_f - bias_flat.shape[1])))
    small = jnp.concatenate(
        [attn_gain[None], moe_gain[None], router_weight.T, bias_flat.reshape(bias_rows, rows_f)]
        + [jnp.zeros((16 - 10 - bias_rows, rows_f), BF)]
    )
    small = from_fsdp(small)
    attn_scale = small[:, 0].reshape(width).astype(F32)
    moe_scale = small[:, 1].reshape(width).astype(F32)
    router_t = jnp.transpose(small[:, 2:10], (1, 0, 2)).reshape(EXPERTS, width)
    bias_full = small[:, 10 : 10 + bias_rows].reshape(n_fsdp, -1)[:, : bias_table.size]
    bias_full = bias_full.reshape(BUCKETS, HEADS)
    cut = [
        lax.dynamic_slice_in_dim(qkv_weight, n * width + h * GWIDTH, GWIDTH, 1) for n in range(3)
    ]
    qkv_heads = from_fsdp(jnp.concatenate(cut, axis=1)).reshape(width, 3 * GWIDTH)
    out_full = from_fsdp(together(out_weight, qkv_heads)[0]).reshape(width, width)

    wide = strip_width(blocks, half)
    top = half * (blocks - 1)
    line = jnp.concatenate(
        [
            bucket_table[: top + 1][::-1],
            jnp.full((wide - length,), -1, jnp.int32),
            bucket_table[top + 1 :][::-1],
        ]
    )
    hot = (line[None] == jnp.arange(BUCKETS, dtype=jnp.int32)[:, None]).astype(BF)
    bias_mine = lax.dynamic_slice_in_dim(bias_full, h * GHEADS, GHEADS, 1)
    strips = make_strips(dot(bias_mine, hot, ((0,), (0,))) * LOG2E, half)

    hot_routes = (routes.reshape(-1)[:, None] == jnp.arange(EXPERTS)[None]).astype(F32)
    earlier = jnp.arange(tok * TOP)
    earlier = (earlier[None, :] < earlier[:, None]).astype(BF)
    before = dot(earlier, hot_routes.astype(BF))
    slot = jnp.sum(before * hot_routes, axis=1).astype(jnp.int32).reshape(tok, TOP)
    target = (routes % here) * n_fsdp + routes // here
    place = target * CAP + slot
    slots = jnp.arange(EXPERTS * CAP, dtype=jnp.int32)
    pick = [slots[:, None] == place[None, :, k] for k in range(TOP)]
    pick_any = (pick[0] | pick[1]).astype(BF)
    exchange = ("h", "fsdp") if spread else ("fsdp",)

    def deal(rows):
        send = rows.reshape(EXPERTS, CAP, rows.shape[-1])
        return lax.all_to_all(send, exchange, 0, 0, tiled=True).reshape(rows.shape)

    mixed, strips = together(mixed, strips)
    ain = normalize(mixed[:, :tok].astype(F32), attn_scale).astype(BF).reshape(GROUPS * tok, width)
    proj = dot(ain, qkv_heads).astype(BF)
    q = proj[:, :GWIDTH]
    kv = proj[:, GWIDTH:].reshape(GROUPS, tok, 2 * GWIDTH)
    kvs = gather_members(jnp.concatenate([kv, mixed[:, tok:, : 2 * GWIDTH]], axis=1))
    dy_send = together(dot(pick_any, cotangent[0]).astype(BF), mixed)[0]
    q, dy_slots = together(q, deal(dy_send))
    o_pre, o_low, stat, *keys = attend(pos, q, kvs, strips, blocks)
    context = swap_groups(o_low)
    context = jnp.transpose(context, (1, 0, 2)).reshape(tok, width)
    x = tokens[0].astype(F32)
    residual = x + dot(context, out_full)

    moe_in = normalize(residual, moe_scale).astype(BF)
    logits = dot(moe_in, router_t, ((1,), (1,)))
    route_hot = hot_routes.reshape(tok, TOP, EXPERTS)
    chosen = jnp.sum(logits[:, None, :] * route_hot, axis=-1)
    gates = jax.nn.softmax(chosen, axis=-1)
    gate_slots = sum(
        jnp.sum(jnp.where(pick[k], gates[None, :, k], 0.0), axis=1, keepdims=True) for k in range(TOP)
    )
    high = lax.reduce_precision(gate_slots, 8, 7)
    mid = lax.reduce_precision(gate_slots - high, 8, 7)
    low = gate_slots - high - mid
    lane = jnp.arange(128)[None]
    extra = jnp.where(lane == 0, high, jnp.where(lane == 1, mid, jnp.where(lane == 2, low, 0.0)))
    rows_out = jnp.concatenate([dot(pick_any, moe_in), extra], axis=1).astype(BF)

    came = deal(rows_out)
    cuts = (GROUPS, members) if spread else (1, 1)
    info = jnp.stack([h if spread else jnp.zeros_like(h), m]).astype(jnp.int32)
    expert_out, back, act, lhs = expert(info, came, dy_slots, up_weight, down_weight, cuts)
    back = deal(back)

    terms = [weight_terms(lhs, act, n) for n in range(2)]
    staged = spread and members == 4
    if staged:
        terms = [(keep, passed, swap(send, "core", 1)) for keep, passed, send in terms]

    dy = cotangent[0].astype(F32)
    gate_grad = jnp.stack(
        [jnp.sum(dot(pick[k].astype(BF), back[:, width:], ((0,), (0,))), axis=1) for k in range(TOP)], axis=1
    )
    chosen_grad = gates * (gate_grad - jnp.sum(gates * gate_grad, axis=1, keepdims=True))
    logit_grad = jnp.sum(chosen_grad[:, :, None] * route_hot, axis=1)
    moe_in_grad = exact_dot(logit_grad, router_t.astype(F32), ((1,), (0,)))
    moe_in_grad = moe_in_grad + dot(pick_any, back[:, :width], ((0,), (0,)))
    norm_grad, moe_gain_grad = jax.vjp(normalize, residual, moe_scale)[1](moe_in_grad)
    resid_grad = dy + norm_grad
    attn_grad = resid_grad.astype(BF)
    router_grad = exact_dot(logit_grad, moe_in.astype(F32), ((0,), (0,)))

    do = dot(attn_grad, out_full, ((1,), (1,))).astype(BF)
    do = jnp.transpose(do.reshape(tok, GROUPS, GWIDTH), (1, 0, 2))
    do, terms = together(do, terms)
    do = swap_groups(do)
    out_term = dot(attn_grad, context, ((0,), (0,))).reshape(shards // 2, 2, rows_c, width)
    out_send = lax.dynamic_index_in_dim(out_term, 1 - core, 1, False).astype(BF)
    do, out_came = together(do, swap(out_send, "core", 1))
    out_term = lax.dynamic_index_in_dim(out_term, core, 1, False) + out_came
    for bit in bits_of(n_fsdp):
        out_term, out_send = part_of(out_term, (f // bit) % 2)
        out_term = out_term + swap(out_send.astype(BF), "fsdp", bit)
    dq, *dkvs, dline = attend_back(pos, q, keys, strips, do, o_pre, stat, members, blocks)
    dkvs[0], out_term = together(dkvs[0], out_term)
    bias_mine = exact_dot(hot.astype(F32), dline, ((1,), (1,)))
    held = dict(enumerate(dkvs))
    for k in range(1, members, 2):
        held[k - 1] = held[k - 1].astype(F32) + swap(held.pop(k), "core", 1)
    if staged:
        first = [(passed.astype(F32) + came[came.shape[0] // 2 :]).astype(BF) for _, passed, came in terms]
        first[0] = swap(first[0], "r", 1)
        held[2], first[0] = together(held[2], first[0])
    bit = 2
    while bit < members:
        for k in [k for k in sorted(held) if k & bit]:
            held[k - bit] = held[k - bit] + swap(held.pop(k).astype(BF), "r", bit // 2)
        bit *= 2
    dkv = held[0].astype(BF).reshape(GROUPS * tok, 2 * GWIDTH)
    if staged:
        first[1], dkv = together(first[1], dkv)
        first[1] = swap(first[1], "r", 1)
    dproj = jnp.concatenate([dq, dkv], axis=1)

    def to_shards(term, came):
        keep, _, from_core = term
        total = (keep.astype(F32) + from_core[: keep.shape[0]] + came).astype(BF)
        total = total.reshape(GROUPS, rows_c, ffn)
        return [total[0]] + [lax.ppermute(total[k], "h", turn(k)) for k in range(1, GROUPS)]

    def in_order(came):
        came = jnp.stack(came)
        return jnp.concatenate(
            [lax.dynamic_index_in_dim(came, group_of(s, h), 0) for s in range(GROUPS)]
        ).astype(F32)

    result = deal(together(expert_out, do)[0])
    back_ain = dot(dproj, qkv_heads, ((1,), (1,)))
    back_low = back_ain.astype(BF).reshape(GROUPS, tok, width)
    if staged:
        up_came = to_shards(terms[0], first[0])
        back_low, up_came, result = together(back_low, up_came, result)

    mid = lax.ppermute(back_low[2], "h", turn(-1))
    side = lax.ppermute(back_low[3], "h", turn(1)).astype(F32)
    mid = (back_low[1].astype(F32) + mid.astype(F32)).astype(BF)
    mid = lax.ppermute(mid, "h", turn(-1)).astype(F32)
    attn_in_grad = back_ain[:tok] + side + mid
    token_grad = jax.vjp(lambda v: normalize(v, attn_scale), x)[1](attn_in_grad)[0]
    tokens_grad = (resid_grad + token_grad).astype(BF)

    picked = [dot(pick[k].astype(BF), result, ((0,), (0,))) for k in range(TOP)]
    layer_out = residual + gates[:, :1] * picked[0] + gates[:, 1:] * picked[1]

    attn_gain_grad = jnp.sum(back_ain * ain.astype(F32), axis=0) / attn_scale
    bias_own = lax.dynamic_update_slice_in_dim(jnp.zeros((BUCKETS, HEADS), F32), bias_mine, h * GHEADS, 1)
    bias_own = jnp.pad(bias_own.reshape(n_fsdp, -1), ((0, 0), (0, rows_f - bias_own.size // n_fsdp)))
    pack = jnp.concatenate(
        [router_grad, attn_gain_grad[None], moe_gain_grad[None], bias_own.reshape(1, width)]
        + [jnp.zeros((5, width), F32)]
    )
    small_rows = pack.shape[0]

    def swap_both(send, pack, axis, bit):
        sent = jnp.concatenate([send.reshape(-1, send.shape[-1]).astype(BF), two_parts(pack)])
        came = swap(sent, axis, bit)
        return came[: -2 * small_rows].reshape(send.shape), came[-2 * small_rows : -small_rows] + came[-small_rows:]

    unit = GWIDTH // members
    term = dot(dproj, ain, ((0,), (0,))).reshape(3, members // 2, 2, unit, width)
    came, pack_came = swap_both(lax.dynamic_index_in_dim(term, 1 - core, 2, False), pack, "core", 1)
    term = (lax.dynamic_index_in_dim(term, core, 2, False) + came).reshape(-1, width)
    pack = pack + pack_came
    for bit in bits_of(n_fsdp):
        term, send = part_of(term, (f // bit) % 2)
        pack, pack_send = part_of(pack, (f // bit) % 2)
        came, pack_came = swap_both(send, pack_send, "fsdp", bit)
        term, pack = term + came, pack + pack_came
    term = jnp.concatenate(
        [term.reshape(3, members // 2, unit, rows_f).swapaxes(0, 1).reshape(members // 2, -1, rows_f)]
        + [out_term.reshape(GROUPS, members // 2, rows_c, rows_f).swapaxes(0, 1).reshape(members // 2, -1, rows_f)],
        axis=1,
    )
    for bit in bits_of(members // 2):
        mine = (lax.axis_index("r") // bit) % 2
        term = term.reshape((2, -1) + term.shape[1:])
        came, pack_came = swap_both(lax.dynamic_index_in_dim(term, 1 - mine, 0, False), pack, "r", bit)
        term = lax.dynamic_index_in_dim(term, mine, 0, False) + came
        pack = pack + pack_came
    term = term[0]
    out_term = term[3 * unit :].reshape(GROUPS, rows_c, rows_f)
    term = term[: 3 * unit].astype(BF).reshape(3, unit, rows_f)
    out_sum, pack_sum = lax.dynamic_index_in_dim(out_term, h, 0, False), pack
    for k in (2, 1, 3):
        piece = lax.dynamic_index_in_dim(out_term, lax.rem(h + k, GROUPS), 0, False)
        came = lax.ppermute(jnp.concatenate([piece.astype(BF), two_parts(pack)]), "h", turn(k)).astype(F32)
        out_sum = out_sum + came[:rows_c]
        pack_sum = pack_sum + came[rows_c : rows_c + small_rows] + came[rows_c + small_rows :]
    at = h * members + m
    parts = []
    for r in range(3):
        pairs = [((3 * d + r) % shards, d) for d in range(shards)]
        entry = [0] * shards
        for s, d in pairs:
            entry[s] = (3 * d + r) // shards
        which = jnp.sum(jnp.where(jnp.arange(shards) == at, jnp.asarray(entry), 0))
        parts.append(lax.ppermute(lax.dynamic_index_in_dim(term, which, 0, False), CTX, pairs))
    qkv_grad = jnp.concatenate(parts).astype(F32).T

    if staged:
        grads = [in_order(up_came), in_order(to_shards(terms[1], first[1]))]
    else:
        grads = [
            lax.psum_scatter(jnp.concatenate(term), CTX, scatter_dimension=0, tiled=True)[None].astype(F32)
            for term in terms
        ]
    return (
        layer_out.astype(BF)[None],
        tokens_grad[None],
        pack_sum[8],
        qkv_grad,
        out_sum.T,
        pack_sum[10, : bias_table.size].reshape(BUCKETS // n_fsdp, HEADS),
        pack_sum[9],
        pack_sum[:8].T,
        grads[0],
        grads[1],
    )


def solution(mesh):
    n_ctx, n_fsdp = mesh.shape["ctx"], mesh.shape["fsdp"]
    cut = mesh.devices.reshape(GROUPS, n_ctx // (2 * GROUPS), 2, n_fsdp)
    row = P("fsdp", CTX, None)
    return jax.shard_map(
        per_device,
        mesh=Mesh(cut, CTX + ("fsdp",)),
        in_specs=(
            row,
            P("fsdp", CTX),
            P(CTX + ("fsdp",), None),
            P(),
            P("fsdp"),
            P("fsdp", None),
            P("fsdp", None),
            P("fsdp", None),
            P("fsdp"),
            P("fsdp", None),
            P("fsdp", None, None),
            P("fsdp", None, None),
            row,
        ),
        out_specs=(
            row,
            row,
            P("fsdp"),
            P("fsdp", CTX),
            P("fsdp", CTX),
            P("fsdp", None),
            P("fsdp"),
            P("fsdp", None),
            row,
            row,
        ),
        check_vma=False,
    )
```

time: 463 us -> 340 us (0.73)
  blocking collectives: 71.5 us -> 0 us
  local copies, waits for them, and re-layouts: 65.8 us -> 39.9 us
  matrix products: 45.1 us -> 21.6 us
  other arithmetic: 32.1 us -> 49.3 us
  between operations: 20.7 us -> 7.62 us
  waiting for transfers between devices: 92.3 us -> 83.8 us
    ppermute x19 -> x36, waiting for transfers between devices: 12.2 us -> 68.1 us  [the longest x6 43.6 us: to_shards(): lax.ppermute(total[k], 'h', turn(k))]
    reduce_scatter x2 -> x0, waiting for transfers between devices: 55.2 us -> none  [the longest x1 55.2 us: per_device(): lax.psum_scatter(out_term, ('h', 'm'), scatter_dimension=0, tiled=True)]
    all_to_all x2 -> x0, blocking collectives: 37.6 us -> none  [the longest x1 27.5 us: deal(): return lax.all_to_all(send, exchange, 0, 0, tiled=True).reshape(rows.shape)]
    all_gather x2 -> x0, blocking collectives: 34 us -> none  [the longest x1 18.4 us: per_device(): small = lax.all_gather(small, 'fsdp', axis=0)]
    dot_general x20 -> x16, matrix products: 42.1 us -> 17.8 us  [dot(): return lax.dot_general(a, b, (dims, ((), ())), preferred_element_type=F32)]
    all_to_all x5 -> x2, starting transfers between devices: 30.2 us -> 9.11 us  [swap_groups(): return lax.all_to_all(x, 'h', 0, 0, tiled=True)]
    convert_element_type x10 -> x24, other arithmetic: 10.8 us -> 29 us  [the longest x7 12.6 us: swap(): return lax.ppermute(x, axis, xor_perm(bit, lax.axis_size(axis))).astype(F32)]
    ppermute x19 -> x36, starting transfers between devices: 32.6 us -> 49.6 us  [the longest x3 12.9 us: per_device(): lax.ppermute(lax.dynamic_index_in_dim(term, which, 0, False), CTX, pairs)]
  transfers between devices with their start and end apart: 29 -> 42, of which waited for: 12 -> 17; matrix products, arithmetic and copies ran while one was open for 21% -> 22% of each run, Pallas kernels for 11% -> 12%
where the time goes in v2:
time: 340 us; the launch traced here: 335 us
  waiting for transfers between devices  83.8 us (25%)
  starting transfers between devices  80.5 us (24%)
  Pallas kernels  52.1 us (15%)
  other arithmetic  49.3 us (14%)
  local copies, waits for them, and re-layouts  39.9 us (12%)
  matrix products  21.6 us (6%)
  between operations  7.62 us (2%)
    ppermute x6, waiting for transfers between devices, to_shards(): lax.ppermute(total[k], 'h', turn(k))  43.6 us
    unnamed x164, local copies, waits for them, and re-layouts  23.9 us
    all_to_all x4, starting transfers between devices, deal(): return lax.all_to_all(send, exchange, 0, 0, tiled=True).reshape(rows.shape)  21.8 us
    dot_general x16, matrix products, dot(): return lax.dot_general(a, b, (dims, ((), ())), preferred_element_type=F32)  17.8 us
    pallas_call x1, Pallas kernels, attend_back(): pl.pallas_call(functools.partial(backward_kernel, half, blocks, members),...  15.4 us
    ppermute x3, starting transfers between devices, per_device(): lax.ppermute(lax.dynamic_index_in_dim(term, which, 0, False), CTX, pairs)  12.9 us
    pallas_call x1, Pallas kernels, attend(): pl.pallas_call(functools.partial(forward_kernel, half, blocks, len(kvs)),...  12.9 us
    convert_element_type x7, other arithmetic, swap(): return lax.ppermute(x, axis, xor_perm(bit, lax.axis_size(axis))).astype(F32)  12.6 us
  transfers between devices with their start and end apart: 42, of which 17 were waited for; matrix products, arithmetic and copies ran while one was open for 22% of the time, Pallas kernels for 12%

profile of v2, /device:TPU:11, one launch (start us, length us, event | category | flops | bytes accessed | tf_op | source)
XLA Modules:
  0.0 334.7 jit_solution(1105570281184119249)
XLA Ops:
  13.0 6.9 %collective-permute-done.3 = bf16[16,384]{1,0:T(8,128)(2,1)S(1)} collective-permute-done((bf16[16,384]{1,0:T(8,128)(2,1)S(1)}, bf16[16,384]{1,0:T(8,128)(2,1)S(1)}, u32[]{:S(2)}, u32[]{:S(2)}) %collective-permute-start.3) | collective-permute-done | bytes 12320 | tf_op jit(solution)/shard_map/ppermute | solution.py:488
  21.6 3.3 strips.1.refs_4_.strip_ref
  26.9 4.4 %all-to-all-start = ((bf16[8,40,768]{2,1,0:T(8,128)(2,1)}), bf16[8,40,768]{2,1,0:T(8,128)(2,1)S(1)}, u32[]{:S(2)}, u32[]{:S(2)}) async-start(bf16[8,40,768]{2,1,0:T(8,128)(2,1)} %bitcast.15), calls=%async_computation | async-start | bytes 983040 | tf_op jit(solution)/shard_map/all_to_all | solution.py:564
  34.4 3.0 collective-permute-start.5
  37.4 4.2 %collective-permute-done.6.refs_2_ = bf16[4,136,384]{2,1,0:T(8,128)(2,1)S(1)} collective-permute-done((bf16[4,136,384]{2,1,0:T(8,128)(2,1)S(1)}, bf16[4,136,384]{2,1,0:T(8,128)(2,1)S(1)}, u32[]{:S(2)}, u32[]{:S(2)}) %collective-permute-start.6) | collective-permute-done | bytes 417824 | tf_op jit(solution)/shard_map/ppermute | solution.py:467
  41.6 3.6 %collective-permute-start.7 = (bf16[4,136,384]{2,1,0:T(8,128)(2,1)S(1)}, bf16[4,136,384]{2,1,0:T(8,128)(2,1)S(1)}, u32[]{:S(2)}, u32[]{:S(2)}) collective-permute-start(bf16[4,136,384]{2,1,0:T(8,128)(2,1)S(1)} %collective-permute-done.6.refs_2_), channel_id=1, source_target_pairs={{0,2},{2,0},{4,6},{6,4},{1,3},{3,1},{5,7},{7,5},{8,10},{10,8},{12,... | collective-permute-start | bytes 1253384 | tf_op jit(solution)/shard_map/ppermute | solution.py:467
  48.3 12.9 %attend.1 = (f32[512,192]{1,0:T(8,128)S(1)}, bf16[4,128,192]{2,1,0:T(8,128)(2,1)S(1)}, f32[8,8,192]{2,1,0:T(8,128)S(1)}, bf16[8,256,192]{2,1,0:T(8,128)(2,1)S(1)...) custom-call(s32[2]{0:T(128)S(1)} %pad_add_fusion.pos, bf16[512,192]{1,0:T(8,128)(2,1)S(1)} %slice.248.q_ref, ...), custom_call_target="tpu_custom_call" | custom-call | flops 10000000000 | bytes 10000000 | tf_op jit(solution)/shard_map/attend/pallas_call | solution.py:291
  64.9 4.6 %all-to-all-start.1 = ((bf16[4,128,192]{1,2,0:T(8,128)(2,1)}), bf16[4,128,192]{1,2,0:T(8,128)(2,1)S(1)}, u32[]{:S(2)}, u32[]{:S(2)}) async-start(bf16[4,128,192]{1,2,0:T(8,128)(2,1)} %copy.107), calls=%async_computation.1 | async-start | bytes 393216 | tf_op jit(solution)/shard_map/all_to_all | solution.py:493
  69.5 1.8 maximum_select_fusion
  71.4 3.4 %all-to-all-done.1 = bf16[4,128,192]{1,2,0:T(8,128)(2,1)S(1)} async-done(((bf16[4,128,192]{1,2,0:T(8,128)(2,1)}), bf16[4,128,192]{1,2,0:T(8,128)(2,1)S(1)}, u32[]{:S(2)}, u32[]{:S(2)}) %all-to-all-start.1) | async-done | bytes 196640 | tf_op jit(solution)/shard_map/all_to_all | solution.py:493
  78.0 5.2 %all-to-all-start.2 = ((bf16[8,40,896]{2,1,0:T(8,128)(2,1)}), bf16[8,40,896]{2,1,0:T(8,128)(2,1)S(1)}, u32[]{:S(2)}, u32[]{:S(2)}) async-start(bf16[8,40,896]{2,1,0:T(8,128)(2,1)} %pad_maximum_fusion.4), calls=%async_computation.2 | async-start | bytes 1146880 | tf_op jit(solution)/shard_map/all_to_all | solution.py:564
  83.2 12.2 %all-to-all-done.2 = bf16[8,40,896]{2,1,0:T(8,128)(2,1)S(1)} async-done(((bf16[8,40,896]{2,1,0:T(8,128)(2,1)}), bf16[8,40,896]{2,1,0:T(8,128)(2,1)S(1)}, u32[]{:S(2)}, u32[]{:S(2)}) %all-to-all-start.2) | async-done | bytes 573472 | tf_op jit(solution)/shard_map/all_to_all | solution.py:564
  95.4 11.8 %expert.1 = (bf16[320,768]{1,0:T(8,128)(2,1)}, bf16[320,896]{1,0:T(8,128)(2,1)}, bf16[2,320,3072]{2,1,0:T(8,128)(2,1)}, bf16[2,768,320]{2,1,0:T(8,128)(2,1)S(1)}) custom-call(s32[2]{0:T(128)S(1)} %pad_add_fusion.1.info, bf16[320,896]{1,0:T(8,128)(2,1)S(1)} %bitcast.164, bf16[320,768]{1,0:T(8,128)(2,1)S(1)} %bitcast.165, bf16[4,768,3072]{2,1,0:T(8,128)(2,1)} %up_ref.1, ...), custom_call_target="tpu_custom_call" | custom-call | flops 11000000512 | bytes 20000000 | tf_op jit(solution)/shard_map/expert/pallas_call | solution.py:393
  107.3 6.3 %all-to-all-start.3 = ((bf16[8,40,896]{2,1,0:T(8,128)(2,1)}), bf16[8,40,896]{2,1,0:T(8,128)(2,1)}, u32[]{:S(2)}, u32[]{:S(2)}) async-start(bf16[8,40,896]{2,1,0:T(8,128)(2,1)} %bitcast.29), calls=%async_computation.3 | async-start | bytes 1146880 | tf_op jit(solution)/shard_map/all_to_all | solution.py:564
  116.7 2.1 copy-done.4
  118.8 4.3 %weight_terms.3 = (bf16[192,3072]{1,0:T(8,128)(2,1)S(1)}, bf16[192,3072]{1,0:T(8,128)(2,1)S(1)}, bf16[384,3072]{1,0:T(8,128)(2,1)}) custom-call(bf16[2,768,320]{2,1,0:T(8,128)(2,1)S(1)} %get-tuple-element.68.lhs_ref, bf16[2,320,3072]{2,1,0:T(8,128)(2,1)S(1)} %copy-done.4), custom_call_target="tpu_custom_call" | custom-call | flops 3500000000 | bytes 10000000 | tf_op jit(solution)/shard_map/weight_terms/pallas_call | solution.py:434
  123.1 2.4 collective-permute-start.10
  126.8 4.3 %weight_terms.2 = (bf16[192,3072]{1,0:T(8,128)(2,1)S(1)}, bf16[192,3072]{1,0:T(8,128)(2,1)S(1)}, bf16[384,3072]{1,0:T(8,128)(2,1)}) custom-call(bf16[2,768,320]{2,1,0:T(8,128)(2,1)S(1)} %copy-done.6, bf16[2,320,3072]{2,1,0:T(8,128)(2,1)S(1)} %copy-done.4), custom_call_target="tpu_custom_call" | custom-call | flops 3500000000 | bytes 10000000 | tf_op jit(solution)/shard_map/weight_terms/pallas_call | solution.py:434
  138.1 1.8 multiply_reduce_fusion.1
  150.7 2.6 convolution_convert_fusion.3
  156.8 2.2 convert_element_type.290
  159.0 4.4 %convert_element_type.287 = f32[384,3072]{1,0:T(8,128)} convert(bf16[384,3072]{1,0:T(8,128)(2,1)} %collective-permute-done.10) | non-fusion elementwise | flops 1179648 | bytes 7077888 | tf_op jit(solution)/shard_map/convert_element_type | solution.py:477
  163.4 4.3 %convert_element_type.286 = f32[384,3072]{1,0:T(8,128)} convert(bf16[384,3072]{1,0:T(8,128)(2,1)} %collective-permute-done.9) | non-fusion elementwise | flops 1179648 | bytes 7077888 | tf_op jit(solution)/shard_map/convert_element_type | solution.py:477
  167.8 4.6 %all-to-all-start.4 = ((bf16[4,128,192]{1,2,0:T(8,128)(2,1)}), bf16[4,128,192]{1,2,0:T(8,128)(2,1)}, u32[]{:S(2)}, u32[]{:S(2)}) async-start(bf16[4,128,192]{1,2,0:T(8,128)(2,1)} %bitcast.190), calls=%async_computation.4 | async-start | bytes 393216 | tf_op jit(solution)/shard_map/all_to_all | solution.py:493
  172.3 3.4 %add_convert_fusion.2 = bf16[192,3072]{1,0:T(8,128)(2,1)} fusion(f32[384,3072]{1,0:T(8,128)} %convert_element_type.286, bf16[192,3072]{1,0:T(8,128)(2,1)} %copy-done), kind=kLoop, calls=%fused_computation.3 | loop fusion | flops 1769472 | bytes 4718592 | tf_op jit(solution)/shard_map/convert_element_type | solution.py:637
  175.8 3.5 %collective-permute-start.15 = (bf16[192,3072]{1,0:T(8,128)(2,1)}, bf16[192,3072]{1,0:T(8,128)(2,1)}, u32[]{:S(2)}, u32[]{:S(2)}) collective-permute-start(bf16[192,3072]{1,0:T(8,128)(2,1)} %add_convert_fusion.2), channel_id=1, source_target_pairs={{0,4},{4,0},{1,5},{5,1},{2,6},{6,2},{3,7},{7,3},{8,12},{12,8},{9,1... | collective-permute-start | bytes 3538952 | tf_op jit(solution)/shard_map/ppermute | solution.py:477
  180.7 1.8 bitcast_add_fusion
  184.5 1.8 copy.111.do_ref
  192.9 15.4 %attend_back.1 = (bf16[512,192]{1,0:T(8,128)(2,1)S(1)}, bf16[4,128,384]{2,1,0:T(8,128)(2,1)S(1)}, bf16[4,128,384]{2,1,0:T(8,128)(2,1)}, bf16[4,128,384]{2,1,0:T(...) custom-call(s32[2]{0:T(128)S(1)} %pad_add_fusion.pos, bf16[512,192]{1,0:T(8,128)(2,1)S(1)} %copy-done.3, ...), custom_call_target="tpu_custom_call" | custom-call | flops 15000000512 | bytes 10000000 | tf_op jit(solution)/shard_map/attend_back/pallas_call | solution.py:313
  209.6 5.9 %all-to-all-start.5 = ((bf16[8,40,768]{2,1,0:T(8,128)(2,1)}), bf16[8,40,768]{2,1,0:T(8,128)(2,1)}, u32[]{:S(2)}, u32[]{:S(2)}) async-start(bf16[8,40,768]{2,1,0:T(8,128)(2,1)} %bitcast.44), calls=%async_computation.5 | async-start | bytes 983040 | tf_op jit(solution)/shard_map/all_to_all | solution.py:564
  222.6 2.2 add_convert_fusion.1
  232.1 1.7 collective-permute-start.32
  234.2 2.2 multiply_reduce_fusion
  236.4 15.2 %collective-permute-done.18 = bf16[48,3072]{1,0:T(8,128)(2,1)} collective-permute-done((bf16[48,3072]{1,0:T(8,128)(2,1)}, bf16[48,3072]{1,0:T(8,128)(2,1)}, u32[]{:S(2)}, u32[]{:S(2)}) %collective-permute-start.18) | collective-permute-done | bytes 294944 | tf_op jit(solution)/shard_map/ppermute | solution.py:655
  251.6 3.2 collective-permute-done.19
  267.2 2.0 fusion.6
  269.3 1.9 collective-permute-done.22
  273.9 4.3 %collective-permute-done.25 = bf16[368,384]{1,0:T(8,128)(2,1)S(1)} collective-permute-done((bf16[368,384]{1,0:T(8,128)(2,1)S(1)}, bf16[368,384]{1,0:T(8,128)(2,1)S(1)}, u32[]{:S(2)}, u32[]{:S(2)}) %collective-permute-start.25) | collective-permute-done | bytes 282656 | tf_op jit(solution)/shard_map/ppermute | solution.py:477
  278.4 2.2 collective-permute-start.29
  280.6 8.8 %collective-permute-start.30 = (bf16[48,384]{1,0:T(8,128)(2,1)S(1)}, bf16[48,384]{1,0:T(8,128)(2,1)S(1)}, u32[]{:S(2)}, u32[]{:S(2)}) collective-permute-start(bf16[48,384]{1,0:T(8,128)(2,1)S(1)} %get-tuple-element.156), channel_id=1, source_target_pairs={{2,0},{8,2},{14,4},{20,6},{26,8},{0,10},{6,12},{12,14},{18,16},{24... | collective-permute-start | bytes 110600 | tf_op jit(solution)/shard_map/ppermute | solution.py:733
  289.4 1.9 collective-permute-start.31
  292.2 1.9 collective-permute-start.27
  296.6 3.8 %collective-permute-done.28 = bf16[80,384]{1,0:T(8,128)(2,1)S(1)} collective-permute-done((bf16[80,384]{1,0:T(8,128)(2,1)S(1)}, bf16[80,384]{1,0:T(8,128)(2,1)S(1)}, u32[]{:S(2)}, u32[]{:S(2)}) %collective-permute-start.28) | collective-permute-done | bytes 61472 | tf_op jit(solution)/shard_map/ppermute | solution.py:722
  301.7 2.5 add_convert_fusion
  304.4 2.0 collective-permute-start.34
  307.7 4.9 %collective-permute-done.33 = bf16[48,3072]{1,0:T(8,128)(2,1)S(1)} collective-permute-done((bf16[48,3072]{1,0:T(8,128)(2,1)S(1)}, bf16[48,3072]{1,0:T(8,128)(2,1)S(1)}, u32[]{:S(2)}, u32[]{:S(2)}) %collective-permute-start.33) | collective-permute-done | bytes 294944 | tf_op jit(solution)/shard_map/ppermute | solution.py:655
  312.6 17.1 %collective-permute-done.34 = bf16[48,3072]{1,0:T(8,128)(2,1)S(1)} collective-permute-done((bf16[48,3072]{1,0:T(8,128)(2,1)S(1)}, bf16[48,3072]{1,0:T(8,128)(2,1)S(1)}, u32[]{:S(2)}, u32[]{:S(2)}) %collective-permute-start.34) | collective-permute-done | bytes 294944 | tf_op jit(solution)/shard_map/ppermute | solution.py:655
  329.7 3.2 collective-permute-done.35
  (366 shorter events, 97.4 us)
Async XLA Ops:
  3.0 21.9 %collective-permute-start = (bf16[136,768]{1,0:T(8,128)(2,1)}, bf16[136,768]{1,0:T(8,128)(2,1)S(1)}, u32[]{:S(2)}, u32[]{:S(2)}) collective-permute-start(bf16[136,768]{1,0:T(8,128)(2,1)} %get-tuple-element.153), channel_id=1, source_target_pairs={{0,8},{8,16},{16,24},{24,0},{1,9},{9,17},{17,25},{25,1},{2,10},{10... | collective-permute-start | bytes 626696 | tf_op jit(solution)/shard_map/ppermute | solution.py:458
  4.3 20.6 %collective-permute-start.1 = (bf16[136,768]{1,0:T(8,128)(2,1)}, bf16[136,768]{1,0:T(8,128)(2,1)S(1)}, u32[]{:S(2)}, u32[]{:S(2)}) collective-permute-start(bf16[136,768]{1,0:T(8,128)(2,1)} %get-tuple-element.153), channel_id=1, source_target_pairs={{0,16},{8,24},{16,0},{24,8},{1,17},{9,25},{17,1},{25,9},{2,18},{10... | collective-permute-start | bytes 626696 | tf_op jit(solution)/shard_map/ppermute | solution.py:458
  5.4 19.5 %collective-permute-start.2 = (bf16[136,768]{1,0:T(8,128)(2,1)}, bf16[136,768]{1,0:T(8,128)(2,1)S(1)}, u32[]{:S(2)}, u32[]{:S(2)}) collective-permute-start(bf16[136,768]{1,0:T(8,128)(2,1)} %get-tuple-element.153), channel_id=1, source_target_pairs={{0,24},{8,0},{16,8},{24,16},{1,25},{9,1},{17,9},{25,17},{2,26},{10... | collective-permute-start | bytes 626696 | tf_op jit(solution)/shard_map/ppermute | solution.py:458
  8.4 23.2 %collective-permute-start.4 = (bf16[384,576]{1,0:T(8,128)(2,1)S(1)}, bf16[384,576]{1,0:T(8,128)(2,1)S(1)}, u32[]{:S(2)}, u32[]{:S(2)}) collective-permute-start(bf16[384,576]{1,0:T(8,128)(2,1)S(1)} %pad_maximum_fusion.5), channel_id=1, source_target_pairs={{0,1},{1,0},{2,3},{3,2},{4,5},{5,4},{6,7},{7,6},{8,9},{9,8},{10,11... | collective-permute-start | bytes 1327112 | tf_op jit(solution)/shard_map/ppermute | solution.py:488
  9.0 10.9 %collective-permute-start.3 = (bf16[16,384]{1,0:T(8,128)(2,1)S(1)}, bf16[16,384]{1,0:T(8,128)(2,1)S(1)}, u32[]{:S(2)}, u32[]{:S(2)}) collective-permute-start(bf16[16,384]{1,0:T(8,128)(2,1)S(1)} %concatenate.79), channel_id=1, source_target_pairs={{0,1},{1,0},{2,3},{3,2},{4,5},{5,4},{6,7},{7,6},{8,9},{9,8},{10,11... | collective-permute-start | bytes 36872 | tf_op jit(solution)/shard_map/ppermute | solution.py:488
  11.3 65.2 %copy-start.52 = (s32[128]{0:T(128)}, s32[128]{0:T(128)S(1)}, u32[]{:S(2)}) copy-start(s32[128]{0:T(128)S(1)} %get-tuple-element.114) | copy-start | bytes 1540
  11.3 65.2 %copy-start.54 = (s32[128]{0:T(128)}, s32[128]{0:T(128)S(1)}, u32[]{:S(2)}) copy-start(s32[128]{0:T(128)S(1)} %get-tuple-element.115) | copy-start | bytes 1540
  13.0 11.9 %copy-start.58 = (s32[2304]{0:T(1024)}, s32[2304]{0:T(1024)S(1)}, u32[]{:S(2)}) copy-start(s32[2304]{0:T(1024)S(1)} %concatenate.80) | copy-start | bytes 27652
  26.9 19.7 %all-to-all-start = ((bf16[8,40,768]{2,1,0:T(8,128)(2,1)}), bf16[8,40,768]{2,1,0:T(8,128)(2,1)S(1)}, u32[]{:S(2)}, u32[]{:S(2)}) async-start(bf16[8,40,768]{2,1,0:T(8,128)(2,1)} %bitcast.15), calls=%async_computation | async-start | bytes 983040 | tf_op jit(solution)/shard_map/all_to_all | solution.py:564
  33.1 8.5 %collective-permute-start.6 = (bf16[4,136,384]{2,1,0:T(8,128)(2,1)S(1)}, bf16[4,136,384]{2,1,0:T(8,128)(2,1)S(1)}, u32[]{:S(2)}, u32[]{:S(2)}) collective-permute-start(bf16[4,136,384]{2,1,0:T(8,128)(2,1)S(1)} %pad_maximum_fusion.8.refs_0_), channel_id=1, source_target_pairs={{0,4},{2,6},{4,0},{6,2},{1,5},{3,7},{5,1},{7,3},{8,12},{10,14},{12... | collective-permute-start | bytes 1253384 | tf_op jit(solution)/shard_map/ppermute | solution.py:467
  34.4 12.2 %collective-permute-start.5 = (bf16[4,136,384]{2,1,0:T(8,128)(2,1)S(1)}, bf16[4,136,384]{2,1,0:T(8,128)(2,1)S(1)}, u32[]{:S(2)}, u32[]{:S(2)}) collective-permute-start(bf16[4,136,384]{2,1,0:T(8,128)(2,1)S(1)} %pad_maximum_fusion.8.refs_0_), channel_id=1, source_target_pairs={{0,2},{2,0},{4,6},{6,4},{1,3},{3,1},{5,7},{7,5},{8,10},{10,8},{12,... | collective-permute-start | bytes 1253384 | tf_op jit(solution)/shard_map/ppermute | solution.py:467
  41.6 5.0 %collective-permute-start.7 = (bf16[4,136,384]{2,1,0:T(8,128)(2,1)S(1)}, bf16[4,136,384]{2,1,0:T(8,128)(2,1)S(1)}, u32[]{:S(2)}, u32[]{:S(2)}) collective-permute-start(bf16[4,136,384]{2,1,0:T(8,128)(2,1)S(1)} %collective-permute-done.6.refs_2_), channel_id=1, source_target_pairs={{0,2},{2,0},{4,6},{6,4},{1,3},{3,1},{5,7},{7,5},{8,10},{10,8},{12,... | collective-permute-start | bytes 1253384 | tf_op jit(solution)/shard_map/ppermute | solution.py:467
  46.3 14.9 %copy-start.2 = (bf16[512,192]{1,0:T(8,128)(2,1)}, bf16[512,192]{1,0:T(8,128)(2,1)S(1)}, u32[]{:S(2)}) copy-start(bf16[512,192]{1,0:T(8,128)(2,1)S(1)} %slice.248.q_ref) | copy-start | bytes 589828
  46.3 23.2 %collective-permute-start.8 = (bf16[384,768]{1,0:T(8,128)(2,1)}, bf16[384,768]{1,0:T(8,128)(2,1)}, u32[]{:S(2)}, u32[]{:S(2)}) collective-permute-start(bf16[384,768]{1,0:T(8,128)(2,1)} %param.22), channel_id=1, source_target_pairs={{0,1},{1,0},{2,3},{3,2},{4,5},{5,4},{6,7},{7,6},{8,9},{9,8},{10,11... | collective-permute-start | bytes 1769480 | tf_op jit(solution)/shard_map/ppermute | solution.py:488
  64.9 9.9 %all-to-all-start.1 = ((bf16[4,128,192]{1,2,0:T(8,128)(2,1)}), bf16[4,128,192]{1,2,0:T(8,128)(2,1)S(1)}, u32[]{:S(2)}, u32[]{:S(2)}) async-start(bf16[4,128,192]{1,2,0:T(8,128)(2,1)} %copy.107), calls=%async_computation.1 | async-start | bytes 393216 | tf_op jit(solution)/shard_map/all_to_all | solution.py:493
  78.0 17.5 %all-to-all-start.2 = ((bf16[8,40,896]{2,1,0:T(8,128)(2,1)}), bf16[8,40,896]{2,1,0:T(8,128)(2,1)S(1)}, u32[]{:S(2)}, u32[]{:S(2)}) async-start(bf16[8,40,896]{2,1,0:T(8,128)(2,1)} %pad_maximum_fusion.4), calls=%async_computation.2 | async-start | bytes 1146880 | tf_op jit(solution)/shard_map/all_to_all | solution.py:564
  107.3 15.8 %copy-start.5 = (bf16[2,768,320]{2,1,0:T(8,128)(2,1)}, bf16[2,768,320]{2,1,0:T(8,128)(2,1)S(1)}, u32[]{:S(2)}) copy-start(bf16[2,768,320]{2,1,0:T(8,128)(2,1)S(1)} %get-tuple-element.68.lhs_ref) | copy-start | bytes 2949124
  107.3 24.9 %all-to-all-start.3 = ((bf16[8,40,896]{2,1,0:T(8,128)(2,1)}), bf16[8,40,896]{2,1,0:T(8,128)(2,1)}, u32[]{:S(2)}, u32[]{:S(2)}) async-start(bf16[8,40,896]{2,1,0:T(8,128)(2,1)} %bitcast.29), calls=%async_computation.3 | async-start | bytes 1146880 | tf_op jit(solution)/shard_map/all_to_all | solution.py:564
  123.1 35.9 %collective-permute-start.10 = (bf16[384,3072]{1,0:T(8,128)(2,1)}, bf16[384,3072]{1,0:T(8,128)(2,1)}, u32[]{:S(2)}, u32[]{:S(2)}) collective-permute-start(bf16[384,3072]{1,0:T(8,128)(2,1)} %get-tuple-element.75), channel_id=1, source_target_pairs={{0,2},{2,0},{1,3},{3,1},{4,6},{6,4},{5,7},{7,5},{8,10},{10,8},{9,1... | collective-permute-start | bytes 7077896 | tf_op jit(solution)/shard_map/ppermute | solution.py:477
  132.2 31.2 %collective-permute-start.9 = (bf16[384,3072]{1,0:T(8,128)(2,1)}, bf16[384,3072]{1,0:T(8,128)(2,1)}, u32[]{:S(2)}, u32[]{:S(2)}) collective-permute-start(bf16[384,3072]{1,0:T(8,128)(2,1)} %get-tuple-element.72), channel_id=1, source_target_pairs={{0,2},{2,0},{1,3},{3,1},{4,6},{6,4},{5,7},{7,5},{8,10},{10,8},{9,1... | collective-permute-start | bytes 7077896 | tf_op jit(solution)/shard_map/ppermute | solution.py:477
  146.4 10.4 %collective-permute-start.11 = (bf16[8,48,768]{2,1,0:T(8,128)(2,1)}, bf16[8,48,768]{2,1,0:T(8,128)(2,1)}, u32[]{:S(2)}, u32[]{:S(2)}) collective-permute-start(bf16[8,48,768]{2,1,0:T(8,128)(2,1)} %fusion.8), channel_id=1, source_target_pairs={{0,2},{2,0},{1,3},{3,1},{4,6},{6,4},{5,7},{7,5},{8,10},{10,8},{9,1... | collective-permute-start | bytes 1769480 | tf_op jit(solution)/shard_map/ppermute | solution.py:477
  167.8 12.9 %all-to-all-start.4 = ((bf16[4,128,192]{1,2,0:T(8,128)(2,1)}), bf16[4,128,192]{1,2,0:T(8,128)(2,1)}, u32[]{:S(2)}, u32[]{:S(2)}) async-start(bf16[4,128,192]{1,2,0:T(8,128)(2,1)} %bitcast.190), calls=%async_computation.4 | async-start | bytes 393216 | tf_op jit(solution)/shard_map/all_to_all | solution.py:493
  175.8 43.9 %collective-permute-start.15 = (bf16[192,3072]{1,0:T(8,128)(2,1)}, bf16[192,3072]{1,0:T(8,128)(2,1)}, u32[]{:S(2)}, u32[]{:S(2)}) collective-permute-start(bf16[192,3072]{1,0:T(8,128)(2,1)} %add_convert_fusion.2), channel_id=1, source_target_pairs={{0,4},{4,0},{1,5},{5,1},{2,6},{6,2},{3,7},{7,3},{8,12},{12,8},{9,1... | collective-permute-start | bytes 3538952 | tf_op jit(solution)/shard_map/ppermute | solution.py:477
  184.2 32.0 %collective-permute-start.12 = (bf16[8,48,384]{2,1,0:T(8,128)(2,1)}, bf16[8,48,384]{2,1,0:T(8,128)(2,1)}, u32[]{:S(2)}, u32[]{:S(2)}) collective-permute-start(bf16[8,48,384]{2,1,0:T(8,128)(2,1)} %select_convert_fusion), channel_id=1, source_target_pairs={{0,1},{1,0},{2,3},{3,2},{4,5},{5,4},{6,7},{7,6},{8,9},{9,8},{10,11... | collective-permute-start | bytes 884744 | tf_op jit(solution)/shard_map/ppermute | solution.py:477
  192.9 22.6 %copy-start.59 = (s32[2304]{0:T(1024)S(1)}, s32[2304]{0:T(1024)}, u32[]{:S(2)}) copy-start(s32[2304]{0:T(1024)} %copy-done.58) | copy-start | bytes 27652
  208.3 10.2 %collective-permute-start.14 = (bf16[4,128,384]{2,1,0:T(8,128)(2,1)}, bf16[4,128,384]{2,1,0:T(8,128)(2,1)}, u32[]{:S(2)}, u32[]{:S(2)}) collective-permute-start(bf16[4,128,384]{2,1,0:T(8,128)(2,1)} %get-tuple-element.91), channel_id=1, source_target_pairs={{0,2},{2,0},{1,3},{3,1},{4,6},{6,4},{5,7},{7,5},{8,10},{10,8},{9,1... | collective-permute-start | bytes 1179656 | tf_op jit(solution)/shard_map/ppermute | solution.py:477
  209.5 19.9 %collective-permute-start.13 = (bf16[4,128,384]{2,1,0:T(8,128)(2,1)}, bf16[4,128,384]{2,1,0:T(8,128)(2,1)}, u32[]{:S(2)}, u32[]{:S(2)}) collective-permute-start(bf16[4,128,384]{2,1,0:T(8,128)(2,1)} %get-tuple-element.89), channel_id=1, source_target_pairs={{0,2},{2,0},{1,3},{3,1},{4,6},{6,4},{5,7},{7,5},{8,10},{10,8},{9,1... | collective-permute-start | bytes 1179656 | tf_op jit(solution)/shard_map/ppermute | solution.py:477
  209.6 26.9 %all-to-all-start.5 = ((bf16[8,40,768]{2,1,0:T(8,128)(2,1)}), bf16[8,40,768]{2,1,0:T(8,128)(2,1)}, u32[]{:S(2)}, u32[]{:S(2)}) async-start(bf16[8,40,768]{2,1,0:T(8,128)(2,1)} %bitcast.44), calls=%async_computation.5 | async-start | bytes 983040 | tf_op jit(solution)/shard_map/all_to_all | solution.py:564
  221.2 9.8 %collective-permute-start.16 = (bf16[4,128,384]{2,1,0:T(8,128)(2,1)S(1)}, bf16[4,128,384]{2,1,0:T(8,128)(2,1)S(1)}, u32[]{:S(2)}, u32[]{:S(2)}) collective-permute-start(bf16[4,128,384]{2,1,0:T(8,128)(2,1)S(1)} %convert_add_fusion), channel_id=1, source_target_pairs={{0,4},{4,0},{1,5},{5,1},{2,6},{6,2},{3,7},{7,3},{8,12},{12,8},{9,1... | collective-permute-start | bytes 1179656 | tf_op jit(solution)/shard_map/ppermute | solution.py:477
  225.8 10.6 %collective-permute-start.17 = (bf16[48,3072]{1,0:T(8,128)(2,1)}, bf16[48,3072]{1,0:T(8,128)(2,1)}, u32[]{:S(2)}, u32[]{:S(2)}) collective-permute-start(bf16[48,3072]{1,0:T(8,128)(2,1)} %get-tuple-element.145), channel_id=1, source_target_pairs={{0,8},{8,16},{16,24},{24,0},{1,9},{9,17},{17,25},{25,1},{2,10},{10... | collective-permute-start | bytes 884744 | tf_op jit(solution)/shard_map/ppermute | solution.py:655
  227.0 24.6 %collective-permute-start.18 = (bf16[48,3072]{1,0:T(8,128)(2,1)}, bf16[48,3072]{1,0:T(8,128)(2,1)}, u32[]{:S(2)}, u32[]{:S(2)}) collective-permute-start(bf16[48,3072]{1,0:T(8,128)(2,1)} %get-tuple-element.144), channel_id=1, source_target_pairs={{0,16},{8,24},{16,0},{24,8},{1,17},{9,25},{17,1},{25,9},{2,18},{10... | collective-permute-start | bytes 884744 | tf_op jit(solution)/shard_map/ppermute | solution.py:655
  228.1 26.8 %collective-permute-start.19 = (bf16[48,3072]{1,0:T(8,128)(2,1)}, bf16[48,3072]{1,0:T(8,128)(2,1)}, u32[]{:S(2)}, u32[]{:S(2)}) collective-permute-start(bf16[48,3072]{1,0:T(8,128)(2,1)} %get-tuple-element.143), channel_id=1, source_target_pairs={{0,24},{8,0},{16,8},{24,16},{1,25},{9,1},{17,9},{25,17},{2,26},{10... | collective-permute-start | bytes 884744 | tf_op jit(solution)/shard_map/ppermute | solution.py:655
  232.1 69.6 %collective-permute-start.32 = (bf16[192,3072]{1,0:T(8,128)(2,1)}, bf16[192,3072]{1,0:T(8,128)(2,1)}, u32[]{:S(2)}, u32[]{:S(2)}) collective-permute-start(bf16[192,3072]{1,0:T(8,128)(2,1)} %add_convert_fusion.3), channel_id=1, source_target_pairs={{0,4},{4,0},{1,5},{5,1},{2,6},{6,2},{3,7},{7,3},{8,12},{12,8},{9,1... | collective-permute-start | bytes 3538952 | tf_op jit(solution)/shard_map/ppermute | solution.py:477
  257.2 8.8 %collective-permute-start.23 = (bf16[320,768]{1,0:T(8,128)(2,1)S(1)}, bf16[320,768]{1,0:T(8,128)(2,1)S(1)}, u32[]{:S(2)}, u32[]{:S(2)}) collective-permute-start(bf16[320,768]{1,0:T(8,128)(2,1)S(1)} %pad_maximum_fusion.6), channel_id=1, source_target_pairs={{0,2},{2,0},{1,3},{3,1},{4,6},{6,4},{5,7},{7,5},{8,10},{10,8},{9,1... | collective-permute-start | bytes 1474568 | tf_op jit(solution)/shard_map/ppermute | solution.py:477
  258.1 7.1 %collective-permute-start.21 = (bf16[128,768]{1,0:T(8,128)(2,1)S(1)}, bf16[128,768]{1,0:T(8,128)(2,1)S(1)}, u32[]{:S(2)}, u32[]{:S(2)}) collective-permute-start(bf16[128,768]{1,0:T(8,128)(2,1)S(1)} %get-tuple-element.148), channel_id=1, source_target_pairs={{0,24},{8,0},{16,8},{24,16},{1,25},{9,1},{17,9},{25,17},{2,26},{10... | collective-permute-start | bytes 589832 | tf_op jit(solution)/shard_map/ppermute | solution.py:670
  258.2 11.1 %collective-permute-start.20 = (bf16[128,768]{1,0:T(8,128)(2,1)S(1)}, bf16[128,768]{1,0:T(8,128)(2,1)S(1)}, u32[]{:S(2)}, u32[]{:S(2)}) collective-permute-start(bf16[128,768]{1,0:T(8,128)(2,1)S(1)} %get-tuple-element.147), channel_id=1, source_target_pairs={{0,8},{8,16},{16,24},{24,0},{1,9},{9,17},{17,25},{25,1},{2,10},{10... | collective-permute-start | bytes 589832 | tf_op jit(solution)/shard_map/ppermute | solution.py:671
  265.3 5.8 %collective-permute-start.22 = (bf16[128,768]{1,0:T(8,128)(2,1)S(1)}, bf16[128,768]{1,0:T(8,128)(2,1)S(1)}, u32[]{:S(2)}, u32[]{:S(2)}) collective-permute-start(bf16[128,768]{1,0:T(8,128)(2,1)S(1)} %fusion.27), channel_id=1, source_target_pairs={{0,24},{8,0},{16,8},{24,16},{1,25},{9,1},{17,9},{25,17},{2,26},{10... | collective-permute-start | bytes 589832 | tf_op jit(solution)/shard_map/ppermute | solution.py:673
  266.4 5.1 %collective-permute-start.24 = (bf16[320,384]{1,0:T(8,128)(2,1)S(1)}, bf16[320,384]{1,0:T(8,128)(2,1)S(1)}, u32[]{:S(2)}, u32[]{:S(2)}) collective-permute-start(bf16[320,384]{1,0:T(8,128)(2,1)S(1)} %pad_maximum_fusion.10), channel_id=1, source_target_pairs={{0,1},{1,0},{2,3},{3,2},{4,5},{5,4},{6,7},{7,6},{8,9},{9,8},{10,11... | collective-permute-start | bytes 737288 | tf_op jit(solution)/shard_map/ppermute | solution.py:477
  272.7 5.5 %collective-permute-start.25 = (bf16[368,384]{1,0:T(8,128)(2,1)S(1)}, bf16[368,384]{1,0:T(8,128)(2,1)S(1)}, u32[]{:S(2)}, u32[]{:S(2)}) collective-permute-start(bf16[368,384]{1,0:T(8,128)(2,1)S(1)} %pad_maximum_fusion.9), channel_id=1, source_target_pairs={{0,4},{4,0},{1,5},{5,1},{2,6},{6,2},{3,7},{7,3},{8,12},{12,8},{9,1... | collective-permute-start | bytes 847880 | tf_op jit(solution)/shard_map/ppermute | solution.py:477
  278.4 13.8 %collective-permute-start.29 = (bf16[48,384]{1,0:T(8,128)(2,1)S(1)}, bf16[48,384]{1,0:T(8,128)(2,1)S(1)}, u32[]{:S(2)}, u32[]{:S(2)}) collective-permute-start(bf16[48,384]{1,0:T(8,128)(2,1)S(1)} %get-tuple-element.154), channel_id=1, source_target_pairs={{0,0},{6,2},{12,4},{18,6},{24,8},{30,10},{4,12},{10,14},{16,16},{2... | collective-permute-start | bytes 110600 | tf_op jit(solution)/shard_map/ppermute | solution.py:733
  280.6 13.5 %collective-permute-start.30 = (bf16[48,384]{1,0:T(8,128)(2,1)S(1)}, bf16[48,384]{1,0:T(8,128)(2,1)S(1)}, u32[]{:S(2)}, u32[]{:S(2)}) collective-permute-start(bf16[48,384]{1,0:T(8,128)(2,1)S(1)} %get-tuple-element.156), channel_id=1, source_target_pairs={{2,0},{8,2},{14,4},{20,6},{26,8},{0,10},{6,12},{12,14},{18,16},{24... | collective-permute-start | bytes 110600 | tf_op jit(solution)/shard_map/ppermute | solution.py:733
  289.4 5.0 %collective-permute-start.31 = (bf16[48,384]{1,0:T(8,128)(2,1)S(1)}, bf16[48,384]{1,0:T(8,128)(2,1)S(1)}, u32[]{:S(2)}, u32[]{:S(2)}) collective-permute-start(bf16[48,384]{1,0:T(8,128)(2,1)S(1)} %get-tuple-element.155), channel_id=1, source_target_pairs={{4,0},{10,2},{16,4},{22,6},{28,8},{2,10},{8,12},{14,14},{20,16},{2... | collective-permute-start | bytes 110600 | tf_op jit(solution)/shard_map/ppermute | solution.py:733
  291.4 5.0 %collective-permute-start.26 = (bf16[80,384]{1,0:T(8,128)(2,1)S(1)}, bf16[80,384]{1,0:T(8,128)(2,1)S(1)}, u32[]{:S(2)}, u32[]{:S(2)}) collective-permute-start(bf16[80,384]{1,0:T(8,128)(2,1)S(1)} %get-tuple-element.161), channel_id=1, source_target_pairs={{0,16},{8,24},{16,0},{24,8},{1,17},{9,25},{17,1},{25,9},{2,18},{10... | collective-permute-start | bytes 184328 | tf_op jit(solution)/shard_map/ppermute | solution.py:722
  292.2 4.4 %collective-permute-start.27 = (bf16[80,384]{1,0:T(8,128)(2,1)S(1)}, bf16[80,384]{1,0:T(8,128)(2,1)S(1)}, u32[]{:S(2)}, u32[]{:S(2)}) collective-permute-start(bf16[80,384]{1,0:T(8,128)(2,1)S(1)} %get-tuple-element.162), channel_id=1, source_target_pairs={{0,8},{8,16},{16,24},{24,0},{1,9},{9,17},{17,25},{25,1},{2,10},{10... | collective-permute-start | bytes 184328 | tf_op jit(solution)/shard_map/ppermute | solution.py:722
  294.1 6.3 %collective-permute-start.28 = (bf16[80,384]{1,0:T(8,128)(2,1)S(1)}, bf16[80,384]{1,0:T(8,128)(2,1)S(1)}, u32[]{:S(2)}, u32[]{:S(2)}) collective-permute-start(bf16[80,384]{1,0:T(8,128)(2,1)S(1)} %get-tuple-element.163), channel_id=1, source_target_pairs={{0,24},{8,0},{16,8},{24,16},{1,25},{9,1},{17,9},{25,17},{2,26},{10... | collective-permute-start | bytes 184328 | tf_op jit(solution)/shard_map/ppermute | solution.py:722
  304.4 8.2 %collective-permute-start.33 = (bf16[48,3072]{1,0:T(8,128)(2,1)S(1)}, bf16[48,3072]{1,0:T(8,128)(2,1)S(1)}, u32[]{:S(2)}, u32[]{:S(2)}) collective-permute-start(bf16[48,3072]{1,0:T(8,128)(2,1)S(1)} %get-tuple-element.138), channel_id=1, source_target_pairs={{0,8},{8,16},{16,24},{24,0},{1,9},{9,17},{17,25},{25,1},{2,10},{10... | collective-permute-start | bytes 884744 | tf_op jit(solution)/shard_map/ppermute | solution.py:655
  304.4 25.3 %collective-permute-start.34 = (bf16[48,3072]{1,0:T(8,128)(2,1)S(1)}, bf16[48,3072]{1,0:T(8,128)(2,1)S(1)}, u32[]{:S(2)}, u32[]{:S(2)}) collective-permute-start(bf16[48,3072]{1,0:T(8,128)(2,1)S(1)} %get-tuple-element.137), channel_id=1, source_target_pairs={{0,16},{8,24},{16,0},{24,8},{1,17},{9,25},{17,1},{25,9},{2,18},{10... | collective-permute-start | bytes 884744 | tf_op jit(solution)/shard_map/ppermute | solution.py:655
  306.4 26.5 %collective-permute-start.35 = (bf16[48,3072]{1,0:T(8,128)(2,1)S(1)}, bf16[48,3072]{1,0:T(8,128)(2,1)S(1)}, u32[]{:S(2)}, u32[]{:S(2)}) collective-permute-start(bf16[48,3072]{1,0:T(8,128)(2,1)S(1)} %get-tuple-element.136), channel_id=1, source_target_pairs={{0,24},{8,0},{16,8},{24,16},{1,25},{9,1},{17,9},{25,17},{2,26},{10... | collective-permute-start | bytes 884744 | tf_op jit(solution)/shard_map/ppermute | solution.py:655
  (73 other events, 240.8 us)

commit v3 on v2

v3 whole, which is shorter than its diff:
```python
import functools

import jax
import jax.numpy as jnp
from jax import lax
from jax.experimental import pallas as pl
from jax.experimental.pallas import tpu as pltpu
from jax.sharding import Mesh, PartitionSpec as P

HEADS = 12
HEAD_DIM = 64
EXPERTS = 8
TOP = 2
BUCKETS = 32
DOCS = 8
CAP = 40
GROUPS = 4
GHEADS = HEADS // GROUPS
GWIDTH = GHEADS * HEAD_DIM
CHUNK = 256

LOG2E = 1.4426950408889634
EPS = 1e-06
LOWEST = -1e30
FULL = lax.Precision.HIGHEST
BF = jnp.bfloat16
F32 = jnp.float32
MEMBERS = ("r", "core")
CTX = ("h", "r", "core")


def normalize(values, weight):
    inv_rms = lax.rsqrt(jnp.mean(values * values, axis=-1, keepdims=True) + EPS)
    return values * inv_rms * weight


def dot(a, b, dims=((1,), (0,))):
    return lax.dot_general(a, b, (dims, ((), ())), preferred_element_type=F32)


def exact_dot(a, b, dims):
    return lax.dot_general(a, b, (dims, ((), ())), precision=FULL)


def xor_perm(mask, size):
    return [(i, i ^ mask) for i in range(size)]


def bits_of(size):
    bit = size // 2
    while bit:
        yield bit
        bit //= 2


def strip_width(blocks, half):
    need = half * (blocks - 1) + CHUNK + half
    return -(-need // 128) * 128


def strips_kernel(g_ref, out_ref):
    half = out_ref.shape[1] // GHEADS
    rolled = [
        pltpu.roll(
            jnp.broadcast_to(g_ref[n : n + 1, :], (half, g_ref.shape[1])), 0, 1, stride=1, stride_axis=0
        )
        for n in range(GHEADS)
    ]
    out_ref[...] = jnp.concatenate(rolled).T


def make_strips(lines, half):
    return pl.pallas_call(
        strips_kernel,
        out_specs=pl.BlockSpec((lines.shape[1], GHEADS * half), lambda: (0, 0)),
        out_shape=pltpu.HBM((lines.shape[1], GHEADS * half), F32),
        cost_estimate=pl.CostEstimate(flops=10**5, bytes_accessed=10**4, transcendentals=0),
        name="strips",
    )(lines)


def own_blocks(size, half):
    a = lax.broadcasted_iota(jnp.int32, (size, size), 0) // half
    b = lax.broadcasted_iota(jnp.int32, (size, size), 1) // half
    return a == b


def spread_rows(x, same):
    return jnp.where(same, jnp.concatenate([x] * GHEADS), 0.0)


def fold_rows(x, same, half):
    y = jnp.where(same, x, 0.0).T
    return sum(y[n * half : (n + 1) * half] for n in range(GHEADS))


def own_columns(x, half):
    return jnp.concatenate(
        [x[n * HEAD_DIM : (n + 1) * HEAD_DIM, n * half : (n + 1) * half] for n in range(GHEADS)]
    )


def spread_columns(x, same):
    return jnp.where(same, jnp.concatenate([x] * GHEADS, axis=1), 0.0)


def group_of(slot, h):
    return lax.rem(h + GROUPS - slot, GROUPS)


def place_of(slot, early, me, h, members, blocks):
    owner = group_of(slot, h) * members + me
    return owner if early else blocks - 1 - owner


def bounds(block, chunk, half, blocks, start):
    top = (blocks - 1 - (block - (CHUNK // half) * chunk)) * half
    lane = lax.broadcasted_iota(jnp.int32, (1, GHEADS * half), 1)
    last = block * half + lax.rem(lane, half) - chunk * CHUNK
    return pl.multiple_of(top, half), last, start - chunk * CHUNK


def forward_kernel(half, blocks, members, pos, q_ref, *refs):
    kvs, refs = refs[:members], refs[members:]
    strip_in, o_ref, *lows, stat_ref, k_out, v_out, kt_out, k_ref, v_ref, kt_ref, vt, strip_ref, sems, strip_sem = refs
    loads = start_copies([(strip_in, strip_ref)], strip_sem)
    size = GHEADS * half
    me, h = pos[0], pos[1]
    tok = 2 * half
    same = own_blocks(size, half)
    key = lax.broadcasted_iota(jnp.int32, (CHUNK, size), 0)
    per = CHUNK // half

    @pl.loop(0, GROUPS)
    def _(slot):
        for j in range(members):
            for early in (True, False):
                block = place_of(slot, early, jnp.bitwise_xor(me, j), h, members, blocks)
                at = pl.ds(pl.multiple_of(lax.rem(block, per) * half, half), half)
                rows = kvs[j][slot, 0 if early else half : half if early else tok, :]
                k_ref[block // per, at, :] = rows[:, :GWIDTH]
                v_ref[block // per, at, :] = rows[:, GWIDTH:]

    @pl.loop(0, blocks // per)
    def _(chunk):
        kt_ref[chunk] = k_ref[chunk].astype(F32).T.astype(BF)
        vt[chunk] = v_ref[chunk].astype(F32).T.astype(BF)

    copies = start_copies([(k_ref, k_out), (v_ref, v_out), (kt_ref, kt_out)], sems)
    docs = jnp.concatenate([kv[a, tok : tok + 1, :tok].astype(F32) for kv in kvs for a in range(GROUPS)])
    begins = [jnp.sum(jnp.where(docs < s, 1.0, 0.0)) for s in range(1, DOCS)]
    for load in loads:
        load.wait()

    @pl.loop(0, q_ref.shape[0] // half)
    def _(i):
        slot, late = i // 2, lax.rem(i, 2)
        owner = group_of(slot, h) * members + me
        block = jnp.where(late == 0, owner, blocks - 1 - owner)
        at = pl.ds(pl.multiple_of(i * half, half), half)
        qt = spread_rows(q_ref[at, :GWIDTH].astype(F32), same).T.astype(BF)
        doc = kvs[0][slot, tok : tok + 1, :tok].astype(F32)
        doc = jnp.where(late == 0, doc[:, :half], doc[:, half:])
        begin = jnp.zeros((1, half), F32)
        for s in range(1, DOCS):
            begin = jnp.where(doc == s, begins[s - 1], begin)
        first = jnp.min(begin).astype(jnp.int32) // CHUNK
        begin = jnp.concatenate([begin] * GHEADS, axis=1)
        start = begin.astype(jnp.int32)

        def visit(chunk, carry):
            peak, total, acc = carry
            top, last, begin = bounds(block, chunk, half, blocks, start)
            t = dot(k_ref[chunk], qt) * (HEAD_DIM**-0.5 * LOG2E) + strip_ref[pl.ds(top, CHUNK), :]
            t = jnp.where((key <= last) & (key >= begin), t, LOWEST)
            new = jnp.maximum(peak, jnp.ceil(jnp.max(t, axis=0, keepdims=True)))
            e = jnp.exp2(t - new)
            fade = jnp.exp2(peak - new)
            total = total * fade + jnp.sum(e, axis=0, keepdims=True)
            acc = acc * fade + dot(vt[chunk], e.astype(BF))
            return new, total, acc

        init = (
            jnp.full((1, size), LOWEST, F32),
            jnp.zeros((1, size), F32),
            jnp.zeros((GWIDTH, size), F32),
        )
        peak, total, acc = lax.fori_loop(first, block // per + 1, visit, init)
        out = own_columns(acc / total, half)
        o_ref[i] = out
        low = out.astype(BF)
        for n in range(GROUPS):
            for part in range(2):

                @pl.when(i == 2 * n + part)
                def _():
                    lows[n][:, part * half : (part + 1) * half] = low

        stat_ref[i, 0:1, :] = peak
        stat_ref[i, 1:2, :] = total
        stat_ref[i, 2:3, :] = begin

    for copy in copies:
        copy.wait()


def backward_kernel(half, blocks, members, pos, *refs):
    dos, refs = refs[:GROUPS], refs[GROUPS:]
    inputs, (dq_ref, *refs) = refs[:7], refs[7:]
    dkvs, refs = refs[:members], refs[members:]
    dline_ref, *held, dk, dv, dstrip, do_ref, sems = refs
    q_ref, strip_ref, o_ref, stat_ref, k_ref, v_ref, kt_ref = held
    size = GHEADS * half
    me, h = pos[0], pos[1]
    width = dstrip.shape[0]
    per = CHUNK // half
    copies = start_copies(list(zip(inputs, held)), sems)
    same = own_blocks(size, half)
    key = lax.broadcasted_iota(jnp.int32, (CHUNK, size), 0)

    @pl.loop(0, blocks // per)
    def _(chunk):
        dk[chunk] = jnp.zeros(dk.shape[1:], F32)
        dv[chunk] = jnp.zeros(dv.shape[1:], F32)

    @pl.loop(0, width // 128)
    def _(j):
        dstrip[pl.ds(pl.multiple_of(j * 128, 128), 128), :] = jnp.zeros((128, size), F32)

    for n in range(GROUPS):
        do_ref[n] = dos[n][...].astype(F32)
    for copy in copies:
        copy.wait()

    @pl.loop(0, q_ref.shape[0] // half)
    def _(i):
        slot, late = i // 2, lax.rem(i, 2)
        owner = group_of(slot, h) * members + me
        block = jnp.where(late == 0, owner, blocks - 1 - owner)
        at = pl.ds(pl.multiple_of(i * half, half), half)
        peak, total, start = (stat_ref[i, n : n + 1, :] for n in range(3))
        first = jnp.min(start).astype(jnp.int32) // CHUNK
        start = start.astype(jnp.int32)
        qs = spread_rows(q_ref[at, :GWIDTH].astype(F32), same)
        qt, qs = qs.T.astype(BF), qs.astype(BF)
        do = do_ref[slot]
        do = jnp.where(late == 0, do[:, :half], do[:, half:])
        corr = jnp.sum(spread_columns(do * o_ref[i], same), axis=0, keepdims=True) / total
        gt = spread_columns(do, same) / total
        gs = gt.T.astype(BF)
        gt = gt.astype(BF)

        def visit(chunk, dq):
            top, last, begin = bounds(block, chunk, half, blocks, start)
            t = dot(k_ref[chunk], qt) * (HEAD_DIM**-0.5 * LOG2E) + strip_ref[pl.ds(top, CHUNK), :]
            t = jnp.where((key <= last) & (key >= begin), t - peak, LOWEST)
            e = jnp.exp2(t)
            s = e * (dot(v_ref[chunk], gt) - corr)
            low = s.astype(BF)
            dk[chunk] += dot(low, qs)
            dv[chunk] += dot(e.astype(BF), gs)
            dstrip[pl.ds(top, CHUNK), :] += s
            return dq + dot(kt_ref[chunk], low)

        dq = lax.fori_loop(first, block // per + 1, visit, jnp.zeros((GWIDTH, size), F32))
        dq_ref[at, :] = (fold_rows(dq, same, half) * HEAD_DIM**-0.5).astype(BF)

    @pl.loop(0, GROUPS)
    def _(slot):
        for j in range(members):
            for early in (True, False):
                block = place_of(slot, early, jnp.bitwise_xor(me, j), h, members, blocks)
                at = pl.ds(pl.multiple_of(lax.rem(block, per) * half, half), half)
                part = jnp.concatenate(
                    [dk[block // per, at, :] * HEAD_DIM**-0.5, dv[block // per, at, :]], axis=1
                )
                dkvs[j][slot, 0 if early else half : half if early else 2 * half, :] = part.astype(BF)

    lines = dstrip[...].T
    for n in range(GHEADS):
        x = lines[n * half : (n + 1) * half]
        rows = half
        while rows > 8:
            rows //= 2
            x = x[:rows] + pltpu.roll(x[rows:], width - rows, 1)
        sub = lax.broadcasted_iota(jnp.int32, x.shape, 0)
        for bit in (4, 2, 1):
            x = jnp.where((sub & bit) != 0, pltpu.roll(x, width - bit, 1), x)
        dline_ref[n : n + 1, :] = jnp.sum(x, axis=0, keepdims=True)


VMEM_SPEC = pl.BlockSpec(memory_space=pltpu.VMEM)
SMEM_SPEC = pl.BlockSpec(memory_space=pltpu.SMEM)
HBM_SPEC = pl.BlockSpec(memory_space=pltpu.HBM)


def in_hbm(*values):
    return [pltpu.with_memory_space_constraint(v, pltpu.HBM) for v in values]


def all_of(x):
    return pl.BlockSpec(x.shape, lambda: (0,) * len(x.shape))


def start_copies(pairs, sems):
    copies = [pltpu.make_async_copy(src, dst, sems.at[i]) for i, (src, dst) in enumerate(pairs)]
    for copy in copies:
        copy.start()
    return copies


def key_shapes(blocks, half):
    chunks = blocks * half // CHUNK
    return ((chunks, CHUNK, GWIDTH), (chunks, CHUNK, GWIDTH), (chunks, GWIDTH, CHUNK))


def attend(pos, q, kvs, strips, blocks):
    rows = q.shape[0]
    half = strips.shape[1] // GHEADS
    shapes = key_shapes(blocks, half)
    o_shape, stat_shape = (rows // half, GWIDTH, half), (rows // half, 8, GHEADS * half)
    return pl.pallas_call(
        functools.partial(forward_kernel, half, blocks, len(kvs)),
        in_specs=[SMEM_SPEC] + [VMEM_SPEC] * (1 + len(kvs)) + [HBM_SPEC],
        out_specs=[all_of(jax.ShapeDtypeStruct(o_shape, F32))]
        + [VMEM_SPEC] * GROUPS
        + [all_of(jax.ShapeDtypeStruct(stat_shape, F32))]
        + [HBM_SPEC] * 3,
        scratch_shapes=[pltpu.VMEM(s, BF) for s in shapes + shapes[2:]]
        + [pltpu.VMEM(strips.shape, F32), pltpu.SemaphoreType.DMA((3,)), pltpu.SemaphoreType.DMA((1,))],
        out_shape=[pltpu.HBM(o_shape, F32)]
        + [jax.ShapeDtypeStruct((GWIDTH, 2 * half), BF)] * GROUPS
        + [pltpu.HBM(stat_shape, F32)]
        + [pltpu.HBM(s, BF) for s in shapes],
        compiler_params=pltpu.CompilerParams(vmem_limit_bytes=32 << 20),
        cost_estimate=pl.CostEstimate(flops=10**5, bytes_accessed=10**4, transcendentals=0),
        name="attend",
    )(pos, q, *kvs, *in_hbm(strips))


def attend_back(pos, q, keys, strips, dos, o, stat, members, blocks):
    rows = q.shape[0]
    half = strips.shape[1] // GHEADS
    shapes = key_shapes(blocks, half)
    kv = jax.ShapeDtypeStruct((GROUPS, 2 * half, 2 * GWIDTH), BF)
    inputs = in_hbm(q, strips, o, stat, *keys)
    return pl.pallas_call(
        functools.partial(backward_kernel, half, blocks, members),
        in_specs=[SMEM_SPEC] + [VMEM_SPEC] * GROUPS + [HBM_SPEC] * len(inputs),
        out_specs=[VMEM_SPEC] * (1 + members) + [pl.BlockSpec((GHEADS, strips.shape[0]), lambda: (0, 0))],
        scratch_shapes=[pltpu.VMEM(x.shape, x.dtype) for x in inputs]
        + [pltpu.VMEM(s, F32) for s in shapes[:2]]
        + [
            pltpu.VMEM(strips.shape, F32),
            pltpu.VMEM((GROUPS, GWIDTH, 2 * half), F32),
            pltpu.SemaphoreType.DMA((len(inputs),)),
        ],
        out_shape=[jax.ShapeDtypeStruct((rows, GWIDTH), BF)]
        + [kv] * members
        + [pltpu.HBM((GHEADS, strips.shape[0]), F32)],
        compiler_params=pltpu.CompilerParams(vmem_limit_bytes=40 << 20),
        cost_estimate=pl.CostEstimate(flops=10**5, bytes_accessed=10**4, transcendentals=0),
        name="attend_back",
    )(pos, *dos, *inputs)


FBLOCK = 768
PIECES = 8


def three_parts(x):
    high = x.astype(BF).astype(F32)
    mid = (x - high).astype(BF).astype(F32)
    low = x - high - mid
    lane = lax.broadcasted_iota(jnp.int32, (x.shape[0], 128), 1)
    return jnp.where(lane == 0, high, jnp.where(lane == 1, mid, jnp.where(lane == 2, low, 0.0))).astype(BF)


def gather_rows(refs):
    return jnp.concatenate([r[...].astype(F32) for r in refs])


def router_kernel(
    pos, x_ref, out_ref, scale_ref, router_ref, routes_ref, place_ref, *refs
):
    lows, refs = refs[:GROUPS], refs[GROUPS:]
    pieces, (context_ref, resid_ref, moe_ref, gates_ref) = refs[:PIECES], refs[PIECES:]
    tok, width = x_ref.shape
    for k in range(GROUPS):
        row = pl.multiple_of(lax.rem(pos[1] + k, GROUPS) * GWIDTH, GWIDTH)
        context_ref[pl.ds(row, GWIDTH), :] = lows[k][...]
    context = context_ref[...].astype(F32).T.astype(BF)
    resid = x_ref[...].astype(F32) + dot(context, out_ref[...])
    resid_ref[...] = resid
    inv = lax.rsqrt(jnp.mean(resid * resid, axis=1, keepdims=True) + EPS)
    moe_in = (resid * inv * scale_ref[...]).astype(BF)
    moe_ref[...] = moe_in
    logits = dot(moe_in, router_ref[...], ((1,), (1,)))
    lane = lax.broadcasted_iota(jnp.int32, logits.shape, 1)
    chosen = [
        jnp.sum(jnp.where(routes_ref[:, k : k + 1] == lane, logits, 0.0), axis=1, keepdims=True)
        for k in range(TOP)
    ]
    most = jnp.maximum(chosen[0], chosen[1])
    powers = [jnp.exp(c - most) for c in chosen]
    gates = [p / (powers[0] + powers[1]) for p in powers]
    slot = lax.broadcasted_iota(jnp.int32, (EXPERTS * CAP, tok), 0)
    pick = [(place_ref[k : k + 1, :] == slot) for k in range(TOP)]
    rows = dot((pick[0] | pick[1]).astype(BF), moe_in)
    extra = sum(dot(pick[k].astype(BF), three_parts(gates[k])) for k in range(TOP))
    for p in range(PIECES):
        pieces[p][:, :width] = rows[p * CAP : (p + 1) * CAP].astype(BF)
        pieces[p][:, width:] = extra[p * CAP : (p + 1) * CAP].astype(BF)
    for k in range(TOP):
        gates_ref[:, k : k + 1] = gates[k]


def router(pos, x, out_full, scale, router_t, routes, places, lows):
    tok, width = x.shape
    kept = [pltpu.HBM(*s) for s in (((width, tok), BF), ((tok, width), F32), ((tok, width), BF), ((tok, TOP), F32))]
    x, out_full = in_hbm(x, out_full)
    return pl.pallas_call(
        router_kernel,
        in_specs=[SMEM_SPEC, all_of(x), all_of(out_full)] + [VMEM_SPEC] * (4 + GROUPS),
        out_specs=[VMEM_SPEC] * PIECES + [all_of(s.inner_aval) for s in kept],
        out_shape=[jax.ShapeDtypeStruct((CAP, width + 128), BF)] * PIECES + kept,
        compiler_params=pltpu.CompilerParams(vmem_limit_bytes=16 << 20),
        cost_estimate=pl.CostEstimate(flops=10**5, bytes_accessed=10**4, transcendentals=0),
        name="router",
    )(pos, x, out_full, scale, router_t, routes, places, *lows)


def expert_kernel(groups, n_fsdp, info, dy_ref, up_ref, down_ref, *refs):
    cames, refs = refs[:PIECES], refs[PIECES:]
    out_refs, (back_ref, act_ref, rows_ref, grad_in, out_acc, back_acc) = refs[:n_fsdp], refs[n_fsdp:]
    step = pl.program_id(0)
    width = grad_in.shape[1]
    h, f = info[0], info[1]
    source = [
        lax.rem(h + groups - p // n_fsdp, groups) * n_fsdp + jnp.bitwise_xor(f, p % n_fsdp) for p in range(PIECES)
    ]

    @pl.when(step == 0)
    def _():
        came = gather_rows(cames)
        gate = jnp.sum(came[:, width:], axis=1, keepdims=True)
        dy = jnp.concatenate([dy_ref[s].astype(F32) for s in source])
        grad_in[...] = dy
        rows_ref[0] = came[:, :width].astype(BF)
        rows_ref[1] = (gate * dy).astype(BF)
        out_acc[...] = jnp.zeros_like(out_acc)
        back_acc[...] = jnp.zeros_like(back_acc)

    up, down = up_ref[0], down_ref[0]
    upper = dot(rows_ref[0], up)
    active_grad = dot(rows_ref[1], down)
    cdf = 0.5 + 0.5 * lax.erf(upper * 0.7071067811865476)
    active = (upper * cdf).astype(BF)
    slope = cdf + upper * (0.3989422804014327 * jnp.exp(-0.5 * upper * upper))
    upper_grad = (active_grad * slope).astype(BF)
    act_ref[0] = upper_grad
    act_ref[1] = active
    back_acc[...] += dot(upper_grad, up, ((1,), (1,)))
    out_acc[...] += dot(active, down, ((1,), (1,)))

    @pl.when(step == pl.num_programs(0) - 1)
    def _():
        out = out_acc[...].astype(BF).astype(F32)
        gate_grad = three_parts(jnp.sum(grad_in[...] * out, axis=1, keepdims=True)).astype(F32)
        for p in range(PIECES):
            rows = slice(p * CAP, (p + 1) * CAP)
            out_refs[p % n_fsdp][lax.rem(h + groups - p // n_fsdp, groups)] = out[rows].astype(BF)
            back_ref[source[p], :, :width] = back_acc[rows, :].astype(BF)
            back_ref[source[p], :, width:] = gate_grad[rows].astype(BF)


def expert(info, cames, dy, up, down, groups, n_fsdp):
    width, ffn = up.shape[1], up.shape[2]
    rows = EXPERTS * CAP
    whole = lambda *shape: pl.BlockSpec(shape, lambda j, info: (0,) * len(shape))
    weight = pl.BlockSpec((1, width, FBLOCK), lambda j, info: (info[0], 0, j))
    return pl.pallas_call(
        functools.partial(expert_kernel, groups, n_fsdp),
        grid_spec=pltpu.PrefetchScalarGridSpec(
            num_scalar_prefetch=1,
            grid=(ffn // FBLOCK,),
            in_specs=[whole(PIECES, CAP, width), weight, weight] + [whole(CAP, width + 128)] * PIECES,
            out_specs=[whole(groups, CAP, width)] * n_fsdp
            + [
                whole(PIECES, CAP, width + 128),
                pl.BlockSpec((2, rows, FBLOCK), lambda j, info: (0, 0, j)),
                whole(2, rows, width),
            ],
            scratch_shapes=[pltpu.VMEM((rows, width), F32)] * 3,
        ),
        out_shape=[pltpu.HBM((groups, CAP, width), BF)] * n_fsdp
        + [
            jax.ShapeDtypeStruct((PIECES, CAP, width + 128), BF),
            pltpu.HBM((2, rows, ffn), BF),
            pltpu.HBM((2, rows, width), BF),
        ],
        compiler_params=pltpu.CompilerParams(vmem_limit_bytes=32 << 20),
        cost_estimate=pl.CostEstimate(flops=10**5, bytes_accessed=10**4, transcendentals=0),
        name="expert",
    )(info, dy, *in_hbm(up, down), *cames)


def weight_kernel(count, members, side, turned_by, pos, *refs):
    rows, acts, (keep_ref, pass_ref, turned, lhs) = refs[:count], refs[count : 2 * count], refs[2 * count :]
    half = keep_ref.shape[0]

    @pl.when(pl.program_id(0) == 0)
    def _():
        for n in range(count):
            turned[...] = rows[n][0].astype(F32).T.astype(BF)
            if side is not None:
                lhs[n] = turned[side * 2 * half : (side + 1) * 2 * half, :]
                continue
            unit = 2 * half // (GROUPS * members // 2)
            for r in range(members // 2):
                member = jnp.bitwise_xor(pos[0], 2 * r)
                for k in range(GROUPS):
                    row = pl.multiple_of((lax.rem(turned_by * pos[1] + k, GROUPS) * members + member) * unit, 16)
                    at = (r * GROUPS + k) * unit
                    lhs[n, at : at + unit, :] = turned[pl.ds(row, unit), :]

    keep_ref[...] = sum(dot(lhs[n, :half, :], acts[n][0]) for n in range(count)).astype(BF)
    pass_ref[...] = sum(dot(lhs[n, half:, :], acts[n][0]) for n in range(count)).astype(BF)


def weight_terms(pos, rows, acts, which, members, side=None):
    _, count, width = rows[0].shape
    ffn = acts[0].shape[2]
    half = pl.BlockSpec((width // 4, FBLOCK), lambda j: (0, j))
    return pl.pallas_call(
        functools.partial(weight_kernel, len(rows), members, side, which),
        grid=(ffn // FBLOCK,),
        in_specs=[SMEM_SPEC]
        + [pl.BlockSpec((1, count, width), lambda j: (which, 0, 0))] * len(rows)
        + [pl.BlockSpec((1, count, FBLOCK), lambda j: (which, 0, j))] * len(rows),
        out_specs=[half, half],
        out_shape=[pltpu.HBM((width // 4, ffn), BF)] * 2,
        scratch_shapes=[pltpu.VMEM((width, count), BF), pltpu.VMEM((len(rows), width // 2, count), BF)],
        compiler_params=pltpu.CompilerParams(vmem_limit_bytes=20 << 20),
        cost_estimate=pl.CostEstimate(flops=10**5, bytes_accessed=10**4, transcendentals=0),
        name="weight_terms",
    )(pos, *rows, *in_hbm(*acts))


def add_kernel(riders, a_ref, b_ref, *refs):
    rides, out = refs[:riders], refs[riders]
    rows, width = a_ref.shape[0] // GROUPS, out.shape[2]
    blocks = a_ref.shape[1] // width
    for k in range(GROUPS):
        for c in range(blocks):
            at = (slice(k * rows, (k + 1) * rows), slice(c * width, (c + 1) * width))
            out[k, c * rows : (c + 1) * rows, :] = (a_ref[at].astype(F32) + b_ref[at].astype(F32)).astype(BF)
        if riders:
            ride = jnp.concatenate([r[k].astype(F32) for r in rides])
            out[k, blocks * rows :, :] = ride.astype(BF)


def add_groups(a, b, width, rides=()):
    rows, cols = a.shape
    count = rows // GROUPS * cols // width + sum(r.shape[1] for r in rides)
    return pl.pallas_call(
        functools.partial(add_kernel, len(rides)),
        in_specs=[all_of(a)] * 2 + [all_of(r) for r in rides],
        out_specs=pl.BlockSpec((GROUPS, count, width), lambda: (0, 0, 0)),
        out_shape=pltpu.HBM((GROUPS, count, width), BF),
        compiler_params=pltpu.CompilerParams(vmem_limit_bytes=16 << 20),
        cost_estimate=pl.CostEstimate(flops=10**5, bytes_accessed=10**4, transcendentals=0),
        name="add_groups",
    )(*in_hbm(a, b, *rides))


def sum_kernel(a_ref, b_ref, *outs):
    rows = outs[0].shape[0]
    for k, out in enumerate(outs):
        at = slice(k * rows, (k + 1) * rows)
        out[...] = (a_ref[at, :].astype(F32) + b_ref[at, :].astype(F32)).astype(BF)


def sum_pieces(a, b):
    rows, cols = a.shape
    return pl.pallas_call(
        sum_kernel,
        in_specs=[all_of(a)] * 2,
        out_specs=[pl.BlockSpec((rows // GROUPS, cols), lambda: (0, 0))] * GROUPS,
        out_shape=[jax.ShapeDtypeStruct((rows // GROUPS, cols), BF)] * GROUPS,
        compiler_params=pltpu.CompilerParams(vmem_limit_bytes=16 << 20),
        cost_estimate=pl.CostEstimate(flops=10**5, bytes_accessed=10**4, transcendentals=0),
        name="sum_pieces",
    )(*in_hbm(a, b))


def order_kernel(pos, *refs):
    for k in range(GROUPS):
        refs[-1][group_of(k, pos[1])] = refs[k][...].astype(F32)


def in_order(pos, parts):
    shape = (GROUPS,) + parts[0].shape
    return pl.pallas_call(
        order_kernel,
        in_specs=[SMEM_SPEC] + [all_of(p) for p in parts],
        out_specs=pl.BlockSpec(shape, lambda: (0, 0, 0)),
        out_shape=jax.ShapeDtypeStruct(shape, F32),
        compiler_params=pltpu.CompilerParams(vmem_limit_bytes=16 << 20),
        cost_estimate=pl.CostEstimate(flops=10**5, bytes_accessed=10**4, transcendentals=0),
        name="in_order",
    )(pos, *parts)


def wide_kernel(blocks, x_ref, out_ref):
    rows, width = out_ref.shape[1], out_ref.shape[2] // blocks
    for k in range(GROUPS):
        for c in range(blocks):
            out_ref[k, :, c * width : (c + 1) * width] = x_ref[k, c * rows : (c + 1) * rows, :].astype(F32)


def to_wide(x, rows, cols):
    width = x.shape[2]
    return pl.pallas_call(
        functools.partial(wide_kernel, cols // width),
        in_specs=[all_of(x)],
        out_specs=pl.BlockSpec((GROUPS, rows, cols), lambda: (0, 0, 0)),
        out_shape=jax.ShapeDtypeStruct((GROUPS, rows, cols), F32),
        compiler_params=pltpu.CompilerParams(vmem_limit_bytes=16 << 20),
        cost_estimate=pl.CostEstimate(flops=10**5, bytes_accessed=10**4, transcendentals=0),
        name="to_wide",
    )(x)


def turn_kernel(
    info, place_ref, routes_ref, gates_ref, resid_ref, moe_ref, dy_ref, router_ref, scale_ref,
    out_ref, context_ref, back_ref, *refs,
):
    dos, (resid_grad_ref, mine_ref, other_ref, send_ref, router_grad_ref, gain_ref, term) = refs[:GROUPS], refs[GROUPS:]
    tok, width = resid_ref.shape
    back = back_ref[...]
    slots = back.shape[0]
    iota = lax.broadcasted_iota(jnp.int32, (tok, slots), 1)
    pick = [place_ref[:, k : k + 1] == iota for k in range(TOP)]
    gates = [gates_ref[:, k : k + 1] for k in range(TOP)]
    gate_grad = [jnp.sum(dot(p.astype(BF), back[:, width:]), axis=1, keepdims=True) for p in pick]
    mean = gates[0] * gate_grad[0] + gates[1] * gate_grad[1]
    lane = lax.broadcasted_iota(jnp.int32, (tok, 128), 1)
    logit_grad = sum(
        jnp.where(routes_ref[:, k : k + 1] == lane, gates[k] * (gate_grad[k] - mean), 0.0) for k in range(TOP)
    )
    grad = dot((pick[0] | pick[1]).astype(BF), back[:, :width])
    for e in range(EXPERTS):
        grad = grad + logit_grad[:, e : e + 1] * router_ref[e : e + 1, :].astype(F32)
    resid = resid_ref[...]
    inv = lax.rsqrt(jnp.mean(resid * resid, axis=1, keepdims=True) + EPS)
    gain_ref[...] = jnp.sum(grad * (resid * inv), axis=0, keepdims=True)
    scaled = grad * scale_ref[...]
    along = jnp.mean(scaled * resid, axis=1, keepdims=True)
    resid_grad = dy_ref[...].astype(F32) + inv * scaled - resid * (inv * inv * inv * along)
    resid_grad_ref[...] = resid_grad
    low = resid_grad.astype(BF)
    term[:, :tok] = dot(out_ref[...], low, ((1,), (1,)))
    for k in range(GROUPS):
        row = pl.multiple_of(lax.rem(info[0] + k, GROUPS) * GWIDTH, GWIDTH)
        dos[k][...] = term[pl.ds(row, GWIDTH), :tok].astype(BF)
    router_grad_ref[...] = lax.dot_general(
        logit_grad.T[:EXPERTS], moe_ref[...].astype(F32), (((1,), (0,)), ((), ())),
        precision=FULL, preferred_element_type=F32,
    )
    term[...] = dot(low.astype(F32).T.astype(BF), context_ref[...].astype(F32).T.astype(BF))
    rows, cols = mine_ref.shape[1:]
    core, top = info[1], info[2]
    mine = pl.ds(pl.multiple_of(top * cols, 128), cols)
    other = pl.ds(pl.multiple_of((1 - top) * cols, 128), cols)
    for g in range(mine_ref.shape[0]):
        keep = pl.ds(pl.multiple_of((2 * g + core) * rows, 8), rows)
        send = pl.ds(pl.multiple_of((2 * g + 1 - core) * rows, 8), rows)
        mine_ref[g] = term[keep, mine]
        other_ref[g] = term[keep, other]
        send_ref[0, g] = term[send, mine].astype(BF)
        send_ref[1, g] = term[send, other].astype(BF)


def turn_back(info, back, place, routes, gates, resid, moe_in, dy, router, scale, out_full, context, shards):
    tok, width = resid.shape
    rows = width // shards
    part = (shards // 2, rows, width // 2)
    gates, resid, moe_in, dy, out_full, context = in_hbm(gates, resid, moe_in, dy, out_full, context)
    inputs = (place, routes, gates, resid, moe_in, dy, router, scale, out_full, context, back)
    kept = [((tok, width), F32), (part, F32), (part, F32), ((2,) + part, BF), ((EXPERTS, width), F32), ((1, width), F32)]
    kept = [pltpu.HBM(*s) for s in kept]
    return pl.pallas_call(
        turn_kernel,
        in_specs=[SMEM_SPEC] + [all_of(x) for x in inputs],
        out_specs=[VMEM_SPEC] * GROUPS + [all_of(s.inner_aval) for s in kept],
        scratch_shapes=[pltpu.VMEM((width, width), F32)],
        out_shape=[jax.ShapeDtypeStruct((GWIDTH, tok), BF)] * GROUPS + kept,
        compiler_params=pltpu.CompilerParams(vmem_limit_bytes=24 << 20),
        cost_estimate=pl.CostEstimate(flops=10**5, bytes_accessed=10**4, transcendentals=0),
        name="turn_back",
    )(info, *inputs)


def pair_kernel(a_ref, b_ref, c_ref, d_ref, keep_ref, send_ref):
    keep_ref[...] = a_ref[...].astype(F32) + b_ref[...].astype(F32)
    send_ref[...] = (c_ref[...].astype(F32) + d_ref[...].astype(F32)).astype(BF)


def add_pairs(a, b, c, d):
    return pl.pallas_call(
        pair_kernel,
        in_specs=[VMEM_SPEC] * 4,
        out_specs=[VMEM_SPEC] * 2,
        out_shape=[jax.ShapeDtypeStruct(a.shape, F32), jax.ShapeDtypeStruct(a.shape, BF)],
        cost_estimate=pl.CostEstimate(flops=10**5, bytes_accessed=10**4, transcendentals=0),
        compiler_params=pltpu.CompilerParams(vmem_limit_bytes=8 << 20),
        name="add_pairs",
    )(a, b, c, d)


SMALL = 16


def input_kernel(
    members, buckets_here, info, dq_ref, keep_ref, came_ref, ain_ref, weight_ref, scale_ref, router_ref,
    gain_ref, line_ref, dline_ref, own_ref, one_ref, two_ref, three_ref, term_ref, sent_ref, pack_ref, dproj, term,
):
    h, core = info[0], info[1]
    width = ain_ref.shape[1]
    tok = own_ref.shape[0]
    dproj[:, :GWIDTH] = dq_ref[...].astype(F32)
    for k in range(GROUPS):
        dkv = keep_ref[k] if came_ref is None else keep_ref[k] + came_ref[k].astype(F32)
        dproj[k * tok : (k + 1) * tok, GWIDTH:] = dkv.astype(BF).astype(F32)
    low = dproj[...].astype(BF)
    ain = ain_ref[...]
    back = dot(low, weight_ref[...], ((1,), (1,)))
    own_ref[...] = back[:tok]
    for k, ref in enumerate((one_ref, two_ref, three_ref)):
        ref[...] = back[(k + 1) * tok : (k + 2) * tok].astype(BF)
    pack_ref[0:EXPERTS, :] = router_ref[...]
    pack_ref[EXPERTS : EXPERTS + 1, :] = jnp.sum(back * ain.astype(F32), axis=0, keepdims=True) / scale_ref[...]
    pack_ref[EXPERTS + 1 : EXPERTS + 2, :] = gain_ref[...]
    col = lax.broadcasted_iota(jnp.int32, (BUCKETS, width), 1)
    cols_f = width * buckets_here // BUCKETS
    within = lax.rem(col, cols_f) - h * buckets_here
    held = jnp.where((within >= 0) & (within < buckets_here), col // cols_f * buckets_here + within, -1)
    held = held == lax.broadcasted_iota(jnp.int32, (BUCKETS, width), 0)
    bucket = line_ref[...] == lax.broadcasted_iota(jnp.int32, (BUCKETS, line_ref.shape[1]), 0)
    for n in range(GHEADS):
        sums = jnp.sum(jnp.where(bucket, dline_ref[n : n + 1, :], 0.0), axis=1, keepdims=True)
        row = EXPERTS + 2 + n
        pack_ref[row : row + 1, :] = jnp.sum(jnp.where(held, sums, 0.0), axis=0, keepdims=True)
    rest = EXPERTS + 2 + GHEADS
    pack_ref[rest:, :] = jnp.zeros((SMALL - rest, width), F32)
    term[...] = dot(dproj[...].T.astype(BF), ain)
    unit = GWIDTH // members
    for t in range(3):
        for r in range(members // 2):
            at = slice((t * (members // 2) + r) * unit, (t * (members // 2) + r + 1) * unit)
            first = (t * members + 2 * r) * unit
            term_ref[at, :] = term[pl.ds(pl.multiple_of(first + core * unit, 8), unit), :]
            sent_ref[at, :] = term[pl.ds(pl.multiple_of(first + (1 - core) * unit, 8), unit), :].astype(BF)
    pack = pack_ref[...]
    high = pack.astype(BF)
    rows = term_ref.shape[0]
    sent_ref[rows : rows + SMALL, :] = high
    sent_ref[rows + SMALL :, :] = (pack - high.astype(F32)).astype(BF)


def input_back(info, members, buckets_here, dq, keep, came, ain, weight, scale, router_grad, gain_grad, line, dline):
    count, width = ain.shape
    tok = count // GROUPS
    rows = 3 * GWIDTH // 2
    ain, weight = in_hbm(ain, weight)
    inputs = [dq, keep] + ([] if came is None else [came]) + [ain, weight, scale, router_grad, gain_grad, line, dline]
    body = functools.partial(input_kernel, members, buckets_here)
    if came is None:
        body = lambda info, dq, keep, *refs: input_kernel(members, buckets_here, info, dq, keep, None, *refs)
    return pl.pallas_call(
        body,
        in_specs=[SMEM_SPEC] + [all_of(x) for x in inputs],
        out_specs=[VMEM_SPEC] * 7,
        out_shape=[jax.ShapeDtypeStruct((tok, width), F32)]
        + [jax.ShapeDtypeStruct((tok, width), BF)] * 3
        + [
            jax.ShapeDtypeStruct((rows, width), F32),
            jax.ShapeDtypeStruct((rows + 2 * SMALL, width), BF),
            jax.ShapeDtypeStruct((SMALL, width), F32),
        ],
        scratch_shapes=[pltpu.VMEM((count, 3 * GWIDTH), F32), pltpu.VMEM((3 * GWIDTH, width), F32)],
        compiler_params=pltpu.CompilerParams(vmem_limit_bytes=24 << 20),
        cost_estimate=pl.CostEstimate(flops=10**5, bytes_accessed=10**4, transcendentals=0),
        name="input_back",
    )(info, *inputs)


def together(*values):
    return lax.optimization_barrier(values)


def turn(shift):
    return [(i, (i + shift) % GROUPS) for i in range(GROUPS)]


def gather_groups(x):
    came = {k: lax.ppermute(x, "h", turn(k)) for k in (2, 1, 3)}
    return jnp.stack([x] + [came[k] for k in range(1, GROUPS)])


def gather_members(x):
    size = lax.axis_size(MEMBERS)
    held = {0: x}
    for bit in bits_of(size):
        for k in sorted(held):
            held[k | bit] = lax.ppermute(held[k], MEMBERS, xor_perm(bit, size))
    return [held[k] for k in range(size)]


def part_of(x, mine):
    low, high = jnp.split(x, 2, axis=-1)
    return jnp.where(mine == 0, low, high), jnp.where(mine == 0, high, low)


def swap(x, axis, bit):
    return lax.ppermute(x, axis, xor_perm(bit, lax.axis_size(axis)))


def two_parts(x):
    high = lax.reduce_precision(x, 8, 7)
    return jnp.concatenate([high, x - high]).astype(BF)


def from_fsdp(part):
    if lax.axis_size("fsdp") != 2:
        return lax.all_gather(part, "fsdp", axis=0)
    came = lax.ppermute(part, "fsdp", xor_perm(1, 2))
    return jnp.where(lax.axis_index("fsdp") == 0, jnp.stack([part, came]), jnp.stack([came, part]))


def swap_groups(x):
    return lax.all_to_all(x, "h", 0, 0, tiled=True)


def group_pieces(pieces, sign):
    came = {k: lax.ppermute(pieces[k], "h", turn(sign * k)) for k in (2, 1, 3)}
    return [pieces[0]] + [came[k] for k in range(1, GROUPS)]


def deal(pieces, spread, sign):
    n_fsdp = lax.axis_size("fsdp")
    out = [pieces[0]] + [None] * (len(pieces) - 1)
    for p in (5, 4, 3, 7, 2, 6, 1):
        k, j = divmod(p, n_fsdp)
        if spread:
            pairs = [
                (g * n_fsdp + i, (g + sign * k) % GROUPS * n_fsdp + (i ^ j))
                for g in range(GROUPS)
                for i in range(n_fsdp)
            ]
            out[p] = lax.ppermute(pieces[p], ("h", "fsdp"), pairs)
        else:
            out[p] = lax.ppermute(pieces[p], "fsdp", xor_perm(j, n_fsdp))
    return out


def per_device(
    tokens, segments, routes, bucket_table, attn_gain, qkv_weight, out_weight, bias_table,
    moe_gain, router_weight, up_weight, down_weight, cotangent,
):
    tok, width = tokens.shape[1], tokens.shape[2]
    half = tok // 2
    h, m, f = lax.axis_index("h"), lax.axis_index(MEMBERS), lax.axis_index("fsdp")
    core = lax.axis_index("core")
    members, n_fsdp = lax.axis_size(MEMBERS), lax.axis_size("fsdp")
    shards = GROUPS * members
    blocks = 2 * shards
    length = shards * tok
    here = EXPERTS // n_fsdp
    spread = here > 1
    ffn = up_weight.shape[2]
    rows_f = width // n_fsdp
    rows_c = width // shards
    pos = jnp.stack([m, h]).astype(jnp.int32)

    extra = jnp.pad(segments.astype(BF), ((0, 7), (0, width - tok)))
    mixed = gather_groups(jnp.concatenate([tokens[0], extra]))

    bias_flat = bias_table.reshape(1, -1)
    bias_rows = -(-bias_flat.shape[1] // rows_f)
    bias_flat = jnp.pad(bias_flat, ((0, 0), (0, bias_rows * rows_f - bias_flat.shape[1])))
    small = jnp.concatenate(
        [attn_gain[None], moe_gain[None], router_weight.T, bias_flat.reshape(bias_rows, rows_f)]
        + [jnp.zeros((16 - 10 - bias_rows, rows_f), BF)]
    )
    small = from_fsdp(small)
    attn_scale = small[:, 0].reshape(width).astype(F32)
    moe_scale = small[:, 1].reshape(width).astype(F32)
    router_t = jnp.transpose(small[:, 2:10], (1, 0, 2)).reshape(EXPERTS, width)
    bias_full = small[:, 10 : 10 + bias_rows].reshape(n_fsdp, -1)[:, : bias_table.size]
    bias_full = bias_full.reshape(BUCKETS, HEADS)
    cut = [
        lax.dynamic_slice_in_dim(qkv_weight, n * width + h * GWIDTH, GWIDTH, 1) for n in range(3)
    ]
    qkv_heads = from_fsdp(jnp.concatenate(cut, axis=1)).reshape(width, 3 * GWIDTH)
    out_full = from_fsdp(together(out_weight, qkv_heads)[0]).reshape(width, width)

    wide = strip_width(blocks, half)
    top = half * (blocks - 1)
    line = jnp.concatenate(
        [
            bucket_table[: top + 1][::-1],
            jnp.full((wide - length,), -1, jnp.int32),
            bucket_table[top + 1 :][::-1],
        ]
    )
    hot = (line[None] == jnp.arange(BUCKETS, dtype=jnp.int32)[:, None]).astype(BF)
    bias_mine = lax.dynamic_slice_in_dim(bias_full, h * GHEADS, GHEADS, 1)
    strips = make_strips(dot(bias_mine, hot, ((0,), (0,))) * LOG2E, half)

    hot_routes = (routes.reshape(-1)[:, None] == jnp.arange(EXPERTS)[None]).astype(F32)
    earlier = jnp.arange(tok * TOP)
    earlier = (earlier[None, :] < earlier[:, None]).astype(BF)
    before = dot(earlier, hot_routes.astype(BF))
    slot = jnp.sum(before * hot_routes, axis=1).astype(jnp.int32).reshape(tok, TOP)
    group = routes % here
    natural = (group * n_fsdp + routes // here) * CAP + slot
    away = lax.rem(group - h + GROUPS, GROUPS) if spread else group
    place = (away * n_fsdp + jnp.bitwise_xor(routes // here, f)) * CAP + slot
    slots = jnp.arange(EXPERTS * CAP, dtype=jnp.int32)
    pick = [slots[:, None] == natural[None, :, k] for k in range(TOP)]
    exchange = ("h", "fsdp") if spread else ("fsdp",)

    def exchange_rows(rows):
        return lax.all_to_all(rows, exchange, 0, 0, tiled=True)

    mixed, strips = together(mixed, strips)
    ain = normalize(mixed[:, :tok].astype(F32), attn_scale).astype(BF).reshape(GROUPS * tok, width)
    proj = dot(ain, qkv_heads).astype(BF)
    kv = proj[:, GWIDTH:].reshape(GROUPS, tok, 2 * GWIDTH)
    kvs = gather_members(jnp.concatenate([kv, mixed[:, tok:, : 2 * GWIDTH]], axis=1))
    dy_send = dot((pick[0] | pick[1]).astype(BF), cotangent[0]).astype(BF).reshape(PIECES, CAP, width)
    dy_send = together(dy_send, qkv_heads)[0]
    kvs[0], dy_slots = together(kvs[0], exchange_rows(dy_send))
    o_pre, *rest = attend(pos, proj, kvs, strips, blocks)
    lows, stat, keys = rest[:GROUPS], rest[GROUPS], rest[GROUPS + 1 :]
    *pieces, context, residual, moe_in, gates = router(
        pos, tokens[0], out_full, moe_scale[None], router_t, routes, place.T, group_pieces(lows, -1)
    )

    came = deal(pieces, spread, 1)
    info = jnp.stack([h if spread else jnp.zeros_like(h), f]).astype(jnp.int32)
    *outs, back, act, rows = expert(
        info, came, dy_slots, up_weight, down_weight, GROUPS if spread else 1, n_fsdp
    )
    back = exchange_rows(back).reshape(EXPERTS * CAP, -1)

    staged = spread and members == 4
    if staged:
        rows, acts = [rows, swap(rows, "core", 1)], [act, swap(act, "core", 1)]
        terms = [weight_terms(pos, rows, acts, n, members) for n in range(2)]
        back, terms = together(back, terms)
    else:
        terms = [weight_terms(pos, [rows], [act], n, members, side) for n in range(2) for side in range(2)]

    top_bit = n_fsdp // 2
    info = jnp.stack([h, core, (f // top_bit) % 2]).astype(jnp.int32)
    *dos, resid_grad, out_mine, out_other, out_send, router_grad, moe_gain_grad = turn_back(
        info, back, natural, routes, gates, residual, moe_in, cotangent[0], router_t,
        moe_scale[None], out_full, context, shards,
    )
    dos = group_pieces(dos, 1)
    out_came = swap(out_send, "core", 1)
    out_far = (out_other + out_came[1].astype(F32)).astype(BF)
    outs = [outs[0]] + [lax.ppermute(outs[j], "fsdp", xor_perm(j, n_fsdp)) for j in range(1, n_fsdp)]
    dos[0], out_far = together(dos[0], out_far)
    out_far = swap(out_far, "fsdp", top_bit)
    dq, *dkvs, dline = attend_back(pos, proj, keys, strips, dos, o_pre, stat, members, blocks)
    dkvs[1], out_far, outs = together(dkvs[1], out_far, outs)
    cames = [swap(dkvs[k], "core", 1) for k in range(1, members, 2)]
    sends = []
    if members == 4:
        keep, send = add_pairs(dkvs[0], cames[0], dkvs[2], cames[1])
        if staged:
            sends = [swap(terms[0][1], "r", 1)]
            send, sends[0] = together(send, sends[0])
        came = swap(send, "r", 1)
    else:
        held = {k: dkvs[k].astype(F32) + cames[k // 2].astype(F32) for k in range(0, members, 2)}
        bit = 2
        while bit < members:
            for k in [k for k in sorted(held) if k & bit]:
                held[k - bit] = held[k - bit] + swap(held.pop(k).astype(BF), "r", bit // 2).astype(F32)
            bit *= 2
        keep, came = held[0], None
    if staged:
        sends.append(swap(terms[1][1], "r", 1))
        up_send, came = together(add_groups(terms[0][0], sends[0], width, outs), came)
        up_came = swap_groups(up_send)

    own_back, back_1, back_2, back_3, term, sent, pack = input_back(
        jnp.stack([h, core]).astype(jnp.int32), members, BUCKETS // n_fsdp, dq, keep, came, ain, qkv_heads,
        attn_scale[None], router_grad, moe_gain_grad, line[None], dline,
    )

    def swap_both(send, pack, axis, bit):
        sent = jnp.concatenate([send.reshape(-1, send.shape[-1]).astype(BF), two_parts(pack)])
        return split_rows(swap(sent, axis, bit).astype(F32), send.shape)

    def split_rows(came, shape):
        return came[: -2 * SMALL].reshape(shape), came[-2 * SMALL : -SMALL] + came[-SMALL:]

    unit = GWIDTH // members
    came, pack_came = split_rows(swap(sent, "core", 1).astype(F32), term.shape)
    term, pack = term + came, pack + pack_came
    out_term = out_mine + out_came[0].astype(F32) + out_far.astype(F32)
    for bit in list(bits_of(n_fsdp))[1:]:
        out_term, out_send = part_of(out_term, (f // bit) % 2)
        out_term = out_term + swap(out_send.astype(BF), "fsdp", bit).astype(F32)
    for bit in bits_of(n_fsdp):
        term, send = part_of(term, (f // bit) % 2)
        pack, pack_send = part_of(pack, (f // bit) % 2)
        came, pack_came = swap_both(send, pack_send, "fsdp", bit)
        term, pack = term + came, pack + pack_came
    term = jnp.concatenate(
        [term.reshape(3, members // 2, unit, rows_f).swapaxes(0, 1).reshape(members // 2, -1, rows_f)]
        + [out_term.reshape(GROUPS, members // 2, rows_c, rows_f).swapaxes(0, 1).reshape(members // 2, -1, rows_f)],
        axis=1,
    )
    if staged:
        term, up_came = together(term, up_came)
    if staged:
        back_2, back_3, term = together(back_2, back_3, term)
    mid = lax.ppermute(back_2, "h", turn(-1))
    side = lax.ppermute(back_3, "h", turn(1)).astype(F32)
    mid = (back_1.astype(F32) + mid.astype(F32)).astype(BF)
    mid = lax.ppermute(mid, "h", turn(-1)).astype(F32)
    attn_in_grad = own_back + side + mid
    x = tokens[0].astype(F32)
    token_grad = jax.vjp(lambda v: normalize(v, attn_scale), x)[1](attn_in_grad)[0]
    tokens_grad = (resid_grad + token_grad).astype(BF)

    for bit in bits_of(members // 2):
        mine = (lax.axis_index("r") // bit) % 2
        term = term.reshape((2, -1) + term.shape[1:])
        came, pack_came = swap_both(lax.dynamic_index_in_dim(term, 1 - mine, 0, False), pack, "r", bit)
        term = lax.dynamic_index_in_dim(term, mine, 0, False) + came
        pack = pack + pack_came
    term = term[0]
    out_term = term[3 * unit :].reshape(GROUPS, rows_c, rows_f)
    term = term[: 3 * unit].astype(BF).reshape(3, unit, rows_f)
    out_sum, pack_sum = lax.dynamic_index_in_dim(out_term, h, 0, False), pack
    for k in (2, 1, 3):
        piece = lax.dynamic_index_in_dim(out_term, lax.rem(h + k, GROUPS), 0, False)
        came = lax.ppermute(jnp.concatenate([piece.astype(BF), two_parts(pack)]), "h", turn(k)).astype(F32)
        out_sum = out_sum + came[:rows_c]
        pack_sum = pack_sum + came[rows_c : rows_c + SMALL] + came[rows_c + SMALL :]
    at = h * members + m
    parts = []
    for r in range(3):
        pairs = [((3 * d + r) % shards, d) for d in range(shards)]
        third = pow(3, -1, shards)
        which = (3 * lax.rem((at + shards - r) * third, shards) + r) // shards
        parts.append(lax.ppermute(lax.dynamic_index_in_dim(term, which, 0, False), CTX, pairs))
    if staged:
        sends[1], parts, pack_sum = together(sends[1], parts, pack_sum)
        down_came = group_pieces(sum_pieces(terms[1][0], sends[1]), 1)
        grads = [to_wide(up_came, rows_c, ffn), in_order(pos, down_came)]
        home = up_came[:, rows_c * ffn // width :].reshape(EXPERTS * CAP, width)
    else:
        terms = [jnp.concatenate(terms[n] + terms[n + 1]) for n in (0, 2)]
        grads = [
            lax.psum_scatter(term, CTX, scatter_dimension=0, tiled=True)[None].astype(F32) for term in terms
        ]
        home = jnp.concatenate([o.reshape(-1, width) for o in outs])
    qkv_grad = jnp.concatenate(parts).astype(F32).T

    place = (group * n_fsdp + jnp.bitwise_xor(routes // here, f)) * CAP + slot
    layer_out = residual
    for k in range(TOP):
        row = (slots[:, None] == place[None, :, k]).astype(BF)
        layer_out = layer_out + gates[:, k : k + 1] * dot(row, home, ((0,), (0,)))
    bias_grad = pack_sum[EXPERTS + 2 : EXPERTS + 2 + GHEADS, : GROUPS * BUCKETS // n_fsdp]
    bias_grad = bias_grad.reshape(GHEADS, GROUPS, BUCKETS // n_fsdp).transpose(2, 1, 0).reshape(-1, HEADS)
    return (
        layer_out.astype(BF)[None],
        tokens_grad[None],
        pack_sum[8],
        qkv_grad,
        out_sum.T,
        bias_grad,
        pack_sum[9],
        pack_sum[:8].T,
        grads[0],
        grads[1],
    )


def solution(mesh):
    n_ctx, n_fsdp = mesh.shape["ctx"], mesh.shape["fsdp"]
    cut = mesh.devices.reshape(GROUPS, n_ctx // (2 * GROUPS), 2, n_fsdp)
    row = P("fsdp", CTX, None)
    return jax.shard_map(
        per_device,
        mesh=Mesh(cut, CTX + ("fsdp",)),
        in_specs=(
            row,
            P("fsdp", CTX),
            P(CTX + ("fsdp",), None),
            P(),
            P("fsdp"),
            P("fsdp", None),
            P("fsdp", None),
            P("fsdp", None),
            P("fsdp"),
            P("fsdp", None),
            P("fsdp", None, None),
            P("fsdp", None, None),
            row,
        ),
        out_specs=(
            row,
            row,
            P("fsdp"),
            P("fsdp", CTX),
            P("fsdp", CTX),
            P("fsdp", None),
            P("fsdp"),
            P("fsdp", None),
            row,
            row,
        ),
        check_vma=False,
    )
```

time: 340 us -> 290 us (0.85)
  other arithmetic: 49.3 us -> 15.2 us
  local copies, waits for them, and re-layouts: 39.9 us -> 11.9 us
  Pallas kernels: 52.1 us -> 76.9 us
  matrix products: 21.6 us -> 4.25 us
  starting transfers between devices: 80.5 us -> 86.9 us
  between operations: 7.62 us -> 1.37 us
  waiting for transfers between devices: 83.8 us -> 88.2 us
    convert_element_type x17 -> x5, other arithmetic: 27.5 us -> 2.57 us  [the longest x1 1.35 us: per_device(): out_far = (out_other + out_came[1].astype(F32)).astype(BF)]
    pallas_call x4 -> x12, Pallas kernels: 23.8 us -> 48.1 us  [the longest x2 12.3 us: weight_terms(): pl.pallas_call(functools.partial(weight_kernel, len(rows), members, side,...]
    ppermute x20 -> x31, starting transfers between devices: 19.6 us -> 42.7 us  [the longest x12 16.8 us: swap(): return lax.ppermute(x, axis, xor_perm(bit, lax.axis_size(axis)))]
    unnamed x164 -> x61, local copies, waits for them, and re-layouts: 23.9 us -> 3.31 us
    all_to_all x2 -> x1, waiting for transfers between devices: 3.41 us -> 21.9 us  [swap_groups(): return lax.all_to_all(x, 'h', 0, 0, tiled=True)]
    dot_general x16 -> x6, matrix products: 17.8 us -> 4.25 us  [dot(): return lax.dot_general(a, b, (dims, ((), ())), preferred_element_type=F32)]
    all_to_all x4 -> x2, starting transfers between devices: 21.8 us -> 9.56 us  [exchange_rows(): return lax.all_to_all(rows, exchange, 0, 0, tiled=True)]
    all_to_all x4 -> x2, waiting for transfers between devices: 12.2 us -> 0.01 us  [exchange_rows(): return lax.all_to_all(rows, exchange, 0, 0, tiled=True)]
  transfers between devices with their start and end apart: 42 -> 50, of which waited for: 17 -> 22; matrix products, arithmetic and copies ran while one was open for 22% -> 9% of each run, Pallas kernels for 12% -> 18%
where the time goes in v3:
time: 290 us; the launch traced here: 285 us
  waiting for transfers between devices  88.2 us (30%)
  starting transfers between devices  86.9 us (30%)
  Pallas kernels  76.9 us (27%)
  other arithmetic  15.2 us (5%)
  local copies, waits for them, and re-layouts  11.9 us (4%)
  matrix products  4.25 us (1%)
    ppermute x9, waiting for transfers between devices, group_pieces(): came = {k: lax.ppermute(pieces[k], 'h', turn(sign * k)) for k in (2, 1, 3)}  27.1 us
    all_to_all x1, waiting for transfers between devices, swap_groups(): return lax.all_to_all(x, 'h', 0, 0, tiled=True)  21.9 us
    ppermute x12, waiting for transfers between devices, swap(): return lax.ppermute(x, axis, xor_perm(bit, lax.axis_size(axis)))  17.2 us
    ppermute x12, starting transfers between devices, swap(): return lax.ppermute(x, axis, xor_perm(bit, lax.axis_size(axis)))  16.8 us
    pallas_call x1, Pallas kernels, attend_back(): pl.pallas_call(functools.partial(backward_kernel, half, blocks, members),...  16.5 us
    pallas_call x1, Pallas kernels, attend(): pl.pallas_call(functools.partial(forward_kernel, half, blocks, len(kvs)),...  12.4 us
    pallas_call x2, Pallas kernels, weight_terms(): pl.pallas_call(functools.partial(weight_kernel, len(rows), members, side,...  12.3 us
    ppermute x7, starting transfers between devices, deal(): out[p] = lax.ppermute(pieces[p], ('h', 'fsdp'), pairs)  12.1 us
  transfers between devices with their start and end apart: 50, of which 22 were waited for; matrix products, arithmetic and copies ran while one was open for 9% of the time, Pallas kernels for 18%

profile of v3, /device:TPU:11, one launch (start us, length us, event | category | flops | bytes accessed | tf_op | source)
XLA Modules:
  0.0 284.8 jit_solution(11417781966198732573)
XLA Ops:
  1.3 1.6 fusion.49
  3.0 2.3 collective-permute-start.4
  17.3 3.3 %strips.1.refs_4_.refs_5_ = f32[2304,192]{1,0:T(8,128)} custom-call(f32[3,2304]{1,0:T(4,128)} %convolution_multiply_fusion.g_ref), custom_call_target="tpu_custom_call" | custom-call | flops 100000 | bytes 10000 | tf_op jit(solution)/shard_map/strips/pallas_call | solution.py:73
  20.7 3.1 %collective-permute-done.3 = bf16[136,768]{1,0:T(8,128)(2,1)S(1)} collective-permute-done((bf16[136,768]{1,0:T(8,128)(2,1)}, bf16[136,768]{1,0:T(8,128)(2,1)S(1)}, u32[]{:S(2)}, u32[]{:S(2)}) %collective-permute-start.3) | collective-permute-done | bytes 208928 | tf_op jit(solution)/shard_map/ppermute | solution.py:808
  26.8 5.5 %all-to-all-start = ((bf16[8,40,768]{2,1,0:T(8,128)(2,1)}), bf16[8,40,768]{2,1,0:T(8,128)(2,1)S(1)}, u32[]{:S(2)}, u32[]{:S(2)}) async-start(bf16[8,40,768]{2,1,0:T(8,128)(2,1)} %bitcast.23), calls=%async_computation | async-start | bytes 983040 | tf_op jit(solution)/shard_map/all_to_all | solution.py:936
  34.9 2.6 collective-permute-start.6
  37.4 5.1 %collective-permute-done.7.refs_2_ = bf16[4,136,384]{2,1,0:T(8,128)(2,1)S(1)} collective-permute-done((bf16[4,136,384]{2,1,0:T(8,128)(2,1)S(1)}, bf16[4,136,384]{2,1,0:T(8,128)(2,1)S(1)}, u32[]{:S(2)}, u32[]{:S(2)}) %collective-permute-start.7) | collective-permute-done | bytes 417824 | tf_op jit(solution)/shard_map/ppermute | solution.py:817
  42.6 2.8 collective-permute-start.8
  46.8 12.4 %attend.1 = (f32[8,192,64]{2,1,0:T(8,128)}, bf16[192,128]{1,0:T(8,128)(2,1)S(1)}, bf16[192,128]{1,0:T(8,128)(2,1)S(1)}, bf16[192,128]{1,0:T(8,128)(2,1)S(1)}, bf...) custom-call(s32[2]{0:T(128)S(1)} %pad_add_fusion.pos, ...), custom_call_target="tpu_custom_call" | custom-call | flops 100000 | bytes 10000 | tf_op jit(solution)/shard_map/attend/pallas_call | solution.py:322
  59.5 2.1 collective-permute-start.10
  61.6 2.1 collective-permute-start.11
  63.7 2.8 maximum_select_fusion
  66.5 2.9 %router.1 = (bf16[40,896]{1,0:T(8,128)(2,1)S(1)}, bf16[40,896]{1,0:T(8,128)(2,1)S(1)}, bf16[40,896]{1,0:T(8,128)(2,1)S(1)}, bf16[40,896]{1,0:T(8,128)(2,1)S(1)},...) custom-call(s32[2]{0:T(128)S(1)} %pad_add_fusion.pos, ...), custom_call_target="tpu_custom_call" | custom-call | flops 100000 | bytes 10000 | tf_op jit(solution)/shard_map/router/pallas_call | solution.py:422
  69.5 4.4 %collective-permute-start.12 = (bf16[40,896]{1,0:T(8,128)(2,1)S(1)}, bf16[40,896]{1,0:T(8,128)(2,1)S(1)}, u32[]{:S(2)}, u32[]{:S(2)}) collective-permute-start(bf16[40,896]{1,0:T(8,128)(2,1)S(1)} %get-tuple-element.115), channel_id=1, source_target_pairs={{0,1},{1,0},{8,9},{9,8},{16,17},{17,16},{24,25},{25,24},{2,3},{3,2... | collective-permute-start | bytes 215048 | tf_op jit(solution)/shard_map/ppermute | solution.py:862
  74.8 2.4 collective-permute-start.15
  79.0 2.6 collective-permute-start.18
  82.5 3.9 %collective-permute-done.16.refs_5_ = bf16[40,896]{1,0:T(8,128)(2,1)S(1)} collective-permute-done((bf16[40,896]{1,0:T(8,128)(2,1)S(1)}, bf16[40,896]{1,0:T(8,128)(2,1)S(1)}, u32[]{:S(2)}, u32[]{:S(2)}) %collective-permute-start.16) | collective-permute-done | bytes 71712 | tf_op jit(solution)/shard_map/ppermute | solution.py:862
  86.4 2.1 collective-permute-done.17.refs_6_
  89.8 11.8 %expert.1 = (bf16[4,40,768]{2,1,0:T(8,128)(2,1)}, bf16[4,40,768]{2,1,0:T(8,128)(2,1)}, bf16[8,40,896]{2,1,0:T(8,128)(2,1)}, bf16[2,320,3072]{2,1,0:T(8,128)(2,1)}, bf16[2,320,768]{2,1,0:T(8,128)(2,1)}) custom-call(s32[2]{0:T(128)S(1)} %pad_add_fusion.3.info, bf16[8,40,768]{2,1,0:T(8,128)(2,1)S(1)} %all-to-all-done.dy_ref, bf16[4,768,3072]{2,1,0:T(8,128)(2,1)} %up_ref.1, ...), custom_call_target="tpu_custom_call" | custom-call | flops 100000 | bytes 10000 | tf_op jit(solution)/shard_map/expert/pallas_call | solution.py:482
  102.2 4.1 %all-to-all-start.1 = ((bf16[8,40,896]{2,1,0:T(8,128)(2,1)}), bf16[8,40,896]{2,1,0:T(8,128)(2,1)S(1)}, u32[]{:S(2)}, u32[]{:S(2)}) async-start(bf16[8,40,896]{2,1,0:T(8,128)(2,1)} %get-tuple-element.122), calls=%async_computation.1 | async-start | bytes 1146880 | tf_op jit(solution)/shard_map/all_to_all | solution.py:936
  107.2 3.0 %collective-permute-done.19.refs_1_ = bf16[2,320,768]{2,1,0:T(8,128)(2,1)S(1)} collective-permute-done((bf16[2,320,768]{2,1,0:T(8,128)(2,1)}, bf16[2,320,768]{2,1,0:T(8,128)(2,1)S(1)}, u32[]{:S(2)}, u32[]{:S(2)}) %collective-permute-start.19) | collective-permute-done | bytes 983072 | tf_op jit(solution)/shard_map/ppermute | solution.py:827
  110.2 6.1 %weight_terms.3 = (bf16[192,3072]{1,0:T(8,128)(2,1)}, bf16[192,3072]{1,0:T(8,128)(2,1)}) custom-call(s32[2]{0:T(128)S(1)} %pad_add_fusion.pos, bf16[2,320,768]{2,1,0:T(8,128)(2,1)S(1)} %copy-done.1, bf16[2,320,768]{2,1,0:T(8,128)(2,1)S(1)} %collective-permute-done.19.refs_1_, bf16[2,320,3072]{2,1,0:T(8,128)(2,1)} %get-tuple-element.124.refs_2_, ...), custom_call_target="tpu_custom_call" | custom-call | flops 100000 | bytes 10000 | tf_op jit(solution)/shard_map/weight_terms/pallas_call | solution.py:535
  116.3 6.1 %weight_terms.2 = (bf16[192,3072]{1,0:T(8,128)(2,1)}, bf16[192,3072]{1,0:T(8,128)(2,1)}) custom-call(s32[2]{0:T(128)S(1)} %pad_add_fusion.pos, bf16[2,320,768]{2,1,0:T(8,128)(2,1)S(1)} %copy-done.1, bf16[2,320,768]{2,1,0:T(8,128)(2,1)S(1)} %collective-permute-done.19.refs_1_, bf16[2,320,3072]{2,1,0:T(8,128)(2,1)} %get-tuple-element.124.refs_2_, ...), custom_call_target="tpu_custom_call" | custom-call | flops 100000 | bytes 10000 | tf_op jit(solution)/shard_map/weight_terms/pallas_call | solution.py:535
  122.5 5.1 %turn_back.1 = (bf16[192,128]{1,0:T(8,128)(2,1)S(1)}, bf16[192,128]{1,0:T(8,128)(2,1)S(1)}, bf16[192,128]{1,0:T(8,128)(2,1)S(1)}, bf16[192,128]{1,0:T(8,128)(2,1...) custom-call(s32[3]{0:T(128)S(1)} %pad_add_fusion.2.info, ...), custom_call_target="tpu_custom_call" | custom-call | flops 100000 | bytes 10000 | tf_op jit(solution)/shard_map/turn_back/pallas_call | solution.py:693
  128.0 2.5 collective-permute-start.29
  137.9 2.6 collective-permute-done.24.refs_3_
  140.5 16.5 %attend_back.1 = (bf16[512,192]{1,0:T(8,128)(2,1)S(1)}, bf16[4,128,384]{2,1,0:T(8,128)(2,1)S(1)}, bf16[4,128,384]{2,1,0:T(8,128)(2,1)S(1)}, bf16[4,128,384]{2,1,...) custom-call(s32[2]{0:T(128)S(1)} %pad_add_fusion.pos, ...), custom_call_target="tpu_custom_call" | custom-call | flops 100000 | bytes 10000 | tf_op jit(solution)/shard_map/attend_back/pallas_call | solution.py:347
  157.0 3.4 %collective-permute-start.28 = (bf16[4,128,384]{2,1,0:T(8,128)(2,1)S(1)}, bf16[4,128,384]{2,1,0:T(8,128)(2,1)S(1)}, u32[]{:S(2)}, u32[]{:S(2)}) collective-permute-start(bf16[4,128,384]{2,1,0:T(8,128)(2,1)S(1)} %get-tuple-element.150), channel_id=1, source_target_pairs={{0,2},{2,0},{1,3},{3,1},{4,6},{6,4},{5,7},{7,5},{8,10},{10,8},{9,1... | collective-permute-start | bytes 1179656 | tf_op jit(solution)/shard_map/ppermute | solution.py:827
  164.1 3.2 %add_groups.1 = bf16[4,272,768]{2,1,0:T(8,128)(2,1)} custom-call(bf16[192,3072]{1,0:T(8,128)(2,1)} %get-tuple-element.152.a_ref, bf16[192,3072]{1,0:T(8,128)(2,1)} %copy-done.12, bf16[4,40,768]{2,1,0:T(8,128)(2,1)} %get-tuple-element.156.refs_0_, bf16[4,40,768]{2,1,0:T(8,128)(2,1)} %copy-done.23), custom_call_target="tpu_custom_call" | custom-call | flops 100000 | bytes 10000 | tf_op jit(solution)/shard_map/add_groups/pallas_call | solution.py:566
  167.3 6.4 %collective-permute-done.30.came_ref = bf16[4,128,384]{2,1,0:T(8,128)(2,1)S(1)} collective-permute-done((bf16[4,128,384]{2,1,0:T(8,128)(2,1)S(1)}, bf16[4,128,384]{2,1,0:T(8,128)(2,1)S(1)}, u32[]{:S(2)}, u32[]{:S(2)}) %collective-permute-start.30) | collective-permute-done | bytes 393248 | tf_op jit(solution)/shard_map/ppermute | solution.py:827
  173.7 3.7 %input_back.1 = (f32[128,768]{1,0:T(8,128)S(1)}, bf16[128,768]{1,0:T(8,128)(2,1)S(1)}, bf16[128,768]{1,0:T(8,128)(2,1)S(1)}, bf16[128,768]{1,0:T(8,128)(2,1)S(1)...) custom-call(s32[2]{0:T(128)S(1)} %pad_add_fusion.1.info, ...), custom_call_target="tpu_custom_call" | custom-call | flops 100000 | bytes 10000 | tf_op jit(solution)/shard_map/input_back/pallas_call | solution.py:781
  179.1 5.5 %all-to-all-start.2 = ((bf16[4,272,768]{2,1,0:T(8,128)(2,1)}), bf16[4,272,768]{2,1,0:T(8,128)(2,1)S(1)}, u32[]{:S(2)}, u32[]{:S(2)}) async-start(bf16[4,272,768]{2,1,0:T(8,128)(2,1)} %add_groups.1), calls=%async_computation.2 | async-start | bytes 3342336 | tf_op jit(solution)/shard_map/all_to_all | solution.py:843
  187.2 4.6 %collective-permute-start.32 = (bf16[320,384]{1,0:T(8,128)(2,1)S(1)}, bf16[320,384]{1,0:T(8,128)(2,1)S(1)}, u32[]{:S(2)}, u32[]{:S(2)}) collective-permute-start(bf16[320,384]{1,0:T(8,128)(2,1)S(1)} %pad_maximum_fusion.5), channel_id=1, source_target_pairs={{0,1},{1,0},{2,3},{3,2},{4,5},{5,4},{6,7},{7,6},{8,9},{9,8},{10,11... | collective-permute-start | bytes 737288 | tf_op jit(solution)/shard_map/ppermute | solution.py:827
  191.9 5.3 %collective-permute-done.32 = bf16[320,384]{1,0:T(8,128)(2,1)S(1)} collective-permute-done((bf16[320,384]{1,0:T(8,128)(2,1)S(1)}, bf16[320,384]{1,0:T(8,128)(2,1)S(1)}, u32[]{:S(2)}, u32[]{:S(2)}) %collective-permute-start.32) | collective-permute-done | bytes 245792 | tf_op jit(solution)/shard_map/ppermute | solution.py:827
  198.5 21.9 %all-to-all-done.2.x_ref = bf16[4,272,768]{2,1,0:T(8,128)(2,1)S(1)} async-done(((bf16[4,272,768]{2,1,0:T(8,128)(2,1)}), bf16[4,272,768]{2,1,0:T(8,128)(2,1)S(1)}, u32[]{:S(2)}, u32[]{:S(2)}) %all-to-all-start.2) | async-done | bytes 1671200 | tf_op jit(solution)/shard_map/all_to_all | solution.py:843
  221.5 1.8 collective-permute-start.34
  226.7 1.6 to_wide.1
  228.3 2.0 collective-permute-done.34
  231.5 2.9 %collective-permute-start.41 = (bf16[80,384]{1,0:T(8,128)(2,1)S(1)}, bf16[80,384]{1,0:T(8,128)(2,1)S(1)}, u32[]{:S(2)}, u32[]{:S(2)}) collective-permute-start(bf16[80,384]{1,0:T(8,128)(2,1)S(1)} %get-tuple-element.230), channel_id=1, source_target_pairs={{0,16},{8,24},{16,0},{24,8},{1,17},{9,25},{17,1},{25,9},{2,18},{10... | collective-permute-start | bytes 184328 | tf_op jit(solution)/shard_map/ppermute | solution.py:1056
  236.0 4.5 %collective-permute-start.40 = (bf16[48,384]{1,0:T(8,128)(2,1)S(1)}, bf16[48,384]{1,0:T(8,128)(2,1)S(1)}, u32[]{:S(2)}, u32[]{:S(2)}) collective-permute-start(bf16[48,384]{1,0:T(8,128)(2,1)S(1)} %get-tuple-element.225), channel_id=1, source_target_pairs={{4,0},{10,2},{16,4},{22,6},{28,8},{2,10},{8,12},{14,14},{20,16},{2... | collective-permute-start | bytes 110600 | tf_op jit(solution)/shard_map/ppermute | solution.py:1065
  240.5 3.7 %collective-permute-start.39 = (bf16[48,384]{1,0:T(8,128)(2,1)S(1)}, bf16[48,384]{1,0:T(8,128)(2,1)S(1)}, u32[]{:S(2)}, u32[]{:S(2)}) collective-permute-start(bf16[48,384]{1,0:T(8,128)(2,1)S(1)} %get-tuple-element.226), channel_id=1, source_target_pairs={{2,0},{8,2},{14,4},{20,6},{26,8},{0,10},{6,12},{12,14},{18,16},{24... | collective-permute-start | bytes 110600 | tf_op jit(solution)/shard_map/ppermute | solution.py:1065
  244.2 3.7 %collective-permute-start.38 = (bf16[48,384]{1,0:T(8,128)(2,1)S(1)}, bf16[48,384]{1,0:T(8,128)(2,1)S(1)}, u32[]{:S(2)}, u32[]{:S(2)}) collective-permute-start(bf16[48,384]{1,0:T(8,128)(2,1)S(1)} %get-tuple-element.227), channel_id=1, source_target_pairs={{0,0},{6,2},{12,4},{18,6},{24,8},{30,10},{4,12},{10,14},{16,16},{2... | collective-permute-start | bytes 110600 | tf_op jit(solution)/shard_map/ppermute | solution.py:1065
  248.5 2.2 collective-permute-done.38
  252.8 1.9 sum_pieces.1
  259.4 4.2 %collective-permute-done.44.refs_1_ = bf16[48,3072]{1,0:T(8,128)(2,1)S(1)} collective-permute-done((bf16[48,3072]{1,0:T(8,128)(2,1)S(1)}, bf16[48,3072]{1,0:T(8,128)(2,1)S(1)}, u32[]{:S(2)}, u32[]{:S(2)}) %collective-permute-start.44) | collective-permute-done | bytes 294944 | tf_op jit(solution)/shard_map/ppermute | solution.py:847
  263.6 16.8 %collective-permute-done.45.refs_2_ = bf16[48,3072]{1,0:T(8,128)(2,1)S(1)} collective-permute-done((bf16[48,3072]{1,0:T(8,128)(2,1)S(1)}, bf16[48,3072]{1,0:T(8,128)(2,1)S(1)}, u32[]{:S(2)}, u32[]{:S(2)}) %collective-permute-start.45) | collective-permute-done | bytes 294944 | tf_op jit(solution)/shard_map/ppermute | solution.py:847
  280.4 2.3 collective-permute-done.46.refs_3_
  282.7 2.1 in_order.1
  (223 shorter events, 57.9 us)
Async XLA Ops:
  3.0 17.7 %collective-permute-start.4 = (bf16[136,768]{1,0:T(8,128)(2,1)}, bf16[136,768]{1,0:T(8,128)(2,1)S(1)}, u32[]{:S(2)}, u32[]{:S(2)}) collective-permute-start(bf16[136,768]{1,0:T(8,128)(2,1)} %get-tuple-element.221), channel_id=1, source_target_pairs={{0,16},{8,24},{16,0},{24,8},{1,17},{9,25},{17,1},{25,9},{2,18},{10... | collective-permute-start | bytes 626696 | tf_op jit(solution)/shard_map/ppermute | solution.py:808
  5.3 18.5 %collective-permute-start.3 = (bf16[136,768]{1,0:T(8,128)(2,1)}, bf16[136,768]{1,0:T(8,128)(2,1)S(1)}, u32[]{:S(2)}, u32[]{:S(2)}) collective-permute-start(bf16[136,768]{1,0:T(8,128)(2,1)} %get-tuple-element.221), channel_id=1, source_target_pairs={{0,8},{8,16},{16,24},{24,0},{1,9},{9,17},{17,25},{25,1},{2,10},{10... | collective-permute-start | bytes 626696 | tf_op jit(solution)/shard_map/ppermute | solution.py:808
  5.3 18.5 %collective-permute-start.5 = (bf16[136,768]{1,0:T(8,128)(2,1)}, bf16[136,768]{1,0:T(8,128)(2,1)S(1)}, u32[]{:S(2)}, u32[]{:S(2)}) collective-permute-start(bf16[136,768]{1,0:T(8,128)(2,1)} %get-tuple-element.221), channel_id=1, source_target_pairs={{0,24},{8,0},{16,8},{24,16},{1,25},{9,1},{17,9},{25,17},{2,26},{10... | collective-permute-start | bytes 626696 | tf_op jit(solution)/shard_map/ppermute | solution.py:808
  9.8 6.3 %collective-permute-start.2 = (bf16[16,384]{1,0:T(8,128)(2,1)S(1)}, bf16[16,384]{1,0:T(8,128)(2,1)S(1)}, u32[]{:S(2)}, u32[]{:S(2)}) collective-permute-start(bf16[16,384]{1,0:T(8,128)(2,1)S(1)} %concatenate.50), channel_id=1, source_target_pairs={{0,1},{1,0},{2,3},{3,2},{4,5},{5,4},{6,7},{7,6},{8,9},{9,8},{10,11... | collective-permute-start | bytes 36872 | tf_op jit(solution)/shard_map/ppermute | solution.py:838
  11.7 12.8 %collective-permute-start = (bf16[384,576]{1,0:T(8,128)(2,1)S(1)}, bf16[384,576]{1,0:T(8,128)(2,1)S(1)}, u32[]{:S(2)}, u32[]{:S(2)}) collective-permute-start(bf16[384,576]{1,0:T(8,128)(2,1)S(1)} %pad_maximum_fusion.2), channel_id=1, source_target_pairs={{0,1},{1,0},{2,3},{3,2},{4,5},{5,4},{6,7},{7,6},{8,9},{9,8},{10,11... | collective-permute-start | bytes 1327112 | tf_op jit(solution)/shard_map/ppermute | solution.py:838
  26.8 18.9 %all-to-all-start = ((bf16[8,40,768]{2,1,0:T(8,128)(2,1)}), bf16[8,40,768]{2,1,0:T(8,128)(2,1)S(1)}, u32[]{:S(2)}, u32[]{:S(2)}) async-start(bf16[8,40,768]{2,1,0:T(8,128)(2,1)} %bitcast.23), calls=%async_computation | async-start | bytes 983040 | tf_op jit(solution)/shard_map/all_to_all | solution.py:936
  33.3 9.3 %collective-permute-start.7 = (bf16[4,136,384]{2,1,0:T(8,128)(2,1)S(1)}, bf16[4,136,384]{2,1,0:T(8,128)(2,1)S(1)}, u32[]{:S(2)}, u32[]{:S(2)}) collective-permute-start(bf16[4,136,384]{2,1,0:T(8,128)(2,1)S(1)} %pad_maximum_fusion.3.refs_0_), channel_id=1, source_target_pairs={{0,4},{2,6},{4,0},{6,2},{1,5},{3,7},{5,1},{7,3},{8,12},{10,14},{12... | collective-permute-start | bytes 1253384 | tf_op jit(solution)/shard_map/ppermute | solution.py:817
  34.6 29.1 %collective-permute-start.1 = (bf16[384,768]{1,0:T(8,128)(2,1)}, bf16[384,768]{1,0:T(8,128)(2,1)}, u32[]{:S(2)}, u32[]{:S(2)}) collective-permute-start(bf16[384,768]{1,0:T(8,128)(2,1)} %param.19), channel_id=1, source_target_pairs={{0,1},{1,0},{2,3},{3,2},{4,5},{5,4},{6,7},{7,6},{8,9},{9,8},{10,11... | collective-permute-start | bytes 1769480 | tf_op jit(solution)/shard_map/ppermute | solution.py:838
  34.9 10.7 %collective-permute-start.6 = (bf16[4,136,384]{2,1,0:T(8,128)(2,1)S(1)}, bf16[4,136,384]{2,1,0:T(8,128)(2,1)S(1)}, u32[]{:S(2)}, u32[]{:S(2)}) collective-permute-start(bf16[4,136,384]{2,1,0:T(8,128)(2,1)S(1)} %pad_maximum_fusion.3.refs_0_), channel_id=1, source_target_pairs={{0,2},{2,0},{4,6},{6,4},{1,3},{3,1},{5,7},{7,5},{8,10},{10,8},{12,... | collective-permute-start | bytes 1253384 | tf_op jit(solution)/shard_map/ppermute | solution.py:817
  42.6 4.2 %collective-permute-start.8 = (bf16[4,136,384]{2,1,0:T(8,128)(2,1)S(1)}, bf16[4,136,384]{2,1,0:T(8,128)(2,1)S(1)}, u32[]{:S(2)}, u32[]{:S(2)}) collective-permute-start(bf16[4,136,384]{2,1,0:T(8,128)(2,1)S(1)} %collective-permute-done.7.refs_2_), channel_id=1, source_target_pairs={{0,2},{2,0},{4,6},{6,4},{1,3},{3,1},{5,7},{7,5},{8,10},{10,8},{12,... | collective-permute-start | bytes 1253384 | tf_op jit(solution)/shard_map/ppermute | solution.py:817
  59.2 7.4 %collective-permute-start.9 = (bf16[192,128]{1,0:T(8,128)(2,1)S(1)}, bf16[192,128]{1,0:T(8,128)(2,1)S(1)}, u32[]{:S(2)}, u32[]{:S(2)}) collective-permute-start(bf16[192,128]{1,0:T(8,128)(2,1)S(1)} %get-tuple-element.106), channel_id=1, source_target_pairs={{0,24},{8,0},{16,8},{24,16},{1,25},{9,1},{17,9},{25,17},{2,26},{10... | collective-permute-start | bytes 147464 | tf_op jit(solution)/shard_map/ppermute | solution.py:847
  59.5 7.0 %collective-permute-start.10 = (bf16[192,128]{1,0:T(8,128)(2,1)S(1)}, bf16[192,128]{1,0:T(8,128)(2,1)S(1)}, u32[]{:S(2)}, u32[]{:S(2)}) collective-permute-start(bf16[192,128]{1,0:T(8,128)(2,1)S(1)} %get-tuple-element.107), channel_id=1, source_target_pairs={{0,16},{8,24},{16,0},{24,8},{1,17},{9,25},{17,1},{25,9},{2,18},{10... | collective-permute-start | bytes 147464 | tf_op jit(solution)/shard_map/ppermute | solution.py:847
  61.6 4.9 %collective-permute-start.11 = (bf16[192,128]{1,0:T(8,128)(2,1)S(1)}, bf16[192,128]{1,0:T(8,128)(2,1)S(1)}, u32[]{:S(2)}, u32[]{:S(2)}) collective-permute-start(bf16[192,128]{1,0:T(8,128)(2,1)S(1)} %get-tuple-element.108), channel_id=1, source_target_pairs={{0,8},{8,16},{16,24},{24,0},{1,9},{9,17},{17,25},{25,1},{2,10},{10... | collective-permute-start | bytes 147464 | tf_op jit(solution)/shard_map/ppermute | solution.py:847
  69.5 8.8 %collective-permute-start.12 = (bf16[40,896]{1,0:T(8,128)(2,1)S(1)}, bf16[40,896]{1,0:T(8,128)(2,1)S(1)}, u32[]{:S(2)}, u32[]{:S(2)}) collective-permute-start(bf16[40,896]{1,0:T(8,128)(2,1)S(1)} %get-tuple-element.115), channel_id=1, source_target_pairs={{0,1},{1,0},{8,9},{9,8},{16,17},{17,16},{24,25},{25,24},{2,3},{3,2... | collective-permute-start | bytes 215048 | tf_op jit(solution)/shard_map/ppermute | solution.py:862
  73.8 5.1 %collective-permute-start.13 = (bf16[40,896]{1,0:T(8,128)(2,1)S(1)}, bf16[40,896]{1,0:T(8,128)(2,1)S(1)}, u32[]{:S(2)}, u32[]{:S(2)}) collective-permute-start(bf16[40,896]{1,0:T(8,128)(2,1)S(1)} %get-tuple-element.116), channel_id=1, source_target_pairs={{0,8},{1,9},{8,16},{9,17},{16,24},{17,25},{24,0},{25,1},{2,10},{3,... | collective-permute-start | bytes 215048 | tf_op jit(solution)/shard_map/ppermute | solution.py:862
  74.0 7.6 %collective-permute-start.14 = (bf16[40,896]{1,0:T(8,128)(2,1)S(1)}, bf16[40,896]{1,0:T(8,128)(2,1)S(1)}, u32[]{:S(2)}, u32[]{:S(2)}) collective-permute-start(bf16[40,896]{1,0:T(8,128)(2,1)S(1)} %get-tuple-element.117), channel_id=1, source_target_pairs={{0,9},{1,8},{8,17},{9,16},{16,25},{17,24},{24,1},{25,0},{2,11},{3,... | collective-permute-start | bytes 215048 | tf_op jit(solution)/shard_map/ppermute | solution.py:862
  74.8 7.7 %collective-permute-start.15 = (bf16[40,896]{1,0:T(8,128)(2,1)S(1)}, bf16[40,896]{1,0:T(8,128)(2,1)S(1)}, u32[]{:S(2)}, u32[]{:S(2)}) collective-permute-start(bf16[40,896]{1,0:T(8,128)(2,1)S(1)} %get-tuple-element.118), channel_id=1, source_target_pairs={{0,16},{1,17},{8,24},{9,25},{16,0},{17,1},{24,8},{25,9},{2,18},{3,... | collective-permute-start | bytes 215048 | tf_op jit(solution)/shard_map/ppermute | solution.py:862
  77.1 9.3 %collective-permute-start.16 = (bf16[40,896]{1,0:T(8,128)(2,1)S(1)}, bf16[40,896]{1,0:T(8,128)(2,1)S(1)}, u32[]{:S(2)}, u32[]{:S(2)}) collective-permute-start(bf16[40,896]{1,0:T(8,128)(2,1)S(1)} %get-tuple-element.119), channel_id=1, source_target_pairs={{0,17},{1,16},{8,25},{9,24},{16,1},{17,0},{24,9},{25,8},{2,19},{3,... | collective-permute-start | bytes 215048 | tf_op jit(solution)/shard_map/ppermute | solution.py:862
  78.3 10.2 %collective-permute-start.17 = (bf16[40,896]{1,0:T(8,128)(2,1)S(1)}, bf16[40,896]{1,0:T(8,128)(2,1)S(1)}, u32[]{:S(2)}, u32[]{:S(2)}) collective-permute-start(bf16[40,896]{1,0:T(8,128)(2,1)S(1)} %get-tuple-element.120), channel_id=1, source_target_pairs={{0,24},{1,25},{8,0},{9,1},{16,8},{17,9},{24,16},{25,17},{2,26},{3,... | collective-permute-start | bytes 215048 | tf_op jit(solution)/shard_map/ppermute | solution.py:862
  79.0 10.8 %collective-permute-start.18 = (bf16[40,896]{1,0:T(8,128)(2,1)S(1)}, bf16[40,896]{1,0:T(8,128)(2,1)S(1)}, u32[]{:S(2)}, u32[]{:S(2)}) collective-permute-start(bf16[40,896]{1,0:T(8,128)(2,1)S(1)} %get-tuple-element.121), channel_id=1, source_target_pairs={{0,25},{1,24},{8,1},{9,0},{16,9},{17,8},{24,17},{25,16},{2,27},{3,... | collective-permute-start | bytes 215048 | tf_op jit(solution)/shard_map/ppermute | solution.py:862
  101.6 8.6 %collective-permute-start.20 = (bf16[2,320,3072]{2,1,0:T(8,128)(2,1)}, bf16[2,320,3072]{2,1,0:T(8,128)(2,1)}, u32[]{:S(2)}, u32[]{:S(2)}) collective-permute-start(bf16[2,320,3072]{2,1,0:T(8,128)(2,1)} %get-tuple-element.124.refs_2_), channel_id=1, source_target_pairs={{0,2},{2,0},{1,3},{3,1},{4,6},{6,4},{5,7},{7,5},{8,10},{10,8},{9,1... | collective-permute-start | bytes 11796488 | tf_op jit(solution)/shard_map/ppermute | solution.py:827
  102.2 20.3 %all-to-all-start.1 = ((bf16[8,40,896]{2,1,0:T(8,128)(2,1)}), bf16[8,40,896]{2,1,0:T(8,128)(2,1)S(1)}, u32[]{:S(2)}, u32[]{:S(2)}) async-start(bf16[8,40,896]{2,1,0:T(8,128)(2,1)} %get-tuple-element.122), calls=%async_computation.1 | async-start | bytes 1146880 | tf_op jit(solution)/shard_map/all_to_all | solution.py:936
  106.3 3.9 %collective-permute-start.19 = (bf16[2,320,768]{2,1,0:T(8,128)(2,1)}, bf16[2,320,768]{2,1,0:T(8,128)(2,1)S(1)}, u32[]{:S(2)}, u32[]{:S(2)}) collective-permute-start(bf16[2,320,768]{2,1,0:T(8,128)(2,1)} %get-tuple-element.123.refs_0_), channel_id=1, source_target_pairs={{0,2},{2,0},{1,3},{3,1},{4,6},{6,4},{5,7},{7,5},{8,10},{10,8},{9,1... | collective-permute-start | bytes 2949128 | tf_op jit(solution)/shard_map/ppermute | solution.py:827
  128.0 35.1 %collective-permute-start.29 = (bf16[192,3072]{1,0:T(8,128)(2,1)S(1)}, bf16[192,3072]{1,0:T(8,128)(2,1)S(1)}, u32[]{:S(2)}, u32[]{:S(2)}) collective-permute-start(bf16[192,3072]{1,0:T(8,128)(2,1)S(1)} %copy-done.26), channel_id=1, source_target_pairs={{0,4},{4,0},{1,5},{5,1},{2,6},{6,2},{3,7},{7,3},{8,12},{12,8},{9,1... | collective-permute-start | bytes 3538952 | tf_op jit(solution)/shard_map/ppermute | solution.py:827
  131.8 28.6 %collective-permute-start.25 = (bf16[8,48,384]{2,1,0:T(8,128)(2,1)S(1)}, bf16[8,48,384]{2,1,0:T(8,128)(2,1)S(1)}, u32[]{:S(2)}, u32[]{:S(2)}) collective-permute-start(bf16[8,48,384]{2,1,0:T(8,128)(2,1)S(1)} %fusion.5), channel_id=1, source_target_pairs={{0,1},{1,0},{2,3},{3,2},{4,5},{5,4},{6,7},{7,6},{8,9},{9,8},{10,11... | collective-permute-start | bytes 884744 | tf_op jit(solution)/shard_map/ppermute | solution.py:827
  132.7 27.7 %collective-permute-start.26 = (bf16[4,40,768]{2,1,0:T(8,128)(2,1)S(1)}, bf16[4,40,768]{2,1,0:T(8,128)(2,1)S(1)}, u32[]{:S(2)}, u32[]{:S(2)}) collective-permute-start(bf16[4,40,768]{2,1,0:T(8,128)(2,1)S(1)} %copy-done.27), channel_id=1, source_target_pairs={{0,1},{1,0},{2,3},{3,2},{4,5},{5,4},{6,7},{7,6},{8,9},{9,8},{10,11... | collective-permute-start | bytes 737288 | tf_op jit(solution)/shard_map/ppermute | solution.py:976
  133.3 3.2 %collective-permute-start.22 = (bf16[192,128]{1,0:T(8,128)(2,1)S(1)}, bf16[192,128]{1,0:T(8,128)(2,1)S(1)}, u32[]{:S(2)}, u32[]{:S(2)}) collective-permute-start(bf16[192,128]{1,0:T(8,128)(2,1)S(1)} %get-tuple-element.134), channel_id=1, source_target_pairs={{0,8},{8,16},{16,24},{24,0},{1,9},{9,17},{17,25},{25,1},{2,10},{10... | collective-permute-start | bytes 147464 | tf_op jit(solution)/shard_map/ppermute | solution.py:847
  133.7 4.2 %collective-permute-start.23 = (bf16[192,128]{1,0:T(8,128)(2,1)S(1)}, bf16[192,128]{1,0:T(8,128)(2,1)S(1)}, u32[]{:S(2)}, u32[]{:S(2)}) collective-permute-start(bf16[192,128]{1,0:T(8,128)(2,1)S(1)} %get-tuple-element.135), channel_id=1, source_target_pairs={{0,16},{8,24},{16,0},{24,8},{1,17},{9,25},{17,1},{25,9},{2,18},{10... | collective-permute-start | bytes 147464 | tf_op jit(solution)/shard_map/ppermute | solution.py:847
  136.5 4.0 %collective-permute-start.24 = (bf16[192,128]{1,0:T(8,128)(2,1)S(1)}, bf16[192,128]{1,0:T(8,128)(2,1)S(1)}, u32[]{:S(2)}, u32[]{:S(2)}) collective-permute-start(bf16[192,128]{1,0:T(8,128)(2,1)S(1)} %get-tuple-element.136), channel_id=1, source_target_pairs={{0,24},{8,0},{16,8},{24,16},{1,25},{9,1},{17,9},{25,17},{2,26},{10... | collective-permute-start | bytes 147464 | tf_op jit(solution)/shard_map/ppermute | solution.py:847
  157.0 4.7 %collective-permute-start.28 = (bf16[4,128,384]{2,1,0:T(8,128)(2,1)S(1)}, bf16[4,128,384]{2,1,0:T(8,128)(2,1)S(1)}, u32[]{:S(2)}, u32[]{:S(2)}) collective-permute-start(bf16[4,128,384]{2,1,0:T(8,128)(2,1)S(1)} %get-tuple-element.150), channel_id=1, source_target_pairs={{0,2},{2,0},{1,3},{3,1},{4,6},{6,4},{5,7},{7,5},{8,10},{10,8},{9,1... | collective-permute-start | bytes 1179656 | tf_op jit(solution)/shard_map/ppermute | solution.py:827
  163.0 10.6 %collective-permute-start.30 = (bf16[4,128,384]{2,1,0:T(8,128)(2,1)S(1)}, bf16[4,128,384]{2,1,0:T(8,128)(2,1)S(1)}, u32[]{:S(2)}, u32[]{:S(2)}) collective-permute-start(bf16[4,128,384]{2,1,0:T(8,128)(2,1)S(1)} %get-tuple-element.158), channel_id=1, source_target_pairs={{0,4},{4,0},{1,5},{5,1},{2,6},{6,2},{3,7},{7,3},{8,12},{12,8},{9,1... | collective-permute-start | bytes 1179656 | tf_op jit(solution)/shard_map/ppermute | solution.py:827
  178.1 7.7 %collective-permute-start.31 = (bf16[320,768]{1,0:T(8,128)(2,1)}, bf16[320,768]{1,0:T(8,128)(2,1)}, u32[]{:S(2)}, u32[]{:S(2)}) collective-permute-start(bf16[320,768]{1,0:T(8,128)(2,1)} %get-tuple-element.164), channel_id=1, source_target_pairs={{0,2},{2,0},{1,3},{3,1},{4,6},{6,4},{5,7},{7,5},{8,10},{10,8},{9,1... | collective-permute-start | bytes 1474568 | tf_op jit(solution)/shard_map/ppermute | solution.py:827
  179.1 41.3 %all-to-all-start.2 = ((bf16[4,272,768]{2,1,0:T(8,128)(2,1)}), bf16[4,272,768]{2,1,0:T(8,128)(2,1)S(1)}, u32[]{:S(2)}, u32[]{:S(2)}) async-start(bf16[4,272,768]{2,1,0:T(8,128)(2,1)} %add_groups.1), calls=%async_computation.2 | async-start | bytes 3342336 | tf_op jit(solution)/shard_map/all_to_all | solution.py:843
  184.9 63.1 %collective-permute-start.36 = (bf16[192,3072]{1,0:T(8,128)(2,1)}, bf16[192,3072]{1,0:T(8,128)(2,1)}, u32[]{:S(2)}, u32[]{:S(2)}) collective-permute-start(bf16[192,3072]{1,0:T(8,128)(2,1)} %get-tuple-element.178), channel_id=1, source_target_pairs={{0,4},{4,0},{1,5},{5,1},{2,6},{6,2},{3,7},{7,3},{8,12},{12,8},{9,1... | collective-permute-start | bytes 3538952 | tf_op jit(solution)/shard_map/ppermute | solution.py:827
  187.2 10.0 %collective-permute-start.32 = (bf16[320,384]{1,0:T(8,128)(2,1)S(1)}, bf16[320,384]{1,0:T(8,128)(2,1)S(1)}, u32[]{:S(2)}, u32[]{:S(2)}) collective-permute-start(bf16[320,384]{1,0:T(8,128)(2,1)S(1)} %pad_maximum_fusion.5), channel_id=1, source_target_pairs={{0,1},{1,0},{2,3},{3,2},{4,5},{5,4},{6,7},{7,6},{8,9},{9,8},{10,11... | collective-permute-start | bytes 737288 | tf_op jit(solution)/shard_map/ppermute | solution.py:827
  220.3 38.0 %collective-permute-start.33 = (bf16[128,768]{1,0:T(8,128)(2,1)S(1)}, bf16[128,768]{1,0:T(8,128)(2,1)S(1)}, u32[]{:S(2)}, u32[]{:S(2)}) collective-permute-start(bf16[128,768]{1,0:T(8,128)(2,1)S(1)} %get-tuple-element.175), channel_id=1, source_target_pairs={{0,8},{8,16},{16,24},{24,0},{1,9},{9,17},{17,25},{25,1},{2,10},{10... | collective-permute-start | bytes 589832 | tf_op jit(solution)/shard_map/ppermute | solution.py:1036
  221.5 8.8 %collective-permute-start.34 = (bf16[128,768]{1,0:T(8,128)(2,1)S(1)}, bf16[128,768]{1,0:T(8,128)(2,1)S(1)}, u32[]{:S(2)}, u32[]{:S(2)}) collective-permute-start(bf16[128,768]{1,0:T(8,128)(2,1)S(1)} %copy-done.6), channel_id=1, source_target_pairs={{0,24},{8,0},{16,8},{24,16},{1,25},{9,1},{17,9},{25,17},{2,26},{10... | collective-permute-start | bytes 589832 | tf_op jit(solution)/shard_map/ppermute | solution.py:1035
  224.4 6.8 %collective-permute-start.37 = (bf16[368,384]{1,0:T(8,128)(2,1)S(1)}, bf16[368,384]{1,0:T(8,128)(2,1)S(1)}, u32[]{:S(2)}, u32[]{:S(2)}) collective-permute-start(bf16[368,384]{1,0:T(8,128)(2,1)S(1)} %pad_maximum_fusion.4), channel_id=1, source_target_pairs={{0,4},{4,0},{1,5},{5,1},{2,6},{6,2},{3,7},{7,3},{8,12},{12,8},{9,1... | collective-permute-start | bytes 847880 | tf_op jit(solution)/shard_map/ppermute | solution.py:827
  231.5 4.5 %collective-permute-start.41 = (bf16[80,384]{1,0:T(8,128)(2,1)S(1)}, bf16[80,384]{1,0:T(8,128)(2,1)S(1)}, u32[]{:S(2)}, u32[]{:S(2)}) collective-permute-start(bf16[80,384]{1,0:T(8,128)(2,1)S(1)} %get-tuple-element.230), channel_id=1, source_target_pairs={{0,16},{8,24},{16,0},{24,8},{1,17},{9,25},{17,1},{25,9},{2,18},{10... | collective-permute-start | bytes 184328 | tf_op jit(solution)/shard_map/ppermute | solution.py:1056
  234.4 6.1 %collective-permute-start.42 = (bf16[80,384]{1,0:T(8,128)(2,1)S(1)}, bf16[80,384]{1,0:T(8,128)(2,1)S(1)}, u32[]{:S(2)}, u32[]{:S(2)}) collective-permute-start(bf16[80,384]{1,0:T(8,128)(2,1)S(1)} %get-tuple-element.231), channel_id=1, source_target_pairs={{0,8},{8,16},{16,24},{24,0},{1,9},{9,17},{17,25},{25,1},{2,10},{10... | collective-permute-start | bytes 184328 | tf_op jit(solution)/shard_map/ppermute | solution.py:1056
  235.7 8.5 %collective-permute-start.43 = (bf16[80,384]{1,0:T(8,128)(2,1)S(1)}, bf16[80,384]{1,0:T(8,128)(2,1)S(1)}, u32[]{:S(2)}, u32[]{:S(2)}) collective-permute-start(bf16[80,384]{1,0:T(8,128)(2,1)S(1)} %get-tuple-element.232), channel_id=1, source_target_pairs={{0,24},{8,0},{16,8},{24,16},{1,25},{9,1},{17,9},{25,17},{2,26},{10... | collective-permute-start | bytes 184328 | tf_op jit(solution)/shard_map/ppermute | solution.py:1056
  236.0 12.6 %collective-permute-start.40 = (bf16[48,384]{1,0:T(8,128)(2,1)S(1)}, bf16[48,384]{1,0:T(8,128)(2,1)S(1)}, u32[]{:S(2)}, u32[]{:S(2)}) collective-permute-start(bf16[48,384]{1,0:T(8,128)(2,1)S(1)} %get-tuple-element.225), channel_id=1, source_target_pairs={{4,0},{10,2},{16,4},{22,6},{28,8},{2,10},{8,12},{14,14},{20,16},{2... | collective-permute-start | bytes 110600 | tf_op jit(solution)/shard_map/ppermute | solution.py:1065
  240.5 8.1 %collective-permute-start.39 = (bf16[48,384]{1,0:T(8,128)(2,1)S(1)}, bf16[48,384]{1,0:T(8,128)(2,1)S(1)}, u32[]{:S(2)}, u32[]{:S(2)}) collective-permute-start(bf16[48,384]{1,0:T(8,128)(2,1)S(1)} %get-tuple-element.226), channel_id=1, source_target_pairs={{2,0},{8,2},{14,4},{20,6},{26,8},{0,10},{6,12},{12,14},{18,16},{24... | collective-permute-start | bytes 110600 | tf_op jit(solution)/shard_map/ppermute | solution.py:1065
  244.2 6.5 %collective-permute-start.38 = (bf16[48,384]{1,0:T(8,128)(2,1)S(1)}, bf16[48,384]{1,0:T(8,128)(2,1)S(1)}, u32[]{:S(2)}, u32[]{:S(2)}) collective-permute-start(bf16[48,384]{1,0:T(8,128)(2,1)S(1)} %get-tuple-element.227), channel_id=1, source_target_pairs={{0,0},{6,2},{12,4},{18,6},{24,8},{30,10},{4,12},{10,14},{16,16},{2... | collective-permute-start | bytes 110600 | tf_op jit(solution)/shard_map/ppermute | solution.py:1065
  248.0 10.3 %collective-permute-start.35 = (bf16[128,768]{1,0:T(8,128)(2,1)S(1)}, bf16[128,768]{1,0:T(8,128)(2,1)S(1)}, u32[]{:S(2)}, u32[]{:S(2)}) collective-permute-start(bf16[128,768]{1,0:T(8,128)(2,1)S(1)} %add_convert_fusion), channel_id=1, source_target_pairs={{0,24},{8,0},{16,8},{24,16},{1,25},{9,1},{17,9},{25,17},{2,26},{10... | collective-permute-start | bytes 589832 | tf_op jit(solution)/shard_map/ppermute | solution.py:1038
  254.7 8.9 %collective-permute-start.44 = (bf16[48,3072]{1,0:T(8,128)(2,1)S(1)}, bf16[48,3072]{1,0:T(8,128)(2,1)S(1)}, u32[]{:S(2)}, u32[]{:S(2)}) collective-permute-start(bf16[48,3072]{1,0:T(8,128)(2,1)S(1)} %get-tuple-element.187), channel_id=1, source_target_pairs={{0,8},{8,16},{16,24},{24,0},{1,9},{9,17},{17,25},{25,1},{2,10},{10... | collective-permute-start | bytes 884744 | tf_op jit(solution)/shard_map/ppermute | solution.py:847
  255.4 25.0 %collective-permute-start.45 = (bf16[48,3072]{1,0:T(8,128)(2,1)S(1)}, bf16[48,3072]{1,0:T(8,128)(2,1)S(1)}, u32[]{:S(2)}, u32[]{:S(2)}) collective-permute-start(bf16[48,3072]{1,0:T(8,128)(2,1)S(1)} %get-tuple-element.188), channel_id=1, source_target_pairs={{0,16},{8,24},{16,0},{24,8},{1,17},{9,25},{17,1},{25,9},{2,18},{10... | collective-permute-start | bytes 884744 | tf_op jit(solution)/shard_map/ppermute | solution.py:847
  256.2 26.5 %collective-permute-start.46 = (bf16[48,3072]{1,0:T(8,128)(2,1)S(1)}, bf16[48,3072]{1,0:T(8,128)(2,1)S(1)}, u32[]{:S(2)}, u32[]{:S(2)}) collective-permute-start(bf16[48,3072]{1,0:T(8,128)(2,1)S(1)} %get-tuple-element.189), channel_id=1, source_target_pairs={{0,24},{8,0},{16,8},{24,16},{1,25},{9,1},{17,9},{25,17},{2,26},{10... | collective-permute-start | bytes 884744 | tf_op jit(solution)/shard_map/ppermute | solution.py:847
  (30 other events, 244.6 us)

commit v4 on v3

--- a/solution.py
+++ b/solution.py
@@ -469,7 +469,7 @@
         gate_grad = three_parts(jnp.sum(grad_in[...] * out, axis=1, keepdims=True)).astype(F32)
         for p in range(PIECES):
             rows = slice(p * CAP, (p + 1) * CAP)
-            out_refs[p % n_fsdp][lax.rem(h + groups - p // n_fsdp, groups)] = out[rows].astype(BF)
+            out_refs[p % n_fsdp][(groups - p // n_fsdp) % groups] = out[rows].astype(BF)
             back_ref[source[p], :, :width] = back_acc[rows, :].astype(BF)
             back_ref[source[p], :, width:] = gate_grad[rows].astype(BF)
 
@@ -505,7 +505,7 @@
     )(info, dy, *in_hbm(up, down), *cames)
 
 
-def weight_kernel(count, members, side, turned_by, pos, *refs):
+def weight_kernel(count, members, side, pos, *refs):
     rows, acts, (keep_ref, pass_ref, turned, lhs) = refs[:count], refs[count : 2 * count], refs[2 * count :]
     half = keep_ref.shape[0]
 
@@ -520,7 +520,7 @@
             for r in range(members // 2):
                 member = jnp.bitwise_xor(pos[0], 2 * r)
                 for k in range(GROUPS):
-                    row = pl.multiple_of((lax.rem(turned_by * pos[1] + k, GROUPS) * members + member) * unit, 16)
+                    row = pl.multiple_of((lax.rem(pos[1] + k, GROUPS) * members + member) * unit, 16)
                     at = (r * GROUPS + k) * unit
                     lhs[n, at : at + unit, :] = turned[pl.ds(row, unit), :]
 
@@ -533,7 +533,7 @@
     ffn = acts[0].shape[2]
     half = pl.BlockSpec((width // 4, FBLOCK), lambda j: (0, j))
     return pl.pallas_call(
-        functools.partial(weight_kernel, len(rows), members, side, which),
+        functools.partial(weight_kernel, len(rows), members, side),
         grid=(ffn // FBLOCK,),
         in_specs=[SMEM_SPEC]
         + [pl.BlockSpec((1, count, width), lambda j: (which, 0, 0))] * len(rows)
@@ -548,16 +548,16 @@
 
 
 def add_kernel(riders, a_ref, b_ref, *refs):
-    rides, out = refs[:riders], refs[riders]
-    rows, width = a_ref.shape[0] // GROUPS, out.shape[2]
+    rides, outs = refs[:riders], refs[riders:]
+    rows, width = a_ref.shape[0] // GROUPS, outs[0].shape[1]
     blocks = a_ref.shape[1] // width
-    for k in range(GROUPS):
+    for k, out in enumerate(outs):
         for c in range(blocks):
             at = (slice(k * rows, (k + 1) * rows), slice(c * width, (c + 1) * width))
-            out[k, c * rows : (c + 1) * rows, :] = (a_ref[at].astype(F32) + b_ref[at].astype(F32)).astype(BF)
+            out[c * rows : (c + 1) * rows, :] = (a_ref[at].astype(F32) + b_ref[at].astype(F32)).astype(BF)
         if riders:
             ride = jnp.concatenate([r[k].astype(F32) for r in rides])
-            out[k, blocks * rows :, :] = ride.astype(BF)
+            out[blocks * rows :, :] = ride.astype(BF)
 
 
 def add_groups(a, b, width, rides=()):
@@ -566,70 +566,34 @@
     return pl.pallas_call(
         functools.partial(add_kernel, len(rides)),
         in_specs=[all_of(a)] * 2 + [all_of(r) for r in rides],
-        out_specs=pl.BlockSpec((GROUPS, count, width), lambda: (0, 0, 0)),
-        out_shape=pltpu.HBM((GROUPS, count, width), BF),
+        out_specs=[pl.BlockSpec((count, width), lambda: (0, 0))] * GROUPS,
+        out_shape=[jax.ShapeDtypeStruct((count, width), BF)] * GROUPS,
         compiler_params=pltpu.CompilerParams(vmem_limit_bytes=16 << 20),
         cost_estimate=pl.CostEstimate(flops=10**5, bytes_accessed=10**4, transcendentals=0),
         name="add_groups",
     )(*in_hbm(a, b, *rides))
 
 
-def sum_kernel(a_ref, b_ref, *outs):
-    rows = outs[0].shape[0]
-    for k, out in enumerate(outs):
-        at = slice(k * rows, (k + 1) * rows)
-        out[...] = (a_ref[at, :].astype(F32) + b_ref[at, :].astype(F32)).astype(BF)
-
-
-def sum_pieces(a, b):
-    rows, cols = a.shape
+def order_kernel(blocks, pos, *refs):
+    out_ref = refs[-1]
+    rows, width = out_ref.shape[1], out_ref.shape[2] // blocks
+    for k in range(GROUPS):
+        group = group_of(k, pos[1])
+        for c in range(blocks):
+            out_ref[group, :, c * width : (c + 1) * width] = refs[k][c * rows : (c + 1) * rows, :].astype(F32)
+
+
+def in_order(pos, parts, rows, cols):
+    width = parts[0].shape[1]
     return pl.pallas_call(
-        sum_kernel,
-        in_specs=[all_of(a)] * 2,
-        out_specs=[pl.BlockSpec((rows // GROUPS, cols), lambda: (0, 0))] * GROUPS,
-        out_shape=[jax.ShapeDtypeStruct((rows // GROUPS, cols), BF)] * GROUPS,
-        compiler_params=pltpu.CompilerParams(vmem_limit_bytes=16 << 20),
-        cost_estimate=pl.CostEstimate(flops=10**5, bytes_accessed=10**4, transcendentals=0),
-        name="sum_pieces",
-    )(*in_hbm(a, b))
-
-
-def order_kernel(pos, *refs):
-    for k in range(GROUPS):
-        refs[-1][group_of(k, pos[1])] = refs[k][...].astype(F32)
-
-
-def in_order(pos, parts):
-    shape = (GROUPS,) + parts[0].shape
-    return pl.pallas_call(
-        order_kernel,
+        functools.partial(order_kernel, cols // width),
         in_specs=[SMEM_SPEC] + [all_of(p) for p in parts],
-        out_specs=pl.BlockSpec(shape, lambda: (0, 0, 0)),
-        out_shape=jax.ShapeDtypeStruct(shape, F32),
+        out_specs=pl.BlockSpec((GROUPS, rows, cols), lambda: (0, 0, 0)),
+        out_shape=jax.ShapeDtypeStruct((GROUPS, rows, cols), F32),
         compiler_params=pltpu.CompilerParams(vmem_limit_bytes=16 << 20),
         cost_estimate=pl.CostEstimate(flops=10**5, bytes_accessed=10**4, transcendentals=0),
         name="in_order",
     )(pos, *parts)
-
-
-def wide_kernel(blocks, x_ref, out_ref):
-    rows, width = out_ref.shape[1], out_ref.shape[2] // blocks
-    for k in range(GROUPS):
-        for c in range(blocks):
-            out_ref[k, :, c * width : (c + 1) * width] = x_ref[k, c * rows : (c + 1) * rows, :].astype(F32)
-
-
-def to_wide(x, rows, cols):
-    width = x.shape[2]
-    return pl.pallas_call(
-        functools.partial(wide_kernel, cols // width),
-        in_specs=[all_of(x)],
-        out_specs=pl.BlockSpec((GROUPS, rows, cols), lambda: (0, 0, 0)),
-        out_shape=jax.ShapeDtypeStruct((GROUPS, rows, cols), F32),
-        compiler_params=pltpu.CompilerParams(vmem_limit_bytes=16 << 20),
-        cost_estimate=pl.CostEstimate(flops=10**5, bytes_accessed=10**4, transcendentals=0),
-        name="to_wide",
-    )(x)
 
 
 def turn_kernel(
@@ -839,10 +803,6 @@
     return jnp.where(lax.axis_index("fsdp") == 0, jnp.stack([part, came]), jnp.stack([came, part]))
 
 
-def swap_groups(x):
-    return lax.all_to_all(x, "h", 0, 0, tiled=True)
-
-
 def group_pieces(pieces, sign):
     came = {k: lax.ppermute(pieces[k], "h", turn(sign * k)) for k in (2, 1, 3)}
     return [pieces[0]] + [came[k] for k in range(1, GROUPS)]
@@ -941,10 +901,10 @@
     kv = proj[:, GWIDTH:].reshape(GROUPS, tok, 2 * GWIDTH)
     kvs = gather_members(jnp.concatenate([kv, mixed[:, tok:, : 2 * GWIDTH]], axis=1))
     dy_send = dot((pick[0] | pick[1]).astype(BF), cotangent[0]).astype(BF).reshape(PIECES, CAP, width)
-    dy_send = together(dy_send, qkv_heads)[0]
-    kvs[0], dy_slots = together(kvs[0], exchange_rows(dy_send))
+    dy_slots = exchange_rows(together(dy_send, proj)[0])
     o_pre, *rest = attend(pos, proj, kvs, strips, blocks)
     lows, stat, keys = rest[:GROUPS], rest[GROUPS], rest[GROUPS + 1 :]
+    lows[1], dy_slots = together(lows[1], dy_slots)
     *pieces, context, residual, moe_in, gates = router(
         pos, tokens[0], out_full, moe_scale[None], router_t, routes, place.T, group_pieces(lows, -1)
     )
@@ -995,9 +955,9 @@
             bit *= 2
         keep, came = held[0], None
     if staged:
-        sends.append(swap(terms[1][1], "r", 1))
-        up_send, came = together(add_groups(terms[0][0], sends[0], width, outs), came)
-        up_came = swap_groups(up_send)
+        up_came = group_pieces(add_groups(terms[0][0], sends[0], width, outs), 1)
+        sends.append(swap(together(terms[1][1], came)[0], "r", 1))
+        came, up_came[2] = together(came, up_came[2])
 
     own_back, back_1, back_2, back_3, term, sent, pack = input_back(
         jnp.stack([h, core]).astype(jnp.int32), members, BUCKETS // n_fsdp, dq, keep, came, ain, qkv_heads,
@@ -1029,9 +989,16 @@
         axis=1,
     )
     if staged:
-        term, up_came = together(term, up_came)
+        term, sends[1], up_came = together(term, sends[1], up_came)
+    for bit in bits_of(members // 2):
+        mine = (lax.axis_index("r") // bit) % 2
+        term = term.reshape((2, -1) + term.shape[1:])
+        came, pack_came = swap_both(lax.dynamic_index_in_dim(term, 1 - mine, 0, False), pack, "r", bit)
+        term = lax.dynamic_index_in_dim(term, mine, 0, False) + came
+        pack = pack + pack_came
+    term = term[0]
     if staged:
-        back_2, back_3, term = together(back_2, back_3, term)
+        back_2, back_3, up_came = together(back_2, back_3, up_came)
     mid = lax.ppermute(back_2, "h", turn(-1))
     side = lax.ppermute(back_3, "h", turn(1)).astype(F32)
     mid = (back_1.astype(F32) + mid.astype(F32)).astype(BF)
@@ -1041,15 +1008,10 @@
     token_grad = jax.vjp(lambda v: normalize(v, attn_scale), x)[1](attn_in_grad)[0]
     tokens_grad = (resid_grad + token_grad).astype(BF)
 
-    for bit in bits_of(members // 2):
-        mine = (lax.axis_index("r") // bit) % 2
-        term = term.reshape((2, -1) + term.shape[1:])
-        came, pack_came = swap_both(lax.dynamic_index_in_dim(term, 1 - mine, 0, False), pack, "r", bit)
-        term = lax.dynamic_index_in_dim(term, mine, 0, False) + came
-        pack = pack + pack_came
-    term = term[0]
     out_term = term[3 * unit :].reshape(GROUPS, rows_c, rows_f)
     term = term[: 3 * unit].astype(BF).reshape(3, unit, rows_f)
+    if staged:
+        down_came = group_pieces(add_groups(terms[1][0], sends[1], width), 1)
     out_sum, pack_sum = lax.dynamic_index_in_dim(out_term, h, 0, False), pack
     for k in (2, 1, 3):
         piece = lax.dynamic_index_in_dim(out_term, lax.rem(h + k, GROUPS), 0, False)
@@ -1064,10 +1026,9 @@
         which = (3 * lax.rem((at + shards - r) * third, shards) + r) // shards
         parts.append(lax.ppermute(lax.dynamic_index_in_dim(term, which, 0, False), CTX, pairs))
     if staged:
-        sends[1], parts, pack_sum = together(sends[1], parts, pack_sum)
-        down_came = group_pieces(sum_pieces(terms[1][0], sends[1]), 1)
-        grads = [to_wide(up_came, rows_c, ffn), in_order(pos, down_came)]
-        home = up_came[:, rows_c * ffn // width :].reshape(EXPERTS * CAP, width)
+        up_came, parts = together(up_came, parts)
+        grads = [in_order(pos, part, rows_c, ffn) for part in (up_came, down_came)]
+        home = jnp.concatenate([part[rows_c * ffn // width :] for part in up_came])
     else:
         terms = [jnp.concatenate(terms[n] + terms[n + 1]) for n in (0, 2)]
         grads = [
@@ -1076,7 +1037,8 @@
         home = jnp.concatenate([o.reshape(-1, width) for o in outs])
     qkv_grad = jnp.concatenate(parts).astype(F32).T
 
-    place = (group * n_fsdp + jnp.bitwise_xor(routes // here, f)) * CAP + slot
+    away = lax.rem(h - group + GROUPS, GROUPS) if spread else group
+    place = (away * n_fsdp + jnp.bitwise_xor(routes // here, f)) * CAP + slot
     layer_out = residual
     for k in range(TOP):
         row = (slots[:, None] == place[None, :, k]).astype(BF)

time: 290 us -> 278 us (0.959)
  starting transfers between devices: 86.9 us -> 80.7 us
    all_to_all x1 -> x0, waiting for transfers between devices: 21.9 us -> none  [swap_groups(): return lax.all_to_all(x, 'h', 0, 0, tiled=True)]
    ppermute x9 -> x12, waiting for transfers between devices: 27.1 us -> 41.2 us  [group_pieces(): came = {k: lax.ppermute(pieces[k], 'h', turn(sign * k)) for k in (2, 1, 3)}]
    ppermute x9 -> x12, starting transfers between devices: 10.2 us -> 18.4 us  [group_pieces(): came = {k: lax.ppermute(pieces[k], 'h', turn(sign * k)) for k in (2, 1, 3)}]
    all_to_all x1 -> x0, starting transfers between devices: 5.5 us -> none  [swap_groups(): return lax.all_to_all(x, 'h', 0, 0, tiled=True)]
    ppermute x3, waiting for transfers between devices: 0.13 us -> 4.87 us  [per_device(): lax.ppermute(jnp.concatenate([piece.astype(BF), two_parts(pack)]), 'h', t...]
    ppermute x12, starting transfers between devices: 16.8 us -> 13.6 us  [swap(): return lax.ppermute(x, axis, xor_perm(bit, lax.axis_size(axis)))]
    pallas_call x5 -> x4, Pallas kernels: 17.9 us -> 16.4 us  [the longest x2 12.2 us: weight_terms(): pl.pallas_call(functools.partial(weight_kernel, len(rows), members, side)...]
  transfers between devices with their start and end apart: 50 -> 52, of which waited for: 22 -> 24; matrix products, arithmetic and copies ran while one was open for 9% -> 8% of each run, Pallas kernels for 18% -> 19%
where the time goes in v4:
time: 278 us; the launch traced here: 276 us
  waiting for transfers between devices  85.8 us (31%)
  starting transfers between devices  80.7 us (29%)
  Pallas kernels  78.3 us (28%)
  other arithmetic  13.5 us (5%)
  local copies, waits for them, and re-layouts  11.7 us (4%)
  matrix products  4.26 us (2%)
    ppermute x12, waiting for transfers between devices, group_pieces(): came = {k: lax.ppermute(pieces[k], 'h', turn(sign * k)) for k in (2, 1, 3)}  41.2 us
    ppermute x12, waiting for transfers between devices, swap(): return lax.ppermute(x, axis, xor_perm(bit, lax.axis_size(axis)))  18.9 us
    ppermute x12, starting transfers between devices, group_pieces(): came = {k: lax.ppermute(pieces[k], 'h', turn(sign * k)) for k in (2, 1, 3)}  18.4 us
    pallas_call x1, Pallas kernels, attend_back(): pl.pallas_call(functools.partial(backward_kernel, half, blocks, members),...  17.9 us
    pallas_call x1, Pallas kernels, attend(): pl.pallas_call(functools.partial(forward_kernel, half, blocks, len(kvs)),...  13.7 us
    ppermute x12, starting transfers between devices, swap(): return lax.ppermute(x, axis, xor_perm(bit, lax.axis_size(axis)))  13.6 us
    pallas_call x2, Pallas kernels, weight_terms(): pl.pallas_call(functools.partial(weight_kernel, len(rows), members, side)...  12.2 us
    pallas_call x1, Pallas kernels, expert(): pl.pallas_call(functools.partial(expert_kernel, groups, n_fsdp), grid_spe...  11.9 us
  transfers between devices with their start and end apart: 52, of which 24 were waited for; matrix products, arithmetic and copies ran while one was open for 8% of the time, Pallas kernels for 19%

profile of v4, /device:TPU:11, one launch (start us, length us, event | category | flops | bytes accessed | tf_op | source)
XLA Modules:
  0.0 275.7 jit_solution(8948674493955086838)
XLA Ops:
  3.0 2.3 collective-permute-start.4
  16.7 3.3 %strips.1.refs_4_.refs_5_ = f32[2304,192]{1,0:T(8,128)} custom-call(f32[3,2304]{1,0:T(4,128)} %convolution_multiply_fusion.g_ref), custom_call_target="tpu_custom_call" | custom-call | flops 100000 | bytes 10000 | tf_op jit(solution)/shard_map/strips/pallas_call | solution.py:73
  20.1 3.7 %collective-permute-done.3 = bf16[136,768]{1,0:T(8,128)(2,1)S(1)} collective-permute-done((bf16[136,768]{1,0:T(8,128)(2,1)}, bf16[136,768]{1,0:T(8,128)(2,1)S(1)}, u32[]{:S(2)}, u32[]{:S(2)}) %collective-permute-start.3) | collective-permute-done | bytes 208928 | tf_op jit(solution)/shard_map/ppermute | solution.py:772
  26.7 5.5 %all-to-all-start = ((bf16[8,40,768]{2,1,0:T(8,128)(2,1)}), bf16[8,40,768]{2,1,0:T(8,128)(2,1)S(1)}, u32[]{:S(2)}, u32[]{:S(2)}) async-start(bf16[8,40,768]{2,1,0:T(8,128)(2,1)} %bitcast.23), calls=%async_computation | async-start | bytes 983040 | tf_op jit(solution)/shard_map/all_to_all | solution.py:896
  35.4 6.9 %collective-permute-done.7.refs_2_ = bf16[4,136,384]{2,1,0:T(8,128)(2,1)S(1)} collective-permute-done((bf16[4,136,384]{2,1,0:T(8,128)(2,1)S(1)}, bf16[4,136,384]{2,1,0:T(8,128)(2,1)S(1)}, u32[]{:S(2)}, u32[]{:S(2)}) %collective-permute-start.7) | collective-permute-done | bytes 417824 | tf_op jit(solution)/shard_map/ppermute | solution.py:781
  42.3 2.0 collective-permute-start.8
  45.7 13.7 %attend.1 = (f32[8,192,64]{2,1,0:T(8,128)}, bf16[192,128]{1,0:T(8,128)(2,1)S(1)}, bf16[192,128]{1,0:T(8,128)(2,1)S(1)}, bf16[192,128]{1,0:T(8,128)(2,1)S(1)}, bf...) custom-call(s32[2]{0:T(128)S(1)} %pad_add_fusion.pos, ...), custom_call_target="tpu_custom_call" | custom-call | flops 100000 | bytes 10000 | tf_op jit(solution)/shard_map/attend/pallas_call | solution.py:322
  59.4 2.1 collective-permute-start.10
  63.0 2.9 %maximum_select_fusion = bf16[2,384,768]{2,1,0:T(8,128)(2,1)} fusion(bf16[1,384,768]{2,1,0:T(8,128)(2,1)} %bitcast.7, bf16[1,384,768]{2,1,0:T(8,128)(2,1)} %bitcast.6, pred[]{:T(512)S(6)} %eq.106), kind=kLoop, calls=%fused_computation.8 | loop fusion | flops 1769472 | bytes 2359297 | tf_op jit(solution)/shard_map/jit(_where)/select_n | solution.py:803
  66.0 2.9 %router.1 = (bf16[40,896]{1,0:T(8,128)(2,1)S(1)}, bf16[40,896]{1,0:T(8,128)(2,1)S(1)}, bf16[40,896]{1,0:T(8,128)(2,1)S(1)}, bf16[40,896]{1,0:T(8,128)(2,1)S(1)},...) custom-call(s32[2]{0:T(128)S(1)} %pad_add_fusion.pos, ...), custom_call_target="tpu_custom_call" | custom-call | flops 100000 | bytes 10000 | tf_op jit(solution)/shard_map/router/pallas_call | solution.py:422
  68.9 2.1 collective-permute-start.12
  75.2 2.1 collective-permute-start.16
  77.5 2.1 collective-permute-start.18
  79.7 3.2 %collective-permute-done.16.refs_5_ = bf16[40,896]{1,0:T(8,128)(2,1)S(1)} collective-permute-done((bf16[40,896]{1,0:T(8,128)(2,1)S(1)}, bf16[40,896]{1,0:T(8,128)(2,1)S(1)}, u32[]{:S(2)}, u32[]{:S(2)}) %collective-permute-start.16) | collective-permute-done | bytes 71712 | tf_op jit(solution)/shard_map/ppermute | solution.py:822
  82.9 4.1 %collective-permute-done.17.refs_6_ = bf16[40,896]{1,0:T(8,128)(2,1)S(1)} collective-permute-done((bf16[40,896]{1,0:T(8,128)(2,1)S(1)}, bf16[40,896]{1,0:T(8,128)(2,1)S(1)}, u32[]{:S(2)}, u32[]{:S(2)}) %collective-permute-start.17) | collective-permute-done | bytes 71712 | tf_op jit(solution)/shard_map/ppermute | solution.py:822
  88.7 11.9 %expert.1 = (bf16[4,40,768]{2,1,0:T(8,128)(2,1)}, bf16[4,40,768]{2,1,0:T(8,128)(2,1)}, bf16[8,40,896]{2,1,0:T(8,128)(2,1)}, bf16[2,320,3072]{2,1,0:T(8,128)(2,1)}, bf16[2,320,768]{2,1,0:T(8,128)(2,1)}) custom-call(s32[2]{0:T(128)S(1)} %pad_add_fusion.3.info, bf16[8,40,768]{2,1,0:T(8,128)(2,1)S(1)} %all-to-all-done.dy_ref, bf16[4,768,3072]{2,1,0:T(8,128)(2,1)} %up_ref.1, ...), custom_call_target="tpu_custom_call" | custom-call | flops 100000 | bytes 10000 | tf_op jit(solution)/shard_map/expert/pallas_call | solution.py:482
  101.2 4.3 %all-to-all-start.1 = ((bf16[8,40,896]{2,1,0:T(8,128)(2,1)}), bf16[8,40,896]{2,1,0:T(8,128)(2,1)S(1)}, u32[]{:S(2)}, u32[]{:S(2)}) async-start(bf16[8,40,896]{2,1,0:T(8,128)(2,1)} %get-tuple-element.136), calls=%async_computation.1 | async-start | bytes 1146880 | tf_op jit(solution)/shard_map/all_to_all | solution.py:896
  106.3 2.9 %collective-permute-done.19.refs_1_ = bf16[2,320,768]{2,1,0:T(8,128)(2,1)S(1)} collective-permute-done((bf16[2,320,768]{2,1,0:T(8,128)(2,1)}, bf16[2,320,768]{2,1,0:T(8,128)(2,1)S(1)}, u32[]{:S(2)}, u32[]{:S(2)}) %collective-permute-start.19) | collective-permute-done | bytes 983072 | tf_op jit(solution)/shard_map/ppermute | solution.py:791
  109.2 6.1 %weight_terms.3 = (bf16[192,3072]{1,0:T(8,128)(2,1)}, bf16[192,3072]{1,0:T(8,128)(2,1)}) custom-call(s32[2]{0:T(128)S(1)} %pad_add_fusion.pos, bf16[2,320,768]{2,1,0:T(8,128)(2,1)S(1)} %copy-done.1, bf16[2,320,768]{2,1,0:T(8,128)(2,1)S(1)} %collective-permute-done.19.refs_1_, bf16[2,320,3072]{2,1,0:T(8,128)(2,1)} %get-tuple-element.138.refs_2_, ...), custom_call_target="tpu_custom_call" | custom-call | flops 100000 | bytes 10000 | tf_op jit(solution)/shard_map/weight_terms/pallas_call | solution.py:535
  115.3 6.1 %weight_terms.2 = (bf16[192,3072]{1,0:T(8,128)(2,1)}, bf16[192,3072]{1,0:T(8,128)(2,1)}) custom-call(s32[2]{0:T(128)S(1)} %pad_add_fusion.pos, bf16[2,320,768]{2,1,0:T(8,128)(2,1)S(1)} %copy-done.1, bf16[2,320,768]{2,1,0:T(8,128)(2,1)S(1)} %collective-permute-done.19.refs_1_, bf16[2,320,3072]{2,1,0:T(8,128)(2,1)} %get-tuple-element.138.refs_2_, ...), custom_call_target="tpu_custom_call" | custom-call | flops 100000 | bytes 10000 | tf_op jit(solution)/shard_map/weight_terms/pallas_call | solution.py:535
  121.5 5.1 %turn_back.1 = (bf16[192,128]{1,0:T(8,128)(2,1)S(1)}, bf16[192,128]{1,0:T(8,128)(2,1)S(1)}, bf16[192,128]{1,0:T(8,128)(2,1)S(1)}, bf16[192,128]{1,0:T(8,128)(2,1...) custom-call(s32[3]{0:T(128)S(1)} %pad_add_fusion.2.info, ...), custom_call_target="tpu_custom_call" | custom-call | flops 100000 | bytes 10000 | tf_op jit(solution)/shard_map/turn_back/pallas_call | solution.py:657
  126.9 2.5 collective-permute-start.29
  135.9 1.8 collective-permute-start.24
  137.7 2.2 collective-permute-done.24.refs_3_
  139.9 17.9 %attend_back.1 = (bf16[512,192]{1,0:T(8,128)(2,1)S(1)}, bf16[4,128,384]{2,1,0:T(8,128)(2,1)S(1)}, bf16[4,128,384]{2,1,0:T(8,128)(2,1)S(1)}, bf16[4,128,384]{2,1,...) custom-call(s32[2]{0:T(128)S(1)} %pad_add_fusion.pos, ...), custom_call_target="tpu_custom_call" | custom-call | flops 100000 | bytes 10000 | tf_op jit(solution)/shard_map/attend_back/pallas_call | solution.py:347
  157.8 2.4 collective-permute-start.28
  163.3 2.0 add_groups.2
  166.1 3.8 %collective-permute-start.31 = (bf16[272,768]{1,0:T(8,128)(2,1)S(1)}, bf16[272,768]{1,0:T(8,128)(2,1)S(1)}, u32[]{:S(2)}, u32[]{:S(2)}) collective-permute-start(bf16[272,768]{1,0:T(8,128)(2,1)S(1)} %get-tuple-element.173), channel_id=1, source_target_pairs={{0,16},{8,24},{16,0},{24,8},{1,17},{9,25},{17,1},{25,9},{2,18},{10... | collective-permute-start | bytes 1253384 | tf_op jit(solution)/shard_map/ppermute | solution.py:807
  170.8 9.1 %collective-permute-done.30.came_ref = bf16[4,128,384]{2,1,0:T(8,128)(2,1)S(1)} collective-permute-done((bf16[4,128,384]{2,1,0:T(8,128)(2,1)S(1)}, bf16[4,128,384]{2,1,0:T(8,128)(2,1)S(1)}, u32[]{:S(2)}, u32[]{:S(2)}) %collective-permute-start.30) | collective-permute-done | bytes 393248 | tf_op jit(solution)/shard_map/ppermute | solution.py:791
  179.9 7.2 %collective-permute-done.31.refs_2_ = bf16[272,768]{1,0:T(8,128)(2,1)S(1)} collective-permute-done((bf16[272,768]{1,0:T(8,128)(2,1)S(1)}, bf16[272,768]{1,0:T(8,128)(2,1)S(1)}, u32[]{:S(2)}, u32[]{:S(2)}) %collective-permute-start.31) | collective-permute-done | bytes 417824 | tf_op jit(solution)/shard_map/ppermute | solution.py:807
  187.1 2.9 %input_back.1 = (f32[128,768]{1,0:T(8,128)S(1)}, bf16[128,768]{1,0:T(8,128)(2,1)S(1)}, bf16[128,768]{1,0:T(8,128)(2,1)S(1)}, bf16[128,768]{1,0:T(8,128)(2,1)S(1)...) custom-call(s32[2]{0:T(128)S(1)} %pad_add_fusion.1.info, ...), custom_call_target="tpu_custom_call" | custom-call | flops 100000 | bytes 10000 | tf_op jit(solution)/shard_map/input_back/pallas_call | solution.py:745
  194.2 2.2 collective-permute-start.33
  197.6 2.0 collective-permute-start.36
  199.6 2.9 %collective-permute-done.33 = bf16[320,384]{1,0:T(8,128)(2,1)S(1)} collective-permute-done((bf16[320,384]{1,0:T(8,128)(2,1)S(1)}, bf16[320,384]{1,0:T(8,128)(2,1)S(1)}, u32[]{:S(2)}, u32[]{:S(2)}) %collective-permute-start.33) | collective-permute-done | bytes 245792 | tf_op jit(solution)/shard_map/ppermute | solution.py:791
  202.8 6.2 %collective-permute-done.35.refs_1_ = bf16[272,768]{1,0:T(8,128)(2,1)S(1)} collective-permute-done((bf16[272,768]{1,0:T(8,128)(2,1)S(1)}, bf16[272,768]{1,0:T(8,128)(2,1)S(1)}, u32[]{:S(2)}, u32[]{:S(2)}) %collective-permute-start.35) | collective-permute-done | bytes 417824 | tf_op jit(solution)/shard_map/ppermute | solution.py:807
  209.0 9.1 %collective-permute-done.36.refs_3_ = bf16[272,768]{1,0:T(8,128)(2,1)S(1)} collective-permute-done((bf16[272,768]{1,0:T(8,128)(2,1)S(1)}, bf16[272,768]{1,0:T(8,128)(2,1)S(1)}, u32[]{:S(2)}, u32[]{:S(2)}) %collective-permute-start.36) | collective-permute-done | bytes 417824 | tf_op jit(solution)/shard_map/ppermute | solution.py:807
  219.2 2.6 collective-permute-start.42
  223.0 1.9 add_groups.3
  225.0 3.7 %collective-permute-start.48 = (bf16[192,768]{1,0:T(8,128)(2,1)S(1)}, bf16[192,768]{1,0:T(8,128)(2,1)S(1)}, u32[]{:S(2)}, u32[]{:S(2)}) collective-permute-start(bf16[192,768]{1,0:T(8,128)(2,1)S(1)} %get-tuple-element.216), channel_id=1, source_target_pairs={{0,16},{8,24},{16,0},{24,8},{1,17},{9,25},{17,1},{25,9},{2,18},{10... | collective-permute-start | bytes 884744 | tf_op jit(solution)/shard_map/ppermute | solution.py:807
  229.3 3.6 %collective-permute-start.40 = (bf16[48,384]{1,0:T(8,128)(2,1)S(1)}, bf16[48,384]{1,0:T(8,128)(2,1)S(1)}, u32[]{:S(2)}, u32[]{:S(2)}) collective-permute-start(bf16[48,384]{1,0:T(8,128)(2,1)S(1)} %get-tuple-element.253), channel_id=1, source_target_pairs={{4,0},{10,2},{16,4},{22,6},{28,8},{2,10},{8,12},{14,14},{20,16},{2... | collective-permute-start | bytes 110600 | tf_op jit(solution)/shard_map/ppermute | solution.py:1027
  232.9 2.9 %collective-permute-start.39 = (bf16[48,384]{1,0:T(8,128)(2,1)S(1)}, bf16[48,384]{1,0:T(8,128)(2,1)S(1)}, u32[]{:S(2)}, u32[]{:S(2)}) collective-permute-start(bf16[48,384]{1,0:T(8,128)(2,1)S(1)} %get-tuple-element.254), channel_id=1, source_target_pairs={{2,0},{8,2},{14,4},{20,6},{26,8},{0,10},{6,12},{12,14},{18,16},{24... | collective-permute-start | bytes 110600 | tf_op jit(solution)/shard_map/ppermute | solution.py:1027
  235.8 2.7 collective-permute-start.38
  238.6 15.3 %collective-permute-done.48.refs_2_ = bf16[192,768]{1,0:T(8,128)(2,1)S(1)} collective-permute-done((bf16[192,768]{1,0:T(8,128)(2,1)S(1)}, bf16[192,768]{1,0:T(8,128)(2,1)S(1)}, u32[]{:S(2)}, u32[]{:S(2)}) %collective-permute-start.48) | collective-permute-done | bytes 294944 | tf_op jit(solution)/shard_map/ppermute | solution.py:807
  255.4 2.1 in_order.3
  257.5 3.1 %collective-permute-start.44 = (bf16[80,384]{1,0:T(8,128)(2,1)S(1)}, bf16[80,384]{1,0:T(8,128)(2,1)S(1)}, u32[]{:S(2)}, u32[]{:S(2)}) collective-permute-start(bf16[80,384]{1,0:T(8,128)(2,1)S(1)} %get-tuple-element.258), channel_id=1, source_target_pairs={{0,16},{8,24},{16,0},{24,8},{1,17},{9,25},{17,1},{25,9},{2,18},{10... | collective-permute-start | bytes 184328 | tf_op jit(solution)/shard_map/ppermute | solution.py:1018
  262.1 2.1 in_order.2
  267.0 2.2 collective-permute-done.45
  269.2 2.6 collective-permute-done.46
  (230 shorter events, 59.7 us)
Async XLA Ops:
  3.0 17.1 %collective-permute-start.4 = (bf16[136,768]{1,0:T(8,128)(2,1)}, bf16[136,768]{1,0:T(8,128)(2,1)S(1)}, u32[]{:S(2)}, u32[]{:S(2)}) collective-permute-start(bf16[136,768]{1,0:T(8,128)(2,1)} %get-tuple-element.249), channel_id=1, source_target_pairs={{0,16},{8,24},{16,0},{24,8},{1,17},{9,25},{17,1},{25,9},{2,18},{10... | collective-permute-start | bytes 626696 | tf_op jit(solution)/shard_map/ppermute | solution.py:772
  5.3 18.5 %collective-permute-start.3 = (bf16[136,768]{1,0:T(8,128)(2,1)}, bf16[136,768]{1,0:T(8,128)(2,1)S(1)}, u32[]{:S(2)}, u32[]{:S(2)}) collective-permute-start(bf16[136,768]{1,0:T(8,128)(2,1)} %get-tuple-element.249), channel_id=1, source_target_pairs={{0,8},{8,16},{16,24},{24,0},{1,9},{9,17},{17,25},{25,1},{2,10},{10... | collective-permute-start | bytes 626696 | tf_op jit(solution)/shard_map/ppermute | solution.py:772
  5.3 18.5 %collective-permute-start.5 = (bf16[136,768]{1,0:T(8,128)(2,1)}, bf16[136,768]{1,0:T(8,128)(2,1)}, u32[]{:S(2)}, u32[]{:S(2)}) collective-permute-start(bf16[136,768]{1,0:T(8,128)(2,1)} %get-tuple-element.249), channel_id=1, source_target_pairs={{0,24},{8,0},{16,8},{24,16},{1,25},{9,1},{17,9},{25,17},{2,26},{10... | collective-permute-start | bytes 626696 | tf_op jit(solution)/shard_map/ppermute | solution.py:772
  9.8 5.7 %collective-permute-start.2 = (bf16[16,384]{1,0:T(8,128)(2,1)S(1)}, bf16[16,384]{1,0:T(8,128)(2,1)S(1)}, u32[]{:S(2)}, u32[]{:S(2)}) collective-permute-start(bf16[16,384]{1,0:T(8,128)(2,1)S(1)} %concatenate.53), channel_id=1, source_target_pairs={{0,1},{1,0},{2,3},{3,2},{4,5},{5,4},{6,7},{7,6},{8,9},{9,8},{10,11... | collective-permute-start | bytes 36872 | tf_op jit(solution)/shard_map/ppermute | solution.py:802
  11.7 13.7 %collective-permute-start = (bf16[384,576]{1,0:T(8,128)(2,1)S(1)}, bf16[384,576]{1,0:T(8,128)(2,1)S(1)}, u32[]{:S(2)}, u32[]{:S(2)}) collective-permute-start(bf16[384,576]{1,0:T(8,128)(2,1)S(1)} %pad_maximum_fusion.2), channel_id=1, source_target_pairs={{0,1},{1,0},{2,3},{3,2},{4,5},{5,4},{6,7},{7,6},{8,9},{9,8},{10,11... | collective-permute-start | bytes 1327112 | tf_op jit(solution)/shard_map/ppermute | solution.py:802
  26.7 34.9 %all-to-all-start = ((bf16[8,40,768]{2,1,0:T(8,128)(2,1)}), bf16[8,40,768]{2,1,0:T(8,128)(2,1)S(1)}, u32[]{:S(2)}, u32[]{:S(2)}) async-start(bf16[8,40,768]{2,1,0:T(8,128)(2,1)} %bitcast.23), calls=%async_computation | async-start | bytes 983040 | tf_op jit(solution)/shard_map/all_to_all | solution.py:896
  32.2 10.2 %collective-permute-start.7 = (bf16[4,136,384]{2,1,0:T(8,128)(2,1)S(1)}, bf16[4,136,384]{2,1,0:T(8,128)(2,1)S(1)}, u32[]{:S(2)}, u32[]{:S(2)}) collective-permute-start(bf16[4,136,384]{2,1,0:T(8,128)(2,1)S(1)} %pad_maximum_fusion.4.refs_0_), channel_id=1, source_target_pairs={{0,4},{2,6},{4,0},{6,2},{1,5},{3,7},{5,1},{7,3},{8,12},{10,14},{12... | collective-permute-start | bytes 1253384 | tf_op jit(solution)/shard_map/ppermute | solution.py:781
  33.5 29.6 %collective-permute-start.1 = (bf16[384,768]{1,0:T(8,128)(2,1)}, bf16[384,768]{1,0:T(8,128)(2,1)}, u32[]{:S(2)}, u32[]{:S(2)}) collective-permute-start(bf16[384,768]{1,0:T(8,128)(2,1)} %param.19), channel_id=1, source_target_pairs={{0,1},{1,0},{2,3},{3,2},{4,5},{5,4},{6,7},{7,6},{8,9},{9,8},{10,11... | collective-permute-start | bytes 1769480 | tf_op jit(solution)/shard_map/ppermute | solution.py:802
  33.7 10.7 %collective-permute-start.6 = (bf16[4,136,384]{2,1,0:T(8,128)(2,1)S(1)}, bf16[4,136,384]{2,1,0:T(8,128)(2,1)S(1)}, u32[]{:S(2)}, u32[]{:S(2)}) collective-permute-start(bf16[4,136,384]{2,1,0:T(8,128)(2,1)S(1)} %pad_maximum_fusion.4.refs_0_), channel_id=1, source_target_pairs={{0,2},{2,0},{4,6},{6,4},{1,3},{3,1},{5,7},{7,5},{8,10},{10,8},{12,... | collective-permute-start | bytes 1253384 | tf_op jit(solution)/shard_map/ppermute | solution.py:781
  42.3 3.3 %collective-permute-start.8 = (bf16[4,136,384]{2,1,0:T(8,128)(2,1)S(1)}, bf16[4,136,384]{2,1,0:T(8,128)(2,1)S(1)}, u32[]{:S(2)}, u32[]{:S(2)}) collective-permute-start(bf16[4,136,384]{2,1,0:T(8,128)(2,1)S(1)} %collective-permute-done.7.refs_2_), channel_id=1, source_target_pairs={{0,2},{2,0},{4,6},{6,4},{1,3},{3,1},{5,7},{7,5},{8,10},{10,8},{12,... | collective-permute-start | bytes 1253384 | tf_op jit(solution)/shard_map/ppermute | solution.py:781
  59.4 6.5 %collective-permute-start.10 = (bf16[192,128]{1,0:T(8,128)(2,1)S(1)}, bf16[192,128]{1,0:T(8,128)(2,1)S(1)}, u32[]{:S(2)}, u32[]{:S(2)}) collective-permute-start(bf16[192,128]{1,0:T(8,128)(2,1)S(1)} %get-tuple-element.121), channel_id=1, source_target_pairs={{0,16},{8,24},{16,0},{24,8},{1,17},{9,25},{17,1},{25,9},{2,18},{10... | collective-permute-start | bytes 147464 | tf_op jit(solution)/shard_map/ppermute | solution.py:807
  61.6 4.4 %collective-permute-start.11 = (bf16[192,128]{1,0:T(8,128)(2,1)S(1)}, bf16[192,128]{1,0:T(8,128)(2,1)S(1)}, u32[]{:S(2)}, u32[]{:S(2)}) collective-permute-start(bf16[192,128]{1,0:T(8,128)(2,1)S(1)} %get-tuple-element.122), channel_id=1, source_target_pairs={{0,8},{8,16},{16,24},{24,0},{1,9},{9,17},{17,25},{25,1},{2,10},{10... | collective-permute-start | bytes 147464 | tf_op jit(solution)/shard_map/ppermute | solution.py:807
  61.6 4.4 %collective-permute-start.9 = (bf16[192,128]{1,0:T(8,128)(2,1)S(1)}, bf16[192,128]{1,0:T(8,128)(2,1)S(1)}, u32[]{:S(2)}, u32[]{:S(2)}) collective-permute-start(bf16[192,128]{1,0:T(8,128)(2,1)S(1)} %get-tuple-element.120), channel_id=1, source_target_pairs={{0,24},{8,0},{16,8},{24,16},{1,25},{9,1},{17,9},{25,17},{2,26},{10... | collective-permute-start | bytes 147464 | tf_op jit(solution)/shard_map/ppermute | solution.py:807
  68.9 8.4 %collective-permute-start.12 = (bf16[40,896]{1,0:T(8,128)(2,1)S(1)}, bf16[40,896]{1,0:T(8,128)(2,1)S(1)}, u32[]{:S(2)}, u32[]{:S(2)}) collective-permute-start(bf16[40,896]{1,0:T(8,128)(2,1)S(1)} %get-tuple-element.129), channel_id=1, source_target_pairs={{0,1},{1,0},{8,9},{9,8},{16,17},{17,16},{24,25},{25,24},{2,3},{3,2... | collective-permute-start | bytes 215048 | tf_op jit(solution)/shard_map/ppermute | solution.py:822
  71.0 6.5 %collective-permute-start.13 = (bf16[40,896]{1,0:T(8,128)(2,1)S(1)}, bf16[40,896]{1,0:T(8,128)(2,1)S(1)}, u32[]{:S(2)}, u32[]{:S(2)}) collective-permute-start(bf16[40,896]{1,0:T(8,128)(2,1)S(1)} %get-tuple-element.130), channel_id=1, source_target_pairs={{0,8},{1,9},{8,16},{9,17},{16,24},{17,25},{24,0},{25,1},{2,10},{3,... | collective-permute-start | bytes 215048 | tf_op jit(solution)/shard_map/ppermute | solution.py:822
  72.2 7.5 %collective-permute-start.14 = (bf16[40,896]{1,0:T(8,128)(2,1)S(1)}, bf16[40,896]{1,0:T(8,128)(2,1)S(1)}, u32[]{:S(2)}, u32[]{:S(2)}) collective-permute-start(bf16[40,896]{1,0:T(8,128)(2,1)S(1)} %get-tuple-element.131), channel_id=1, source_target_pairs={{0,9},{1,8},{8,17},{9,16},{16,25},{17,24},{24,1},{25,0},{2,11},{3,... | collective-permute-start | bytes 215048 | tf_op jit(solution)/shard_map/ppermute | solution.py:822
  73.7 6.0 %collective-permute-start.15 = (bf16[40,896]{1,0:T(8,128)(2,1)S(1)}, bf16[40,896]{1,0:T(8,128)(2,1)S(1)}, u32[]{:S(2)}, u32[]{:S(2)}) collective-permute-start(bf16[40,896]{1,0:T(8,128)(2,1)S(1)} %get-tuple-element.132), channel_id=1, source_target_pairs={{0,16},{1,17},{8,24},{9,25},{16,0},{17,1},{24,8},{25,9},{2,18},{3,... | collective-permute-start | bytes 215048 | tf_op jit(solution)/shard_map/ppermute | solution.py:822
  75.2 7.8 %collective-permute-start.16 = (bf16[40,896]{1,0:T(8,128)(2,1)S(1)}, bf16[40,896]{1,0:T(8,128)(2,1)S(1)}, u32[]{:S(2)}, u32[]{:S(2)}) collective-permute-start(bf16[40,896]{1,0:T(8,128)(2,1)S(1)} %get-tuple-element.133), channel_id=1, source_target_pairs={{0,17},{1,16},{8,25},{9,24},{16,1},{17,0},{24,9},{25,8},{2,19},{3,... | collective-permute-start | bytes 215048 | tf_op jit(solution)/shard_map/ppermute | solution.py:822
  77.3 9.8 %collective-permute-start.17 = (bf16[40,896]{1,0:T(8,128)(2,1)S(1)}, bf16[40,896]{1,0:T(8,128)(2,1)S(1)}, u32[]{:S(2)}, u32[]{:S(2)}) collective-permute-start(bf16[40,896]{1,0:T(8,128)(2,1)S(1)} %get-tuple-element.134), channel_id=1, source_target_pairs={{0,24},{1,25},{8,0},{9,1},{16,8},{17,9},{24,16},{25,17},{2,26},{3,... | collective-permute-start | bytes 215048 | tf_op jit(solution)/shard_map/ppermute | solution.py:822
  77.5 11.2 %collective-permute-start.18 = (bf16[40,896]{1,0:T(8,128)(2,1)S(1)}, bf16[40,896]{1,0:T(8,128)(2,1)S(1)}, u32[]{:S(2)}, u32[]{:S(2)}) collective-permute-start(bf16[40,896]{1,0:T(8,128)(2,1)S(1)} %get-tuple-element.135), channel_id=1, source_target_pairs={{0,25},{1,24},{8,1},{9,0},{16,9},{17,8},{24,17},{25,16},{2,27},{3,... | collective-permute-start | bytes 215048 | tf_op jit(solution)/shard_map/ppermute | solution.py:822
  100.6 8.6 %collective-permute-start.20 = (bf16[2,320,3072]{2,1,0:T(8,128)(2,1)}, bf16[2,320,3072]{2,1,0:T(8,128)(2,1)}, u32[]{:S(2)}, u32[]{:S(2)}) collective-permute-start(bf16[2,320,3072]{2,1,0:T(8,128)(2,1)} %get-tuple-element.138.refs_2_), channel_id=1, source_target_pairs={{0,2},{2,0},{1,3},{3,1},{4,6},{6,4},{5,7},{7,5},{8,10},{10,8},{9,1... | collective-permute-start | bytes 11796488 | tf_op jit(solution)/shard_map/ppermute | solution.py:791
  101.2 20.2 %all-to-all-start.1 = ((bf16[8,40,896]{2,1,0:T(8,128)(2,1)}), bf16[8,40,896]{2,1,0:T(8,128)(2,1)S(1)}, u32[]{:S(2)}, u32[]{:S(2)}) async-start(bf16[8,40,896]{2,1,0:T(8,128)(2,1)} %get-tuple-element.136), calls=%async_computation.1 | async-start | bytes 1146880 | tf_op jit(solution)/shard_map/all_to_all | solution.py:896
  105.5 3.7 %collective-permute-start.19 = (bf16[2,320,768]{2,1,0:T(8,128)(2,1)}, bf16[2,320,768]{2,1,0:T(8,128)(2,1)S(1)}, u32[]{:S(2)}, u32[]{:S(2)}) collective-permute-start(bf16[2,320,768]{2,1,0:T(8,128)(2,1)} %get-tuple-element.137.refs_0_), channel_id=1, source_target_pairs={{0,2},{2,0},{1,3},{3,1},{4,6},{6,4},{5,7},{7,5},{8,10},{10,8},{9,1... | collective-permute-start | bytes 2949128 | tf_op jit(solution)/shard_map/ppermute | solution.py:791
  126.9 35.4 %collective-permute-start.29 = (bf16[192,3072]{1,0:T(8,128)(2,1)S(1)}, bf16[192,3072]{1,0:T(8,128)(2,1)S(1)}, u32[]{:S(2)}, u32[]{:S(2)}) collective-permute-start(bf16[192,3072]{1,0:T(8,128)(2,1)S(1)} %copy-done.26), channel_id=1, source_target_pairs={{0,4},{4,0},{1,5},{5,1},{2,6},{6,2},{3,7},{7,3},{8,12},{12,8},{9,1... | collective-permute-start | bytes 3538952 | tf_op jit(solution)/shard_map/ppermute | solution.py:791
  130.8 29.4 %collective-permute-start.25 = (bf16[8,48,384]{2,1,0:T(8,128)(2,1)S(1)}, bf16[8,48,384]{2,1,0:T(8,128)(2,1)S(1)}, u32[]{:S(2)}, u32[]{:S(2)}) collective-permute-start(bf16[8,48,384]{2,1,0:T(8,128)(2,1)S(1)} %fusion.5), channel_id=1, source_target_pairs={{0,1},{1,0},{2,3},{3,2},{4,5},{5,4},{6,7},{7,6},{8,9},{9,8},{10,11... | collective-permute-start | bytes 884744 | tf_op jit(solution)/shard_map/ppermute | solution.py:791
  132.5 27.7 %collective-permute-start.26 = (bf16[4,40,768]{2,1,0:T(8,128)(2,1)S(1)}, bf16[4,40,768]{2,1,0:T(8,128)(2,1)S(1)}, u32[]{:S(2)}, u32[]{:S(2)}) collective-permute-start(bf16[4,40,768]{2,1,0:T(8,128)(2,1)S(1)} %copy-done.27), channel_id=1, source_target_pairs={{0,1},{1,0},{2,3},{3,2},{4,5},{5,4},{6,7},{7,6},{8,9},{9,8},{10,11... | collective-permute-start | bytes 737288 | tf_op jit(solution)/shard_map/ppermute | solution.py:936
  133.4 4.3 %collective-permute-start.23 = (bf16[192,128]{1,0:T(8,128)(2,1)S(1)}, bf16[192,128]{1,0:T(8,128)(2,1)S(1)}, u32[]{:S(2)}, u32[]{:S(2)}) collective-permute-start(bf16[192,128]{1,0:T(8,128)(2,1)S(1)} %get-tuple-element.149), channel_id=1, source_target_pairs={{0,16},{8,24},{16,0},{24,8},{1,17},{9,25},{17,1},{25,9},{2,18},{10... | collective-permute-start | bytes 147464 | tf_op jit(solution)/shard_map/ppermute | solution.py:807
  135.9 4.1 %collective-permute-start.24 = (bf16[192,128]{1,0:T(8,128)(2,1)S(1)}, bf16[192,128]{1,0:T(8,128)(2,1)S(1)}, u32[]{:S(2)}, u32[]{:S(2)}) collective-permute-start(bf16[192,128]{1,0:T(8,128)(2,1)S(1)} %get-tuple-element.150), channel_id=1, source_target_pairs={{0,24},{8,0},{16,8},{24,16},{1,25},{9,1},{17,9},{25,17},{2,26},{10... | collective-permute-start | bytes 147464 | tf_op jit(solution)/shard_map/ppermute | solution.py:807
  157.8 3.7 %collective-permute-start.28 = (bf16[4,128,384]{2,1,0:T(8,128)(2,1)S(1)}, bf16[4,128,384]{2,1,0:T(8,128)(2,1)S(1)}, u32[]{:S(2)}, u32[]{:S(2)}) collective-permute-start(bf16[4,128,384]{2,1,0:T(8,128)(2,1)S(1)} %get-tuple-element.164), channel_id=1, source_target_pairs={{0,2},{2,0},{1,3},{3,1},{4,6},{6,4},{5,7},{7,5},{8,10},{10,8},{9,1... | collective-permute-start | bytes 1179656 | tf_op jit(solution)/shard_map/ppermute | solution.py:791
  166.1 21.0 %collective-permute-start.31 = (bf16[272,768]{1,0:T(8,128)(2,1)S(1)}, bf16[272,768]{1,0:T(8,128)(2,1)S(1)}, u32[]{:S(2)}, u32[]{:S(2)}) collective-permute-start(bf16[272,768]{1,0:T(8,128)(2,1)S(1)} %get-tuple-element.173), channel_id=1, source_target_pairs={{0,16},{8,24},{16,0},{24,8},{1,17},{9,25},{17,1},{25,9},{2,18},{10... | collective-permute-start | bytes 1253384 | tf_op jit(solution)/shard_map/ppermute | solution.py:807
  169.9 10.0 %collective-permute-start.30 = (bf16[4,128,384]{2,1,0:T(8,128)(2,1)S(1)}, bf16[4,128,384]{2,1,0:T(8,128)(2,1)S(1)}, u32[]{:S(2)}, u32[]{:S(2)}) collective-permute-start(bf16[4,128,384]{2,1,0:T(8,128)(2,1)S(1)} %get-tuple-element.168), channel_id=1, source_target_pairs={{0,4},{4,0},{1,5},{5,1},{2,6},{6,2},{3,7},{7,3},{8,12},{12,8},{9,1... | collective-permute-start | bytes 1179656 | tf_op jit(solution)/shard_map/ppermute | solution.py:791
  191.4 27.8 %collective-permute-start.34 = (bf16[192,3072]{1,0:T(8,128)(2,1)}, bf16[192,3072]{1,0:T(8,128)(2,1)S(1)}, u32[]{:S(2)}, u32[]{:S(2)}) collective-permute-start(bf16[192,3072]{1,0:T(8,128)(2,1)} %get-tuple-element.186), channel_id=1, source_target_pairs={{0,4},{4,0},{1,5},{5,1},{2,6},{6,2},{3,7},{7,3},{8,12},{12,8},{9,1... | collective-permute-start | bytes 3538952 | tf_op jit(solution)/shard_map/ppermute | solution.py:791
  194.2 8.3 %collective-permute-start.33 = (bf16[320,384]{1,0:T(8,128)(2,1)S(1)}, bf16[320,384]{1,0:T(8,128)(2,1)S(1)}, u32[]{:S(2)}, u32[]{:S(2)}) collective-permute-start(bf16[320,384]{1,0:T(8,128)(2,1)S(1)} %pad_maximum_fusion.6), channel_id=1, source_target_pairs={{0,1},{1,0},{2,3},{3,2},{4,5},{5,4},{6,7},{7,6},{8,9},{9,8},{10,11... | collective-permute-start | bytes 737288 | tf_op jit(solution)/shard_map/ppermute | solution.py:791
  196.5 12.5 %collective-permute-start.35 = (bf16[272,768]{1,0:T(8,128)(2,1)S(1)}, bf16[272,768]{1,0:T(8,128)(2,1)S(1)}, u32[]{:S(2)}, u32[]{:S(2)}) collective-permute-start(bf16[272,768]{1,0:T(8,128)(2,1)S(1)} %copy-done.6), channel_id=1, source_target_pairs={{0,8},{8,16},{16,24},{24,0},{1,9},{9,17},{17,25},{25,1},{2,10},{10... | collective-permute-start | bytes 1253384 | tf_op jit(solution)/shard_map/ppermute | solution.py:807
  197.6 20.5 %collective-permute-start.36 = (bf16[272,768]{1,0:T(8,128)(2,1)S(1)}, bf16[272,768]{1,0:T(8,128)(2,1)S(1)}, u32[]{:S(2)}, u32[]{:S(2)}) collective-permute-start(bf16[272,768]{1,0:T(8,128)(2,1)S(1)} %get-tuple-element.190), channel_id=1, source_target_pairs={{0,24},{8,0},{16,8},{24,16},{1,25},{9,1},{17,9},{25,17},{2,26},{10... | collective-permute-start | bytes 1253384 | tf_op jit(solution)/shard_map/ppermute | solution.py:807
  219.2 9.4 %collective-permute-start.42 = (bf16[128,768]{1,0:T(8,128)(2,1)S(1)}, bf16[128,768]{1,0:T(8,128)(2,1)S(1)}, u32[]{:S(2)}, u32[]{:S(2)}) collective-permute-start(bf16[128,768]{1,0:T(8,128)(2,1)S(1)} %copy-done.8), channel_id=1, source_target_pairs={{0,24},{8,0},{16,8},{24,16},{1,25},{9,1},{17,9},{25,17},{2,26},{10... | collective-permute-start | bytes 589832 | tf_op jit(solution)/shard_map/ppermute | solution.py:1002
  221.8 7.2 %collective-permute-start.37 = (bf16[368,384]{1,0:T(8,128)(2,1)S(1)}, bf16[368,384]{1,0:T(8,128)(2,1)S(1)}, u32[]{:S(2)}, u32[]{:S(2)}) collective-permute-start(bf16[368,384]{1,0:T(8,128)(2,1)S(1)} %pad_maximum_fusion.5), channel_id=1, source_target_pairs={{0,4},{4,0},{1,5},{5,1},{2,6},{6,2},{3,7},{7,3},{8,12},{12,8},{9,1... | collective-permute-start | bytes 847880 | tf_op jit(solution)/shard_map/ppermute | solution.py:791
  224.9 10.9 %collective-permute-start.47 = (bf16[192,768]{1,0:T(8,128)(2,1)S(1)}, bf16[192,768]{1,0:T(8,128)(2,1)S(1)}, u32[]{:S(2)}, u32[]{:S(2)}) collective-permute-start(bf16[192,768]{1,0:T(8,128)(2,1)S(1)} %get-tuple-element.215), channel_id=1, source_target_pairs={{0,8},{8,16},{16,24},{24,0},{1,9},{9,17},{17,25},{25,1},{2,10},{10... | collective-permute-start | bytes 884744 | tf_op jit(solution)/shard_map/ppermute | solution.py:807
  225.0 28.9 %collective-permute-start.48 = (bf16[192,768]{1,0:T(8,128)(2,1)S(1)}, bf16[192,768]{1,0:T(8,128)(2,1)S(1)}, u32[]{:S(2)}, u32[]{:S(2)}) collective-permute-start(bf16[192,768]{1,0:T(8,128)(2,1)S(1)} %get-tuple-element.216), channel_id=1, source_target_pairs={{0,16},{8,24},{16,0},{24,8},{1,17},{9,25},{17,1},{25,9},{2,18},{10... | collective-permute-start | bytes 884744 | tf_op jit(solution)/shard_map/ppermute | solution.py:807
  228.6 25.6 %collective-permute-start.49 = (bf16[192,768]{1,0:T(8,128)(2,1)S(1)}, bf16[192,768]{1,0:T(8,128)(2,1)S(1)}, u32[]{:S(2)}, u32[]{:S(2)}) collective-permute-start(bf16[192,768]{1,0:T(8,128)(2,1)S(1)} %get-tuple-element.217), channel_id=1, source_target_pairs={{0,24},{8,0},{16,8},{24,16},{1,25},{9,1},{17,9},{25,17},{2,26},{10... | collective-permute-start | bytes 884744 | tf_op jit(solution)/shard_map/ppermute | solution.py:807
  229.3 28.2 %collective-permute-start.40 = (bf16[48,384]{1,0:T(8,128)(2,1)S(1)}, bf16[48,384]{1,0:T(8,128)(2,1)S(1)}, u32[]{:S(2)}, u32[]{:S(2)}) collective-permute-start(bf16[48,384]{1,0:T(8,128)(2,1)S(1)} %get-tuple-element.253), channel_id=1, source_target_pairs={{4,0},{10,2},{16,4},{22,6},{28,8},{2,10},{8,12},{14,14},{20,16},{2... | collective-permute-start | bytes 110600 | tf_op jit(solution)/shard_map/ppermute | solution.py:1027
  232.9 27.7 %collective-permute-start.39 = (bf16[48,384]{1,0:T(8,128)(2,1)S(1)}, bf16[48,384]{1,0:T(8,128)(2,1)S(1)}, u32[]{:S(2)}, u32[]{:S(2)}) collective-permute-start(bf16[48,384]{1,0:T(8,128)(2,1)S(1)} %get-tuple-element.254), channel_id=1, source_target_pairs={{2,0},{8,2},{14,4},{20,6},{26,8},{0,10},{6,12},{12,14},{18,16},{24... | collective-permute-start | bytes 110600 | tf_op jit(solution)/shard_map/ppermute | solution.py:1027
  235.8 25.7 %collective-permute-start.38 = (bf16[48,384]{1,0:T(8,128)(2,1)S(1)}, bf16[48,384]{1,0:T(8,128)(2,1)S(1)}, u32[]{:S(2)}, u32[]{:S(2)}) collective-permute-start(bf16[48,384]{1,0:T(8,128)(2,1)S(1)} %get-tuple-element.255), channel_id=1, source_target_pairs={{0,0},{6,2},{12,4},{18,6},{24,8},{30,10},{4,12},{10,14},{16,16},{2... | collective-permute-start | bytes 110600 | tf_op jit(solution)/shard_map/ppermute | solution.py:1027
  253.9 20.6 %collective-permute-start.41 = (bf16[128,768]{1,0:T(8,128)(2,1)S(1)}, bf16[128,768]{1,0:T(8,128)(2,1)S(1)}, u32[]{:S(2)}, u32[]{:S(2)}) collective-permute-start(bf16[128,768]{1,0:T(8,128)(2,1)S(1)} %get-tuple-element.206), channel_id=1, source_target_pairs={{0,8},{8,16},{16,24},{24,0},{1,9},{9,17},{17,25},{25,1},{2,10},{10... | collective-permute-start | bytes 589832 | tf_op jit(solution)/shard_map/ppermute | solution.py:1003
  254.2 20.3 %collective-permute-start.43 = (bf16[128,768]{1,0:T(8,128)(2,1)S(1)}, bf16[128,768]{1,0:T(8,128)(2,1)S(1)}, u32[]{:S(2)}, u32[]{:S(2)}) collective-permute-start(bf16[128,768]{1,0:T(8,128)(2,1)S(1)} %add_convert_fusion), channel_id=1, source_target_pairs={{0,24},{8,0},{16,8},{24,16},{1,25},{9,1},{17,9},{25,17},{2,26},{10... | collective-permute-start | bytes 589832 | tf_op jit(solution)/shard_map/ppermute | solution.py:1005
  257.5 9.5 %collective-permute-start.44 = (bf16[80,384]{1,0:T(8,128)(2,1)S(1)}, bf16[80,384]{1,0:T(8,128)(2,1)S(1)}, u32[]{:S(2)}, u32[]{:S(2)}) collective-permute-start(bf16[80,384]{1,0:T(8,128)(2,1)S(1)} %get-tuple-element.258), channel_id=1, source_target_pairs={{0,16},{8,24},{16,0},{24,8},{1,17},{9,25},{17,1},{25,9},{2,18},{10... | collective-permute-start | bytes 184328 | tf_op jit(solution)/shard_map/ppermute | solution.py:1018
  260.6 8.6 %collective-permute-start.45 = (bf16[80,384]{1,0:T(8,128)(2,1)S(1)}, bf16[80,384]{1,0:T(8,128)(2,1)S(1)}, u32[]{:S(2)}, u32[]{:S(2)}) collective-permute-start(bf16[80,384]{1,0:T(8,128)(2,1)S(1)} %get-tuple-element.259), channel_id=1, source_target_pairs={{0,8},{8,16},{16,24},{24,0},{1,9},{9,17},{17,25},{25,1},{2,10},{10... | collective-permute-start | bytes 184328 | tf_op jit(solution)/shard_map/ppermute | solution.py:1018
  261.5 10.4 %collective-permute-start.46 = (bf16[80,384]{1,0:T(8,128)(2,1)S(1)}, bf16[80,384]{1,0:T(8,128)(2,1)S(1)}, u32[]{:S(2)}, u32[]{:S(2)}) collective-permute-start(bf16[80,384]{1,0:T(8,128)(2,1)S(1)} %get-tuple-element.260), channel_id=1, source_target_pairs={{0,24},{8,0},{16,8},{24,16},{1,25},{9,1},{17,9},{25,17},{2,26},{10... | collective-permute-start | bytes 184328 | tf_op jit(solution)/shard_map/ppermute | solution.py:1018
  (32 other events, 276.0 us)

commit v5 on v4

--- a/solution.py
+++ b/solution.py
@@ -89,15 +89,20 @@
     return jnp.where(same, jnp.concatenate([x] * GHEADS), 0.0)
 
 
+def identity(size):
+    a, b = (lax.broadcasted_iota(jnp.int32, (size, size), n) for n in range(2))
+    return jnp.where(a == b, 1.0, 0.0).astype(BF)
+
+
+def own_columns(x, half):
+    return jnp.concatenate(
+        [x[n * HEAD_DIM : (n + 1) * HEAD_DIM, n * half : (n + 1) * half] for n in range(GHEADS)]
+    )
+
+
 def fold_rows(x, same, half):
     y = jnp.where(same, x, 0.0).T
     return sum(y[n * half : (n + 1) * half] for n in range(GHEADS))
-
-
-def own_columns(x, half):
-    return jnp.concatenate(
-        [x[n * HEAD_DIM : (n + 1) * HEAD_DIM, n * half : (n + 1) * half] for n in range(GHEADS)]
-    )
 
 
 def spread_columns(x, same):
@@ -122,7 +127,7 @@
 
 def forward_kernel(half, blocks, members, pos, q_ref, *refs):
     kvs, refs = refs[:members], refs[members:]
-    strip_in, o_ref, *lows, stat_ref, k_out, v_out, kt_out, k_ref, v_ref, kt_ref, vt, strip_ref, sems, strip_sem = refs
+    strip_in, o_ref, *lows, stat_ref, k_out, v_out, kt_out, k_ref, v_ref, kt_ref, vt, strip_ref, low, sems, strip_sem = refs
     loads = start_copies([(strip_in, strip_ref)], strip_sem)
     size = GHEADS * half
     me, h = pos[0], pos[1]
@@ -141,10 +146,12 @@
                 k_ref[block // per, at, :] = rows[:, :GWIDTH]
                 v_ref[block // per, at, :] = rows[:, GWIDTH:]
 
-    @pl.loop(0, blocks // per)
+    eye = identity(GWIDTH)
+
+    @pl.loop(0, blocks // per, unroll=4)
     def _(chunk):
-        kt_ref[chunk] = k_ref[chunk].astype(F32).T.astype(BF)
-        vt[chunk] = v_ref[chunk].astype(F32).T.astype(BF)
+        kt_ref[chunk] = dot(eye, k_ref[chunk], ((1,), (1,))).astype(BF)
+        vt[chunk] = dot(eye, v_ref[chunk], ((1,), (1,))).astype(BF)
 
     copies = start_copies([(k_ref, k_out), (v_ref, v_out), (kt_ref, kt_out)], sems)
     docs = jnp.concatenate([kv[a, tok : tok + 1, :tok].astype(F32) for kv in kvs for a in range(GROUPS)])
@@ -152,54 +159,63 @@
     for load in loads:
         load.wait()
 
-    @pl.loop(0, q_ref.shape[0] // half)
-    def _(i):
-        slot, late = i // 2, lax.rem(i, 2)
+    def prepare(slot, late):
         owner = group_of(slot, h) * members + me
-        block = jnp.where(late == 0, owner, blocks - 1 - owner)
-        at = pl.ds(pl.multiple_of(i * half, half), half)
-        qt = spread_rows(q_ref[at, :GWIDTH].astype(F32), same).T.astype(BF)
-        doc = kvs[0][slot, tok : tok + 1, :tok].astype(F32)
-        doc = jnp.where(late == 0, doc[:, :half], doc[:, half:])
+        block = owner if late == 0 else blocks - 1 - owner
+        at = pl.ds(pl.multiple_of(slot * tok + late * half, half), half)
+        qs = spread_rows(q_ref[at, :GWIDTH].astype(F32), same).astype(BF)
+        qt = dot(eye, qs, ((1,), (1,))).astype(BF)
+        doc = kvs[0][slot, tok : tok + 1, :tok].astype(F32)[:, late * half : (late + 1) * half]
         begin = jnp.zeros((1, half), F32)
         for s in range(1, DOCS):
             begin = jnp.where(doc == s, begins[s - 1], begin)
         first = jnp.min(begin).astype(jnp.int32) // CHUNK
         begin = jnp.concatenate([begin] * GHEADS, axis=1)
-        start = begin.astype(jnp.int32)
-
-        def visit(chunk, carry):
-            peak, total, acc = carry
-            top, last, begin = bounds(block, chunk, half, blocks, start)
-            t = dot(k_ref[chunk], qt) * (HEAD_DIM**-0.5 * LOG2E) + strip_ref[pl.ds(top, CHUNK), :]
-            t = jnp.where((key <= last) & (key >= begin), t, LOWEST)
-            new = jnp.maximum(peak, jnp.ceil(jnp.max(t, axis=0, keepdims=True)))
-            e = jnp.exp2(t - new)
-            fade = jnp.exp2(peak - new)
-            total = total * fade + jnp.sum(e, axis=0, keepdims=True)
-            acc = acc * fade + dot(vt[chunk], e.astype(BF))
-            return new, total, acc
-
-        init = (
-            jnp.full((1, size), LOWEST, F32),
-            jnp.zeros((1, size), F32),
-            jnp.zeros((GWIDTH, size), F32),
+        return block, first, block // per, begin, qt
+
+    def advance(state, step, carry):
+        block, first, final, begin, qt = state
+        peak, total, acc = carry
+        chunk = jnp.minimum(first + step, final)
+        top, last, begin = bounds(block, chunk, half, blocks, begin.astype(jnp.int32))
+        last = jnp.where(first + step <= final, last, -1)
+        t = dot(k_ref[chunk], qt) * (HEAD_DIM**-0.5 * LOG2E) + strip_ref[pl.ds(top, CHUNK), :]
+        t = jnp.where((key <= last) & (key >= begin), t, LOWEST)
+        new = jnp.maximum(peak, jnp.ceil(jnp.max(t, axis=0, keepdims=True)))
+        e = jnp.exp2(t - new)
+        fade = jnp.exp2(peak - new)
+        total = total * fade + jnp.sum(e, axis=0, keepdims=True)
+        acc = acc * fade + dot(vt[chunk], e.astype(BF))
+        return new, total, acc
+
+    init = (
+        jnp.full((1, size), LOWEST, F32),
+        jnp.zeros((1, size), F32),
+        jnp.zeros((GWIDTH, size), F32),
+    )
+
+    def pair_of(pair, late):
+        slots = [group_of(2 * pair + n, h) for n in range(2)]
+        states = [prepare(slot, late) for slot in slots]
+        steps = functools.reduce(jnp.maximum, [s[2] - s[1] + 1 for s in states])
+        done = lax.fori_loop(
+            0, steps, lambda i, c: tuple(advance(s, i, x) for s, x in zip(states, c)), (init,) * 2
         )
-        peak, total, acc = lax.fori_loop(first, block // per + 1, visit, init)
-        out = own_columns(acc / total, half)
-        o_ref[i] = out
-        low = out.astype(BF)
-        for n in range(GROUPS):
-            for part in range(2):
-
-                @pl.when(i == 2 * n + part)
-                def _():
-                    lows[n][:, part * half : (part + 1) * half] = low
-
-        stat_ref[i, 0:1, :] = peak
-        stat_ref[i, 1:2, :] = total
-        stat_ref[i, 2:3, :] = begin
-
+        for slot, state, (peak, total, acc) in zip(slots, states, done):
+            out = own_columns(acc / total, half)
+            o_ref[2 * slot + late] = out
+            low[slot, :, late * half : (late + 1) * half] = out.astype(BF)
+            stat_ref[2 * slot + late, 0:1, :] = peak
+            stat_ref[2 * slot + late, 1:2, :] = total
+            stat_ref[2 * slot + late, 2:3, :] = state[3]
+
+    @pl.loop(0, GROUPS // 2)
+    def _(pair):
+        pair_of(pair, 0)
+        pair_of(pair, 1)
+
+    for n in range(GROUPS):
+        lows[n][...] = low[n]
     for copy in copies:
         copy.wait()
 
@@ -232,38 +248,54 @@
     for copy in copies:
         copy.wait()
 
-    @pl.loop(0, q_ref.shape[0] // half)
-    def _(i):
-        slot, late = i // 2, lax.rem(i, 2)
+    def prepare(slot, late):
+        i = 2 * slot + late
         owner = group_of(slot, h) * members + me
-        block = jnp.where(late == 0, owner, blocks - 1 - owner)
-        at = pl.ds(pl.multiple_of(i * half, half), half)
+        block = owner if late == 0 else blocks - 1 - owner
+        at = pl.ds(pl.multiple_of(slot * 2 * half + late * half, half), half)
         peak, total, start = (stat_ref[i, n : n + 1, :] for n in range(3))
         first = jnp.min(start).astype(jnp.int32) // CHUNK
-        start = start.astype(jnp.int32)
         qs = spread_rows(q_ref[at, :GWIDTH].astype(F32), same)
         qt, qs = qs.T.astype(BF), qs.astype(BF)
-        do = do_ref[slot]
-        do = jnp.where(late == 0, do[:, :half], do[:, half:])
+        do = do_ref[slot][:, late * half : (late + 1) * half]
         corr = jnp.sum(spread_columns(do * o_ref[i], same), axis=0, keepdims=True) / total
         gt = spread_columns(do, same) / total
         gs = gt.T.astype(BF)
-        gt = gt.astype(BF)
-
-        def visit(chunk, dq):
-            top, last, begin = bounds(block, chunk, half, blocks, start)
-            t = dot(k_ref[chunk], qt) * (HEAD_DIM**-0.5 * LOG2E) + strip_ref[pl.ds(top, CHUNK), :]
-            t = jnp.where((key <= last) & (key >= begin), t - peak, LOWEST)
-            e = jnp.exp2(t)
-            s = e * (dot(v_ref[chunk], gt) - corr)
-            low = s.astype(BF)
-            dk[chunk] += dot(low, qs)
-            dv[chunk] += dot(e.astype(BF), gs)
-            dstrip[pl.ds(top, CHUNK), :] += s
-            return dq + dot(kt_ref[chunk], low)
-
-        dq = lax.fori_loop(first, block // per + 1, visit, jnp.zeros((GWIDTH, size), F32))
-        dq_ref[at, :] = (fold_rows(dq, same, half) * HEAD_DIM**-0.5).astype(BF)
+        return block, first, block // per, start.astype(jnp.int32), peak, corr, qt, qs, gt.astype(BF), gs, at
+
+    def scores(state, step):
+        block, first, final, start, peak, corr, qt, _, gt = state[:9]
+        chunk = jnp.minimum(first + step, final)
+        top, last, begin = bounds(block, chunk, half, blocks, start)
+        last = jnp.where(first + step <= final, last, -1)
+        t = dot(k_ref[chunk], qt) * (HEAD_DIM**-0.5 * LOG2E) + strip_ref[pl.ds(top, CHUNK), :]
+        t = jnp.where((key <= last) & (key >= begin), t - peak, LOWEST)
+        e = jnp.exp2(t)
+        return chunk, top, e.astype(BF), e * (dot(v_ref[chunk], gt) - corr)
+
+    def pair_of(pair, late):
+        states = [prepare(group_of(2 * pair + n, h), late) for n in range(2)]
+
+        def visit(step, carry):
+            found = [scores(s, step) for s in states]
+            out = []
+            for (chunk, top, e, s), state, dq in zip(found, states, carry):
+                low = s.astype(BF)
+                dk[chunk] += dot(low, state[7])
+                dv[chunk] += dot(e, state[9])
+                dstrip[pl.ds(top, CHUNK), :] += s
+                out.append(dq + dot(kt_ref[chunk], low))
+            return tuple(out)
+
+        steps = functools.reduce(jnp.maximum, [s[2] - s[1] + 1 for s in states])
+        done = lax.fori_loop(0, steps, visit, (jnp.zeros((GWIDTH, size), F32),) * 2)
+        for state, dq in zip(states, done):
+            dq_ref[state[10], :] = (fold_rows(dq, same, half) * HEAD_DIM**-0.5).astype(BF)
+
+    @pl.loop(0, GROUPS // 2)
+    def _(pair):
+        pair_of(pair, 0)
+        pair_of(pair, 1)
 
     @pl.loop(0, GROUPS)
     def _(slot):
@@ -327,7 +359,12 @@
         + [all_of(jax.ShapeDtypeStruct(stat_shape, F32))]
         + [HBM_SPEC] * 3,
         scratch_shapes=[pltpu.VMEM(s, BF) for s in shapes + shapes[2:]]
-        + [pltpu.VMEM(strips.shape, F32), pltpu.SemaphoreType.DMA((3,)), pltpu.SemaphoreType.DMA((1,))],
+        + [
+            pltpu.VMEM(strips.shape, F32),
+            pltpu.VMEM((GROUPS, GWIDTH, 2 * half), BF),
+            pltpu.SemaphoreType.DMA((3,)),
+            pltpu.SemaphoreType.DMA((1,)),
+        ],
         out_shape=[pltpu.HBM(o_shape, F32)]
         + [jax.ShapeDtypeStruct((GWIDTH, 2 * half), BF)] * GROUPS
         + [pltpu.HBM(stat_shape, F32)]

time: 278 us -> 271 us (0.975)
  Pallas kernels: 78.3 us -> 73.7 us
  transfers between devices with their start and end apart: 52 -> 52, of which waited for: 24 -> 23; matrix products, arithmetic and copies ran while one was open for 8% -> 8% of each run, Pallas kernels for 19% -> 18%
where the time goes in v5:
time: 271 us; the launch traced here: 269 us
  waiting for transfers between devices  84.7 us (31%)
  starting transfers between devices  78.9 us (29%)
  Pallas kernels  73.7 us (27%)
  other arithmetic  13.5 us (5%)
  local copies, waits for them, and re-layouts  12.7 us (5%)
  matrix products  4.25 us (2%)
    ppermute x12, waiting for transfers between devices, group_pieces(): came = {k: lax.ppermute(pieces[k], 'h', turn(sign * k)) for k in (2, 1, 3)}  40 us
    ppermute x12, waiting for transfers between devices, swap(): return lax.ppermute(x, axis, xor_perm(bit, lax.axis_size(axis)))  19 us
    ppermute x12, starting transfers between devices, group_pieces(): came = {k: lax.ppermute(pieces[k], 'h', turn(sign * k)) for k in (2, 1, 3)}  17.2 us
    pallas_call x1, Pallas kernels, attend_back(): pl.pallas_call(functools.partial(backward_kernel, half, blocks, members),...  15.2 us
    ppermute x12, starting transfers between devices, swap(): return lax.ppermute(x, axis, xor_perm(bit, lax.axis_size(axis)))  14 us
    pallas_call x2, Pallas kernels, weight_terms(): pl.pallas_call(functools.partial(weight_kernel, len(rows), members, side)...  12.2 us
    pallas_call x1, Pallas kernels, expert(): pl.pallas_call(functools.partial(expert_kernel, groups, n_fsdp), grid_spe...  11.9 us
    pallas_call x1, Pallas kernels, attend(): pl.pallas_call(functools.partial(forward_kernel, half, blocks, len(kvs)),...  11.8 us
  transfers between devices with their start and end apart: 52, of which 23 were waited for; matrix products, arithmetic and copies ran while one was open for 8% of the time, Pallas kernels for 18%

profile of v5, /device:TPU:11, one launch (start us, length us, event | category | flops | bytes accessed | tf_op | source)
XLA Modules:
  0.0 269.1 jit_solution(15182044040217853475)
XLA Ops:
  3.0 2.3 collective-permute-start.4
  16.7 3.3 %strips.1.refs_4_.refs_5_ = f32[2304,192]{1,0:T(8,128)} custom-call(f32[3,2304]{1,0:T(4,128)} %convolution_multiply_fusion.g_ref), custom_call_target="tpu_custom_call" | custom-call | flops 100000 | bytes 10000 | tf_op jit(solution)/shard_map/strips/pallas_call | solution.py:73
  20.1 3.7 %collective-permute-done.3 = bf16[136,768]{1,0:T(8,128)(2,1)S(1)} collective-permute-done((bf16[136,768]{1,0:T(8,128)(2,1)}, bf16[136,768]{1,0:T(8,128)(2,1)S(1)}, u32[]{:S(2)}, u32[]{:S(2)}) %collective-permute-start.3) | collective-permute-done | bytes 208928 | tf_op jit(solution)/shard_map/ppermute | solution.py:809
  26.7 5.5 %all-to-all-start = ((bf16[8,40,768]{2,1,0:T(8,128)(2,1)}), bf16[8,40,768]{2,1,0:T(8,128)(2,1)S(1)}, u32[]{:S(2)}, u32[]{:S(2)}) async-start(bf16[8,40,768]{2,1,0:T(8,128)(2,1)} %bitcast.23), calls=%async_computation | async-start | bytes 983040 | tf_op jit(solution)/shard_map/all_to_all | solution.py:933
  35.4 6.9 %collective-permute-done.7.refs_2_ = bf16[4,136,384]{2,1,0:T(8,128)(2,1)S(1)} collective-permute-done((bf16[4,136,384]{2,1,0:T(8,128)(2,1)S(1)}, bf16[4,136,384]{2,1,0:T(8,128)(2,1)S(1)}, u32[]{:S(2)}, u32[]{:S(2)}) %collective-permute-start.7) | collective-permute-done | bytes 417824 | tf_op jit(solution)/shard_map/ppermute | solution.py:818
  42.3 2.0 collective-permute-start.8
  45.7 11.8 %attend.1 = (f32[8,192,64]{2,1,0:T(8,128)}, bf16[192,128]{1,0:T(8,128)(2,1)S(1)}, bf16[192,128]{1,0:T(8,128)(2,1)S(1)}, bf16[192,128]{1,0:T(8,128)(2,1)S(1)}, bf...) custom-call(s32[2]{0:T(128)S(1)} %pad_add_fusion.pos, ...), custom_call_target="tpu_custom_call" | custom-call | flops 100000 | bytes 10000 | tf_op jit(solution)/shard_map/attend/pallas_call | solution.py:354
  57.5 2.2 collective-permute-start.10
  61.1 2.9 %maximum_select_fusion = bf16[2,384,768]{2,1,0:T(8,128)(2,1)} fusion(bf16[1,384,768]{2,1,0:T(8,128)(2,1)} %bitcast.7, bf16[1,384,768]{2,1,0:T(8,128)(2,1)} %bitcast.6, pred[]{:T(512)S(6)} %eq.106), kind=kLoop, calls=%fused_computation.8 | loop fusion | flops 1769472 | bytes 2359297 | tf_op jit(solution)/shard_map/jit(_where)/select_n | solution.py:840
  64.1 2.9 %router.1 = (bf16[40,896]{1,0:T(8,128)(2,1)S(1)}, bf16[40,896]{1,0:T(8,128)(2,1)S(1)}, bf16[40,896]{1,0:T(8,128)(2,1)S(1)}, bf16[40,896]{1,0:T(8,128)(2,1)S(1)},...) custom-call(s32[2]{0:T(128)S(1)} %pad_add_fusion.pos, ...), custom_call_target="tpu_custom_call" | custom-call | flops 100000 | bytes 10000 | tf_op jit(solution)/shard_map/router/pallas_call | solution.py:459
  72.3 2.0 collective-permute-start.16
  74.6 2.2 collective-permute-start.18
  76.9 4.2 %collective-permute-done.16.refs_5_ = bf16[40,896]{1,0:T(8,128)(2,1)S(1)} collective-permute-done((bf16[40,896]{1,0:T(8,128)(2,1)S(1)}, bf16[40,896]{1,0:T(8,128)(2,1)S(1)}, u32[]{:S(2)}, u32[]{:S(2)}) %collective-permute-start.16) | collective-permute-done | bytes 71712 | tf_op jit(solution)/shard_map/ppermute | solution.py:859
  81.0 3.1 %collective-permute-done.17.refs_6_ = bf16[40,896]{1,0:T(8,128)(2,1)S(1)} collective-permute-done((bf16[40,896]{1,0:T(8,128)(2,1)S(1)}, bf16[40,896]{1,0:T(8,128)(2,1)S(1)}, u32[]{:S(2)}, u32[]{:S(2)}) %collective-permute-start.17) | collective-permute-done | bytes 71712 | tf_op jit(solution)/shard_map/ppermute | solution.py:859
  85.8 11.9 %expert.1 = (bf16[4,40,768]{2,1,0:T(8,128)(2,1)}, bf16[4,40,768]{2,1,0:T(8,128)(2,1)}, bf16[8,40,896]{2,1,0:T(8,128)(2,1)}, bf16[2,320,3072]{2,1,0:T(8,128)(2,1)}, bf16[2,320,768]{2,1,0:T(8,128)(2,1)}) custom-call(s32[2]{0:T(128)S(1)} %pad_add_fusion.3.info, bf16[8,40,768]{2,1,0:T(8,128)(2,1)S(1)} %all-to-all-done.dy_ref, bf16[4,768,3072]{2,1,0:T(8,128)(2,1)} %up_ref.1, ...), custom_call_target="tpu_custom_call" | custom-call | flops 100000 | bytes 10000 | tf_op jit(solution)/shard_map/expert/pallas_call | solution.py:519
  98.3 4.5 %all-to-all-start.1 = ((bf16[8,40,896]{2,1,0:T(8,128)(2,1)}), bf16[8,40,896]{2,1,0:T(8,128)(2,1)S(1)}, u32[]{:S(2)}, u32[]{:S(2)}) async-start(bf16[8,40,896]{2,1,0:T(8,128)(2,1)} %get-tuple-element.136), calls=%async_computation.1 | async-start | bytes 1146880 | tf_op jit(solution)/shard_map/all_to_all | solution.py:933
  103.6 2.7 %collective-permute-done.19.refs_1_ = bf16[2,320,768]{2,1,0:T(8,128)(2,1)S(1)} collective-permute-done((bf16[2,320,768]{2,1,0:T(8,128)(2,1)}, bf16[2,320,768]{2,1,0:T(8,128)(2,1)S(1)}, u32[]{:S(2)}, u32[]{:S(2)}) %collective-permute-start.19) | collective-permute-done | bytes 983072 | tf_op jit(solution)/shard_map/ppermute | solution.py:828
  106.3 6.1 %weight_terms.3 = (bf16[192,3072]{1,0:T(8,128)(2,1)}, bf16[192,3072]{1,0:T(8,128)(2,1)}) custom-call(s32[2]{0:T(128)S(1)} %pad_add_fusion.pos, bf16[2,320,768]{2,1,0:T(8,128)(2,1)S(1)} %copy-done.1, bf16[2,320,768]{2,1,0:T(8,128)(2,1)S(1)} %collective-permute-done.19.refs_1_, bf16[2,320,3072]{2,1,0:T(8,128)(2,1)} %get-tuple-element.138.refs_2_, ...), custom_call_target="tpu_custom_call" | custom-call | flops 100000 | bytes 10000 | tf_op jit(solution)/shard_map/weight_terms/pallas_call | solution.py:572
  112.4 6.1 %weight_terms.2 = (bf16[192,3072]{1,0:T(8,128)(2,1)}, bf16[192,3072]{1,0:T(8,128)(2,1)}) custom-call(s32[2]{0:T(128)S(1)} %pad_add_fusion.pos, bf16[2,320,768]{2,1,0:T(8,128)(2,1)S(1)} %copy-done.1, bf16[2,320,768]{2,1,0:T(8,128)(2,1)S(1)} %collective-permute-done.19.refs_1_, bf16[2,320,3072]{2,1,0:T(8,128)(2,1)} %get-tuple-element.138.refs_2_, ...), custom_call_target="tpu_custom_call" | custom-call | flops 100000 | bytes 10000 | tf_op jit(solution)/shard_map/weight_terms/pallas_call | solution.py:572
  118.5 5.1 %turn_back.1 = (bf16[192,128]{1,0:T(8,128)(2,1)S(1)}, bf16[192,128]{1,0:T(8,128)(2,1)S(1)}, bf16[192,128]{1,0:T(8,128)(2,1)S(1)}, bf16[192,128]{1,0:T(8,128)(2,1...) custom-call(s32[3]{0:T(128)S(1)} %pad_add_fusion.2.info, ...), custom_call_target="tpu_custom_call" | custom-call | flops 100000 | bytes 10000 | tf_op jit(solution)/shard_map/turn_back/pallas_call | solution.py:694
  124.0 2.0 collective-permute-start.29
  133.8 2.3 collective-permute-done.24.refs_3_
  136.1 15.2 %attend_back.1 = (bf16[512,192]{1,0:T(8,128)(2,1)S(1)}, bf16[4,128,384]{2,1,0:T(8,128)(2,1)S(1)}, bf16[4,128,384]{2,1,0:T(8,128)(2,1)S(1)}, bf16[4,128,384]{2,1,...) custom-call(s32[2]{0:T(128)S(1)} %pad_add_fusion.pos, ...), custom_call_target="tpu_custom_call" | custom-call | flops 100000 | bytes 10000 | tf_op jit(solution)/shard_map/attend_back/pallas_call | solution.py:384
  151.3 1.8 collective-permute-start.28
  156.2 2.0 add_groups.2
  159.0 3.2 %collective-permute-start.31 = (bf16[272,768]{1,0:T(8,128)(2,1)S(1)}, bf16[272,768]{1,0:T(8,128)(2,1)S(1)}, u32[]{:S(2)}, u32[]{:S(2)}) collective-permute-start(bf16[272,768]{1,0:T(8,128)(2,1)S(1)} %get-tuple-element.173), channel_id=1, source_target_pairs={{0,16},{8,24},{16,0},{24,8},{1,17},{9,25},{17,1},{25,9},{2,18},{10... | collective-permute-start | bytes 1253384 | tf_op jit(solution)/shard_map/ppermute | solution.py:844
  162.1 2.6 collective-permute-start.30
  164.9 8.8 %collective-permute-done.30.came_ref = bf16[4,128,384]{2,1,0:T(8,128)(2,1)S(1)} collective-permute-done((bf16[4,128,384]{2,1,0:T(8,128)(2,1)S(1)}, bf16[4,128,384]{2,1,0:T(8,128)(2,1)S(1)}, u32[]{:S(2)}, u32[]{:S(2)}) %collective-permute-start.30) | collective-permute-done | bytes 393248 | tf_op jit(solution)/shard_map/ppermute | solution.py:828
  173.7 5.2 %collective-permute-done.31.refs_2_ = bf16[272,768]{1,0:T(8,128)(2,1)S(1)} collective-permute-done((bf16[272,768]{1,0:T(8,128)(2,1)S(1)}, bf16[272,768]{1,0:T(8,128)(2,1)S(1)}, u32[]{:S(2)}, u32[]{:S(2)}) %collective-permute-start.31) | collective-permute-done | bytes 417824 | tf_op jit(solution)/shard_map/ppermute | solution.py:844
  178.8 2.9 %input_back.1 = (f32[128,768]{1,0:T(8,128)S(1)}, bf16[128,768]{1,0:T(8,128)(2,1)S(1)}, bf16[128,768]{1,0:T(8,128)(2,1)S(1)}, bf16[128,768]{1,0:T(8,128)(2,1)S(1)...) custom-call(s32[2]{0:T(128)S(1)} %pad_add_fusion.1.info, ...), custom_call_target="tpu_custom_call" | custom-call | flops 100000 | bytes 10000 | tf_op jit(solution)/shard_map/input_back/pallas_call | solution.py:782
  183.1 3.0 %collective-permute-start.34 = (bf16[192,3072]{1,0:T(8,128)(2,1)}, bf16[192,3072]{1,0:T(8,128)(2,1)S(1)}, u32[]{:S(2)}, u32[]{:S(2)}) collective-permute-start(bf16[192,3072]{1,0:T(8,128)(2,1)} %get-tuple-element.186), channel_id=1, source_target_pairs={{0,4},{4,0},{1,5},{5,1},{2,6},{6,2},{3,7},{7,3},{8,12},{12,8},{9,1... | collective-permute-start | bytes 3538952 | tf_op jit(solution)/shard_map/ppermute | solution.py:828
  189.6 2.0 collective-permute-start.36
  191.6 3.2 %collective-permute-done.33 = bf16[320,384]{1,0:T(8,128)(2,1)S(1)} collective-permute-done((bf16[320,384]{1,0:T(8,128)(2,1)S(1)}, bf16[320,384]{1,0:T(8,128)(2,1)S(1)}, u32[]{:S(2)}, u32[]{:S(2)}) %collective-permute-start.33) | collective-permute-done | bytes 245792 | tf_op jit(solution)/shard_map/ppermute | solution.py:828
  195.1 6.3 %collective-permute-done.35.refs_1_ = bf16[272,768]{1,0:T(8,128)(2,1)S(1)} collective-permute-done((bf16[272,768]{1,0:T(8,128)(2,1)S(1)}, bf16[272,768]{1,0:T(8,128)(2,1)S(1)}, u32[]{:S(2)}, u32[]{:S(2)}) %collective-permute-start.35) | collective-permute-done | bytes 417824 | tf_op jit(solution)/shard_map/ppermute | solution.py:844
  201.4 9.2 %collective-permute-done.36.refs_3_ = bf16[272,768]{1,0:T(8,128)(2,1)S(1)} collective-permute-done((bf16[272,768]{1,0:T(8,128)(2,1)S(1)}, bf16[272,768]{1,0:T(8,128)(2,1)S(1)}, u32[]{:S(2)}, u32[]{:S(2)}) %collective-permute-start.36) | collective-permute-done | bytes 417824 | tf_op jit(solution)/shard_map/ppermute | solution.py:844
  210.6 2.1 collective-permute-done.34.b_ref
  212.7 2.8 %collective-permute-start.42 = (bf16[128,768]{1,0:T(8,128)(2,1)S(1)}, bf16[128,768]{1,0:T(8,128)(2,1)S(1)}, u32[]{:S(2)}, u32[]{:S(2)}) collective-permute-start(bf16[128,768]{1,0:T(8,128)(2,1)S(1)} %copy-done.8), channel_id=1, source_target_pairs={{0,24},{8,0},{16,8},{24,16},{1,25},{9,1},{17,9},{25,17},{2,26},{10... | collective-permute-start | bytes 589832 | tf_op jit(solution)/shard_map/ppermute | solution.py:1039
  217.1 1.9 add_groups.3
  219.0 3.5 %collective-permute-start.48 = (bf16[192,768]{1,0:T(8,128)(2,1)S(1)}, bf16[192,768]{1,0:T(8,128)(2,1)S(1)}, u32[]{:S(2)}, u32[]{:S(2)}) collective-permute-start(bf16[192,768]{1,0:T(8,128)(2,1)S(1)} %get-tuple-element.216), channel_id=1, source_target_pairs={{0,16},{8,24},{16,0},{24,8},{1,17},{9,25},{17,1},{25,9},{2,18},{10... | collective-permute-start | bytes 884744 | tf_op jit(solution)/shard_map/ppermute | solution.py:844
  223.2 3.4 %collective-permute-start.40 = (bf16[48,384]{1,0:T(8,128)(2,1)S(1)}, bf16[48,384]{1,0:T(8,128)(2,1)S(1)}, u32[]{:S(2)}, u32[]{:S(2)}) collective-permute-start(bf16[48,384]{1,0:T(8,128)(2,1)S(1)} %get-tuple-element.253), channel_id=1, source_target_pairs={{4,0},{10,2},{16,4},{22,6},{28,8},{2,10},{8,12},{14,14},{20,16},{2... | collective-permute-start | bytes 110600 | tf_op jit(solution)/shard_map/ppermute | solution.py:1064
  226.6 3.3 %collective-permute-start.39 = (bf16[48,384]{1,0:T(8,128)(2,1)S(1)}, bf16[48,384]{1,0:T(8,128)(2,1)S(1)}, u32[]{:S(2)}, u32[]{:S(2)}) collective-permute-start(bf16[48,384]{1,0:T(8,128)(2,1)S(1)} %get-tuple-element.254), channel_id=1, source_target_pairs={{2,0},{8,2},{14,4},{20,6},{26,8},{0,10},{6,12},{12,14},{18,16},{24... | collective-permute-start | bytes 110600 | tf_op jit(solution)/shard_map/ppermute | solution.py:1064
  229.9 2.1 collective-permute-start.38
  232.1 15.3 %collective-permute-done.48.refs_2_ = bf16[192,768]{1,0:T(8,128)(2,1)S(1)} collective-permute-done((bf16[192,768]{1,0:T(8,128)(2,1)S(1)}, bf16[192,768]{1,0:T(8,128)(2,1)S(1)}, u32[]{:S(2)}, u32[]{:S(2)}) %collective-permute-start.48) | collective-permute-done | bytes 294944 | tf_op jit(solution)/shard_map/ppermute | solution.py:844
  248.8 2.1 in_order.3
  250.9 3.1 %collective-permute-start.44 = (bf16[80,384]{1,0:T(8,128)(2,1)S(1)}, bf16[80,384]{1,0:T(8,128)(2,1)S(1)}, u32[]{:S(2)}, u32[]{:S(2)}) collective-permute-start(bf16[80,384]{1,0:T(8,128)(2,1)S(1)} %get-tuple-element.258), channel_id=1, source_target_pairs={{0,16},{8,24},{16,0},{24,8},{1,17},{9,25},{17,1},{25,9},{2,18},{10... | collective-permute-start | bytes 184328 | tf_op jit(solution)/shard_map/ppermute | solution.py:1055
  255.6 2.1 in_order.2
  260.5 2.1 collective-permute-done.45
  262.6 2.6 collective-permute-done.46
  (230 shorter events, 60.3 us)
Async XLA Ops:
  3.0 17.1 %collective-permute-start.4 = (bf16[136,768]{1,0:T(8,128)(2,1)}, bf16[136,768]{1,0:T(8,128)(2,1)S(1)}, u32[]{:S(2)}, u32[]{:S(2)}) collective-permute-start(bf16[136,768]{1,0:T(8,128)(2,1)} %get-tuple-element.249), channel_id=1, source_target_pairs={{0,16},{8,24},{16,0},{24,8},{1,17},{9,25},{17,1},{25,9},{2,18},{10... | collective-permute-start | bytes 626696 | tf_op jit(solution)/shard_map/ppermute | solution.py:809
  5.3 18.5 %collective-permute-start.3 = (bf16[136,768]{1,0:T(8,128)(2,1)}, bf16[136,768]{1,0:T(8,128)(2,1)S(1)}, u32[]{:S(2)}, u32[]{:S(2)}) collective-permute-start(bf16[136,768]{1,0:T(8,128)(2,1)} %get-tuple-element.249), channel_id=1, source_target_pairs={{0,8},{8,16},{16,24},{24,0},{1,9},{9,17},{17,25},{25,1},{2,10},{10... | collective-permute-start | bytes 626696 | tf_op jit(solution)/shard_map/ppermute | solution.py:809
  5.3 18.5 %collective-permute-start.5 = (bf16[136,768]{1,0:T(8,128)(2,1)}, bf16[136,768]{1,0:T(8,128)(2,1)}, u32[]{:S(2)}, u32[]{:S(2)}) collective-permute-start(bf16[136,768]{1,0:T(8,128)(2,1)} %get-tuple-element.249), channel_id=1, source_target_pairs={{0,24},{8,0},{16,8},{24,16},{1,25},{9,1},{17,9},{25,17},{2,26},{10... | collective-permute-start | bytes 626696 | tf_op jit(solution)/shard_map/ppermute | solution.py:809
  9.8 5.7 %collective-permute-start.2 = (bf16[16,384]{1,0:T(8,128)(2,1)S(1)}, bf16[16,384]{1,0:T(8,128)(2,1)S(1)}, u32[]{:S(2)}, u32[]{:S(2)}) collective-permute-start(bf16[16,384]{1,0:T(8,128)(2,1)S(1)} %concatenate.53), channel_id=1, source_target_pairs={{0,1},{1,0},{2,3},{3,2},{4,5},{5,4},{6,7},{7,6},{8,9},{9,8},{10,11... | collective-permute-start | bytes 36872 | tf_op jit(solution)/shard_map/ppermute | solution.py:839
  11.7 13.7 %collective-permute-start = (bf16[384,576]{1,0:T(8,128)(2,1)S(1)}, bf16[384,576]{1,0:T(8,128)(2,1)S(1)}, u32[]{:S(2)}, u32[]{:S(2)}) collective-permute-start(bf16[384,576]{1,0:T(8,128)(2,1)S(1)} %pad_maximum_fusion.2), channel_id=1, source_target_pairs={{0,1},{1,0},{2,3},{3,2},{4,5},{5,4},{6,7},{7,6},{8,9},{9,8},{10,11... | collective-permute-start | bytes 1327112 | tf_op jit(solution)/shard_map/ppermute | solution.py:839
  26.7 33.0 %all-to-all-start = ((bf16[8,40,768]{2,1,0:T(8,128)(2,1)}), bf16[8,40,768]{2,1,0:T(8,128)(2,1)S(1)}, u32[]{:S(2)}, u32[]{:S(2)}) async-start(bf16[8,40,768]{2,1,0:T(8,128)(2,1)} %bitcast.23), calls=%async_computation | async-start | bytes 983040 | tf_op jit(solution)/shard_map/all_to_all | solution.py:933
  32.2 10.2 %collective-permute-start.7 = (bf16[4,136,384]{2,1,0:T(8,128)(2,1)S(1)}, bf16[4,136,384]{2,1,0:T(8,128)(2,1)S(1)}, u32[]{:S(2)}, u32[]{:S(2)}) collective-permute-start(bf16[4,136,384]{2,1,0:T(8,128)(2,1)S(1)} %pad_maximum_fusion.4.refs_0_), channel_id=1, source_target_pairs={{0,4},{2,6},{4,0},{6,2},{1,5},{3,7},{5,1},{7,3},{8,12},{10,14},{12... | collective-permute-start | bytes 1253384 | tf_op jit(solution)/shard_map/ppermute | solution.py:818
  33.5 27.7 %collective-permute-start.1 = (bf16[384,768]{1,0:T(8,128)(2,1)}, bf16[384,768]{1,0:T(8,128)(2,1)}, u32[]{:S(2)}, u32[]{:S(2)}) collective-permute-start(bf16[384,768]{1,0:T(8,128)(2,1)} %param.19), channel_id=1, source_target_pairs={{0,1},{1,0},{2,3},{3,2},{4,5},{5,4},{6,7},{7,6},{8,9},{9,8},{10,11... | collective-permute-start | bytes 1769480 | tf_op jit(solution)/shard_map/ppermute | solution.py:839
  33.7 10.7 %collective-permute-start.6 = (bf16[4,136,384]{2,1,0:T(8,128)(2,1)S(1)}, bf16[4,136,384]{2,1,0:T(8,128)(2,1)S(1)}, u32[]{:S(2)}, u32[]{:S(2)}) collective-permute-start(bf16[4,136,384]{2,1,0:T(8,128)(2,1)S(1)} %pad_maximum_fusion.4.refs_0_), channel_id=1, source_target_pairs={{0,2},{2,0},{4,6},{6,4},{1,3},{3,1},{5,7},{7,5},{8,10},{10,8},{12,... | collective-permute-start | bytes 1253384 | tf_op jit(solution)/shard_map/ppermute | solution.py:818
  42.3 3.3 %collective-permute-start.8 = (bf16[4,136,384]{2,1,0:T(8,128)(2,1)S(1)}, bf16[4,136,384]{2,1,0:T(8,128)(2,1)S(1)}, u32[]{:S(2)}, u32[]{:S(2)}) collective-permute-start(bf16[4,136,384]{2,1,0:T(8,128)(2,1)S(1)} %collective-permute-done.7.refs_2_), channel_id=1, source_target_pairs={{0,2},{2,0},{4,6},{6,4},{1,3},{3,1},{5,7},{7,5},{8,10},{10,8},{12,... | collective-permute-start | bytes 1253384 | tf_op jit(solution)/shard_map/ppermute | solution.py:818
  57.5 6.5 %collective-permute-start.10 = (bf16[192,128]{1,0:T(8,128)(2,1)S(1)}, bf16[192,128]{1,0:T(8,128)(2,1)S(1)}, u32[]{:S(2)}, u32[]{:S(2)}) collective-permute-start(bf16[192,128]{1,0:T(8,128)(2,1)S(1)} %get-tuple-element.121), channel_id=1, source_target_pairs={{0,16},{8,24},{16,0},{24,8},{1,17},{9,25},{17,1},{25,9},{2,18},{10... | collective-permute-start | bytes 147464 | tf_op jit(solution)/shard_map/ppermute | solution.py:844
  59.7 4.4 %collective-permute-start.11 = (bf16[192,128]{1,0:T(8,128)(2,1)S(1)}, bf16[192,128]{1,0:T(8,128)(2,1)S(1)}, u32[]{:S(2)}, u32[]{:S(2)}) collective-permute-start(bf16[192,128]{1,0:T(8,128)(2,1)S(1)} %get-tuple-element.122), channel_id=1, source_target_pairs={{0,8},{8,16},{16,24},{24,0},{1,9},{9,17},{17,25},{25,1},{2,10},{10... | collective-permute-start | bytes 147464 | tf_op jit(solution)/shard_map/ppermute | solution.py:844
  59.7 4.4 %collective-permute-start.9 = (bf16[192,128]{1,0:T(8,128)(2,1)S(1)}, bf16[192,128]{1,0:T(8,128)(2,1)S(1)}, u32[]{:S(2)}, u32[]{:S(2)}) collective-permute-start(bf16[192,128]{1,0:T(8,128)(2,1)S(1)} %get-tuple-element.120), channel_id=1, source_target_pairs={{0,24},{8,0},{16,8},{24,16},{1,25},{9,1},{17,9},{25,17},{2,26},{10... | collective-permute-start | bytes 147464 | tf_op jit(solution)/shard_map/ppermute | solution.py:844
  67.0 7.3 %collective-permute-start.12 = (bf16[40,896]{1,0:T(8,128)(2,1)S(1)}, bf16[40,896]{1,0:T(8,128)(2,1)S(1)}, u32[]{:S(2)}, u32[]{:S(2)}) collective-permute-start(bf16[40,896]{1,0:T(8,128)(2,1)S(1)} %get-tuple-element.129), channel_id=1, source_target_pairs={{0,1},{1,0},{8,9},{9,8},{16,17},{17,16},{24,25},{25,24},{2,3},{3,2... | collective-permute-start | bytes 215048 | tf_op jit(solution)/shard_map/ppermute | solution.py:859
  68.0 6.5 %collective-permute-start.13 = (bf16[40,896]{1,0:T(8,128)(2,1)S(1)}, bf16[40,896]{1,0:T(8,128)(2,1)S(1)}, u32[]{:S(2)}, u32[]{:S(2)}) collective-permute-start(bf16[40,896]{1,0:T(8,128)(2,1)S(1)} %get-tuple-element.130), channel_id=1, source_target_pairs={{0,8},{1,9},{8,16},{9,17},{16,24},{17,25},{24,0},{25,1},{2,10},{3,... | collective-permute-start | bytes 215048 | tf_op jit(solution)/shard_map/ppermute | solution.py:859
  69.5 7.4 %collective-permute-start.14 = (bf16[40,896]{1,0:T(8,128)(2,1)S(1)}, bf16[40,896]{1,0:T(8,128)(2,1)S(1)}, u32[]{:S(2)}, u32[]{:S(2)}) collective-permute-start(bf16[40,896]{1,0:T(8,128)(2,1)S(1)} %get-tuple-element.131), channel_id=1, source_target_pairs={{0,9},{1,8},{8,17},{9,16},{16,25},{17,24},{24,1},{25,0},{2,11},{3,... | collective-permute-start | bytes 215048 | tf_op jit(solution)/shard_map/ppermute | solution.py:859
  71.1 5.7 %collective-permute-start.15 = (bf16[40,896]{1,0:T(8,128)(2,1)S(1)}, bf16[40,896]{1,0:T(8,128)(2,1)S(1)}, u32[]{:S(2)}, u32[]{:S(2)}) collective-permute-start(bf16[40,896]{1,0:T(8,128)(2,1)S(1)} %get-tuple-element.132), channel_id=1, source_target_pairs={{0,16},{1,17},{8,24},{9,25},{16,0},{17,1},{24,8},{25,9},{2,18},{3,... | collective-permute-start | bytes 215048 | tf_op jit(solution)/shard_map/ppermute | solution.py:859
  72.3 8.7 %collective-permute-start.16 = (bf16[40,896]{1,0:T(8,128)(2,1)S(1)}, bf16[40,896]{1,0:T(8,128)(2,1)S(1)}, u32[]{:S(2)}, u32[]{:S(2)}) collective-permute-start(bf16[40,896]{1,0:T(8,128)(2,1)S(1)} %get-tuple-element.133), channel_id=1, source_target_pairs={{0,17},{1,16},{8,25},{9,24},{16,1},{17,0},{24,9},{25,8},{2,19},{3,... | collective-permute-start | bytes 215048 | tf_op jit(solution)/shard_map/ppermute | solution.py:859
  74.3 9.9 %collective-permute-start.17 = (bf16[40,896]{1,0:T(8,128)(2,1)S(1)}, bf16[40,896]{1,0:T(8,128)(2,1)S(1)}, u32[]{:S(2)}, u32[]{:S(2)}) collective-permute-start(bf16[40,896]{1,0:T(8,128)(2,1)S(1)} %get-tuple-element.134), channel_id=1, source_target_pairs={{0,24},{1,25},{8,0},{9,1},{16,8},{17,9},{24,16},{25,17},{2,26},{3,... | collective-permute-start | bytes 215048 | tf_op jit(solution)/shard_map/ppermute | solution.py:859
  74.6 11.2 %collective-permute-start.18 = (bf16[40,896]{1,0:T(8,128)(2,1)S(1)}, bf16[40,896]{1,0:T(8,128)(2,1)S(1)}, u32[]{:S(2)}, u32[]{:S(2)}) collective-permute-start(bf16[40,896]{1,0:T(8,128)(2,1)S(1)} %get-tuple-element.135), channel_id=1, source_target_pairs={{0,25},{1,24},{8,1},{9,0},{16,9},{17,8},{24,17},{25,16},{2,27},{3,... | collective-permute-start | bytes 215048 | tf_op jit(solution)/shard_map/ppermute | solution.py:859
  97.7 8.6 %collective-permute-start.20 = (bf16[2,320,3072]{2,1,0:T(8,128)(2,1)}, bf16[2,320,3072]{2,1,0:T(8,128)(2,1)}, u32[]{:S(2)}, u32[]{:S(2)}) collective-permute-start(bf16[2,320,3072]{2,1,0:T(8,128)(2,1)} %get-tuple-element.138.refs_2_), channel_id=1, source_target_pairs={{0,2},{2,0},{1,3},{3,1},{4,6},{6,4},{5,7},{7,5},{8,10},{10,8},{9,1... | collective-permute-start | bytes 11796488 | tf_op jit(solution)/shard_map/ppermute | solution.py:828
  98.3 20.2 %all-to-all-start.1 = ((bf16[8,40,896]{2,1,0:T(8,128)(2,1)}), bf16[8,40,896]{2,1,0:T(8,128)(2,1)S(1)}, u32[]{:S(2)}, u32[]{:S(2)}) async-start(bf16[8,40,896]{2,1,0:T(8,128)(2,1)} %get-tuple-element.136), calls=%async_computation.1 | async-start | bytes 1146880 | tf_op jit(solution)/shard_map/all_to_all | solution.py:933
  102.8 3.5 %collective-permute-start.19 = (bf16[2,320,768]{2,1,0:T(8,128)(2,1)}, bf16[2,320,768]{2,1,0:T(8,128)(2,1)S(1)}, u32[]{:S(2)}, u32[]{:S(2)}) collective-permute-start(bf16[2,320,768]{2,1,0:T(8,128)(2,1)} %get-tuple-element.137.refs_0_), channel_id=1, source_target_pairs={{0,2},{2,0},{1,3},{3,1},{4,6},{6,4},{5,7},{7,5},{8,10},{10,8},{9,1... | collective-permute-start | bytes 2949128 | tf_op jit(solution)/shard_map/ppermute | solution.py:828
  124.0 31.1 %collective-permute-start.29 = (bf16[192,3072]{1,0:T(8,128)(2,1)S(1)}, bf16[192,3072]{1,0:T(8,128)(2,1)S(1)}, u32[]{:S(2)}, u32[]{:S(2)}) collective-permute-start(bf16[192,3072]{1,0:T(8,128)(2,1)S(1)} %copy-done.26), channel_id=1, source_target_pairs={{0,4},{4,0},{1,5},{5,1},{2,6},{6,2},{3,7},{7,3},{8,12},{12,8},{9,1... | collective-permute-start | bytes 3538952 | tf_op jit(solution)/shard_map/ppermute | solution.py:828
  127.3 25.7 %collective-permute-start.25 = (bf16[8,48,384]{2,1,0:T(8,128)(2,1)S(1)}, bf16[8,48,384]{2,1,0:T(8,128)(2,1)S(1)}, u32[]{:S(2)}, u32[]{:S(2)}) collective-permute-start(bf16[8,48,384]{2,1,0:T(8,128)(2,1)S(1)} %fusion.5), channel_id=1, source_target_pairs={{0,1},{1,0},{2,3},{3,2},{4,5},{5,4},{6,7},{7,6},{8,9},{9,8},{10,11... | collective-permute-start | bytes 884744 | tf_op jit(solution)/shard_map/ppermute | solution.py:828
  128.3 24.7 %collective-permute-start.26 = (bf16[4,40,768]{2,1,0:T(8,128)(2,1)S(1)}, bf16[4,40,768]{2,1,0:T(8,128)(2,1)S(1)}, u32[]{:S(2)}, u32[]{:S(2)}) collective-permute-start(bf16[4,40,768]{2,1,0:T(8,128)(2,1)S(1)} %copy-done.27), channel_id=1, source_target_pairs={{0,1},{1,0},{2,3},{3,2},{4,5},{5,4},{6,7},{7,6},{8,9},{9,8},{10,11... | collective-permute-start | bytes 737288 | tf_op jit(solution)/shard_map/ppermute | solution.py:973
  129.6 4.3 %collective-permute-start.23 = (bf16[192,128]{1,0:T(8,128)(2,1)S(1)}, bf16[192,128]{1,0:T(8,128)(2,1)S(1)}, u32[]{:S(2)}, u32[]{:S(2)}) collective-permute-start(bf16[192,128]{1,0:T(8,128)(2,1)S(1)} %get-tuple-element.149), channel_id=1, source_target_pairs={{0,16},{8,24},{16,0},{24,8},{1,17},{9,25},{17,1},{25,9},{2,18},{10... | collective-permute-start | bytes 147464 | tf_op jit(solution)/shard_map/ppermute | solution.py:844
  132.1 4.0 %collective-permute-start.24 = (bf16[192,128]{1,0:T(8,128)(2,1)S(1)}, bf16[192,128]{1,0:T(8,128)(2,1)S(1)}, u32[]{:S(2)}, u32[]{:S(2)}) collective-permute-start(bf16[192,128]{1,0:T(8,128)(2,1)S(1)} %get-tuple-element.150), channel_id=1, source_target_pairs={{0,24},{8,0},{16,8},{24,16},{1,25},{9,1},{17,9},{25,17},{2,26},{10... | collective-permute-start | bytes 147464 | tf_op jit(solution)/shard_map/ppermute | solution.py:844
  159.0 19.9 %collective-permute-start.31 = (bf16[272,768]{1,0:T(8,128)(2,1)S(1)}, bf16[272,768]{1,0:T(8,128)(2,1)S(1)}, u32[]{:S(2)}, u32[]{:S(2)}) collective-permute-start(bf16[272,768]{1,0:T(8,128)(2,1)S(1)} %get-tuple-element.173), channel_id=1, source_target_pairs={{0,16},{8,24},{16,0},{24,8},{1,17},{9,25},{17,1},{25,9},{2,18},{10... | collective-permute-start | bytes 1253384 | tf_op jit(solution)/shard_map/ppermute | solution.py:844
  162.1 11.5 %collective-permute-start.30 = (bf16[4,128,384]{2,1,0:T(8,128)(2,1)S(1)}, bf16[4,128,384]{2,1,0:T(8,128)(2,1)S(1)}, u32[]{:S(2)}, u32[]{:S(2)}) collective-permute-start(bf16[4,128,384]{2,1,0:T(8,128)(2,1)S(1)} %get-tuple-element.168), channel_id=1, source_target_pairs={{0,4},{4,0},{1,5},{5,1},{2,6},{6,2},{3,7},{7,3},{8,12},{12,8},{9,1... | collective-permute-start | bytes 1179656 | tf_op jit(solution)/shard_map/ppermute | solution.py:828
  182.5 3.7 %collective-permute-start.32 = (bf16[320,768]{1,0:T(8,128)(2,1)S(1)}, bf16[320,768]{1,0:T(8,128)(2,1)}, u32[]{:S(2)}, u32[]{:S(2)}) collective-permute-start(bf16[320,768]{1,0:T(8,128)(2,1)S(1)} %get-tuple-element.181), channel_id=1, source_target_pairs={{0,2},{2,0},{1,3},{3,1},{4,6},{6,4},{5,7},{7,5},{8,10},{10,8},{9,1... | collective-permute-start | bytes 1474568 | tf_op jit(solution)/shard_map/ppermute | solution.py:828
  183.1 29.5 %collective-permute-start.34 = (bf16[192,3072]{1,0:T(8,128)(2,1)}, bf16[192,3072]{1,0:T(8,128)(2,1)S(1)}, u32[]{:S(2)}, u32[]{:S(2)}) collective-permute-start(bf16[192,3072]{1,0:T(8,128)(2,1)} %get-tuple-element.186), channel_id=1, source_target_pairs={{0,4},{4,0},{1,5},{5,1},{2,6},{6,2},{3,7},{7,3},{8,12},{12,8},{9,1... | collective-permute-start | bytes 3538952 | tf_op jit(solution)/shard_map/ppermute | solution.py:828
  187.5 7.3 %collective-permute-start.33 = (bf16[320,384]{1,0:T(8,128)(2,1)S(1)}, bf16[320,384]{1,0:T(8,128)(2,1)S(1)}, u32[]{:S(2)}, u32[]{:S(2)}) collective-permute-start(bf16[320,384]{1,0:T(8,128)(2,1)S(1)} %pad_maximum_fusion.6), channel_id=1, source_target_pairs={{0,1},{1,0},{2,3},{3,2},{4,5},{5,4},{6,7},{7,6},{8,9},{9,8},{10,11... | collective-permute-start | bytes 737288 | tf_op jit(solution)/shard_map/ppermute | solution.py:828
  188.8 12.6 %collective-permute-start.35 = (bf16[272,768]{1,0:T(8,128)(2,1)S(1)}, bf16[272,768]{1,0:T(8,128)(2,1)S(1)}, u32[]{:S(2)}, u32[]{:S(2)}) collective-permute-start(bf16[272,768]{1,0:T(8,128)(2,1)S(1)} %copy-done.6), channel_id=1, source_target_pairs={{0,8},{8,16},{16,24},{24,0},{1,9},{9,17},{17,25},{25,1},{2,10},{10... | collective-permute-start | bytes 1253384 | tf_op jit(solution)/shard_map/ppermute | solution.py:844
  189.6 20.9 %collective-permute-start.36 = (bf16[272,768]{1,0:T(8,128)(2,1)S(1)}, bf16[272,768]{1,0:T(8,128)(2,1)S(1)}, u32[]{:S(2)}, u32[]{:S(2)}) collective-permute-start(bf16[272,768]{1,0:T(8,128)(2,1)S(1)} %get-tuple-element.190), channel_id=1, source_target_pairs={{0,24},{8,0},{16,8},{24,16},{1,25},{9,1},{17,9},{25,17},{2,26},{10... | collective-permute-start | bytes 1253384 | tf_op jit(solution)/shard_map/ppermute | solution.py:844
  212.7 9.9 %collective-permute-start.42 = (bf16[128,768]{1,0:T(8,128)(2,1)S(1)}, bf16[128,768]{1,0:T(8,128)(2,1)S(1)}, u32[]{:S(2)}, u32[]{:S(2)}) collective-permute-start(bf16[128,768]{1,0:T(8,128)(2,1)S(1)} %copy-done.8), channel_id=1, source_target_pairs={{0,24},{8,0},{16,8},{24,16},{1,25},{9,1},{17,9},{25,17},{2,26},{10... | collective-permute-start | bytes 589832 | tf_op jit(solution)/shard_map/ppermute | solution.py:1039
  215.6 7.5 %collective-permute-start.37 = (bf16[368,384]{1,0:T(8,128)(2,1)S(1)}, bf16[368,384]{1,0:T(8,128)(2,1)S(1)}, u32[]{:S(2)}, u32[]{:S(2)}) collective-permute-start(bf16[368,384]{1,0:T(8,128)(2,1)S(1)} %pad_maximum_fusion.5), channel_id=1, source_target_pairs={{0,4},{4,0},{1,5},{5,1},{2,6},{6,2},{3,7},{7,3},{8,12},{12,8},{9,1... | collective-permute-start | bytes 847880 | tf_op jit(solution)/shard_map/ppermute | solution.py:828
  219.0 11.0 %collective-permute-start.47 = (bf16[192,768]{1,0:T(8,128)(2,1)S(1)}, bf16[192,768]{1,0:T(8,128)(2,1)S(1)}, u32[]{:S(2)}, u32[]{:S(2)}) collective-permute-start(bf16[192,768]{1,0:T(8,128)(2,1)S(1)} %get-tuple-element.215), channel_id=1, source_target_pairs={{0,8},{8,16},{16,24},{24,0},{1,9},{9,17},{17,25},{25,1},{2,10},{10... | collective-permute-start | bytes 884744 | tf_op jit(solution)/shard_map/ppermute | solution.py:844
  219.0 28.3 %collective-permute-start.48 = (bf16[192,768]{1,0:T(8,128)(2,1)S(1)}, bf16[192,768]{1,0:T(8,128)(2,1)S(1)}, u32[]{:S(2)}, u32[]{:S(2)}) collective-permute-start(bf16[192,768]{1,0:T(8,128)(2,1)S(1)} %get-tuple-element.216), channel_id=1, source_target_pairs={{0,16},{8,24},{16,0},{24,8},{1,17},{9,25},{17,1},{25,9},{2,18},{10... | collective-permute-start | bytes 884744 | tf_op jit(solution)/shard_map/ppermute | solution.py:844
  222.6 25.6 %collective-permute-start.49 = (bf16[192,768]{1,0:T(8,128)(2,1)S(1)}, bf16[192,768]{1,0:T(8,128)(2,1)S(1)}, u32[]{:S(2)}, u32[]{:S(2)}) collective-permute-start(bf16[192,768]{1,0:T(8,128)(2,1)S(1)} %get-tuple-element.217), channel_id=1, source_target_pairs={{0,24},{8,0},{16,8},{24,16},{1,25},{9,1},{17,9},{25,17},{2,26},{10... | collective-permute-start | bytes 884744 | tf_op jit(solution)/shard_map/ppermute | solution.py:844
  223.2 27.7 %collective-permute-start.40 = (bf16[48,384]{1,0:T(8,128)(2,1)S(1)}, bf16[48,384]{1,0:T(8,128)(2,1)S(1)}, u32[]{:S(2)}, u32[]{:S(2)}) collective-permute-start(bf16[48,384]{1,0:T(8,128)(2,1)S(1)} %get-tuple-element.253), channel_id=1, source_target_pairs={{4,0},{10,2},{16,4},{22,6},{28,8},{2,10},{8,12},{14,14},{20,16},{2... | collective-permute-start | bytes 110600 | tf_op jit(solution)/shard_map/ppermute | solution.py:1064
  226.6 27.4 %collective-permute-start.39 = (bf16[48,384]{1,0:T(8,128)(2,1)S(1)}, bf16[48,384]{1,0:T(8,128)(2,1)S(1)}, u32[]{:S(2)}, u32[]{:S(2)}) collective-permute-start(bf16[48,384]{1,0:T(8,128)(2,1)S(1)} %get-tuple-element.254), channel_id=1, source_target_pairs={{2,0},{8,2},{14,4},{20,6},{26,8},{0,10},{6,12},{12,14},{18,16},{24... | collective-permute-start | bytes 110600 | tf_op jit(solution)/shard_map/ppermute | solution.py:1064
  229.9 25.0 %collective-permute-start.38 = (bf16[48,384]{1,0:T(8,128)(2,1)S(1)}, bf16[48,384]{1,0:T(8,128)(2,1)S(1)}, u32[]{:S(2)}, u32[]{:S(2)}) collective-permute-start(bf16[48,384]{1,0:T(8,128)(2,1)S(1)} %get-tuple-element.255), channel_id=1, source_target_pairs={{0,0},{6,2},{12,4},{18,6},{24,8},{30,10},{4,12},{10,14},{16,16},{2... | collective-permute-start | bytes 110600 | tf_op jit(solution)/shard_map/ppermute | solution.py:1064
  247.3 20.6 %collective-permute-start.41 = (bf16[128,768]{1,0:T(8,128)(2,1)S(1)}, bf16[128,768]{1,0:T(8,128)(2,1)S(1)}, u32[]{:S(2)}, u32[]{:S(2)}) collective-permute-start(bf16[128,768]{1,0:T(8,128)(2,1)S(1)} %get-tuple-element.206), channel_id=1, source_target_pairs={{0,8},{8,16},{16,24},{24,0},{1,9},{9,17},{17,25},{25,1},{2,10},{10... | collective-permute-start | bytes 589832 | tf_op jit(solution)/shard_map/ppermute | solution.py:1040
  248.2 19.8 %collective-permute-start.43 = (bf16[128,768]{1,0:T(8,128)(2,1)S(1)}, bf16[128,768]{1,0:T(8,128)(2,1)S(1)}, u32[]{:S(2)}, u32[]{:S(2)}) collective-permute-start(bf16[128,768]{1,0:T(8,128)(2,1)S(1)} %add_convert_fusion), channel_id=1, source_target_pairs={{0,24},{8,0},{16,8},{24,16},{1,25},{9,1},{17,9},{25,17},{2,26},{10... | collective-permute-start | bytes 589832 | tf_op jit(solution)/shard_map/ppermute | solution.py:1042
  250.9 9.6 %collective-permute-start.44 = (bf16[80,384]{1,0:T(8,128)(2,1)S(1)}, bf16[80,384]{1,0:T(8,128)(2,1)S(1)}, u32[]{:S(2)}, u32[]{:S(2)}) collective-permute-start(bf16[80,384]{1,0:T(8,128)(2,1)S(1)} %get-tuple-element.258), channel_id=1, source_target_pairs={{0,16},{8,24},{16,0},{24,8},{1,17},{9,25},{17,1},{25,9},{2,18},{10... | collective-permute-start | bytes 184328 | tf_op jit(solution)/shard_map/ppermute | solution.py:1055
  254.0 8.6 %collective-permute-start.45 = (bf16[80,384]{1,0:T(8,128)(2,1)S(1)}, bf16[80,384]{1,0:T(8,128)(2,1)S(1)}, u32[]{:S(2)}, u32[]{:S(2)}) collective-permute-start(bf16[80,384]{1,0:T(8,128)(2,1)S(1)} %get-tuple-element.259), channel_id=1, source_target_pairs={{0,8},{8,16},{16,24},{24,0},{1,9},{9,17},{17,25},{25,1},{2,10},{10... | collective-permute-start | bytes 184328 | tf_op jit(solution)/shard_map/ppermute | solution.py:1055
  254.9 10.4 %collective-permute-start.46 = (bf16[80,384]{1,0:T(8,128)(2,1)S(1)}, bf16[80,384]{1,0:T(8,128)(2,1)S(1)}, u32[]{:S(2)}, u32[]{:S(2)}) collective-permute-start(bf16[80,384]{1,0:T(8,128)(2,1)S(1)} %get-tuple-element.260), channel_id=1, source_target_pairs={{0,24},{8,0},{16,8},{24,16},{1,25},{9,1},{17,9},{25,17},{2,26},{10... | collective-permute-start | bytes 184328 | tf_op jit(solution)/shard_map/ppermute | solution.py:1055
  (32 other events, 265.5 us)

commit v6 on v5

--- a/solution.py
+++ b/solution.py
@@ -994,7 +994,7 @@
     if staged:
         up_came = group_pieces(add_groups(terms[0][0], sends[0], width, outs), 1)
         sends.append(swap(together(terms[1][1], came)[0], "r", 1))
-        came, up_came[2] = together(came, up_came[2])
+        came, up_came[1] = together(came, up_came[1])
 
     own_back, back_1, back_2, back_3, term, sent, pack = input_back(
         jnp.stack([h, core]).astype(jnp.int32), members, BUCKETS // n_fsdp, dq, keep, came, ain, qkv_heads,
@@ -1035,7 +1035,8 @@
         pack = pack + pack_came
     term = term[0]
     if staged:
-        back_2, back_3, up_came = together(back_2, back_3, up_came)
+        back_2, up_came = together(back_2, up_came)
+        back_3, term = together(back_3, term)
     mid = lax.ppermute(back_2, "h", turn(-1))
     side = lax.ppermute(back_3, "h", turn(1)).astype(F32)
     mid = (back_1.astype(F32) + mid.astype(F32)).astype(BF)

time: 271 us -> 269 us (level)
  waiting for transfers between devices: 84.7 us -> 81.4 us
    ppermute x3, waiting for transfers between devices: 4.88 us -> 0.01 us  [per_device(): lax.ppermute(jnp.concatenate([piece.astype(BF), two_parts(pack)]), 'h', t...]
    ppermute x12, waiting for transfers between devices: 40 us -> 44.7 us  [group_pieces(): came = {k: lax.ppermute(pieces[k], 'h', turn(sign * k)) for k in (2, 1, 3)}]
    ppermute x12, waiting for transfers between devices: 19 us -> 16.1 us  [swap(): return lax.ppermute(x, axis, xor_perm(bit, lax.axis_size(axis)))]
  transfers between devices with their start and end apart: 52 -> 52, of which waited for: 23 -> 18; matrix products, arithmetic and copies ran while one was open for 8% -> 8% of each run, Pallas kernels for 18% -> 18%
where the time goes in v6:
time: 269 us; the launch traced here: 266 us
  waiting for transfers between devices  81.4 us (30%)
  starting transfers between devices  78.8 us (29%)
  Pallas kernels  73.7 us (27%)
  other arithmetic  13.5 us (5%)
  local copies, waits for them, and re-layouts  12.7 us (5%)
  matrix products  4.24 us (2%)
    ppermute x12, waiting for transfers between devices, group_pieces(): came = {k: lax.ppermute(pieces[k], 'h', turn(sign * k)) for k in (2, 1, 3)}  44.7 us
    ppermute x12, starting transfers between devices, swap(): return lax.ppermute(x, axis, xor_perm(bit, lax.axis_size(axis)))  16.6 us
    ppermute x12, waiting for transfers between devices, swap(): return lax.ppermute(x, axis, xor_perm(bit, lax.axis_size(axis)))  16.1 us
    ppermute x12, starting transfers between devices, group_pieces(): came = {k: lax.ppermute(pieces[k], 'h', turn(sign * k)) for k in (2, 1, 3)}  15.4 us
    pallas_call x1, Pallas kernels, attend_back(): pl.pallas_call(functools.partial(backward_kernel, half, blocks, members),...  15.2 us
    pallas_call x2, Pallas kernels, weight_terms(): pl.pallas_call(functools.partial(weight_kernel, len(rows), members, side)...  12.2 us
    pallas_call x1, Pallas kernels, expert(): pl.pallas_call(functools.partial(expert_kernel, groups, n_fsdp), grid_spe...  11.9 us
    pallas_call x1, Pallas kernels, attend(): pl.pallas_call(functools.partial(forward_kernel, half, blocks, len(kvs)),...  11.8 us
  transfers between devices with their start and end apart: 52, of which 18 were waited for; matrix products, arithmetic and copies ran while one was open for 8% of the time, Pallas kernels for 18%

profile of v6, /device:TPU:11, one launch (start us, length us, event | category | flops | bytes accessed | tf_op | source)
XLA Modules:
  0.0 265.8 jit_solution(13542425227324930655)
XLA Ops:
  1.3 1.6 fusion.55
  3.0 2.3 collective-permute-start.4
  16.7 3.3 %strips.1.refs_4_.refs_5_ = f32[2304,192]{1,0:T(8,128)} custom-call(f32[3,2304]{1,0:T(4,128)} %convolution_multiply_fusion.g_ref), custom_call_target="tpu_custom_call" | custom-call | flops 100000 | bytes 10000 | tf_op jit(solution)/shard_map/strips/pallas_call | solution.py:73
  20.1 3.7 %collective-permute-done.3 = bf16[136,768]{1,0:T(8,128)(2,1)S(1)} collective-permute-done((bf16[136,768]{1,0:T(8,128)(2,1)}, bf16[136,768]{1,0:T(8,128)(2,1)S(1)}, u32[]{:S(2)}, u32[]{:S(2)}) %collective-permute-start.3) | collective-permute-done | bytes 208928 | tf_op jit(solution)/shard_map/ppermute | solution.py:809
  26.7 5.5 %all-to-all-start = ((bf16[8,40,768]{2,1,0:T(8,128)(2,1)}), bf16[8,40,768]{2,1,0:T(8,128)(2,1)S(1)}, u32[]{:S(2)}, u32[]{:S(2)}) async-start(bf16[8,40,768]{2,1,0:T(8,128)(2,1)} %bitcast.23), calls=%async_computation | async-start | bytes 983040 | tf_op jit(solution)/shard_map/all_to_all | solution.py:933
  33.7 1.7 collective-permute-start.6
  35.4 6.9 %collective-permute-done.7.refs_2_ = bf16[4,136,384]{2,1,0:T(8,128)(2,1)S(1)} collective-permute-done((bf16[4,136,384]{2,1,0:T(8,128)(2,1)S(1)}, bf16[4,136,384]{2,1,0:T(8,128)(2,1)S(1)}, u32[]{:S(2)}, u32[]{:S(2)}) %collective-permute-start.7) | collective-permute-done | bytes 417824 | tf_op jit(solution)/shard_map/ppermute | solution.py:818
  42.3 2.0 collective-permute-start.8
  45.7 11.8 %attend.1 = (f32[8,192,64]{2,1,0:T(8,128)}, bf16[192,128]{1,0:T(8,128)(2,1)S(1)}, bf16[192,128]{1,0:T(8,128)(2,1)S(1)}, bf16[192,128]{1,0:T(8,128)(2,1)S(1)}, bf...) custom-call(s32[2]{0:T(128)S(1)} %pad_add_fusion.pos, ...), custom_call_target="tpu_custom_call" | custom-call | flops 100000 | bytes 10000 | tf_op jit(solution)/shard_map/attend/pallas_call | solution.py:354
  57.5 2.2 collective-permute-start.10
  59.7 1.5 collective-permute-start.9
  61.1 2.9 %maximum_select_fusion = bf16[2,384,768]{2,1,0:T(8,128)(2,1)} fusion(bf16[1,384,768]{2,1,0:T(8,128)(2,1)} %bitcast.7, bf16[1,384,768]{2,1,0:T(8,128)(2,1)} %bitcast.6, pred[]{:T(512)S(6)} %eq.106), kind=kLoop, calls=%fused_computation.8 | loop fusion | flops 1769472 | bytes 2359297 | tf_op jit(solution)/shard_map/jit(_where)/select_n | solution.py:840
  64.1 2.9 %router.1 = (bf16[40,896]{1,0:T(8,128)(2,1)S(1)}, bf16[40,896]{1,0:T(8,128)(2,1)S(1)}, bf16[40,896]{1,0:T(8,128)(2,1)S(1)}, bf16[40,896]{1,0:T(8,128)(2,1)S(1)},...) custom-call(s32[2]{0:T(128)S(1)} %pad_add_fusion.pos, ...), custom_call_target="tpu_custom_call" | custom-call | flops 100000 | bytes 10000 | tf_op jit(solution)/shard_map/router/pallas_call | solution.py:459
  68.7 2.8 %collective-permute-start.14 = (bf16[40,896]{1,0:T(8,128)(2,1)S(1)}, bf16[40,896]{1,0:T(8,128)(2,1)S(1)}, u32[]{:S(2)}, u32[]{:S(2)}) collective-permute-start(bf16[40,896]{1,0:T(8,128)(2,1)S(1)} %get-tuple-element.132), channel_id=1, source_target_pairs={{0,9},{1,8},{8,17},{9,16},{16,25},{17,24},{24,1},{25,0},{2,11},{3,... | collective-permute-start | bytes 215048 | tf_op jit(solution)/shard_map/ppermute | solution.py:859
  73.8 3.0 %collective-permute-start.18 = (bf16[40,896]{1,0:T(8,128)(2,1)S(1)}, bf16[40,896]{1,0:T(8,128)(2,1)S(1)}, u32[]{:S(2)}, u32[]{:S(2)}) collective-permute-start(bf16[40,896]{1,0:T(8,128)(2,1)S(1)} %get-tuple-element.136), channel_id=1, source_target_pairs={{0,25},{1,24},{8,1},{9,0},{16,9},{17,8},{24,17},{25,16},{2,27},{3,... | collective-permute-start | bytes 215048 | tf_op jit(solution)/shard_map/ppermute | solution.py:859
  78.0 4.9 %collective-permute-done.17.refs_6_ = bf16[40,896]{1,0:T(8,128)(2,1)S(1)} collective-permute-done((bf16[40,896]{1,0:T(8,128)(2,1)S(1)}, bf16[40,896]{1,0:T(8,128)(2,1)S(1)}, u32[]{:S(2)}, u32[]{:S(2)}) %collective-permute-start.17) | collective-permute-done | bytes 71712 | tf_op jit(solution)/shard_map/ppermute | solution.py:859
  82.9 2.5 collective-permute-done.18.refs_7_
  85.4 11.9 %expert.1 = (bf16[4,40,768]{2,1,0:T(8,128)(2,1)}, bf16[4,40,768]{2,1,0:T(8,128)(2,1)}, bf16[8,40,896]{2,1,0:T(8,128)(2,1)}, bf16[2,320,3072]{2,1,0:T(8,128)(2,1)}, bf16[2,320,768]{2,1,0:T(8,128)(2,1)}) custom-call(s32[2]{0:T(128)S(1)} %pad_add_fusion.3.info, bf16[8,40,768]{2,1,0:T(8,128)(2,1)S(1)} %all-to-all-done.dy_ref, bf16[4,768,3072]{2,1,0:T(8,128)(2,1)} %up_ref.1, ...), custom_call_target="tpu_custom_call" | custom-call | flops 100000 | bytes 10000 | tf_op jit(solution)/shard_map/expert/pallas_call | solution.py:519
  98.2 4.3 %all-to-all-start.1 = ((bf16[8,40,896]{2,1,0:T(8,128)(2,1)}), bf16[8,40,896]{2,1,0:T(8,128)(2,1)S(1)}, u32[]{:S(2)}, u32[]{:S(2)}) async-start(bf16[8,40,896]{2,1,0:T(8,128)(2,1)} %get-tuple-element.137), calls=%async_computation.1 | async-start | bytes 1146880 | tf_op jit(solution)/shard_map/all_to_all | solution.py:933
  103.3 3.0 %collective-permute-done.19.refs_1_ = bf16[2,320,768]{2,1,0:T(8,128)(2,1)S(1)} collective-permute-done((bf16[2,320,768]{2,1,0:T(8,128)(2,1)}, bf16[2,320,768]{2,1,0:T(8,128)(2,1)S(1)}, u32[]{:S(2)}, u32[]{:S(2)}) %collective-permute-start.19) | collective-permute-done | bytes 983072 | tf_op jit(solution)/shard_map/ppermute | solution.py:828
  106.3 6.1 %weight_terms.3 = (bf16[192,3072]{1,0:T(8,128)(2,1)}, bf16[192,3072]{1,0:T(8,128)(2,1)}) custom-call(s32[2]{0:T(128)S(1)} %pad_add_fusion.pos, bf16[2,320,768]{2,1,0:T(8,128)(2,1)S(1)} %copy-done.1, bf16[2,320,768]{2,1,0:T(8,128)(2,1)S(1)} %collective-permute-done.19.refs_1_, bf16[2,320,3072]{2,1,0:T(8,128)(2,1)} %get-tuple-element.139.refs_2_, ...), custom_call_target="tpu_custom_call" | custom-call | flops 100000 | bytes 10000 | tf_op jit(solution)/shard_map/weight_terms/pallas_call | solution.py:572
  112.4 6.1 %weight_terms.2 = (bf16[192,3072]{1,0:T(8,128)(2,1)}, bf16[192,3072]{1,0:T(8,128)(2,1)}) custom-call(s32[2]{0:T(128)S(1)} %pad_add_fusion.pos, bf16[2,320,768]{2,1,0:T(8,128)(2,1)S(1)} %copy-done.1, bf16[2,320,768]{2,1,0:T(8,128)(2,1)S(1)} %collective-permute-done.19.refs_1_, bf16[2,320,3072]{2,1,0:T(8,128)(2,1)} %get-tuple-element.139.refs_2_, ...), custom_call_target="tpu_custom_call" | custom-call | flops 100000 | bytes 10000 | tf_op jit(solution)/shard_map/weight_terms/pallas_call | solution.py:572
  118.5 5.1 %turn_back.1 = (bf16[192,128]{1,0:T(8,128)(2,1)S(1)}, bf16[192,128]{1,0:T(8,128)(2,1)S(1)}, bf16[192,128]{1,0:T(8,128)(2,1)S(1)}, bf16[192,128]{1,0:T(8,128)(2,1...) custom-call(s32[3]{0:T(128)S(1)} %pad_add_fusion.2.info, ...), custom_call_target="tpu_custom_call" | custom-call | flops 100000 | bytes 10000 | tf_op jit(solution)/shard_map/turn_back/pallas_call | solution.py:694
  124.0 3.6 %collective-permute-start.29 = (bf16[192,3072]{1,0:T(8,128)(2,1)S(1)}, bf16[192,3072]{1,0:T(8,128)(2,1)S(1)}, u32[]{:S(2)}, u32[]{:S(2)}) collective-permute-start(bf16[192,3072]{1,0:T(8,128)(2,1)S(1)} %copy-done.26), channel_id=1, source_target_pairs={{0,4},{4,0},{1,5},{5,1},{2,6},{6,2},{3,7},{7,3},{8,12},{12,8},{9,1... | collective-permute-start | bytes 3538952 | tf_op jit(solution)/shard_map/ppermute | solution.py:828
  130.5 1.5 collective-permute-start.23
  132.0 1.7 collective-permute-done.22.refs_1_
  134.6 2.7 %collective-permute-done.24.refs_3_ = bf16[192,128]{1,0:T(8,128)(2,1)S(1)} collective-permute-done((bf16[192,128]{1,0:T(8,128)(2,1)S(1)}, bf16[192,128]{1,0:T(8,128)(2,1)S(1)}, u32[]{:S(2)}, u32[]{:S(2)}) %collective-permute-start.24) | collective-permute-done | bytes 49184 | tf_op jit(solution)/shard_map/ppermute | solution.py:844
  137.3 15.2 %attend_back.1 = (bf16[512,192]{1,0:T(8,128)(2,1)S(1)}, bf16[4,128,384]{2,1,0:T(8,128)(2,1)S(1)}, bf16[4,128,384]{2,1,0:T(8,128)(2,1)S(1)}, bf16[4,128,384]{2,1,...) custom-call(s32[2]{0:T(128)S(1)} %pad_add_fusion.pos, ...), custom_call_target="tpu_custom_call" | custom-call | flops 100000 | bytes 10000 | tf_op jit(solution)/shard_map/attend_back/pallas_call | solution.py:384
  152.5 3.1 %collective-permute-start.28 = (bf16[4,128,384]{2,1,0:T(8,128)(2,1)S(1)}, bf16[4,128,384]{2,1,0:T(8,128)(2,1)S(1)}, u32[]{:S(2)}, u32[]{:S(2)}) collective-permute-start(bf16[4,128,384]{2,1,0:T(8,128)(2,1)S(1)} %get-tuple-element.165), channel_id=1, source_target_pairs={{0,2},{2,0},{1,3},{3,1},{4,6},{6,4},{5,7},{7,5},{8,10},{10,8},{9,1... | collective-permute-start | bytes 1179656 | tf_op jit(solution)/shard_map/ppermute | solution.py:828
  158.7 2.0 add_groups.2
  162.3 3.1 %collective-permute-start.30 = (bf16[4,128,384]{2,1,0:T(8,128)(2,1)S(1)}, bf16[4,128,384]{2,1,0:T(8,128)(2,1)S(1)}, u32[]{:S(2)}, u32[]{:S(2)}) collective-permute-start(bf16[4,128,384]{2,1,0:T(8,128)(2,1)S(1)} %get-tuple-element.169), channel_id=1, source_target_pairs={{0,4},{4,0},{1,5},{5,1},{2,6},{6,2},{3,7},{7,3},{8,12},{12,8},{9,1... | collective-permute-start | bytes 1179656 | tf_op jit(solution)/shard_map/ppermute | solution.py:828
  165.5 8.8 %collective-permute-done.30.came_ref = bf16[4,128,384]{2,1,0:T(8,128)(2,1)S(1)} collective-permute-done((bf16[4,128,384]{2,1,0:T(8,128)(2,1)S(1)}, bf16[4,128,384]{2,1,0:T(8,128)(2,1)S(1)}, u32[]{:S(2)}, u32[]{:S(2)}) %collective-permute-start.30) | collective-permute-done | bytes 393248 | tf_op jit(solution)/shard_map/ppermute | solution.py:828
  174.3 3.0 %input_back.1 = (f32[128,768]{1,0:T(8,128)S(1)}, bf16[128,768]{1,0:T(8,128)(2,1)S(1)}, bf16[128,768]{1,0:T(8,128)(2,1)S(1)}, bf16[128,768]{1,0:T(8,128)(2,1)S(1)...) custom-call(s32[2]{0:T(128)S(1)} %pad_add_fusion.1.info, ...), custom_call_target="tpu_custom_call" | custom-call | flops 100000 | bytes 10000 | tf_op jit(solution)/shard_map/input_back/pallas_call | solution.py:782
  179.3 1.5 collective-permute-start.34
  183.5 2.6 collective-permute-start.35
  187.0 2.5 collective-permute-done.33
  189.8 22.9 %collective-permute-done.35.refs_2_ = bf16[272,768]{1,0:T(8,128)(2,1)S(1)} collective-permute-done((bf16[272,768]{1,0:T(8,128)(2,1)S(1)}, bf16[272,768]{1,0:T(8,128)(2,1)S(1)}, u32[]{:S(2)}, u32[]{:S(2)}) %collective-permute-start.35) | collective-permute-done | bytes 417824 | tf_op jit(solution)/shard_map/ppermute | solution.py:844
  216.2 1.9 add_groups.3
  218.1 1.5 collective-permute-start.47
  219.6 3.5 %collective-permute-start.48 = (bf16[192,768]{1,0:T(8,128)(2,1)S(1)}, bf16[192,768]{1,0:T(8,128)(2,1)S(1)}, u32[]{:S(2)}, u32[]{:S(2)}) collective-permute-start(bf16[192,768]{1,0:T(8,128)(2,1)S(1)} %get-tuple-element.218), channel_id=1, source_target_pairs={{0,16},{8,24},{16,0},{24,8},{1,17},{9,25},{17,1},{25,9},{2,18},{10... | collective-permute-start | bytes 884744 | tf_op jit(solution)/shard_map/ppermute | solution.py:844
  223.3 3.1 %collective-permute-start.40 = (bf16[48,384]{1,0:T(8,128)(2,1)S(1)}, bf16[48,384]{1,0:T(8,128)(2,1)S(1)}, u32[]{:S(2)}, u32[]{:S(2)}) collective-permute-start(bf16[48,384]{1,0:T(8,128)(2,1)S(1)} %get-tuple-element.255), channel_id=1, source_target_pairs={{4,0},{10,2},{16,4},{22,6},{28,8},{2,10},{8,12},{14,14},{20,16},{2... | collective-permute-start | bytes 110600 | tf_op jit(solution)/shard_map/ppermute | solution.py:1065
  226.5 4.2 %collective-permute-start.39 = (bf16[48,384]{1,0:T(8,128)(2,1)S(1)}, bf16[48,384]{1,0:T(8,128)(2,1)S(1)}, u32[]{:S(2)}, u32[]{:S(2)}) collective-permute-start(bf16[48,384]{1,0:T(8,128)(2,1)S(1)} %get-tuple-element.256), channel_id=1, source_target_pairs={{2,0},{8,2},{14,4},{20,6},{26,8},{0,10},{6,12},{12,14},{18,16},{24... | collective-permute-start | bytes 110600 | tf_op jit(solution)/shard_map/ppermute | solution.py:1065
  230.7 1.9 collective-permute-start.38
  232.7 15.0 %collective-permute-done.48.refs_2_ = bf16[192,768]{1,0:T(8,128)(2,1)S(1)} collective-permute-done((bf16[192,768]{1,0:T(8,128)(2,1)S(1)}, bf16[192,768]{1,0:T(8,128)(2,1)S(1)}, u32[]{:S(2)}, u32[]{:S(2)}) %collective-permute-start.48) | collective-permute-done | bytes 294944 | tf_op jit(solution)/shard_map/ppermute | solution.py:844
  248.6 2.2 collective-permute-start.44
  250.8 2.1 in_order.3
  252.9 2.4 collective-permute-start.45
  256.8 2.1 in_order.2
  (230 shorter events, 52.4 us)
Async XLA Ops:
  3.0 17.1 %collective-permute-start.4 = (bf16[136,768]{1,0:T(8,128)(2,1)}, bf16[136,768]{1,0:T(8,128)(2,1)S(1)}, u32[]{:S(2)}, u32[]{:S(2)}) collective-permute-start(bf16[136,768]{1,0:T(8,128)(2,1)} %get-tuple-element.251), channel_id=1, source_target_pairs={{0,16},{8,24},{16,0},{24,8},{1,17},{9,25},{17,1},{25,9},{2,18},{10... | collective-permute-start | bytes 626696 | tf_op jit(solution)/shard_map/ppermute | solution.py:809
  5.3 18.5 %collective-permute-start.3 = (bf16[136,768]{1,0:T(8,128)(2,1)}, bf16[136,768]{1,0:T(8,128)(2,1)S(1)}, u32[]{:S(2)}, u32[]{:S(2)}) collective-permute-start(bf16[136,768]{1,0:T(8,128)(2,1)} %get-tuple-element.251), channel_id=1, source_target_pairs={{0,8},{8,16},{16,24},{24,0},{1,9},{9,17},{17,25},{25,1},{2,10},{10... | collective-permute-start | bytes 626696 | tf_op jit(solution)/shard_map/ppermute | solution.py:809
  5.3 18.5 %collective-permute-start.5 = (bf16[136,768]{1,0:T(8,128)(2,1)}, bf16[136,768]{1,0:T(8,128)(2,1)}, u32[]{:S(2)}, u32[]{:S(2)}) collective-permute-start(bf16[136,768]{1,0:T(8,128)(2,1)} %get-tuple-element.251), channel_id=1, source_target_pairs={{0,24},{8,0},{16,8},{24,16},{1,25},{9,1},{17,9},{25,17},{2,26},{10... | collective-permute-start | bytes 626696 | tf_op jit(solution)/shard_map/ppermute | solution.py:809
  9.8 5.7 %collective-permute-start.2 = (bf16[16,384]{1,0:T(8,128)(2,1)S(1)}, bf16[16,384]{1,0:T(8,128)(2,1)S(1)}, u32[]{:S(2)}, u32[]{:S(2)}) collective-permute-start(bf16[16,384]{1,0:T(8,128)(2,1)S(1)} %concatenate.53), channel_id=1, source_target_pairs={{0,1},{1,0},{2,3},{3,2},{4,5},{5,4},{6,7},{7,6},{8,9},{9,8},{10,11... | collective-permute-start | bytes 36872 | tf_op jit(solution)/shard_map/ppermute | solution.py:839
  11.7 13.7 %collective-permute-start = (bf16[384,576]{1,0:T(8,128)(2,1)S(1)}, bf16[384,576]{1,0:T(8,128)(2,1)S(1)}, u32[]{:S(2)}, u32[]{:S(2)}) collective-permute-start(bf16[384,576]{1,0:T(8,128)(2,1)S(1)} %pad_maximum_fusion.2), channel_id=1, source_target_pairs={{0,1},{1,0},{2,3},{3,2},{4,5},{5,4},{6,7},{7,6},{8,9},{9,8},{10,11... | collective-permute-start | bytes 1327112 | tf_op jit(solution)/shard_map/ppermute | solution.py:839
  26.7 33.0 %all-to-all-start = ((bf16[8,40,768]{2,1,0:T(8,128)(2,1)}), bf16[8,40,768]{2,1,0:T(8,128)(2,1)S(1)}, u32[]{:S(2)}, u32[]{:S(2)}) async-start(bf16[8,40,768]{2,1,0:T(8,128)(2,1)} %bitcast.23), calls=%async_computation | async-start | bytes 983040 | tf_op jit(solution)/shard_map/all_to_all | solution.py:933
  32.2 10.2 %collective-permute-start.7 = (bf16[4,136,384]{2,1,0:T(8,128)(2,1)S(1)}, bf16[4,136,384]{2,1,0:T(8,128)(2,1)S(1)}, u32[]{:S(2)}, u32[]{:S(2)}) collective-permute-start(bf16[4,136,384]{2,1,0:T(8,128)(2,1)S(1)} %pad_maximum_fusion.4.refs_0_), channel_id=1, source_target_pairs={{0,4},{2,6},{4,0},{6,2},{1,5},{3,7},{5,1},{7,3},{8,12},{10,14},{12... | collective-permute-start | bytes 1253384 | tf_op jit(solution)/shard_map/ppermute | solution.py:818
  33.5 27.7 %collective-permute-start.1 = (bf16[384,768]{1,0:T(8,128)(2,1)}, bf16[384,768]{1,0:T(8,128)(2,1)}, u32[]{:S(2)}, u32[]{:S(2)}) collective-permute-start(bf16[384,768]{1,0:T(8,128)(2,1)} %param.19), channel_id=1, source_target_pairs={{0,1},{1,0},{2,3},{3,2},{4,5},{5,4},{6,7},{7,6},{8,9},{9,8},{10,11... | collective-permute-start | bytes 1769480 | tf_op jit(solution)/shard_map/ppermute | solution.py:839
  33.7 10.7 %collective-permute-start.6 = (bf16[4,136,384]{2,1,0:T(8,128)(2,1)S(1)}, bf16[4,136,384]{2,1,0:T(8,128)(2,1)S(1)}, u32[]{:S(2)}, u32[]{:S(2)}) collective-permute-start(bf16[4,136,384]{2,1,0:T(8,128)(2,1)S(1)} %pad_maximum_fusion.4.refs_0_), channel_id=1, source_target_pairs={{0,2},{2,0},{4,6},{6,4},{1,3},{3,1},{5,7},{7,5},{8,10},{10,8},{12,... | collective-permute-start | bytes 1253384 | tf_op jit(solution)/shard_map/ppermute | solution.py:818
  57.5 6.5 %collective-permute-start.10 = (bf16[192,128]{1,0:T(8,128)(2,1)S(1)}, bf16[192,128]{1,0:T(8,128)(2,1)S(1)}, u32[]{:S(2)}, u32[]{:S(2)}) collective-permute-start(bf16[192,128]{1,0:T(8,128)(2,1)S(1)} %get-tuple-element.122), channel_id=1, source_target_pairs={{0,16},{8,24},{16,0},{24,8},{1,17},{9,25},{17,1},{25,9},{2,18},{10... | collective-permute-start | bytes 147464 | tf_op jit(solution)/shard_map/ppermute | solution.py:844
  59.7 4.4 %collective-permute-start.11 = (bf16[192,128]{1,0:T(8,128)(2,1)S(1)}, bf16[192,128]{1,0:T(8,128)(2,1)S(1)}, u32[]{:S(2)}, u32[]{:S(2)}) collective-permute-start(bf16[192,128]{1,0:T(8,128)(2,1)S(1)} %get-tuple-element.123), channel_id=1, source_target_pairs={{0,8},{8,16},{16,24},{24,0},{1,9},{9,17},{17,25},{25,1},{2,10},{10... | collective-permute-start | bytes 147464 | tf_op jit(solution)/shard_map/ppermute | solution.py:844
  59.7 4.4 %collective-permute-start.9 = (bf16[192,128]{1,0:T(8,128)(2,1)S(1)}, bf16[192,128]{1,0:T(8,128)(2,1)S(1)}, u32[]{:S(2)}, u32[]{:S(2)}) collective-permute-start(bf16[192,128]{1,0:T(8,128)(2,1)S(1)} %get-tuple-element.121), channel_id=1, source_target_pairs={{0,24},{8,0},{16,8},{24,16},{1,25},{9,1},{17,9},{25,17},{2,26},{10... | collective-permute-start | bytes 147464 | tf_op jit(solution)/shard_map/ppermute | solution.py:844
  67.0 6.6 %collective-permute-start.12 = (bf16[40,896]{1,0:T(8,128)(2,1)S(1)}, bf16[40,896]{1,0:T(8,128)(2,1)S(1)}, u32[]{:S(2)}, u32[]{:S(2)}) collective-permute-start(bf16[40,896]{1,0:T(8,128)(2,1)S(1)} %get-tuple-element.130), channel_id=1, source_target_pairs={{0,1},{1,0},{8,9},{9,8},{16,17},{17,16},{24,25},{25,24},{2,3},{3,2... | collective-permute-start | bytes 215048 | tf_op jit(solution)/shard_map/ppermute | solution.py:859
  67.3 6.5 %collective-permute-start.13 = (bf16[40,896]{1,0:T(8,128)(2,1)S(1)}, bf16[40,896]{1,0:T(8,128)(2,1)S(1)}, u32[]{:S(2)}, u32[]{:S(2)}) collective-permute-start(bf16[40,896]{1,0:T(8,128)(2,1)S(1)} %get-tuple-element.131), channel_id=1, source_target_pairs={{0,8},{1,9},{8,16},{9,17},{16,24},{17,25},{24,0},{25,1},{2,10},{3,... | collective-permute-start | bytes 215048 | tf_op jit(solution)/shard_map/ppermute | solution.py:859
  68.7 8.2 %collective-permute-start.14 = (bf16[40,896]{1,0:T(8,128)(2,1)S(1)}, bf16[40,896]{1,0:T(8,128)(2,1)S(1)}, u32[]{:S(2)}, u32[]{:S(2)}) collective-permute-start(bf16[40,896]{1,0:T(8,128)(2,1)S(1)} %get-tuple-element.132), channel_id=1, source_target_pairs={{0,9},{1,8},{8,17},{9,16},{16,25},{17,24},{24,1},{25,0},{2,11},{3,... | collective-permute-start | bytes 215048 | tf_op jit(solution)/shard_map/ppermute | solution.py:859
  71.5 5.4 %collective-permute-start.15 = (bf16[40,896]{1,0:T(8,128)(2,1)S(1)}, bf16[40,896]{1,0:T(8,128)(2,1)S(1)}, u32[]{:S(2)}, u32[]{:S(2)}) collective-permute-start(bf16[40,896]{1,0:T(8,128)(2,1)S(1)} %get-tuple-element.133), channel_id=1, source_target_pairs={{0,16},{1,17},{8,24},{9,25},{16,0},{17,1},{24,8},{25,9},{2,18},{3,... | collective-permute-start | bytes 215048 | tf_op jit(solution)/shard_map/ppermute | solution.py:859
  72.3 5.7 %collective-permute-start.16 = (bf16[40,896]{1,0:T(8,128)(2,1)S(1)}, bf16[40,896]{1,0:T(8,128)(2,1)S(1)}, u32[]{:S(2)}, u32[]{:S(2)}) collective-permute-start(bf16[40,896]{1,0:T(8,128)(2,1)S(1)} %get-tuple-element.134), channel_id=1, source_target_pairs={{0,17},{1,16},{8,25},{9,24},{16,1},{17,0},{24,9},{25,8},{2,19},{3,... | collective-permute-start | bytes 215048 | tf_op jit(solution)/shard_map/ppermute | solution.py:859
  73.6 9.3 %collective-permute-start.17 = (bf16[40,896]{1,0:T(8,128)(2,1)S(1)}, bf16[40,896]{1,0:T(8,128)(2,1)S(1)}, u32[]{:S(2)}, u32[]{:S(2)}) collective-permute-start(bf16[40,896]{1,0:T(8,128)(2,1)S(1)} %get-tuple-element.135), channel_id=1, source_target_pairs={{0,24},{1,25},{8,0},{9,1},{16,8},{17,9},{24,16},{25,17},{2,26},{3,... | collective-permute-start | bytes 215048 | tf_op jit(solution)/shard_map/ppermute | solution.py:859
  73.8 11.6 %collective-permute-start.18 = (bf16[40,896]{1,0:T(8,128)(2,1)S(1)}, bf16[40,896]{1,0:T(8,128)(2,1)S(1)}, u32[]{:S(2)}, u32[]{:S(2)}) collective-permute-start(bf16[40,896]{1,0:T(8,128)(2,1)S(1)} %get-tuple-element.136), channel_id=1, source_target_pairs={{0,25},{1,24},{8,1},{9,0},{16,9},{17,8},{24,17},{25,16},{2,27},{3,... | collective-permute-start | bytes 215048 | tf_op jit(solution)/shard_map/ppermute | solution.py:859
  97.3 9.0 %collective-permute-start.20 = (bf16[2,320,3072]{2,1,0:T(8,128)(2,1)}, bf16[2,320,3072]{2,1,0:T(8,128)(2,1)}, u32[]{:S(2)}, u32[]{:S(2)}) collective-permute-start(bf16[2,320,3072]{2,1,0:T(8,128)(2,1)} %get-tuple-element.139.refs_2_), channel_id=1, source_target_pairs={{0,2},{2,0},{1,3},{3,1},{4,6},{6,4},{5,7},{7,5},{8,10},{10,8},{9,1... | collective-permute-start | bytes 11796488 | tf_op jit(solution)/shard_map/ppermute | solution.py:828
  98.2 20.3 %all-to-all-start.1 = ((bf16[8,40,896]{2,1,0:T(8,128)(2,1)}), bf16[8,40,896]{2,1,0:T(8,128)(2,1)S(1)}, u32[]{:S(2)}, u32[]{:S(2)}) async-start(bf16[8,40,896]{2,1,0:T(8,128)(2,1)} %get-tuple-element.137), calls=%async_computation.1 | async-start | bytes 1146880 | tf_op jit(solution)/shard_map/all_to_all | solution.py:933
  102.5 3.8 %collective-permute-start.19 = (bf16[2,320,768]{2,1,0:T(8,128)(2,1)}, bf16[2,320,768]{2,1,0:T(8,128)(2,1)S(1)}, u32[]{:S(2)}, u32[]{:S(2)}) collective-permute-start(bf16[2,320,768]{2,1,0:T(8,128)(2,1)} %get-tuple-element.138.refs_0_), channel_id=1, source_target_pairs={{0,2},{2,0},{1,3},{3,1},{4,6},{6,4},{5,7},{7,5},{8,10},{10,8},{9,1... | collective-permute-start | bytes 2949128 | tf_op jit(solution)/shard_map/ppermute | solution.py:828
  123.6 4.0 %collective-permute-start.21 = (bf16[2,8,48,384]{3,2,1,0:T(8,128)(2,1)}, bf16[2,8,48,384]{3,2,1,0:T(8,128)(2,1)S(1)}, u32[]{:S(2)}, u32[]{:S(2)}) collective-permute-start(bf16[2,8,48,384]{3,2,1,0:T(8,128)(2,1)} %get-tuple-element.147), channel_id=1, source_target_pairs={{0,2},{2,0},{1,3},{3,1},{4,6},{6,4},{5,7},{7,5},{8,10},{10,8},{9,1... | collective-permute-start | bytes 1769480 | tf_op jit(solution)/shard_map/ppermute | solution.py:828
  124.0 33.7 %collective-permute-start.29 = (bf16[192,3072]{1,0:T(8,128)(2,1)S(1)}, bf16[192,3072]{1,0:T(8,128)(2,1)S(1)}, u32[]{:S(2)}, u32[]{:S(2)}) collective-permute-start(bf16[192,3072]{1,0:T(8,128)(2,1)S(1)} %copy-done.26), channel_id=1, source_target_pairs={{0,4},{4,0},{1,5},{5,1},{2,6},{6,2},{3,7},{7,3},{8,12},{12,8},{9,1... | collective-permute-start | bytes 3538952 | tf_op jit(solution)/shard_map/ppermute | solution.py:828
  128.9 26.7 %collective-permute-start.25 = (bf16[8,48,384]{2,1,0:T(8,128)(2,1)S(1)}, bf16[8,48,384]{2,1,0:T(8,128)(2,1)S(1)}, u32[]{:S(2)}, u32[]{:S(2)}) collective-permute-start(bf16[8,48,384]{2,1,0:T(8,128)(2,1)S(1)} %fusion.5), channel_id=1, source_target_pairs={{0,1},{1,0},{2,3},{3,2},{4,5},{5,4},{6,7},{7,6},{8,9},{9,8},{10,11... | collective-permute-start | bytes 884744 | tf_op jit(solution)/shard_map/ppermute | solution.py:828
  129.4 26.2 %collective-permute-start.26 = (bf16[4,40,768]{2,1,0:T(8,128)(2,1)S(1)}, bf16[4,40,768]{2,1,0:T(8,128)(2,1)S(1)}, u32[]{:S(2)}, u32[]{:S(2)}) collective-permute-start(bf16[4,40,768]{2,1,0:T(8,128)(2,1)S(1)} %copy-done.27), channel_id=1, source_target_pairs={{0,1},{1,0},{2,3},{3,2},{4,5},{5,4},{6,7},{7,6},{8,9},{9,8},{10,11... | collective-permute-start | bytes 737288 | tf_op jit(solution)/shard_map/ppermute | solution.py:973
  130.5 4.2 %collective-permute-start.23 = (bf16[192,128]{1,0:T(8,128)(2,1)S(1)}, bf16[192,128]{1,0:T(8,128)(2,1)S(1)}, u32[]{:S(2)}, u32[]{:S(2)}) collective-permute-start(bf16[192,128]{1,0:T(8,128)(2,1)S(1)} %get-tuple-element.150), channel_id=1, source_target_pairs={{0,16},{8,24},{16,0},{24,8},{1,17},{9,25},{17,1},{25,9},{2,18},{10... | collective-permute-start | bytes 147464 | tf_op jit(solution)/shard_map/ppermute | solution.py:844
  133.7 3.6 %collective-permute-start.24 = (bf16[192,128]{1,0:T(8,128)(2,1)S(1)}, bf16[192,128]{1,0:T(8,128)(2,1)S(1)}, u32[]{:S(2)}, u32[]{:S(2)}) collective-permute-start(bf16[192,128]{1,0:T(8,128)(2,1)S(1)} %get-tuple-element.151), channel_id=1, source_target_pairs={{0,24},{8,0},{16,8},{24,16},{1,25},{9,1},{17,9},{25,17},{2,26},{10... | collective-permute-start | bytes 147464 | tf_op jit(solution)/shard_map/ppermute | solution.py:844
  152.5 4.4 %collective-permute-start.28 = (bf16[4,128,384]{2,1,0:T(8,128)(2,1)S(1)}, bf16[4,128,384]{2,1,0:T(8,128)(2,1)S(1)}, u32[]{:S(2)}, u32[]{:S(2)}) collective-permute-start(bf16[4,128,384]{2,1,0:T(8,128)(2,1)S(1)} %get-tuple-element.165), channel_id=1, source_target_pairs={{0,2},{2,0},{1,3},{3,1},{4,6},{6,4},{5,7},{7,5},{8,10},{10,8},{9,1... | collective-permute-start | bytes 1179656 | tf_op jit(solution)/shard_map/ppermute | solution.py:828
  161.5 12.8 %collective-permute-start.31 = (bf16[272,768]{1,0:T(8,128)(2,1)S(1)}, bf16[272,768]{1,0:T(8,128)(2,1)S(1)}, u32[]{:S(2)}, u32[]{:S(2)}) collective-permute-start(bf16[272,768]{1,0:T(8,128)(2,1)S(1)} %get-tuple-element.174), channel_id=1, source_target_pairs={{0,8},{8,16},{16,24},{24,0},{1,9},{9,17},{17,25},{25,1},{2,10},{10... | collective-permute-start | bytes 1253384 | tf_op jit(solution)/shard_map/ppermute | solution.py:844
  162.3 11.9 %collective-permute-start.30 = (bf16[4,128,384]{2,1,0:T(8,128)(2,1)S(1)}, bf16[4,128,384]{2,1,0:T(8,128)(2,1)S(1)}, u32[]{:S(2)}, u32[]{:S(2)}) collective-permute-start(bf16[4,128,384]{2,1,0:T(8,128)(2,1)S(1)} %get-tuple-element.169), channel_id=1, source_target_pairs={{0,4},{4,0},{1,5},{5,1},{2,6},{6,2},{3,7},{7,3},{8,12},{12,8},{9,1... | collective-permute-start | bytes 1179656 | tf_op jit(solution)/shard_map/ppermute | solution.py:828
  179.3 34.9 %collective-permute-start.34 = (bf16[192,3072]{1,0:T(8,128)(2,1)}, bf16[192,3072]{1,0:T(8,128)(2,1)S(1)}, u32[]{:S(2)}, u32[]{:S(2)}) collective-permute-start(bf16[192,3072]{1,0:T(8,128)(2,1)} %get-tuple-element.186), channel_id=1, source_target_pairs={{0,4},{4,0},{1,5},{5,1},{2,6},{6,2},{3,7},{7,3},{8,12},{12,8},{9,1... | collective-permute-start | bytes 3538952 | tf_op jit(solution)/shard_map/ppermute | solution.py:828
  182.2 7.3 %collective-permute-start.33 = (bf16[320,384]{1,0:T(8,128)(2,1)S(1)}, bf16[320,384]{1,0:T(8,128)(2,1)S(1)}, u32[]{:S(2)}, u32[]{:S(2)}) collective-permute-start(bf16[320,384]{1,0:T(8,128)(2,1)S(1)} %pad_maximum_fusion.6), channel_id=1, source_target_pairs={{0,1},{1,0},{2,3},{3,2},{4,5},{5,4},{6,7},{7,6},{8,9},{9,8},{10,11... | collective-permute-start | bytes 737288 | tf_op jit(solution)/shard_map/ppermute | solution.py:828
  183.5 29.3 %collective-permute-start.35 = (bf16[272,768]{1,0:T(8,128)(2,1)S(1)}, bf16[272,768]{1,0:T(8,128)(2,1)S(1)}, u32[]{:S(2)}, u32[]{:S(2)}) collective-permute-start(bf16[272,768]{1,0:T(8,128)(2,1)S(1)} %copy-done.6), channel_id=1, source_target_pairs={{0,16},{8,24},{16,0},{24,8},{1,17},{9,25},{17,1},{25,9},{2,18},{10... | collective-permute-start | bytes 1253384 | tf_op jit(solution)/shard_map/ppermute | solution.py:844
  186.1 28.1 %collective-permute-start.36 = (bf16[272,768]{1,0:T(8,128)(2,1)S(1)}, bf16[272,768]{1,0:T(8,128)(2,1)S(1)}, u32[]{:S(2)}, u32[]{:S(2)}) collective-permute-start(bf16[272,768]{1,0:T(8,128)(2,1)S(1)} %get-tuple-element.190), channel_id=1, source_target_pairs={{0,24},{8,0},{16,8},{24,16},{1,25},{9,1},{17,9},{25,17},{2,26},{10... | collective-permute-start | bytes 1253384 | tf_op jit(solution)/shard_map/ppermute | solution.py:844
  214.2 8.9 %collective-permute-start.42 = (bf16[128,768]{1,0:T(8,128)(2,1)S(1)}, bf16[128,768]{1,0:T(8,128)(2,1)S(1)}, u32[]{:S(2)}, u32[]{:S(2)}) collective-permute-start(bf16[128,768]{1,0:T(8,128)(2,1)S(1)} %copy-done.8), channel_id=1, source_target_pairs={{0,24},{8,0},{16,8},{24,16},{1,25},{9,1},{17,9},{25,17},{2,26},{10... | collective-permute-start | bytes 589832 | tf_op jit(solution)/shard_map/ppermute | solution.py:1040
  214.6 8.5 %collective-permute-start.37 = (bf16[368,384]{1,0:T(8,128)(2,1)S(1)}, bf16[368,384]{1,0:T(8,128)(2,1)S(1)}, u32[]{:S(2)}, u32[]{:S(2)}) collective-permute-start(bf16[368,384]{1,0:T(8,128)(2,1)S(1)} %pad_maximum_fusion.5), channel_id=1, source_target_pairs={{0,4},{4,0},{1,5},{5,1},{2,6},{6,2},{3,7},{7,3},{8,12},{12,8},{9,1... | collective-permute-start | bytes 847880 | tf_op jit(solution)/shard_map/ppermute | solution.py:828
  218.1 12.6 %collective-permute-start.47 = (bf16[192,768]{1,0:T(8,128)(2,1)S(1)}, bf16[192,768]{1,0:T(8,128)(2,1)S(1)}, u32[]{:S(2)}, u32[]{:S(2)}) collective-permute-start(bf16[192,768]{1,0:T(8,128)(2,1)S(1)} %get-tuple-element.217), channel_id=1, source_target_pairs={{0,8},{8,16},{16,24},{24,0},{1,9},{9,17},{17,25},{25,1},{2,10},{10... | collective-permute-start | bytes 884744 | tf_op jit(solution)/shard_map/ppermute | solution.py:844
  219.6 28.1 %collective-permute-start.48 = (bf16[192,768]{1,0:T(8,128)(2,1)S(1)}, bf16[192,768]{1,0:T(8,128)(2,1)S(1)}, u32[]{:S(2)}, u32[]{:S(2)}) collective-permute-start(bf16[192,768]{1,0:T(8,128)(2,1)S(1)} %get-tuple-element.218), channel_id=1, source_target_pairs={{0,16},{8,24},{16,0},{24,8},{1,17},{9,25},{17,1},{25,9},{2,18},{10... | collective-permute-start | bytes 884744 | tf_op jit(solution)/shard_map/ppermute | solution.py:844
  223.0 25.6 %collective-permute-start.49 = (bf16[192,768]{1,0:T(8,128)(2,1)S(1)}, bf16[192,768]{1,0:T(8,128)(2,1)S(1)}, u32[]{:S(2)}, u32[]{:S(2)}) collective-permute-start(bf16[192,768]{1,0:T(8,128)(2,1)S(1)} %get-tuple-element.219), channel_id=1, source_target_pairs={{0,24},{8,0},{16,8},{24,16},{1,25},{9,1},{17,9},{25,17},{2,26},{10... | collective-permute-start | bytes 884744 | tf_op jit(solution)/shard_map/ppermute | solution.py:844
  223.3 29.6 %collective-permute-start.40 = (bf16[48,384]{1,0:T(8,128)(2,1)S(1)}, bf16[48,384]{1,0:T(8,128)(2,1)S(1)}, u32[]{:S(2)}, u32[]{:S(2)}) collective-permute-start(bf16[48,384]{1,0:T(8,128)(2,1)S(1)} %get-tuple-element.255), channel_id=1, source_target_pairs={{4,0},{10,2},{16,4},{22,6},{28,8},{2,10},{8,12},{14,14},{20,16},{2... | collective-permute-start | bytes 110600 | tf_op jit(solution)/shard_map/ppermute | solution.py:1065
  226.5 28.8 %collective-permute-start.39 = (bf16[48,384]{1,0:T(8,128)(2,1)S(1)}, bf16[48,384]{1,0:T(8,128)(2,1)S(1)}, u32[]{:S(2)}, u32[]{:S(2)}) collective-permute-start(bf16[48,384]{1,0:T(8,128)(2,1)S(1)} %get-tuple-element.256), channel_id=1, source_target_pairs={{2,0},{8,2},{14,4},{20,6},{26,8},{0,10},{6,12},{12,14},{18,16},{24... | collective-permute-start | bytes 110600 | tf_op jit(solution)/shard_map/ppermute | solution.py:1065
  230.7 24.5 %collective-permute-start.38 = (bf16[48,384]{1,0:T(8,128)(2,1)S(1)}, bf16[48,384]{1,0:T(8,128)(2,1)S(1)}, u32[]{:S(2)}, u32[]{:S(2)}) collective-permute-start(bf16[48,384]{1,0:T(8,128)(2,1)S(1)} %get-tuple-element.257), channel_id=1, source_target_pairs={{0,0},{6,2},{12,4},{18,6},{24,8},{30,10},{4,12},{10,14},{16,16},{2... | collective-permute-start | bytes 110600 | tf_op jit(solution)/shard_map/ppermute | solution.py:1065
  247.7 16.7 %collective-permute-start.43 = (bf16[128,768]{1,0:T(8,128)(2,1)S(1)}, bf16[128,768]{1,0:T(8,128)(2,1)S(1)}, u32[]{:S(2)}, u32[]{:S(2)}) collective-permute-start(bf16[128,768]{1,0:T(8,128)(2,1)S(1)} %add_convert_fusion), channel_id=1, source_target_pairs={{0,24},{8,0},{16,8},{24,16},{1,25},{9,1},{17,9},{25,17},{2,26},{10... | collective-permute-start | bytes 589832 | tf_op jit(solution)/shard_map/ppermute | solution.py:1043
  248.6 13.0 %collective-permute-start.44 = (bf16[80,384]{1,0:T(8,128)(2,1)S(1)}, bf16[80,384]{1,0:T(8,128)(2,1)S(1)}, u32[]{:S(2)}, u32[]{:S(2)}) collective-permute-start(bf16[80,384]{1,0:T(8,128)(2,1)S(1)} %get-tuple-element.260), channel_id=1, source_target_pairs={{0,16},{8,24},{16,0},{24,8},{1,17},{9,25},{17,1},{25,9},{2,18},{10... | collective-permute-start | bytes 184328 | tf_op jit(solution)/shard_map/ppermute | solution.py:1056
  252.9 8.7 %collective-permute-start.45 = (bf16[80,384]{1,0:T(8,128)(2,1)S(1)}, bf16[80,384]{1,0:T(8,128)(2,1)S(1)}, u32[]{:S(2)}, u32[]{:S(2)}) collective-permute-start(bf16[80,384]{1,0:T(8,128)(2,1)S(1)} %get-tuple-element.261), channel_id=1, source_target_pairs={{0,8},{8,16},{16,24},{24,0},{1,9},{9,17},{17,25},{25,1},{2,10},{10... | collective-permute-start | bytes 184328 | tf_op jit(solution)/shard_map/ppermute | solution.py:1056
  255.3 6.4 %collective-permute-start.46 = (bf16[80,384]{1,0:T(8,128)(2,1)S(1)}, bf16[80,384]{1,0:T(8,128)(2,1)S(1)}, u32[]{:S(2)}, u32[]{:S(2)}) collective-permute-start(bf16[80,384]{1,0:T(8,128)(2,1)S(1)} %get-tuple-element.262), channel_id=1, source_target_pairs={{0,24},{8,0},{16,8},{24,16},{1,25},{9,1},{17,9},{25,17},{2,26},{10... | collective-permute-start | bytes 184328 | tf_op jit(solution)/shard_map/ppermute | solution.py:1056
  255.3 9.4 %collective-permute-start.41 = (bf16[128,768]{1,0:T(8,128)(2,1)S(1)}, bf16[128,768]{1,0:T(8,128)(2,1)S(1)}, u32[]{:S(2)}, u32[]{:S(2)}) collective-permute-start(bf16[128,768]{1,0:T(8,128)(2,1)S(1)} %get-tuple-element.208), channel_id=1, source_target_pairs={{0,8},{8,16},{16,24},{24,0},{1,9},{9,17},{17,25},{25,1},{2,10},{10... | collective-permute-start | bytes 589832 | tf_op jit(solution)/shard_map/ppermute | solution.py:1041
  (32 other events, 245.7 us)

commit v7 on v6

--- a/solution.py
+++ b/solution.py
@@ -136,7 +136,7 @@
     key = lax.broadcasted_iota(jnp.int32, (CHUNK, size), 0)
     per = CHUNK // half
 
-    @pl.loop(0, GROUPS)
+    @pl.loop(0, GROUPS, unroll=2)
     def _(slot):
         for j in range(members):
             for early in (True, False):
@@ -234,12 +234,12 @@
     same = own_blocks(size, half)
     key = lax.broadcasted_iota(jnp.int32, (CHUNK, size), 0)
 
-    @pl.loop(0, blocks // per)
+    @pl.loop(0, blocks // per, unroll=4)
     def _(chunk):
         dk[chunk] = jnp.zeros(dk.shape[1:], F32)
         dv[chunk] = jnp.zeros(dv.shape[1:], F32)
 
-    @pl.loop(0, width // 128)
+    @pl.loop(0, width // 128, unroll=2)
     def _(j):
         dstrip[pl.ds(pl.multiple_of(j * 128, 128), 128), :] = jnp.zeros((128, size), F32)
 
@@ -297,7 +297,7 @@
         pair_of(pair, 0)
         pair_of(pair, 1)
 
-    @pl.loop(0, GROUPS)
+    @pl.loop(0, GROUPS, unroll=2)
     def _(slot):
         for j in range(members):
             for early in (True, False):
@@ -938,7 +938,7 @@
     kv = proj[:, GWIDTH:].reshape(GROUPS, tok, 2 * GWIDTH)
     kvs = gather_members(jnp.concatenate([kv, mixed[:, tok:, : 2 * GWIDTH]], axis=1))
     dy_send = dot((pick[0] | pick[1]).astype(BF), cotangent[0]).astype(BF).reshape(PIECES, CAP, width)
-    dy_slots = exchange_rows(together(dy_send, proj)[0])
+    dy_slots = exchange_rows(together(dy_send, small)[0])
     o_pre, *rest = attend(pos, proj, kvs, strips, blocks)
     lows, stat, keys = rest[:GROUPS], rest[GROUPS], rest[GROUPS + 1 :]
     lows[1], dy_slots = together(lows[1], dy_slots)

time: 269 us -> 268 us (level)
  waiting for transfers between devices: 81.4 us -> 73.9 us
  Pallas kernels: 73.7 us -> 78.7 us
    ppermute x12, starting transfers between devices: 16.6 us -> 10.7 us  [swap(): return lax.ppermute(x, axis, xor_perm(bit, lax.axis_size(axis)))]
    ppermute x3, waiting for transfers between devices: 3.72 us -> 0.01 us  [gather_groups(): came = {k: lax.ppermute(x, 'h', turn(k)) for k in (2, 1, 3)}]
    ppermute x12, starting transfers between devices: 15.4 us -> 18.4 us  [group_pieces(): came = {k: lax.ppermute(pieces[k], 'h', turn(sign * k)) for k in (2, 1, 3)}]
    pallas_call x1, Pallas kernels: 11.8 us -> 14.7 us  [attend(): pl.pallas_call(functools.partial(forward_kernel, half, blocks, len(kvs)),...]
  transfers between devices with their start and end apart: 52 -> 52, of which waited for: 18 -> 19; matrix products, arithmetic and copies ran while one was open for 8% -> 10% of each run, Pallas kernels for 18% -> 20%
where the time goes in v7:
time: 268 us; the launch traced here: 265 us
  Pallas kernels  78.7 us (29%)
  starting transfers between devices  78.1 us (29%)
  waiting for transfers between devices  73.9 us (28%)
  other arithmetic  15 us (6%)
  local copies, waits for them, and re-layouts  13.8 us (5%)
  matrix products  4.25 us (2%)
    ppermute x12, waiting for transfers between devices, group_pieces(): came = {k: lax.ppermute(pieces[k], 'h', turn(sign * k)) for k in (2, 1, 3)}  43.7 us
    ppermute x12, starting transfers between devices, group_pieces(): came = {k: lax.ppermute(pieces[k], 'h', turn(sign * k)) for k in (2, 1, 3)}  18.4 us
    pallas_call x1, Pallas kernels, attend_back(): pl.pallas_call(functools.partial(backward_kernel, half, blocks, members),...  17.2 us
    ppermute x12, waiting for transfers between devices, swap(): return lax.ppermute(x, axis, xor_perm(bit, lax.axis_size(axis)))  16.2 us
    pallas_call x1, Pallas kernels, attend(): pl.pallas_call(functools.partial(forward_kernel, half, blocks, len(kvs)),...  14.7 us
    pallas_call x2, Pallas kernels, weight_terms(): pl.pallas_call(functools.partial(weight_kernel, len(rows), members, side)...  12.2 us
    pallas_call x1, Pallas kernels, expert(): pl.pallas_call(functools.partial(expert_kernel, groups, n_fsdp), grid_spe...  11.9 us
    ppermute x12, starting transfers between devices, swap(): return lax.ppermute(x, axis, xor_perm(bit, lax.axis_size(axis)))  10.7 us
  transfers between devices with their start and end apart: 52, of which 19 were waited for; matrix products, arithmetic and copies ran while one was open for 10% of the time, Pallas kernels for 20%

profile of v7, /device:TPU:11, one launch (start us, length us, event | category | flops | bytes accessed | tf_op | source)
XLA Modules:
  0.0 265.2 jit_solution(17423671811835108810)
XLA Ops:
  2.3 2.4 collective-permute-start.4
  4.7 1.5 collective-permute-start.5
  9.5 1.4 constant_dynamic-slice_fusion.2
  16.8 5.3 %all-to-all-start = ((bf16[8,40,768]{2,1,0:T(8,128)(2,1)}), bf16[8,40,768]{2,1,0:T(8,128)(2,1)S(1)}, u32[]{:S(2)}, u32[]{:S(2)}) async-start(bf16[8,40,768]{2,1,0:T(8,128)(2,1)} %bitcast.23), calls=%async_computation | async-start | bytes 983040 | tf_op jit(solution)/shard_map/all_to_all | solution.py:933
  22.1 3.3 %strips.1.refs_4_.refs_5_ = f32[2304,192]{1,0:T(8,128)} custom-call(f32[3,2304]{1,0:T(4,128)} %convolution_multiply_fusion.g_ref), custom_call_target="tpu_custom_call" | custom-call | flops 100000 | bytes 10000 | tf_op jit(solution)/shard_map/strips/pallas_call | solution.py:73
  27.1 1.7 maximum_select_fusion.1
  31.5 2.9 %collective-permute-start.6 = (bf16[4,136,384]{2,1,0:T(8,128)(2,1)S(1)}, bf16[4,136,384]{2,1,0:T(8,128)(2,1)S(1)}, u32[]{:S(2)}, u32[]{:S(2)}) collective-permute-start(bf16[4,136,384]{2,1,0:T(8,128)(2,1)S(1)} %pad_maximum_fusion.4.refs_0_), channel_id=1, source_target_pairs={{0,2},{2,0},{4,6},{6,4},{1,3},{3,1},{5,7},{7,5},{8,10},{10,8},{12,... | collective-permute-start | bytes 1253384 | tf_op jit(solution)/shard_map/ppermute | solution.py:818
  34.4 4.5 %collective-permute-done.7.refs_2_ = bf16[4,136,384]{2,1,0:T(8,128)(2,1)S(1)} collective-permute-done((bf16[4,136,384]{2,1,0:T(8,128)(2,1)S(1)}, bf16[4,136,384]{2,1,0:T(8,128)(2,1)S(1)}, u32[]{:S(2)}, u32[]{:S(2)}) %collective-permute-start.7) | collective-permute-done | bytes 417824 | tf_op jit(solution)/shard_map/ppermute | solution.py:818
  38.9 3.2 %collective-permute-start.8 = (bf16[4,136,384]{2,1,0:T(8,128)(2,1)S(1)}, bf16[4,136,384]{2,1,0:T(8,128)(2,1)S(1)}, u32[]{:S(2)}, u32[]{:S(2)}) collective-permute-start(bf16[4,136,384]{2,1,0:T(8,128)(2,1)S(1)} %collective-permute-done.7.refs_2_), channel_id=1, source_target_pairs={{0,2},{2,0},{4,6},{6,4},{1,3},{3,1},{5,7},{7,5},{8,10},{10,8},{12,... | collective-permute-start | bytes 1253384 | tf_op jit(solution)/shard_map/ppermute | solution.py:818
  43.4 14.7 %attend.1 = (f32[8,192,64]{2,1,0:T(8,128)}, bf16[192,128]{1,0:T(8,128)(2,1)S(1)}, bf16[192,128]{1,0:T(8,128)(2,1)S(1)}, bf16[192,128]{1,0:T(8,128)(2,1)S(1)}, bf...) custom-call(s32[2]{0:T(128)S(1)} %pad_add_fusion.pos, ...), custom_call_target="tpu_custom_call" | custom-call | flops 100000 | bytes 10000 | tf_op jit(solution)/shard_map/attend/pallas_call | solution.py:354
  58.5 2.1 collective-permute-start.10
  60.6 2.1 collective-permute-start.11
  62.7 2.9 %maximum_select_fusion = bf16[2,384,768]{2,1,0:T(8,128)(2,1)} fusion(bf16[1,384,768]{2,1,0:T(8,128)(2,1)} %bitcast.7, bf16[1,384,768]{2,1,0:T(8,128)(2,1)} %bitcast.6, pred[]{:T(512)S(6)} %eq.106), kind=kLoop, calls=%fused_computation.8 | loop fusion | flops 1769472 | bytes 2359297 | tf_op jit(solution)/shard_map/jit(_where)/select_n | solution.py:840
  65.6 2.9 %router.1 = (bf16[40,896]{1,0:T(8,128)(2,1)S(1)}, bf16[40,896]{1,0:T(8,128)(2,1)S(1)}, bf16[40,896]{1,0:T(8,128)(2,1)S(1)}, bf16[40,896]{1,0:T(8,128)(2,1)S(1)},...) custom-call(s32[2]{0:T(128)S(1)} %pad_add_fusion.pos, ...), custom_call_target="tpu_custom_call" | custom-call | flops 100000 | bytes 10000 | tf_op jit(solution)/shard_map/router/pallas_call | solution.py:459
  68.6 1.5 collective-permute-start.13
  71.3 2.0 collective-permute-start.15
  74.8 2.9 %collective-permute-start.18 = (bf16[40,896]{1,0:T(8,128)(2,1)S(1)}, bf16[40,896]{1,0:T(8,128)(2,1)S(1)}, u32[]{:S(2)}, u32[]{:S(2)}) collective-permute-start(bf16[40,896]{1,0:T(8,128)(2,1)S(1)} %get-tuple-element.136), channel_id=1, source_target_pairs={{0,25},{1,24},{8,1},{9,0},{16,9},{17,8},{24,17},{25,16},{2,27},{3,... | collective-permute-start | bytes 215048 | tf_op jit(solution)/shard_map/ppermute | solution.py:859
  77.8 4.1 %collective-permute-done.16.refs_5_ = bf16[40,896]{1,0:T(8,128)(2,1)S(1)} collective-permute-done((bf16[40,896]{1,0:T(8,128)(2,1)S(1)}, bf16[40,896]{1,0:T(8,128)(2,1)S(1)}, u32[]{:S(2)}, u32[]{:S(2)}) %collective-permute-start.16) | collective-permute-done | bytes 71712 | tf_op jit(solution)/shard_map/ppermute | solution.py:859
  81.9 2.5 collective-permute-done.17.refs_6_
  84.5 1.4 collective-permute-done.18.refs_7_
  85.9 11.9 %expert.1 = (bf16[4,40,768]{2,1,0:T(8,128)(2,1)}, bf16[4,40,768]{2,1,0:T(8,128)(2,1)}, bf16[8,40,896]{2,1,0:T(8,128)(2,1)}, bf16[2,320,3072]{2,1,0:T(8,128)(2,1)}, bf16[2,320,768]{2,1,0:T(8,128)(2,1)}) custom-call(s32[2]{0:T(128)S(1)} %pad_add_fusion.3.info, bf16[8,40,768]{2,1,0:T(8,128)(2,1)S(1)} %all-to-all-done.dy_ref, bf16[4,768,3072]{2,1,0:T(8,128)(2,1)} %up_ref.1, ...), custom_call_target="tpu_custom_call" | custom-call | flops 100000 | bytes 10000 | tf_op jit(solution)/shard_map/expert/pallas_call | solution.py:519
  98.5 4.5 %all-to-all-start.1 = ((bf16[8,40,896]{2,1,0:T(8,128)(2,1)}), bf16[8,40,896]{2,1,0:T(8,128)(2,1)S(1)}, u32[]{:S(2)}, u32[]{:S(2)}) async-start(bf16[8,40,896]{2,1,0:T(8,128)(2,1)} %get-tuple-element.137), calls=%async_computation.1 | async-start | bytes 1146880 | tf_op jit(solution)/shard_map/all_to_all | solution.py:933
  103.7 2.7 %collective-permute-done.19.refs_1_ = bf16[2,320,768]{2,1,0:T(8,128)(2,1)S(1)} collective-permute-done((bf16[2,320,768]{2,1,0:T(8,128)(2,1)}, bf16[2,320,768]{2,1,0:T(8,128)(2,1)S(1)}, u32[]{:S(2)}, u32[]{:S(2)}) %collective-permute-start.19) | collective-permute-done | bytes 983072 | tf_op jit(solution)/shard_map/ppermute | solution.py:828
  106.5 6.1 %weight_terms.3 = (bf16[192,3072]{1,0:T(8,128)(2,1)}, bf16[192,3072]{1,0:T(8,128)(2,1)}) custom-call(s32[2]{0:T(128)S(1)} %pad_add_fusion.pos, bf16[2,320,768]{2,1,0:T(8,128)(2,1)S(1)} %copy-done.1, bf16[2,320,768]{2,1,0:T(8,128)(2,1)S(1)} %collective-permute-done.19.refs_1_, bf16[2,320,3072]{2,1,0:T(8,128)(2,1)} %get-tuple-element.139.refs_2_, ...), custom_call_target="tpu_custom_call" | custom-call | flops 100000 | bytes 10000 | tf_op jit(solution)/shard_map/weight_terms/pallas_call | solution.py:572
  112.6 6.1 %weight_terms.2 = (bf16[192,3072]{1,0:T(8,128)(2,1)}, bf16[192,3072]{1,0:T(8,128)(2,1)}) custom-call(s32[2]{0:T(128)S(1)} %pad_add_fusion.pos, bf16[2,320,768]{2,1,0:T(8,128)(2,1)S(1)} %copy-done.1, bf16[2,320,768]{2,1,0:T(8,128)(2,1)S(1)} %collective-permute-done.19.refs_1_, bf16[2,320,3072]{2,1,0:T(8,128)(2,1)} %get-tuple-element.139.refs_2_, ...), custom_call_target="tpu_custom_call" | custom-call | flops 100000 | bytes 10000 | tf_op jit(solution)/shard_map/weight_terms/pallas_call | solution.py:572
  118.7 5.1 %turn_back.1 = (bf16[192,128]{1,0:T(8,128)(2,1)S(1)}, bf16[192,128]{1,0:T(8,128)(2,1)S(1)}, bf16[192,128]{1,0:T(8,128)(2,1)S(1)}, bf16[192,128]{1,0:T(8,128)(2,1...) custom-call(s32[3]{0:T(128)S(1)} %pad_add_fusion.2.info, ...), custom_call_target="tpu_custom_call" | custom-call | flops 100000 | bytes 10000 | tf_op jit(solution)/shard_map/turn_back/pallas_call | solution.py:694
  129.7 1.6 collective-permute-start.23
  132.2 1.8 collective-permute-start.24
  134.0 2.2 collective-permute-done.24.refs_3_
  136.2 17.2 %attend_back.1 = (bf16[512,192]{1,0:T(8,128)(2,1)S(1)}, bf16[4,128,384]{2,1,0:T(8,128)(2,1)S(1)}, bf16[4,128,384]{2,1,0:T(8,128)(2,1)S(1)}, bf16[4,128,384]{2,1,...) custom-call(s32[2]{0:T(128)S(1)} %pad_add_fusion.pos, ...), custom_call_target="tpu_custom_call" | custom-call | flops 100000 | bytes 10000 | tf_op jit(solution)/shard_map/attend_back/pallas_call | solution.py:384
  153.5 2.1 collective-permute-start.28
  158.7 2.0 add_groups.2
  163.9 8.6 %collective-permute-done.30.came_ref = bf16[4,128,384]{2,1,0:T(8,128)(2,1)S(1)} collective-permute-done((bf16[4,128,384]{2,1,0:T(8,128)(2,1)S(1)}, bf16[4,128,384]{2,1,0:T(8,128)(2,1)S(1)}, u32[]{:S(2)}, u32[]{:S(2)}) %collective-permute-start.30) | collective-permute-done | bytes 393248 | tf_op jit(solution)/shard_map/ppermute | solution.py:828
  173.1 3.0 %input_back.1 = (f32[128,768]{1,0:T(8,128)S(1)}, bf16[128,768]{1,0:T(8,128)(2,1)S(1)}, bf16[128,768]{1,0:T(8,128)(2,1)S(1)}, bf16[128,768]{1,0:T(8,128)(2,1)S(1)...) custom-call(s32[2]{0:T(128)S(1)} %pad_add_fusion.1.info, ...), custom_call_target="tpu_custom_call" | custom-call | flops 100000 | bytes 10000 | tf_op jit(solution)/shard_map/input_back/pallas_call | solution.py:782
  182.8 3.0 %collective-permute-start.35 = (bf16[272,768]{1,0:T(8,128)(2,1)S(1)}, bf16[272,768]{1,0:T(8,128)(2,1)S(1)}, u32[]{:S(2)}, u32[]{:S(2)}) collective-permute-start(bf16[272,768]{1,0:T(8,128)(2,1)S(1)} %copy-done.6), channel_id=1, source_target_pairs={{0,16},{8,24},{16,0},{24,8},{1,17},{9,25},{17,1},{25,9},{2,18},{10... | collective-permute-start | bytes 1253384 | tf_op jit(solution)/shard_map/ppermute | solution.py:844
  186.7 2.2 collective-permute-done.33
  189.2 23.3 %collective-permute-done.35.refs_2_ = bf16[272,768]{1,0:T(8,128)(2,1)S(1)} collective-permute-done((bf16[272,768]{1,0:T(8,128)(2,1)S(1)}, bf16[272,768]{1,0:T(8,128)(2,1)S(1)}, u32[]{:S(2)}, u32[]{:S(2)}) %collective-permute-start.35) | collective-permute-done | bytes 417824 | tf_op jit(solution)/shard_map/ppermute | solution.py:844
  214.9 1.9 add_groups.3
  218.1 3.5 %collective-permute-start.48 = (bf16[192,768]{1,0:T(8,128)(2,1)S(1)}, bf16[192,768]{1,0:T(8,128)(2,1)S(1)}, u32[]{:S(2)}, u32[]{:S(2)}) collective-permute-start(bf16[192,768]{1,0:T(8,128)(2,1)S(1)} %get-tuple-element.218), channel_id=1, source_target_pairs={{0,16},{8,24},{16,0},{24,8},{1,17},{9,25},{17,1},{25,9},{2,18},{10... | collective-permute-start | bytes 884744 | tf_op jit(solution)/shard_map/ppermute | solution.py:844
  222.1 3.8 %collective-permute-start.40 = (bf16[48,384]{1,0:T(8,128)(2,1)S(1)}, bf16[48,384]{1,0:T(8,128)(2,1)S(1)}, u32[]{:S(2)}, u32[]{:S(2)}) collective-permute-start(bf16[48,384]{1,0:T(8,128)(2,1)S(1)} %get-tuple-element.255), channel_id=1, source_target_pairs={{4,0},{10,2},{16,4},{22,6},{28,8},{2,10},{8,12},{14,14},{20,16},{2... | collective-permute-start | bytes 110600 | tf_op jit(solution)/shard_map/ppermute | solution.py:1065
  225.9 2.5 collective-permute-start.39
  228.4 3.4 %collective-permute-start.38 = (bf16[48,384]{1,0:T(8,128)(2,1)S(1)}, bf16[48,384]{1,0:T(8,128)(2,1)S(1)}, u32[]{:S(2)}, u32[]{:S(2)}) collective-permute-start(bf16[48,384]{1,0:T(8,128)(2,1)S(1)} %get-tuple-element.257), channel_id=1, source_target_pairs={{0,0},{6,2},{12,4},{18,6},{24,8},{30,10},{4,12},{10,14},{16,16},{2... | collective-permute-start | bytes 110600 | tf_op jit(solution)/shard_map/ppermute | solution.py:1065
  231.9 15.2 %collective-permute-done.48.refs_2_ = bf16[192,768]{1,0:T(8,128)(2,1)S(1)} collective-permute-done((bf16[192,768]{1,0:T(8,128)(2,1)S(1)}, bf16[192,768]{1,0:T(8,128)(2,1)S(1)}, u32[]{:S(2)}, u32[]{:S(2)}) %collective-permute-start.48) | collective-permute-done | bytes 294944 | tf_op jit(solution)/shard_map/ppermute | solution.py:844
  247.2 3.1 %collective-permute-start.44 = (bf16[80,384]{1,0:T(8,128)(2,1)S(1)}, bf16[80,384]{1,0:T(8,128)(2,1)S(1)}, u32[]{:S(2)}, u32[]{:S(2)}) collective-permute-start(bf16[80,384]{1,0:T(8,128)(2,1)S(1)} %get-tuple-element.260), channel_id=1, source_target_pairs={{0,16},{8,24},{16,0},{24,8},{1,17},{9,25},{17,1},{25,9},{2,18},{10... | collective-permute-start | bytes 184328 | tf_op jit(solution)/shard_map/ppermute | solution.py:1056
  250.2 2.1 in_order.3
  252.3 2.4 collective-permute-start.45
  254.7 1.5 collective-permute-start.41
  256.2 2.1 in_order.2
  (230 shorter events, 53.5 us)
Async XLA Ops:
  2.3 23.1 %collective-permute-start.4 = (bf16[136,768]{1,0:T(8,128)(2,1)S(1)}, bf16[136,768]{1,0:T(8,128)(2,1)S(1)}, u32[]{:S(2)}, u32[]{:S(2)}) collective-permute-start(bf16[136,768]{1,0:T(8,128)(2,1)S(1)} %get-tuple-element.251), channel_id=1, source_target_pairs={{0,16},{8,24},{16,0},{24,8},{1,17},{9,25},{17,1},{25,9},{2,18},{10... | collective-permute-start | bytes 626696 | tf_op jit(solution)/shard_map/ppermute | solution.py:809
  4.7 20.8 %collective-permute-start.3 = (bf16[136,768]{1,0:T(8,128)(2,1)S(1)}, bf16[136,768]{1,0:T(8,128)(2,1)}, u32[]{:S(2)}, u32[]{:S(2)}) collective-permute-start(bf16[136,768]{1,0:T(8,128)(2,1)S(1)} %get-tuple-element.251), channel_id=1, source_target_pairs={{0,8},{8,16},{16,24},{24,0},{1,9},{9,17},{17,25},{25,1},{2,10},{10... | collective-permute-start | bytes 626696 | tf_op jit(solution)/shard_map/ppermute | solution.py:809
  4.7 20.8 %collective-permute-start.5 = (bf16[136,768]{1,0:T(8,128)(2,1)S(1)}, bf16[136,768]{1,0:T(8,128)(2,1)}, u32[]{:S(2)}, u32[]{:S(2)}) collective-permute-start(bf16[136,768]{1,0:T(8,128)(2,1)S(1)} %get-tuple-element.251), channel_id=1, source_target_pairs={{0,24},{8,0},{16,8},{24,16},{1,25},{9,1},{17,9},{25,17},{2,26},{10... | collective-permute-start | bytes 626696 | tf_op jit(solution)/shard_map/ppermute | solution.py:809
  9.2 6.5 %collective-permute-start.2 = (bf16[16,384]{1,0:T(8,128)(2,1)S(1)}, bf16[16,384]{1,0:T(8,128)(2,1)S(1)}, u32[]{:S(2)}, u32[]{:S(2)}) collective-permute-start(bf16[16,384]{1,0:T(8,128)(2,1)S(1)} %concatenate.53), channel_id=1, source_target_pairs={{0,1},{1,0},{2,3},{3,2},{4,5},{5,4},{6,7},{7,6},{8,9},{9,8},{10,11... | collective-permute-start | bytes 36872 | tf_op jit(solution)/shard_map/ppermute | solution.py:839
  11.1 16.0 %collective-permute-start = (bf16[384,576]{1,0:T(8,128)(2,1)S(1)}, bf16[384,576]{1,0:T(8,128)(2,1)}, u32[]{:S(2)}, u32[]{:S(2)}) collective-permute-start(bf16[384,576]{1,0:T(8,128)(2,1)S(1)} %pad_maximum_fusion.2), channel_id=1, source_target_pairs={{0,1},{1,0},{2,3},{3,2},{4,5},{5,4},{6,7},{7,6},{8,9},{9,8},{10,11... | collective-permute-start | bytes 1327112 | tf_op jit(solution)/shard_map/ppermute | solution.py:839
  16.8 41.4 %all-to-all-start = ((bf16[8,40,768]{2,1,0:T(8,128)(2,1)}), bf16[8,40,768]{2,1,0:T(8,128)(2,1)S(1)}, u32[]{:S(2)}, u32[]{:S(2)}) async-start(bf16[8,40,768]{2,1,0:T(8,128)(2,1)} %bitcast.23), calls=%async_computation | async-start | bytes 983040 | tf_op jit(solution)/shard_map/all_to_all | solution.py:933
  29.9 9.0 %collective-permute-start.7 = (bf16[4,136,384]{2,1,0:T(8,128)(2,1)S(1)}, bf16[4,136,384]{2,1,0:T(8,128)(2,1)S(1)}, u32[]{:S(2)}, u32[]{:S(2)}) collective-permute-start(bf16[4,136,384]{2,1,0:T(8,128)(2,1)S(1)} %pad_maximum_fusion.4.refs_0_), channel_id=1, source_target_pairs={{0,4},{2,6},{4,0},{6,2},{1,5},{3,7},{5,1},{7,3},{8,12},{10,14},{12... | collective-permute-start | bytes 1253384 | tf_op jit(solution)/shard_map/ppermute | solution.py:818
  31.2 31.5 %collective-permute-start.1 = (bf16[384,768]{1,0:T(8,128)(2,1)}, bf16[384,768]{1,0:T(8,128)(2,1)}, u32[]{:S(2)}, u32[]{:S(2)}) collective-permute-start(bf16[384,768]{1,0:T(8,128)(2,1)} %param.19), channel_id=1, source_target_pairs={{0,1},{1,0},{2,3},{3,2},{4,5},{5,4},{6,7},{7,6},{8,9},{9,8},{10,11... | collective-permute-start | bytes 1769480 | tf_op jit(solution)/shard_map/ppermute | solution.py:839
  31.5 10.7 %collective-permute-start.6 = (bf16[4,136,384]{2,1,0:T(8,128)(2,1)S(1)}, bf16[4,136,384]{2,1,0:T(8,128)(2,1)S(1)}, u32[]{:S(2)}, u32[]{:S(2)}) collective-permute-start(bf16[4,136,384]{2,1,0:T(8,128)(2,1)S(1)} %pad_maximum_fusion.4.refs_0_), channel_id=1, source_target_pairs={{0,2},{2,0},{4,6},{6,4},{1,3},{3,1},{5,7},{7,5},{8,10},{10,8},{12,... | collective-permute-start | bytes 1253384 | tf_op jit(solution)/shard_map/ppermute | solution.py:818
  38.9 4.6 %collective-permute-start.8 = (bf16[4,136,384]{2,1,0:T(8,128)(2,1)S(1)}, bf16[4,136,384]{2,1,0:T(8,128)(2,1)S(1)}, u32[]{:S(2)}, u32[]{:S(2)}) collective-permute-start(bf16[4,136,384]{2,1,0:T(8,128)(2,1)S(1)} %collective-permute-done.7.refs_2_), channel_id=1, source_target_pairs={{0,2},{2,0},{4,6},{6,4},{1,3},{3,1},{5,7},{7,5},{8,10},{10,8},{12,... | collective-permute-start | bytes 1253384 | tf_op jit(solution)/shard_map/ppermute | solution.py:818
  58.2 7.4 %collective-permute-start.9 = (bf16[192,128]{1,0:T(8,128)(2,1)S(1)}, bf16[192,128]{1,0:T(8,128)(2,1)S(1)}, u32[]{:S(2)}, u32[]{:S(2)}) collective-permute-start(bf16[192,128]{1,0:T(8,128)(2,1)S(1)} %get-tuple-element.121), channel_id=1, source_target_pairs={{0,24},{8,0},{16,8},{24,16},{1,25},{9,1},{17,9},{25,17},{2,26},{10... | collective-permute-start | bytes 147464 | tf_op jit(solution)/shard_map/ppermute | solution.py:844
  58.5 7.1 %collective-permute-start.10 = (bf16[192,128]{1,0:T(8,128)(2,1)S(1)}, bf16[192,128]{1,0:T(8,128)(2,1)S(1)}, u32[]{:S(2)}, u32[]{:S(2)}) collective-permute-start(bf16[192,128]{1,0:T(8,128)(2,1)S(1)} %get-tuple-element.122), channel_id=1, source_target_pairs={{0,16},{8,24},{16,0},{24,8},{1,17},{9,25},{17,1},{25,9},{2,18},{10... | collective-permute-start | bytes 147464 | tf_op jit(solution)/shard_map/ppermute | solution.py:844
  60.6 5.0 %collective-permute-start.11 = (bf16[192,128]{1,0:T(8,128)(2,1)S(1)}, bf16[192,128]{1,0:T(8,128)(2,1)S(1)}, u32[]{:S(2)}, u32[]{:S(2)}) collective-permute-start(bf16[192,128]{1,0:T(8,128)(2,1)S(1)} %get-tuple-element.123), channel_id=1, source_target_pairs={{0,8},{8,16},{16,24},{24,0},{1,9},{9,17},{17,25},{25,1},{2,10},{10... | collective-permute-start | bytes 147464 | tf_op jit(solution)/shard_map/ppermute | solution.py:844
  68.6 5.1 %collective-permute-start.12 = (bf16[40,896]{1,0:T(8,128)(2,1)S(1)}, bf16[40,896]{1,0:T(8,128)(2,1)S(1)}, u32[]{:S(2)}, u32[]{:S(2)}) collective-permute-start(bf16[40,896]{1,0:T(8,128)(2,1)S(1)} %get-tuple-element.130), channel_id=1, source_target_pairs={{0,1},{1,0},{8,9},{9,8},{16,17},{17,16},{24,25},{25,24},{2,3},{3,2... | collective-permute-start | bytes 215048 | tf_op jit(solution)/shard_map/ppermute | solution.py:859
  68.6 6.3 %collective-permute-start.13 = (bf16[40,896]{1,0:T(8,128)(2,1)S(1)}, bf16[40,896]{1,0:T(8,128)(2,1)S(1)}, u32[]{:S(2)}, u32[]{:S(2)}) collective-permute-start(bf16[40,896]{1,0:T(8,128)(2,1)S(1)} %get-tuple-element.131), channel_id=1, source_target_pairs={{0,8},{1,9},{8,16},{9,17},{16,24},{17,25},{24,0},{25,1},{2,10},{3,... | collective-permute-start | bytes 215048 | tf_op jit(solution)/shard_map/ppermute | solution.py:859
  70.1 7.7 %collective-permute-start.14 = (bf16[40,896]{1,0:T(8,128)(2,1)S(1)}, bf16[40,896]{1,0:T(8,128)(2,1)S(1)}, u32[]{:S(2)}, u32[]{:S(2)}) collective-permute-start(bf16[40,896]{1,0:T(8,128)(2,1)S(1)} %get-tuple-element.132), channel_id=1, source_target_pairs={{0,9},{1,8},{8,17},{9,16},{16,25},{17,24},{24,1},{25,0},{2,11},{3,... | collective-permute-start | bytes 215048 | tf_op jit(solution)/shard_map/ppermute | solution.py:859
  71.3 6.5 %collective-permute-start.15 = (bf16[40,896]{1,0:T(8,128)(2,1)S(1)}, bf16[40,896]{1,0:T(8,128)(2,1)S(1)}, u32[]{:S(2)}, u32[]{:S(2)}) collective-permute-start(bf16[40,896]{1,0:T(8,128)(2,1)S(1)} %get-tuple-element.133), channel_id=1, source_target_pairs={{0,16},{1,17},{8,24},{9,25},{16,0},{17,1},{24,8},{25,9},{2,18},{3,... | collective-permute-start | bytes 215048 | tf_op jit(solution)/shard_map/ppermute | solution.py:859
  73.3 8.6 %collective-permute-start.16 = (bf16[40,896]{1,0:T(8,128)(2,1)S(1)}, bf16[40,896]{1,0:T(8,128)(2,1)S(1)}, u32[]{:S(2)}, u32[]{:S(2)}) collective-permute-start(bf16[40,896]{1,0:T(8,128)(2,1)S(1)} %get-tuple-element.134), channel_id=1, source_target_pairs={{0,17},{1,16},{8,25},{9,24},{16,1},{17,0},{24,9},{25,8},{2,19},{3,... | collective-permute-start | bytes 215048 | tf_op jit(solution)/shard_map/ppermute | solution.py:859
  73.7 10.8 %collective-permute-start.17 = (bf16[40,896]{1,0:T(8,128)(2,1)S(1)}, bf16[40,896]{1,0:T(8,128)(2,1)S(1)}, u32[]{:S(2)}, u32[]{:S(2)}) collective-permute-start(bf16[40,896]{1,0:T(8,128)(2,1)S(1)} %get-tuple-element.135), channel_id=1, source_target_pairs={{0,24},{1,25},{8,0},{9,1},{16,8},{17,9},{24,16},{25,17},{2,26},{3,... | collective-permute-start | bytes 215048 | tf_op jit(solution)/shard_map/ppermute | solution.py:859
  74.8 11.0 %collective-permute-start.18 = (bf16[40,896]{1,0:T(8,128)(2,1)S(1)}, bf16[40,896]{1,0:T(8,128)(2,1)S(1)}, u32[]{:S(2)}, u32[]{:S(2)}) collective-permute-start(bf16[40,896]{1,0:T(8,128)(2,1)S(1)} %get-tuple-element.136), channel_id=1, source_target_pairs={{0,25},{1,24},{8,1},{9,0},{16,9},{17,8},{24,17},{25,16},{2,27},{3,... | collective-permute-start | bytes 215048 | tf_op jit(solution)/shard_map/ppermute | solution.py:859
  97.8 8.7 %collective-permute-start.20 = (bf16[2,320,3072]{2,1,0:T(8,128)(2,1)}, bf16[2,320,3072]{2,1,0:T(8,128)(2,1)}, u32[]{:S(2)}, u32[]{:S(2)}) collective-permute-start(bf16[2,320,3072]{2,1,0:T(8,128)(2,1)} %get-tuple-element.139.refs_2_), channel_id=1, source_target_pairs={{0,2},{2,0},{1,3},{3,1},{4,6},{6,4},{5,7},{7,5},{8,10},{10,8},{9,1... | collective-permute-start | bytes 11796488 | tf_op jit(solution)/shard_map/ppermute | solution.py:828
  98.5 20.2 %all-to-all-start.1 = ((bf16[8,40,896]{2,1,0:T(8,128)(2,1)}), bf16[8,40,896]{2,1,0:T(8,128)(2,1)S(1)}, u32[]{:S(2)}, u32[]{:S(2)}) async-start(bf16[8,40,896]{2,1,0:T(8,128)(2,1)} %get-tuple-element.137), calls=%async_computation.1 | async-start | bytes 1146880 | tf_op jit(solution)/shard_map/all_to_all | solution.py:933
  102.9 3.5 %collective-permute-start.19 = (bf16[2,320,768]{2,1,0:T(8,128)(2,1)}, bf16[2,320,768]{2,1,0:T(8,128)(2,1)S(1)}, u32[]{:S(2)}, u32[]{:S(2)}) collective-permute-start(bf16[2,320,768]{2,1,0:T(8,128)(2,1)} %get-tuple-element.138.refs_0_), channel_id=1, source_target_pairs={{0,2},{2,0},{1,3},{3,1},{4,6},{6,4},{5,7},{7,5},{8,10},{10,8},{9,1... | collective-permute-start | bytes 2949128 | tf_op jit(solution)/shard_map/ppermute | solution.py:828
  124.2 33.5 %collective-permute-start.29 = (bf16[192,3072]{1,0:T(8,128)(2,1)S(1)}, bf16[192,3072]{1,0:T(8,128)(2,1)S(1)}, u32[]{:S(2)}, u32[]{:S(2)}) collective-permute-start(bf16[192,3072]{1,0:T(8,128)(2,1)S(1)} %copy-done.26), channel_id=1, source_target_pairs={{0,4},{4,0},{1,5},{5,1},{2,6},{6,2},{3,7},{7,3},{8,12},{12,8},{9,1... | collective-permute-start | bytes 3538952 | tf_op jit(solution)/shard_map/ppermute | solution.py:828
  127.4 28.2 %collective-permute-start.25 = (bf16[8,48,384]{2,1,0:T(8,128)(2,1)S(1)}, bf16[8,48,384]{2,1,0:T(8,128)(2,1)S(1)}, u32[]{:S(2)}, u32[]{:S(2)}) collective-permute-start(bf16[8,48,384]{2,1,0:T(8,128)(2,1)S(1)} %fusion.5), channel_id=1, source_target_pairs={{0,1},{1,0},{2,3},{3,2},{4,5},{5,4},{6,7},{7,6},{8,9},{9,8},{10,11... | collective-permute-start | bytes 884744 | tf_op jit(solution)/shard_map/ppermute | solution.py:828
  128.6 26.9 %collective-permute-start.26 = (bf16[4,40,768]{2,1,0:T(8,128)(2,1)S(1)}, bf16[4,40,768]{2,1,0:T(8,128)(2,1)S(1)}, u32[]{:S(2)}, u32[]{:S(2)}) collective-permute-start(bf16[4,40,768]{2,1,0:T(8,128)(2,1)S(1)} %copy-done.27), channel_id=1, source_target_pairs={{0,1},{1,0},{2,3},{3,2},{4,5},{5,4},{6,7},{7,6},{8,9},{9,8},{10,11... | collective-permute-start | bytes 737288 | tf_op jit(solution)/shard_map/ppermute | solution.py:973
  129.7 4.3 %collective-permute-start.23 = (bf16[192,128]{1,0:T(8,128)(2,1)S(1)}, bf16[192,128]{1,0:T(8,128)(2,1)S(1)}, u32[]{:S(2)}, u32[]{:S(2)}) collective-permute-start(bf16[192,128]{1,0:T(8,128)(2,1)S(1)} %get-tuple-element.150), channel_id=1, source_target_pairs={{0,16},{8,24},{16,0},{24,8},{1,17},{9,25},{17,1},{25,9},{2,18},{10... | collective-permute-start | bytes 147464 | tf_op jit(solution)/shard_map/ppermute | solution.py:844
  132.2 4.0 %collective-permute-start.24 = (bf16[192,128]{1,0:T(8,128)(2,1)S(1)}, bf16[192,128]{1,0:T(8,128)(2,1)S(1)}, u32[]{:S(2)}, u32[]{:S(2)}) collective-permute-start(bf16[192,128]{1,0:T(8,128)(2,1)S(1)} %get-tuple-element.151), channel_id=1, source_target_pairs={{0,24},{8,0},{16,8},{24,16},{1,25},{9,1},{17,9},{25,17},{2,26},{10... | collective-permute-start | bytes 147464 | tf_op jit(solution)/shard_map/ppermute | solution.py:844
  153.5 3.5 %collective-permute-start.28 = (bf16[4,128,384]{2,1,0:T(8,128)(2,1)S(1)}, bf16[4,128,384]{2,1,0:T(8,128)(2,1)S(1)}, u32[]{:S(2)}, u32[]{:S(2)}) collective-permute-start(bf16[4,128,384]{2,1,0:T(8,128)(2,1)S(1)} %get-tuple-element.165), channel_id=1, source_target_pairs={{0,2},{2,0},{1,3},{3,1},{4,6},{6,4},{5,7},{7,5},{8,10},{10,8},{9,1... | collective-permute-start | bytes 1179656 | tf_op jit(solution)/shard_map/ppermute | solution.py:828
  161.5 11.6 %collective-permute-start.31 = (bf16[272,768]{1,0:T(8,128)(2,1)S(1)}, bf16[272,768]{1,0:T(8,128)(2,1)S(1)}, u32[]{:S(2)}, u32[]{:S(2)}) collective-permute-start(bf16[272,768]{1,0:T(8,128)(2,1)S(1)} %get-tuple-element.174), channel_id=1, source_target_pairs={{0,8},{8,16},{16,24},{24,0},{1,9},{9,17},{17,25},{25,1},{2,10},{10... | collective-permute-start | bytes 1253384 | tf_op jit(solution)/shard_map/ppermute | solution.py:844
  162.5 10.0 %collective-permute-start.30 = (bf16[4,128,384]{2,1,0:T(8,128)(2,1)S(1)}, bf16[4,128,384]{2,1,0:T(8,128)(2,1)S(1)}, u32[]{:S(2)}, u32[]{:S(2)}) collective-permute-start(bf16[4,128,384]{2,1,0:T(8,128)(2,1)S(1)} %get-tuple-element.169), channel_id=1, source_target_pairs={{0,4},{4,0},{1,5},{5,1},{2,6},{6,2},{3,7},{7,3},{8,12},{12,8},{9,1... | collective-permute-start | bytes 1179656 | tf_op jit(solution)/shard_map/ppermute | solution.py:828
  178.8 35.1 %collective-permute-start.34 = (bf16[192,3072]{1,0:T(8,128)(2,1)}, bf16[192,3072]{1,0:T(8,128)(2,1)S(1)}, u32[]{:S(2)}, u32[]{:S(2)}) collective-permute-start(bf16[192,3072]{1,0:T(8,128)(2,1)} %get-tuple-element.186), channel_id=1, source_target_pairs={{0,4},{4,0},{1,5},{5,1},{2,6},{6,2},{3,7},{7,3},{8,12},{12,8},{9,1... | collective-permute-start | bytes 3538952 | tf_op jit(solution)/shard_map/ppermute | solution.py:828
  181.6 7.3 %collective-permute-start.33 = (bf16[320,384]{1,0:T(8,128)(2,1)S(1)}, bf16[320,384]{1,0:T(8,128)(2,1)S(1)}, u32[]{:S(2)}, u32[]{:S(2)}) collective-permute-start(bf16[320,384]{1,0:T(8,128)(2,1)S(1)} %pad_maximum_fusion.6), channel_id=1, source_target_pairs={{0,1},{1,0},{2,3},{3,2},{4,5},{5,4},{6,7},{7,6},{8,9},{9,8},{10,11... | collective-permute-start | bytes 737288 | tf_op jit(solution)/shard_map/ppermute | solution.py:828
  182.8 29.7 %collective-permute-start.35 = (bf16[272,768]{1,0:T(8,128)(2,1)S(1)}, bf16[272,768]{1,0:T(8,128)(2,1)S(1)}, u32[]{:S(2)}, u32[]{:S(2)}) collective-permute-start(bf16[272,768]{1,0:T(8,128)(2,1)S(1)} %copy-done.6), channel_id=1, source_target_pairs={{0,16},{8,24},{16,0},{24,8},{1,17},{9,25},{17,1},{25,9},{2,18},{10... | collective-permute-start | bytes 1253384 | tf_op jit(solution)/shard_map/ppermute | solution.py:844
  185.8 28.1 %collective-permute-start.36 = (bf16[272,768]{1,0:T(8,128)(2,1)S(1)}, bf16[272,768]{1,0:T(8,128)(2,1)S(1)}, u32[]{:S(2)}, u32[]{:S(2)}) collective-permute-start(bf16[272,768]{1,0:T(8,128)(2,1)S(1)} %get-tuple-element.190), channel_id=1, source_target_pairs={{0,24},{8,0},{16,8},{24,16},{1,25},{9,1},{17,9},{25,17},{2,26},{10... | collective-permute-start | bytes 1253384 | tf_op jit(solution)/shard_map/ppermute | solution.py:844
  213.9 7.7 %collective-permute-start.42 = (bf16[128,768]{1,0:T(8,128)(2,1)S(1)}, bf16[128,768]{1,0:T(8,128)(2,1)S(1)}, u32[]{:S(2)}, u32[]{:S(2)}) collective-permute-start(bf16[128,768]{1,0:T(8,128)(2,1)S(1)} %copy-done.8), channel_id=1, source_target_pairs={{0,24},{8,0},{16,8},{24,16},{1,25},{9,1},{17,9},{25,17},{2,26},{10... | collective-permute-start | bytes 589832 | tf_op jit(solution)/shard_map/ppermute | solution.py:1040
  214.0 7.9 %collective-permute-start.37 = (bf16[368,384]{1,0:T(8,128)(2,1)S(1)}, bf16[368,384]{1,0:T(8,128)(2,1)S(1)}, u32[]{:S(2)}, u32[]{:S(2)}) collective-permute-start(bf16[368,384]{1,0:T(8,128)(2,1)S(1)} %pad_maximum_fusion.5), channel_id=1, source_target_pairs={{0,4},{4,0},{1,5},{5,1},{2,6},{6,2},{3,7},{7,3},{8,12},{12,8},{9,1... | collective-permute-start | bytes 847880 | tf_op jit(solution)/shard_map/ppermute | solution.py:828
  216.8 11.7 %collective-permute-start.47 = (bf16[192,768]{1,0:T(8,128)(2,1)S(1)}, bf16[192,768]{1,0:T(8,128)(2,1)S(1)}, u32[]{:S(2)}, u32[]{:S(2)}) collective-permute-start(bf16[192,768]{1,0:T(8,128)(2,1)S(1)} %get-tuple-element.217), channel_id=1, source_target_pairs={{0,8},{8,16},{16,24},{24,0},{1,9},{9,17},{17,25},{25,1},{2,10},{10... | collective-permute-start | bytes 884744 | tf_op jit(solution)/shard_map/ppermute | solution.py:844
  218.1 29.0 %collective-permute-start.48 = (bf16[192,768]{1,0:T(8,128)(2,1)S(1)}, bf16[192,768]{1,0:T(8,128)(2,1)S(1)}, u32[]{:S(2)}, u32[]{:S(2)}) collective-permute-start(bf16[192,768]{1,0:T(8,128)(2,1)S(1)} %get-tuple-element.218), channel_id=1, source_target_pairs={{0,16},{8,24},{16,0},{24,8},{1,17},{9,25},{17,1},{25,9},{2,18},{10... | collective-permute-start | bytes 884744 | tf_op jit(solution)/shard_map/ppermute | solution.py:844
  221.6 25.6 %collective-permute-start.49 = (bf16[192,768]{1,0:T(8,128)(2,1)S(1)}, bf16[192,768]{1,0:T(8,128)(2,1)S(1)}, u32[]{:S(2)}, u32[]{:S(2)}) collective-permute-start(bf16[192,768]{1,0:T(8,128)(2,1)S(1)} %get-tuple-element.219), channel_id=1, source_target_pairs={{0,24},{8,0},{16,8},{24,16},{1,25},{9,1},{17,9},{25,17},{2,26},{10... | collective-permute-start | bytes 884744 | tf_op jit(solution)/shard_map/ppermute | solution.py:844
  222.1 30.2 %collective-permute-start.40 = (bf16[48,384]{1,0:T(8,128)(2,1)S(1)}, bf16[48,384]{1,0:T(8,128)(2,1)S(1)}, u32[]{:S(2)}, u32[]{:S(2)}) collective-permute-start(bf16[48,384]{1,0:T(8,128)(2,1)S(1)} %get-tuple-element.255), channel_id=1, source_target_pairs={{4,0},{10,2},{16,4},{22,6},{28,8},{2,10},{8,12},{14,14},{20,16},{2... | collective-permute-start | bytes 110600 | tf_op jit(solution)/shard_map/ppermute | solution.py:1065
  225.9 28.8 %collective-permute-start.39 = (bf16[48,384]{1,0:T(8,128)(2,1)S(1)}, bf16[48,384]{1,0:T(8,128)(2,1)S(1)}, u32[]{:S(2)}, u32[]{:S(2)}) collective-permute-start(bf16[48,384]{1,0:T(8,128)(2,1)S(1)} %get-tuple-element.256), channel_id=1, source_target_pairs={{2,0},{8,2},{14,4},{20,6},{26,8},{0,10},{6,12},{12,14},{18,16},{24... | collective-permute-start | bytes 110600 | tf_op jit(solution)/shard_map/ppermute | solution.py:1065
  228.4 26.3 %collective-permute-start.38 = (bf16[48,384]{1,0:T(8,128)(2,1)S(1)}, bf16[48,384]{1,0:T(8,128)(2,1)S(1)}, u32[]{:S(2)}, u32[]{:S(2)}) collective-permute-start(bf16[48,384]{1,0:T(8,128)(2,1)S(1)} %get-tuple-element.257), channel_id=1, source_target_pairs={{0,0},{6,2},{12,4},{18,6},{24,8},{30,10},{4,12},{10,14},{16,16},{2... | collective-permute-start | bytes 110600 | tf_op jit(solution)/shard_map/ppermute | solution.py:1065
  247.1 16.7 %collective-permute-start.43 = (bf16[128,768]{1,0:T(8,128)(2,1)S(1)}, bf16[128,768]{1,0:T(8,128)(2,1)S(1)}, u32[]{:S(2)}, u32[]{:S(2)}) collective-permute-start(bf16[128,768]{1,0:T(8,128)(2,1)S(1)} %add_convert_fusion), channel_id=1, source_target_pairs={{0,24},{8,0},{16,8},{24,16},{1,25},{9,1},{17,9},{25,17},{2,26},{10... | collective-permute-start | bytes 589832 | tf_op jit(solution)/shard_map/ppermute | solution.py:1043
  247.2 13.9 %collective-permute-start.44 = (bf16[80,384]{1,0:T(8,128)(2,1)S(1)}, bf16[80,384]{1,0:T(8,128)(2,1)S(1)}, u32[]{:S(2)}, u32[]{:S(2)}) collective-permute-start(bf16[80,384]{1,0:T(8,128)(2,1)S(1)} %get-tuple-element.260), channel_id=1, source_target_pairs={{0,16},{8,24},{16,0},{24,8},{1,17},{9,25},{17,1},{25,9},{2,18},{10... | collective-permute-start | bytes 184328 | tf_op jit(solution)/shard_map/ppermute | solution.py:1056
  252.3 8.7 %collective-permute-start.45 = (bf16[80,384]{1,0:T(8,128)(2,1)S(1)}, bf16[80,384]{1,0:T(8,128)(2,1)S(1)}, u32[]{:S(2)}, u32[]{:S(2)}) collective-permute-start(bf16[80,384]{1,0:T(8,128)(2,1)S(1)} %get-tuple-element.261), channel_id=1, source_target_pairs={{0,8},{8,16},{16,24},{24,0},{1,9},{9,17},{17,25},{25,1},{2,10},{10... | collective-permute-start | bytes 184328 | tf_op jit(solution)/shard_map/ppermute | solution.py:1056
  254.7 6.4 %collective-permute-start.46 = (bf16[80,384]{1,0:T(8,128)(2,1)S(1)}, bf16[80,384]{1,0:T(8,128)(2,1)S(1)}, u32[]{:S(2)}, u32[]{:S(2)}) collective-permute-start(bf16[80,384]{1,0:T(8,128)(2,1)S(1)} %get-tuple-element.262), channel_id=1, source_target_pairs={{0,24},{8,0},{16,8},{24,16},{1,25},{9,1},{17,9},{25,17},{2,26},{10... | collective-permute-start | bytes 184328 | tf_op jit(solution)/shard_map/ppermute | solution.py:1056
  254.7 9.4 %collective-permute-start.41 = (bf16[128,768]{1,0:T(8,128)(2,1)S(1)}, bf16[128,768]{1,0:T(8,128)(2,1)S(1)}, u32[]{:S(2)}, u32[]{:S(2)}) collective-permute-start(bf16[128,768]{1,0:T(8,128)(2,1)S(1)} %get-tuple-element.208), channel_id=1, source_target_pairs={{0,8},{8,16},{16,24},{24,0},{1,9},{9,17},{17,25},{25,1},{2,10},{10... | collective-permute-start | bytes 589832 | tf_op jit(solution)/shard_map/ppermute | solution.py:1041
  (32 other events, 220.4 us)

commit v8 on v7

--- a/solution.py
+++ b/solution.py
@@ -968,13 +968,11 @@
         moe_scale[None], out_full, context, shards,
     )
     dos = group_pieces(dos, 1)
-    out_came = swap(out_send, "core", 1)
-    out_far = (out_other + out_came[1].astype(F32)).astype(BF)
     outs = [outs[0]] + [lax.ppermute(outs[j], "fsdp", xor_perm(j, n_fsdp)) for j in range(1, n_fsdp)]
-    dos[0], out_far = together(dos[0], out_far)
-    out_far = swap(out_far, "fsdp", top_bit)
     dq, *dkvs, dline = attend_back(pos, proj, keys, strips, dos, o_pre, stat, members, blocks)
-    dkvs[1], out_far, outs = together(dkvs[1], out_far, outs)
+    dkvs[1], outs = together(dkvs[1], outs)
+    out_came = swap(together(out_send, dq)[0], "core", 1)
+    out_far = swap((out_other + out_came[1].astype(F32)).astype(BF), "fsdp", top_bit)
     cames = [swap(dkvs[k], "core", 1) for k in range(1, members, 2)]
     sends = []
     if members == 4:

time: 268 us -> 266 us (level)
  waiting for transfers between devices: 73.9 us -> 81 us
  Pallas kernels: 78.7 us -> 74.2 us
  starting transfers between devices: 78.1 us -> 75.4 us
    ppermute x12, waiting for transfers between devices: 16.2 us -> 19.9 us  [swap(): return lax.ppermute(x, axis, xor_perm(bit, lax.axis_size(axis)))]
  transfers between devices with their start and end apart: 52 -> 52, of which waited for: 19 -> 21; matrix products, arithmetic and copies ran while one was open for 10% -> 9% of each run, Pallas kernels for 20% -> 22%
where the time goes in v8:
time: 266 us; the launch traced here: 262 us
  waiting for transfers between devices  81 us (30%)
  starting transfers between devices  75.4 us (28%)
  Pallas kernels  74.2 us (28%)
  other arithmetic  13.3 us (5%)
  local copies, waits for them, and re-layouts  12.8 us (5%)
  matrix products  4.25 us (2%)
    ppermute x12, waiting for transfers between devices, group_pieces(): came = {k: lax.ppermute(pieces[k], 'h', turn(sign * k)) for k in (2, 1, 3)}  46.1 us
    ppermute x12, waiting for transfers between devices, swap(): return lax.ppermute(x, axis, xor_perm(bit, lax.axis_size(axis)))  19.9 us
    ppermute x12, starting transfers between devices, group_pieces(): came = {k: lax.ppermute(pieces[k], 'h', turn(sign * k)) for k in (2, 1, 3)}  15.8 us
    pallas_call x1, Pallas kernels, attend_back(): pl.pallas_call(functools.partial(backward_kernel, half, blocks, members),...  15.3 us
    pallas_call x1, Pallas kernels, attend(): pl.pallas_call(functools.partial(forward_kernel, half, blocks, len(kvs)),...  12.4 us
    pallas_call x2, Pallas kernels, weight_terms(): pl.pallas_call(functools.partial(weight_kernel, len(rows), members, side)...  12.3 us
    pallas_call x1, Pallas kernels, expert(): pl.pallas_call(functools.partial(expert_kernel, groups, n_fsdp), grid_spe...  11.8 us
    ppermute x7, starting transfers between devices, deal(): out[p] = lax.ppermute(pieces[p], ('h', 'fsdp'), pairs)  9.82 us
  transfers between devices with their start and end apart: 52, of which 21 were waited for; matrix products, arithmetic and copies ran while one was open for 9% of the time, Pallas kernels for 22%

profile of v8, /device:TPU:11, one launch (start us, length us, event | category | flops | bytes accessed | tf_op | source)
XLA Modules:
  0.0 262.4 jit_solution(12623841298670560728)
XLA Ops:
  1.3 1.6 fusion.55
  3.0 2.3 collective-permute-start.4
  5.3 1.5 collective-permute-start.5
  10.1 1.4 constant_dynamic-slice_fusion.2
  16.7 5.3 %all-to-all-start = ((bf16[8,40,768]{2,1,0:T(8,128)(2,1)}), bf16[8,40,768]{2,1,0:T(8,128)(2,1)S(1)}, u32[]{:S(2)}, u32[]{:S(2)}) async-start(bf16[8,40,768]{2,1,0:T(8,128)(2,1)} %bitcast.23), calls=%async_computation | async-start | bytes 983040 | tf_op jit(solution)/shard_map/all_to_all | solution.py:933
  22.1 3.3 %strips.1.refs_4_.refs_5_ = f32[2304,192]{1,0:T(8,128)} custom-call(f32[3,2304]{1,0:T(4,128)} %convolution_multiply_fusion.g_ref), custom_call_target="tpu_custom_call" | custom-call | flops 100000 | bytes 10000 | tf_op jit(solution)/shard_map/strips/pallas_call | solution.py:73
  29.0 2.9 %collective-permute-start.6 = (bf16[4,136,384]{2,1,0:T(8,128)(2,1)S(1)}, bf16[4,136,384]{2,1,0:T(8,128)(2,1)S(1)}, u32[]{:S(2)}, u32[]{:S(2)}) collective-permute-start(bf16[4,136,384]{2,1,0:T(8,128)(2,1)S(1)} %pad_maximum_fusion.4.refs_0_), channel_id=1, source_target_pairs={{0,2},{2,0},{4,6},{6,4},{1,3},{3,1},{5,7},{7,5},{8,10},{10,8},{12,... | collective-permute-start | bytes 1253384 | tf_op jit(solution)/shard_map/ppermute | solution.py:818
  31.9 4.4 %collective-permute-done.7.refs_2_ = bf16[4,136,384]{2,1,0:T(8,128)(2,1)S(1)} collective-permute-done((bf16[4,136,384]{2,1,0:T(8,128)(2,1)S(1)}, bf16[4,136,384]{2,1,0:T(8,128)(2,1)S(1)}, u32[]{:S(2)}, u32[]{:S(2)}) %collective-permute-start.7) | collective-permute-done | bytes 417824 | tf_op jit(solution)/shard_map/ppermute | solution.py:818
  36.4 3.2 %collective-permute-start.8 = (bf16[4,136,384]{2,1,0:T(8,128)(2,1)S(1)}, bf16[4,136,384]{2,1,0:T(8,128)(2,1)S(1)}, u32[]{:S(2)}, u32[]{:S(2)}) collective-permute-start(bf16[4,136,384]{2,1,0:T(8,128)(2,1)S(1)} %collective-permute-done.7.refs_2_), channel_id=1, source_target_pairs={{0,2},{2,0},{4,6},{6,4},{1,3},{3,1},{5,7},{7,5},{8,10},{10,8},{12,... | collective-permute-start | bytes 1253384 | tf_op jit(solution)/shard_map/ppermute | solution.py:818
  40.9 12.4 %attend.1 = (f32[8,192,64]{2,1,0:T(8,128)}, bf16[192,128]{1,0:T(8,128)(2,1)S(1)}, bf16[192,128]{1,0:T(8,128)(2,1)S(1)}, bf16[192,128]{1,0:T(8,128)(2,1)S(1)}, bf...) custom-call(s32[2]{0:T(128)S(1)} %pad_add_fusion.pos, ...), custom_call_target="tpu_custom_call" | custom-call | flops 100000 | bytes 10000 | tf_op jit(solution)/shard_map/attend/pallas_call | solution.py:354
  54.1 3.2 %collective-permute-start.10 = (bf16[192,128]{1,0:T(8,128)(2,1)S(1)}, bf16[192,128]{1,0:T(8,128)(2,1)S(1)}, u32[]{:S(2)}, u32[]{:S(2)}) collective-permute-start(bf16[192,128]{1,0:T(8,128)(2,1)S(1)} %get-tuple-element.120), channel_id=1, source_target_pairs={{0,16},{8,24},{16,0},{24,8},{1,17},{9,25},{17,1},{25,9},{2,18},{10... | collective-permute-start | bytes 147464 | tf_op jit(solution)/shard_map/ppermute | solution.py:844
  57.9 2.9 %maximum_select_fusion = bf16[2,384,768]{2,1,0:T(8,128)(2,1)} fusion(bf16[1,384,768]{2,1,0:T(8,128)(2,1)} %bitcast.7, bf16[1,384,768]{2,1,0:T(8,128)(2,1)} %bitcast.6, pred[]{:T(512)S(6)} %eq.106), kind=kLoop, calls=%fused_computation.8 | loop fusion | flops 1769472 | bytes 2359297 | tf_op jit(solution)/shard_map/jit(_where)/select_n | solution.py:840
  61.1 2.9 %router.1 = (bf16[40,896]{1,0:T(8,128)(2,1)S(1)}, bf16[40,896]{1,0:T(8,128)(2,1)S(1)}, bf16[40,896]{1,0:T(8,128)(2,1)S(1)}, bf16[40,896]{1,0:T(8,128)(2,1)S(1)},...) custom-call(s32[2]{0:T(128)S(1)} %pad_add_fusion.pos, ...), custom_call_target="tpu_custom_call" | custom-call | flops 100000 | bytes 10000 | tf_op jit(solution)/shard_map/router/pallas_call | solution.py:459
  64.0 1.7 collective-permute-start.12
  65.7 2.2 collective-permute-start.13
  67.9 1.4 collective-permute-start.15
  69.4 2.0 collective-permute-start.16
  73.9 4.6 %collective-permute-done.16.refs_5_ = bf16[40,896]{1,0:T(8,128)(2,1)S(1)} collective-permute-done((bf16[40,896]{1,0:T(8,128)(2,1)S(1)}, bf16[40,896]{1,0:T(8,128)(2,1)S(1)}, u32[]{:S(2)}, u32[]{:S(2)}) %collective-permute-start.16) | collective-permute-done | bytes 71712 | tf_op jit(solution)/shard_map/ppermute | solution.py:859
  78.6 2.2 collective-permute-done.17.refs_6_
  80.7 2.2 collective-permute-done.18.refs_7_
  82.9 11.8 %expert.1 = (bf16[4,40,768]{2,1,0:T(8,128)(2,1)}, bf16[4,40,768]{2,1,0:T(8,128)(2,1)}, bf16[8,40,896]{2,1,0:T(8,128)(2,1)}, bf16[2,320,3072]{2,1,0:T(8,128)(2,1)}, bf16[2,320,768]{2,1,0:T(8,128)(2,1)}) custom-call(s32[2]{0:T(128)S(1)} %pad_add_fusion.3.info, bf16[8,40,768]{2,1,0:T(8,128)(2,1)S(1)} %all-to-all-done.dy_ref, bf16[4,768,3072]{2,1,0:T(8,128)(2,1)} %up_ref.1, ...), custom_call_target="tpu_custom_call" | custom-call | flops 100000 | bytes 10000 | tf_op jit(solution)/shard_map/expert/pallas_call | solution.py:519
  95.2 4.2 %all-to-all-start.1 = ((bf16[8,40,896]{2,1,0:T(8,128)(2,1)}), bf16[8,40,896]{2,1,0:T(8,128)(2,1)S(1)}, u32[]{:S(2)}, u32[]{:S(2)}) async-start(bf16[8,40,896]{2,1,0:T(8,128)(2,1)} %get-tuple-element.135), calls=%async_computation.1 | async-start | bytes 1146880 | tf_op jit(solution)/shard_map/all_to_all | solution.py:933
  100.2 3.1 %collective-permute-done.19.refs_1_ = bf16[2,320,768]{2,1,0:T(8,128)(2,1)S(1)} collective-permute-done((bf16[2,320,768]{2,1,0:T(8,128)(2,1)}, bf16[2,320,768]{2,1,0:T(8,128)(2,1)S(1)}, u32[]{:S(2)}, u32[]{:S(2)}) %collective-permute-start.19) | collective-permute-done | bytes 983072 | tf_op jit(solution)/shard_map/ppermute | solution.py:828
  103.3 6.1 %weight_terms.3 = (bf16[192,3072]{1,0:T(8,128)(2,1)}, bf16[192,3072]{1,0:T(8,128)(2,1)}) custom-call(s32[2]{0:T(128)S(1)} %pad_add_fusion.pos, bf16[2,320,768]{2,1,0:T(8,128)(2,1)S(1)} %copy-done.1, bf16[2,320,768]{2,1,0:T(8,128)(2,1)S(1)} %collective-permute-done.19.refs_1_, bf16[2,320,3072]{2,1,0:T(8,128)(2,1)} %get-tuple-element.137.refs_2_, ...), custom_call_target="tpu_custom_call" | custom-call | flops 100000 | bytes 10000 | tf_op jit(solution)/shard_map/weight_terms/pallas_call | solution.py:572
  109.4 6.2 %weight_terms.2 = (bf16[192,3072]{1,0:T(8,128)(2,1)}, bf16[192,3072]{1,0:T(8,128)(2,1)}) custom-call(s32[2]{0:T(128)S(1)} %pad_add_fusion.pos, bf16[2,320,768]{2,1,0:T(8,128)(2,1)S(1)} %copy-done.1, bf16[2,320,768]{2,1,0:T(8,128)(2,1)S(1)} %collective-permute-done.19.refs_1_, bf16[2,320,3072]{2,1,0:T(8,128)(2,1)} %get-tuple-element.137.refs_2_, ...), custom_call_target="tpu_custom_call" | custom-call | flops 100000 | bytes 10000 | tf_op jit(solution)/shard_map/weight_terms/pallas_call | solution.py:572
  117.5 5.0 %turn_back.1 = (bf16[192,128]{1,0:T(8,128)(2,1)S(1)}, bf16[192,128]{1,0:T(8,128)(2,1)S(1)}, bf16[192,128]{1,0:T(8,128)(2,1)S(1)}, bf16[192,128]{1,0:T(8,128)(2,1...) custom-call(s32[3]{0:T(128)S(1)} %pad_add_fusion.2.info, ...), custom_call_target="tpu_custom_call" | custom-call | flops 100000 | bytes 10000 | tf_op jit(solution)/shard_map/turn_back/pallas_call | solution.py:694
  122.7 1.3 collective-permute-start.22
  124.0 1.4 collective-permute-start.23
  126.6 2.7 %collective-permute-done.23.refs_3_ = bf16[192,128]{1,0:T(8,128)(2,1)S(1)} collective-permute-done((bf16[192,128]{1,0:T(8,128)(2,1)S(1)}, bf16[192,128]{1,0:T(8,128)(2,1)S(1)}, u32[]{:S(2)}, u32[]{:S(2)}) %collective-permute-start.23) | collective-permute-done | bytes 49184 | tf_op jit(solution)/shard_map/ppermute | solution.py:844
  129.2 15.3 %attend_back.1 = (bf16[512,192]{1,0:T(8,128)(2,1)S(1)}, bf16[4,128,384]{2,1,0:T(8,128)(2,1)S(1)}, bf16[4,128,384]{2,1,0:T(8,128)(2,1)S(1)}, bf16[4,128,384]{2,1,...) custom-call(s32[2]{0:T(128)S(1)} %pad_add_fusion.pos, ...), custom_call_target="tpu_custom_call" | custom-call | flops 100000 | bytes 10000 | tf_op jit(solution)/shard_map/attend_back/pallas_call | solution.py:384
  148.3 2.0 add_groups.2
  153.3 8.1 %collective-permute-done.28.came_ref = bf16[4,128,384]{2,1,0:T(8,128)(2,1)S(1)} collective-permute-done((bf16[4,128,384]{2,1,0:T(8,128)(2,1)S(1)}, bf16[4,128,384]{2,1,0:T(8,128)(2,1)S(1)}, u32[]{:S(2)}, u32[]{:S(2)}) %collective-permute-start.28) | collective-permute-done | bytes 393248 | tf_op jit(solution)/shard_map/ppermute | solution.py:828
  161.9 2.9 %input_back.1 = (f32[128,768]{1,0:T(8,128)S(1)}, bf16[128,768]{1,0:T(8,128)(2,1)S(1)}, bf16[128,768]{1,0:T(8,128)(2,1)S(1)}, bf16[128,768]{1,0:T(8,128)(2,1)S(1)...) custom-call(s32[2]{0:T(128)S(1)} %pad_add_fusion.1.info, ...), custom_call_target="tpu_custom_call" | custom-call | flops 100000 | bytes 10000 | tf_op jit(solution)/shard_map/input_back/pallas_call | solution.py:782
  168.8 3.0 %collective-permute-start.33 = (bf16[8,48,384]{2,1,0:T(8,128)(2,1)S(1)}, bf16[8,48,384]{2,1,0:T(8,128)(2,1)S(1)}, u32[]{:S(2)}, u32[]{:S(2)}) collective-permute-start(bf16[8,48,384]{2,1,0:T(8,128)(2,1)S(1)} %fusion.4), channel_id=1, source_target_pairs={{0,1},{1,0},{2,3},{3,2},{4,5},{5,4},{6,7},{7,6},{8,9},{9,8},{10,11... | collective-permute-start | bytes 884744 | tf_op jit(solution)/shard_map/ppermute | solution.py:828
  173.5 5.7 %collective-permute-done.33 = bf16[8,48,384]{2,1,0:T(8,128)(2,1)S(1)} collective-permute-done((bf16[8,48,384]{2,1,0:T(8,128)(2,1)S(1)}, bf16[8,48,384]{2,1,0:T(8,128)(2,1)S(1)}, u32[]{:S(2)}, u32[]{:S(2)}) %collective-permute-start.33) | collective-permute-done | bytes 294944 | tf_op jit(solution)/shard_map/ppermute | solution.py:828
  180.3 2.5 collective-permute-start.35
  184.7 24.9 %collective-permute-done.35.refs_2_ = bf16[272,768]{1,0:T(8,128)(2,1)S(1)} collective-permute-done((bf16[272,768]{1,0:T(8,128)(2,1)S(1)}, bf16[272,768]{1,0:T(8,128)(2,1)S(1)}, u32[]{:S(2)}, u32[]{:S(2)}) %collective-permute-start.35) | collective-permute-done | bytes 417824 | tf_op jit(solution)/shard_map/ppermute | solution.py:844
  211.9 1.9 add_groups.3
  214.9 3.6 %collective-permute-start.48 = (bf16[192,768]{1,0:T(8,128)(2,1)S(1)}, bf16[192,768]{1,0:T(8,128)(2,1)S(1)}, u32[]{:S(2)}, u32[]{:S(2)}) collective-permute-start(bf16[192,768]{1,0:T(8,128)(2,1)S(1)} %get-tuple-element.214), channel_id=1, source_target_pairs={{0,16},{8,24},{16,0},{24,8},{1,17},{9,25},{17,1},{25,9},{2,18},{10... | collective-permute-start | bytes 884744 | tf_op jit(solution)/shard_map/ppermute | solution.py:844
  219.1 4.0 %collective-permute-start.40 = (bf16[48,384]{1,0:T(8,128)(2,1)S(1)}, bf16[48,384]{1,0:T(8,128)(2,1)S(1)}, u32[]{:S(2)}, u32[]{:S(2)}) collective-permute-start(bf16[48,384]{1,0:T(8,128)(2,1)S(1)} %get-tuple-element.251), channel_id=1, source_target_pairs={{4,0},{10,2},{16,4},{22,6},{28,8},{2,10},{8,12},{14,14},{20,16},{2... | collective-permute-start | bytes 110600 | tf_op jit(solution)/shard_map/ppermute | solution.py:1063
  223.2 2.4 collective-permute-start.39
  225.6 3.4 %collective-permute-start.38 = (bf16[48,384]{1,0:T(8,128)(2,1)S(1)}, bf16[48,384]{1,0:T(8,128)(2,1)S(1)}, u32[]{:S(2)}, u32[]{:S(2)}) collective-permute-start(bf16[48,384]{1,0:T(8,128)(2,1)S(1)} %get-tuple-element.253), channel_id=1, source_target_pairs={{0,0},{6,2},{12,4},{18,6},{24,8},{30,10},{4,12},{10,14},{16,16},{2... | collective-permute-start | bytes 110600 | tf_op jit(solution)/shard_map/ppermute | solution.py:1063
  229.0 15.3 %collective-permute-done.48.refs_2_ = bf16[192,768]{1,0:T(8,128)(2,1)S(1)} collective-permute-done((bf16[192,768]{1,0:T(8,128)(2,1)S(1)}, bf16[192,768]{1,0:T(8,128)(2,1)S(1)}, u32[]{:S(2)}, u32[]{:S(2)}) %collective-permute-start.48) | collective-permute-done | bytes 294944 | tf_op jit(solution)/shard_map/ppermute | solution.py:844
  244.4 3.1 %collective-permute-start.44 = (bf16[80,384]{1,0:T(8,128)(2,1)S(1)}, bf16[80,384]{1,0:T(8,128)(2,1)S(1)}, u32[]{:S(2)}, u32[]{:S(2)}) collective-permute-start(bf16[80,384]{1,0:T(8,128)(2,1)S(1)} %get-tuple-element.256), channel_id=1, source_target_pairs={{0,16},{8,24},{16,0},{24,8},{1,17},{9,25},{17,1},{25,9},{2,18},{10... | collective-permute-start | bytes 184328 | tf_op jit(solution)/shard_map/ppermute | solution.py:1054
  247.5 2.1 in_order.3
  249.6 2.4 collective-permute-start.45
  251.9 1.5 collective-permute-start.41
  253.5 2.1 in_order.2
  (228 shorter events, 49.3 us)
Async XLA Ops:
  3.0 22.5 %collective-permute-start.4 = (bf16[136,768]{1,0:T(8,128)(2,1)}, bf16[136,768]{1,0:T(8,128)(2,1)S(1)}, u32[]{:S(2)}, u32[]{:S(2)}) collective-permute-start(bf16[136,768]{1,0:T(8,128)(2,1)} %get-tuple-element.247), channel_id=1, source_target_pairs={{0,16},{8,24},{16,0},{24,8},{1,17},{9,25},{17,1},{25,9},{2,18},{10... | collective-permute-start | bytes 626696 | tf_op jit(solution)/shard_map/ppermute | solution.py:809
  5.3 20.2 %collective-permute-start.3 = (bf16[136,768]{1,0:T(8,128)(2,1)}, bf16[136,768]{1,0:T(8,128)(2,1)S(1)}, u32[]{:S(2)}, u32[]{:S(2)}) collective-permute-start(bf16[136,768]{1,0:T(8,128)(2,1)} %get-tuple-element.247), channel_id=1, source_target_pairs={{0,8},{8,16},{16,24},{24,0},{1,9},{9,17},{17,25},{25,1},{2,10},{10... | collective-permute-start | bytes 626696 | tf_op jit(solution)/shard_map/ppermute | solution.py:809
  5.3 20.2 %collective-permute-start.5 = (bf16[136,768]{1,0:T(8,128)(2,1)}, bf16[136,768]{1,0:T(8,128)(2,1)S(1)}, u32[]{:S(2)}, u32[]{:S(2)}) collective-permute-start(bf16[136,768]{1,0:T(8,128)(2,1)} %get-tuple-element.247), channel_id=1, source_target_pairs={{0,24},{8,0},{16,8},{24,16},{1,25},{9,1},{17,9},{25,17},{2,26},{10... | collective-permute-start | bytes 626696 | tf_op jit(solution)/shard_map/ppermute | solution.py:809
  9.8 5.9 %collective-permute-start.2 = (bf16[16,384]{1,0:T(8,128)(2,1)S(1)}, bf16[16,384]{1,0:T(8,128)(2,1)S(1)}, u32[]{:S(2)}, u32[]{:S(2)}) collective-permute-start(bf16[16,384]{1,0:T(8,128)(2,1)S(1)} %concatenate.53), channel_id=1, source_target_pairs={{0,1},{1,0},{2,3},{3,2},{4,5},{5,4},{6,7},{7,6},{8,9},{9,8},{10,11... | collective-permute-start | bytes 36872 | tf_op jit(solution)/shard_map/ppermute | solution.py:839
  11.7 14.4 %collective-permute-start = (bf16[384,576]{1,0:T(8,128)(2,1)S(1)}, bf16[384,576]{1,0:T(8,128)(2,1)S(1)}, u32[]{:S(2)}, u32[]{:S(2)}) collective-permute-start(bf16[384,576]{1,0:T(8,128)(2,1)S(1)} %pad_maximum_fusion.2), channel_id=1, source_target_pairs={{0,1},{1,0},{2,3},{3,2},{4,5},{5,4},{6,7},{7,6},{8,9},{9,8},{10,11... | collective-permute-start | bytes 1327112 | tf_op jit(solution)/shard_map/ppermute | solution.py:839
  16.7 36.6 %all-to-all-start = ((bf16[8,40,768]{2,1,0:T(8,128)(2,1)}), bf16[8,40,768]{2,1,0:T(8,128)(2,1)S(1)}, u32[]{:S(2)}, u32[]{:S(2)}) async-start(bf16[8,40,768]{2,1,0:T(8,128)(2,1)} %bitcast.23), calls=%async_computation | async-start | bytes 983040 | tf_op jit(solution)/shard_map/all_to_all | solution.py:933
  27.4 8.9 %collective-permute-start.7 = (bf16[4,136,384]{2,1,0:T(8,128)(2,1)S(1)}, bf16[4,136,384]{2,1,0:T(8,128)(2,1)S(1)}, u32[]{:S(2)}, u32[]{:S(2)}) collective-permute-start(bf16[4,136,384]{2,1,0:T(8,128)(2,1)S(1)} %pad_maximum_fusion.4.refs_0_), channel_id=1, source_target_pairs={{0,4},{2,6},{4,0},{6,2},{1,5},{3,7},{5,1},{7,3},{8,12},{10,14},{12... | collective-permute-start | bytes 1253384 | tf_op jit(solution)/shard_map/ppermute | solution.py:818
  28.7 29.2 %collective-permute-start.1 = (bf16[384,768]{1,0:T(8,128)(2,1)}, bf16[384,768]{1,0:T(8,128)(2,1)}, u32[]{:S(2)}, u32[]{:S(2)}) collective-permute-start(bf16[384,768]{1,0:T(8,128)(2,1)} %param.19), channel_id=1, source_target_pairs={{0,1},{1,0},{2,3},{3,2},{4,5},{5,4},{6,7},{7,6},{8,9},{9,8},{10,11... | collective-permute-start | bytes 1769480 | tf_op jit(solution)/shard_map/ppermute | solution.py:839
  29.0 10.7 %collective-permute-start.6 = (bf16[4,136,384]{2,1,0:T(8,128)(2,1)S(1)}, bf16[4,136,384]{2,1,0:T(8,128)(2,1)S(1)}, u32[]{:S(2)}, u32[]{:S(2)}) collective-permute-start(bf16[4,136,384]{2,1,0:T(8,128)(2,1)S(1)} %pad_maximum_fusion.4.refs_0_), channel_id=1, source_target_pairs={{0,2},{2,0},{4,6},{6,4},{1,3},{3,1},{5,7},{7,5},{8,10},{10,8},{12,... | collective-permute-start | bytes 1253384 | tf_op jit(solution)/shard_map/ppermute | solution.py:818
  36.4 4.6 %collective-permute-start.8 = (bf16[4,136,384]{2,1,0:T(8,128)(2,1)S(1)}, bf16[4,136,384]{2,1,0:T(8,128)(2,1)S(1)}, u32[]{:S(2)}, u32[]{:S(2)}) collective-permute-start(bf16[4,136,384]{2,1,0:T(8,128)(2,1)S(1)} %collective-permute-done.7.refs_2_), channel_id=1, source_target_pairs={{0,2},{2,0},{4,6},{6,4},{1,3},{3,1},{5,7},{7,5},{8,10},{10,8},{12,... | collective-permute-start | bytes 1253384 | tf_op jit(solution)/shard_map/ppermute | solution.py:818
  53.3 7.4 %collective-permute-start.9 = (bf16[192,128]{1,0:T(8,128)(2,1)S(1)}, bf16[192,128]{1,0:T(8,128)(2,1)S(1)}, u32[]{:S(2)}, u32[]{:S(2)}) collective-permute-start(bf16[192,128]{1,0:T(8,128)(2,1)S(1)} %get-tuple-element.119), channel_id=1, source_target_pairs={{0,24},{8,0},{16,8},{24,16},{1,25},{9,1},{17,9},{25,17},{2,26},{10... | collective-permute-start | bytes 147464 | tf_op jit(solution)/shard_map/ppermute | solution.py:844
  54.1 6.7 %collective-permute-start.10 = (bf16[192,128]{1,0:T(8,128)(2,1)S(1)}, bf16[192,128]{1,0:T(8,128)(2,1)S(1)}, u32[]{:S(2)}, u32[]{:S(2)}) collective-permute-start(bf16[192,128]{1,0:T(8,128)(2,1)S(1)} %get-tuple-element.120), channel_id=1, source_target_pairs={{0,16},{8,24},{16,0},{24,8},{1,17},{9,25},{17,1},{25,9},{2,18},{10... | collective-permute-start | bytes 147464 | tf_op jit(solution)/shard_map/ppermute | solution.py:844
  57.3 3.8 %collective-permute-start.11 = (bf16[192,128]{1,0:T(8,128)(2,1)S(1)}, bf16[192,128]{1,0:T(8,128)(2,1)S(1)}, u32[]{:S(2)}, u32[]{:S(2)}) collective-permute-start(bf16[192,128]{1,0:T(8,128)(2,1)S(1)} %get-tuple-element.121), channel_id=1, source_target_pairs={{0,8},{8,16},{16,24},{24,0},{1,9},{9,17},{17,25},{25,1},{2,10},{10... | collective-permute-start | bytes 147464 | tf_op jit(solution)/shard_map/ppermute | solution.py:844
  64.0 7.3 %collective-permute-start.12 = (bf16[40,896]{1,0:T(8,128)(2,1)S(1)}, bf16[40,896]{1,0:T(8,128)(2,1)S(1)}, u32[]{:S(2)}, u32[]{:S(2)}) collective-permute-start(bf16[40,896]{1,0:T(8,128)(2,1)S(1)} %get-tuple-element.128), channel_id=1, source_target_pairs={{0,1},{1,0},{8,9},{9,8},{16,17},{17,16},{24,25},{25,24},{2,3},{3,2... | collective-permute-start | bytes 215048 | tf_op jit(solution)/shard_map/ppermute | solution.py:859
  65.7 6.9 %collective-permute-start.13 = (bf16[40,896]{1,0:T(8,128)(2,1)S(1)}, bf16[40,896]{1,0:T(8,128)(2,1)S(1)}, u32[]{:S(2)}, u32[]{:S(2)}) collective-permute-start(bf16[40,896]{1,0:T(8,128)(2,1)S(1)} %get-tuple-element.129), channel_id=1, source_target_pairs={{0,8},{1,9},{8,16},{9,17},{16,24},{17,25},{24,0},{25,1},{2,10},{3,... | collective-permute-start | bytes 215048 | tf_op jit(solution)/shard_map/ppermute | solution.py:859
  67.9 6.0 %collective-permute-start.14 = (bf16[40,896]{1,0:T(8,128)(2,1)S(1)}, bf16[40,896]{1,0:T(8,128)(2,1)S(1)}, u32[]{:S(2)}, u32[]{:S(2)}) collective-permute-start(bf16[40,896]{1,0:T(8,128)(2,1)S(1)} %get-tuple-element.130), channel_id=1, source_target_pairs={{0,9},{1,8},{8,17},{9,16},{16,25},{17,24},{24,1},{25,0},{2,11},{3,... | collective-permute-start | bytes 215048 | tf_op jit(solution)/shard_map/ppermute | solution.py:859
  67.9 6.0 %collective-permute-start.15 = (bf16[40,896]{1,0:T(8,128)(2,1)S(1)}, bf16[40,896]{1,0:T(8,128)(2,1)S(1)}, u32[]{:S(2)}, u32[]{:S(2)}) collective-permute-start(bf16[40,896]{1,0:T(8,128)(2,1)S(1)} %get-tuple-element.131), channel_id=1, source_target_pairs={{0,16},{1,17},{8,24},{9,25},{16,0},{17,1},{24,8},{25,9},{2,18},{3,... | collective-permute-start | bytes 215048 | tf_op jit(solution)/shard_map/ppermute | solution.py:859
  69.4 9.2 %collective-permute-start.16 = (bf16[40,896]{1,0:T(8,128)(2,1)S(1)}, bf16[40,896]{1,0:T(8,128)(2,1)S(1)}, u32[]{:S(2)}, u32[]{:S(2)}) collective-permute-start(bf16[40,896]{1,0:T(8,128)(2,1)S(1)} %get-tuple-element.132), channel_id=1, source_target_pairs={{0,17},{1,16},{8,25},{9,24},{16,1},{17,0},{24,9},{25,8},{2,19},{3,... | collective-permute-start | bytes 215048 | tf_op jit(solution)/shard_map/ppermute | solution.py:859
  71.3 9.4 %collective-permute-start.17 = (bf16[40,896]{1,0:T(8,128)(2,1)S(1)}, bf16[40,896]{1,0:T(8,128)(2,1)S(1)}, u32[]{:S(2)}, u32[]{:S(2)}) collective-permute-start(bf16[40,896]{1,0:T(8,128)(2,1)S(1)} %get-tuple-element.133), channel_id=1, source_target_pairs={{0,24},{1,25},{8,0},{9,1},{16,8},{17,9},{24,16},{25,17},{2,26},{3,... | collective-permute-start | bytes 215048 | tf_op jit(solution)/shard_map/ppermute | solution.py:859
  72.7 10.2 %collective-permute-start.18 = (bf16[40,896]{1,0:T(8,128)(2,1)S(1)}, bf16[40,896]{1,0:T(8,128)(2,1)S(1)}, u32[]{:S(2)}, u32[]{:S(2)}) collective-permute-start(bf16[40,896]{1,0:T(8,128)(2,1)S(1)} %get-tuple-element.134), channel_id=1, source_target_pairs={{0,25},{1,24},{8,1},{9,0},{16,9},{17,8},{24,17},{25,16},{2,27},{3,... | collective-permute-start | bytes 215048 | tf_op jit(solution)/shard_map/ppermute | solution.py:859
  94.7 8.6 %collective-permute-start.20 = (bf16[2,320,3072]{2,1,0:T(8,128)(2,1)}, bf16[2,320,3072]{2,1,0:T(8,128)(2,1)}, u32[]{:S(2)}, u32[]{:S(2)}) collective-permute-start(bf16[2,320,3072]{2,1,0:T(8,128)(2,1)} %get-tuple-element.137.refs_2_), channel_id=1, source_target_pairs={{0,2},{2,0},{1,3},{3,1},{4,6},{6,4},{5,7},{7,5},{8,10},{10,8},{9,1... | collective-permute-start | bytes 11796488 | tf_op jit(solution)/shard_map/ppermute | solution.py:828
  95.2 20.4 %all-to-all-start.1 = ((bf16[8,40,896]{2,1,0:T(8,128)(2,1)}), bf16[8,40,896]{2,1,0:T(8,128)(2,1)S(1)}, u32[]{:S(2)}, u32[]{:S(2)}) async-start(bf16[8,40,896]{2,1,0:T(8,128)(2,1)} %get-tuple-element.135), calls=%async_computation.1 | async-start | bytes 1146880 | tf_op jit(solution)/shard_map/all_to_all | solution.py:933
  115.6 31.7 %collective-permute-start.27 = (bf16[192,3072]{1,0:T(8,128)(2,1)}, bf16[192,3072]{1,0:T(8,128)(2,1)S(1)}, u32[]{:S(2)}, u32[]{:S(2)}) collective-permute-start(bf16[192,3072]{1,0:T(8,128)(2,1)} %get-tuple-element.162), channel_id=1, source_target_pairs={{0,4},{4,0},{1,5},{5,1},{2,6},{6,2},{3,7},{7,3},{8,12},{12,8},{9,1... | collective-permute-start | bytes 3538952 | tf_op jit(solution)/shard_map/ppermute | solution.py:828
  116.9 27.7 %collective-permute-start.24 = (bf16[4,40,768]{2,1,0:T(8,128)(2,1)S(1)}, bf16[4,40,768]{2,1,0:T(8,128)(2,1)S(1)}, u32[]{:S(2)}, u32[]{:S(2)}) collective-permute-start(bf16[4,40,768]{2,1,0:T(8,128)(2,1)S(1)} %copy-done.26), channel_id=1, source_target_pairs={{0,1},{1,0},{2,3},{3,2},{4,5},{5,4},{6,7},{7,6},{8,9},{9,8},{10,11... | collective-permute-start | bytes 737288 | tf_op jit(solution)/shard_map/ppermute | solution.py:971
  122.7 3.9 %collective-permute-start.22 = (bf16[192,128]{1,0:T(8,128)(2,1)S(1)}, bf16[192,128]{1,0:T(8,128)(2,1)S(1)}, u32[]{:S(2)}, u32[]{:S(2)}) collective-permute-start(bf16[192,128]{1,0:T(8,128)(2,1)S(1)} %get-tuple-element.145), channel_id=1, source_target_pairs={{0,16},{8,24},{16,0},{24,8},{1,17},{9,25},{17,1},{25,9},{2,18},{10... | collective-permute-start | bytes 147464 | tf_op jit(solution)/shard_map/ppermute | solution.py:844
  124.0 5.2 %collective-permute-start.23 = (bf16[192,128]{1,0:T(8,128)(2,1)S(1)}, bf16[192,128]{1,0:T(8,128)(2,1)S(1)}, u32[]{:S(2)}, u32[]{:S(2)}) collective-permute-start(bf16[192,128]{1,0:T(8,128)(2,1)S(1)} %get-tuple-element.146), channel_id=1, source_target_pairs={{0,24},{8,0},{16,8},{24,16},{1,25},{9,1},{17,9},{25,17},{2,26},{10... | collective-permute-start | bytes 147464 | tf_op jit(solution)/shard_map/ppermute | solution.py:844
  151.1 10.9 %collective-permute-start.29 = (bf16[272,768]{1,0:T(8,128)(2,1)S(1)}, bf16[272,768]{1,0:T(8,128)(2,1)S(1)}, u32[]{:S(2)}, u32[]{:S(2)}) collective-permute-start(bf16[272,768]{1,0:T(8,128)(2,1)S(1)} %get-tuple-element.168), channel_id=1, source_target_pairs={{0,8},{8,16},{16,24},{24,0},{1,9},{9,17},{17,25},{25,1},{2,10},{10... | collective-permute-start | bytes 1253384 | tf_op jit(solution)/shard_map/ppermute | solution.py:844
  151.4 10.0 %collective-permute-start.28 = (bf16[4,128,384]{2,1,0:T(8,128)(2,1)S(1)}, bf16[4,128,384]{2,1,0:T(8,128)(2,1)S(1)}, u32[]{:S(2)}, u32[]{:S(2)}) collective-permute-start(bf16[4,128,384]{2,1,0:T(8,128)(2,1)S(1)} %get-tuple-element.163), channel_id=1, source_target_pairs={{0,4},{4,0},{1,5},{5,1},{2,6},{6,2},{3,7},{7,3},{8,12},{12,8},{9,1... | collective-permute-start | bytes 1179656 | tf_op jit(solution)/shard_map/ppermute | solution.py:828
  152.3 15.3 %collective-permute-start.32 = (bf16[2,8,48,384]{3,2,1,0:T(8,128)(2,1)}, bf16[2,8,48,384]{3,2,1,0:T(8,128)(2,1)}, u32[]{:S(2)}, u32[]{:S(2)}) collective-permute-start(bf16[2,8,48,384]{3,2,1,0:T(8,128)(2,1)} %get-tuple-element.179), channel_id=1, source_target_pairs={{0,2},{2,0},{1,3},{3,1},{4,6},{6,4},{5,7},{7,5},{8,10},{10,8},{9,1... | collective-permute-start | bytes 1769480 | tf_op jit(solution)/shard_map/ppermute | solution.py:828
  166.2 5.8 %collective-permute-start.30 = (bf16[320,768]{1,0:T(8,128)(2,1)S(1)}, bf16[320,768]{1,0:T(8,128)(2,1)}, u32[]{:S(2)}, u32[]{:S(2)}) collective-permute-start(bf16[320,768]{1,0:T(8,128)(2,1)S(1)} %get-tuple-element.175), channel_id=1, source_target_pairs={{0,2},{2,0},{1,3},{3,1},{4,6},{6,4},{5,7},{7,5},{8,10},{10,8},{9,1... | collective-permute-start | bytes 1474568 | tf_op jit(solution)/shard_map/ppermute | solution.py:828
  168.8 10.3 %collective-permute-start.33 = (bf16[8,48,384]{2,1,0:T(8,128)(2,1)S(1)}, bf16[8,48,384]{2,1,0:T(8,128)(2,1)S(1)}, u32[]{:S(2)}, u32[]{:S(2)}) collective-permute-start(bf16[8,48,384]{2,1,0:T(8,128)(2,1)S(1)} %fusion.4), channel_id=1, source_target_pairs={{0,1},{1,0},{2,3},{3,2},{4,5},{5,4},{6,7},{7,6},{8,9},{9,8},{10,11... | collective-permute-start | bytes 884744 | tf_op jit(solution)/shard_map/ppermute | solution.py:828
  171.8 39.1 %collective-permute-start.34 = (bf16[192,3072]{1,0:T(8,128)(2,1)}, bf16[192,3072]{1,0:T(8,128)(2,1)S(1)}, u32[]{:S(2)}, u32[]{:S(2)}) collective-permute-start(bf16[192,3072]{1,0:T(8,128)(2,1)} %get-tuple-element.182), channel_id=1, source_target_pairs={{0,4},{4,0},{1,5},{5,1},{2,6},{6,2},{3,7},{7,3},{8,12},{12,8},{9,1... | collective-permute-start | bytes 3538952 | tf_op jit(solution)/shard_map/ppermute | solution.py:828
  173.4 11.1 %collective-permute-start.31 = (bf16[320,384]{1,0:T(8,128)(2,1)S(1)}, bf16[320,384]{1,0:T(8,128)(2,1)S(1)}, u32[]{:S(2)}, u32[]{:S(2)}) collective-permute-start(bf16[320,384]{1,0:T(8,128)(2,1)S(1)} %pad_maximum_fusion.6), channel_id=1, source_target_pairs={{0,1},{1,0},{2,3},{3,2},{4,5},{5,4},{6,7},{7,6},{8,9},{9,8},{10,11... | collective-permute-start | bytes 737288 | tf_op jit(solution)/shard_map/ppermute | solution.py:828
  180.3 29.3 %collective-permute-start.35 = (bf16[272,768]{1,0:T(8,128)(2,1)S(1)}, bf16[272,768]{1,0:T(8,128)(2,1)S(1)}, u32[]{:S(2)}, u32[]{:S(2)}) collective-permute-start(bf16[272,768]{1,0:T(8,128)(2,1)S(1)} %copy-done.6), channel_id=1, source_target_pairs={{0,16},{8,24},{16,0},{24,8},{1,17},{9,25},{17,1},{25,9},{2,18},{10... | collective-permute-start | bytes 1253384 | tf_op jit(solution)/shard_map/ppermute | solution.py:844
  182.8 28.1 %collective-permute-start.36 = (bf16[272,768]{1,0:T(8,128)(2,1)S(1)}, bf16[272,768]{1,0:T(8,128)(2,1)S(1)}, u32[]{:S(2)}, u32[]{:S(2)}) collective-permute-start(bf16[272,768]{1,0:T(8,128)(2,1)S(1)} %get-tuple-element.186), channel_id=1, source_target_pairs={{0,24},{8,0},{16,8},{24,16},{1,25},{9,1},{17,9},{25,17},{2,26},{10... | collective-permute-start | bytes 1253384 | tf_op jit(solution)/shard_map/ppermute | solution.py:844
  210.9 7.7 %collective-permute-start.42 = (bf16[128,768]{1,0:T(8,128)(2,1)S(1)}, bf16[128,768]{1,0:T(8,128)(2,1)S(1)}, u32[]{:S(2)}, u32[]{:S(2)}) collective-permute-start(bf16[128,768]{1,0:T(8,128)(2,1)S(1)} %copy-done.10), channel_id=1, source_target_pairs={{0,24},{8,0},{16,8},{24,16},{1,25},{9,1},{17,9},{25,17},{2,26},{10... | collective-permute-start | bytes 589832 | tf_op jit(solution)/shard_map/ppermute | solution.py:1038
  211.0 7.9 %collective-permute-start.37 = (bf16[368,384]{1,0:T(8,128)(2,1)S(1)}, bf16[368,384]{1,0:T(8,128)(2,1)S(1)}, u32[]{:S(2)}, u32[]{:S(2)}) collective-permute-start(bf16[368,384]{1,0:T(8,128)(2,1)S(1)} %pad_maximum_fusion.5), channel_id=1, source_target_pairs={{0,4},{4,0},{1,5},{5,1},{2,6},{6,2},{3,7},{7,3},{8,12},{12,8},{9,1... | collective-permute-start | bytes 847880 | tf_op jit(solution)/shard_map/ppermute | solution.py:828
  213.8 11.8 %collective-permute-start.47 = (bf16[192,768]{1,0:T(8,128)(2,1)S(1)}, bf16[192,768]{1,0:T(8,128)(2,1)S(1)}, u32[]{:S(2)}, u32[]{:S(2)}) collective-permute-start(bf16[192,768]{1,0:T(8,128)(2,1)S(1)} %get-tuple-element.213), channel_id=1, source_target_pairs={{0,8},{8,16},{16,24},{24,0},{1,9},{9,17},{17,25},{25,1},{2,10},{10... | collective-permute-start | bytes 884744 | tf_op jit(solution)/shard_map/ppermute | solution.py:844
  214.9 29.4 %collective-permute-start.48 = (bf16[192,768]{1,0:T(8,128)(2,1)S(1)}, bf16[192,768]{1,0:T(8,128)(2,1)S(1)}, u32[]{:S(2)}, u32[]{:S(2)}) collective-permute-start(bf16[192,768]{1,0:T(8,128)(2,1)S(1)} %get-tuple-element.214), channel_id=1, source_target_pairs={{0,16},{8,24},{16,0},{24,8},{1,17},{9,25},{17,1},{25,9},{2,18},{10... | collective-permute-start | bytes 884744 | tf_op jit(solution)/shard_map/ppermute | solution.py:844
  218.5 25.8 %collective-permute-start.49 = (bf16[192,768]{1,0:T(8,128)(2,1)S(1)}, bf16[192,768]{1,0:T(8,128)(2,1)S(1)}, u32[]{:S(2)}, u32[]{:S(2)}) collective-permute-start(bf16[192,768]{1,0:T(8,128)(2,1)S(1)} %get-tuple-element.215), channel_id=1, source_target_pairs={{0,24},{8,0},{16,8},{24,16},{1,25},{9,1},{17,9},{25,17},{2,26},{10... | collective-permute-start | bytes 884744 | tf_op jit(solution)/shard_map/ppermute | solution.py:844
  219.1 30.4 %collective-permute-start.40 = (bf16[48,384]{1,0:T(8,128)(2,1)S(1)}, bf16[48,384]{1,0:T(8,128)(2,1)S(1)}, u32[]{:S(2)}, u32[]{:S(2)}) collective-permute-start(bf16[48,384]{1,0:T(8,128)(2,1)S(1)} %get-tuple-element.251), channel_id=1, source_target_pairs={{4,0},{10,2},{16,4},{22,6},{28,8},{2,10},{8,12},{14,14},{20,16},{2... | collective-permute-start | bytes 110600 | tf_op jit(solution)/shard_map/ppermute | solution.py:1063
  223.2 28.8 %collective-permute-start.39 = (bf16[48,384]{1,0:T(8,128)(2,1)S(1)}, bf16[48,384]{1,0:T(8,128)(2,1)S(1)}, u32[]{:S(2)}, u32[]{:S(2)}) collective-permute-start(bf16[48,384]{1,0:T(8,128)(2,1)S(1)} %get-tuple-element.252), channel_id=1, source_target_pairs={{2,0},{8,2},{14,4},{20,6},{26,8},{0,10},{6,12},{12,14},{18,16},{24... | collective-permute-start | bytes 110600 | tf_op jit(solution)/shard_map/ppermute | solution.py:1063
  225.6 26.4 %collective-permute-start.38 = (bf16[48,384]{1,0:T(8,128)(2,1)S(1)}, bf16[48,384]{1,0:T(8,128)(2,1)S(1)}, u32[]{:S(2)}, u32[]{:S(2)}) collective-permute-start(bf16[48,384]{1,0:T(8,128)(2,1)S(1)} %get-tuple-element.253), channel_id=1, source_target_pairs={{0,0},{6,2},{12,4},{18,6},{24,8},{30,10},{4,12},{10,14},{16,16},{2... | collective-permute-start | bytes 110600 | tf_op jit(solution)/shard_map/ppermute | solution.py:1063
  244.3 16.7 %collective-permute-start.43 = (bf16[128,768]{1,0:T(8,128)(2,1)S(1)}, bf16[128,768]{1,0:T(8,128)(2,1)S(1)}, u32[]{:S(2)}, u32[]{:S(2)}) collective-permute-start(bf16[128,768]{1,0:T(8,128)(2,1)S(1)} %add_convert_fusion), channel_id=1, source_target_pairs={{0,24},{8,0},{16,8},{24,16},{1,25},{9,1},{17,9},{25,17},{2,26},{10... | collective-permute-start | bytes 589832 | tf_op jit(solution)/shard_map/ppermute | solution.py:1041
  244.4 13.9 %collective-permute-start.44 = (bf16[80,384]{1,0:T(8,128)(2,1)S(1)}, bf16[80,384]{1,0:T(8,128)(2,1)S(1)}, u32[]{:S(2)}, u32[]{:S(2)}) collective-permute-start(bf16[80,384]{1,0:T(8,128)(2,1)S(1)} %get-tuple-element.256), channel_id=1, source_target_pairs={{0,16},{8,24},{16,0},{24,8},{1,17},{9,25},{17,1},{25,9},{2,18},{10... | collective-permute-start | bytes 184328 | tf_op jit(solution)/shard_map/ppermute | solution.py:1054
  249.6 8.7 %collective-permute-start.45 = (bf16[80,384]{1,0:T(8,128)(2,1)S(1)}, bf16[80,384]{1,0:T(8,128)(2,1)S(1)}, u32[]{:S(2)}, u32[]{:S(2)}) collective-permute-start(bf16[80,384]{1,0:T(8,128)(2,1)S(1)} %get-tuple-element.257), channel_id=1, source_target_pairs={{0,8},{8,16},{16,24},{24,0},{1,9},{9,17},{17,25},{25,1},{2,10},{10... | collective-permute-start | bytes 184328 | tf_op jit(solution)/shard_map/ppermute | solution.py:1054
  251.9 6.4 %collective-permute-start.46 = (bf16[80,384]{1,0:T(8,128)(2,1)S(1)}, bf16[80,384]{1,0:T(8,128)(2,1)S(1)}, u32[]{:S(2)}, u32[]{:S(2)}) collective-permute-start(bf16[80,384]{1,0:T(8,128)(2,1)S(1)} %get-tuple-element.258), channel_id=1, source_target_pairs={{0,24},{8,0},{16,8},{24,16},{1,25},{9,1},{17,9},{25,17},{2,26},{10... | collective-permute-start | bytes 184328 | tf_op jit(solution)/shard_map/ppermute | solution.py:1054
  251.9 9.4 %collective-permute-start.41 = (bf16[128,768]{1,0:T(8,128)(2,1)S(1)}, bf16[128,768]{1,0:T(8,128)(2,1)S(1)}, u32[]{:S(2)}, u32[]{:S(2)}) collective-permute-start(bf16[128,768]{1,0:T(8,128)(2,1)S(1)} %copy-done.8), channel_id=1, source_target_pairs={{0,8},{8,16},{16,24},{24,0},{1,9},{9,17},{17,25},{25,1},{2,10},{10... | collective-permute-start | bytes 589832 | tf_op jit(solution)/shard_map/ppermute | solution.py:1039
  (31 other events, 230.2 us)
